TPU v7x, 32 devices: a whole 2x2x4 slice. The times are simulated.
32 devices in a mesh: rows: 8 (over z, y), heads: 4 (over x, core).
Axes of the slice: x: 2, y: 2, z: 4, core: 2. Of those that a mesh axis runs over, the one named last changes fastest.
Arguments:
- patches: bfloat16 [8192, 1152], P(('rows', 'heads')), may hold values from -6 to 6
- time_table: bfloat16 [1024, 1152], P('rows', 'heads'), may hold values from -6 to 6
- class_table: bfloat16 [1024, 1152], P('rows', 'heads'), may hold values from -6 to 6
- w_ada: bfloat16 [1152, 6912], P('heads', 'rows'), may hold values from -0.1875 to 0.1875
- b_ada: bfloat16 [6912], replicated, may hold values from -3 to 3
- w_qkv: bfloat16 [1152, 3456], P('rows', 'heads'), may hold values from -0.1875 to 0.1875
- b_qv: bfloat16 [16, 144], P('heads'), may hold values from -0.59765625 to 0.59765625
- w_out: bfloat16 [1152, 1152], P('rows', 'heads'), may hold values from -1 to 1
- b_out: bfloat16 [1152], replicated, may hold values from -3 to 3
- w_fc1: bfloat16 [1152, 4608], P('rows', 'heads'), may hold values from -0.1875 to 0.1875
- b_fc1: bfloat16 [4608], P('heads'), may hold values from -3 to 3
- w_fc2: bfloat16 [1152, 4608], P('rows', 'heads'), may hold values from -0.09375 to 0.09375
- b_fc2: bfloat16 [1152], replicated, may hold values from -3 to 3
- image_lengths: int32 [8, 4], P('rows'), may hold values from 0 to 1024, as said below
- segment_ids: int32 [8, 1024], P('rows'), may hold values from 0 to 3, as said below
- bucket_ids: int32 [8, 4], P('rows'), may hold values from 0 to 1023
- class_labels: int32 [8, 4], P('rows'), may hold values from 0 to 1023
- cotangent: bfloat16 [8192, 1152], P(('rows', 'heads')), may hold values from -6 to 6
Outputs:
- block_out: bfloat16 [8192, 1152], P(('rows', 'heads'))
- grad_patches: float32 [8192, 1152], P(('rows', 'heads'))
- grad_time_table: float32 [1024, 1152], P('rows', 'heads')
- grad_class_table: float32 [1024, 1152], P('rows', 'heads')
- grad_w_ada: float32 [1152, 6912], P('heads', 'rows')
- grad_b_ada: float32 [6912], P('rows')
- grad_w_qkv: float32 [1152, 3456], P('rows', 'heads')
- grad_b_qv: float32 [16, 144], P('heads')
- grad_w_out: float32 [1152, 1152], P('rows', 'heads')
- grad_b_out: float32 [1152], P('rows')
- grad_w_fc1: float32 [1152, 4608], P('rows', 'heads')
- grad_b_fc1: float32 [4608], P('heads')
- grad_w_fc2: float32 [1152, 4608], P('rows', 'heads')
- grad_b_fc2: float32 [1152], P('rows')
Inputs may be any that keep to these rules, and one draw needn't show every extreme that they name: `image_lengths`: each packed row holds either one image of 1024 patches in slot 0, its other slots of length 0, or 4 images of 256 patches; both kinds occur in every draw. `segment_ids`: the slot of each patch's image, consistent with image_lengths: patches are in slot order, slot k covering the patches after the first k slots' lengths.
All inputs are finite; a program needn't handle non-finite values.
Results may differ from a plain program's by a relative error of at most 0.019.
The roundings to bfloat16 on the way count: a program that leaves them out, or rounds other values in their place, can miss the bound.
Values may be sent and summed in bfloat16 or wider, within the bound.
A program may use at most 192 MiB of HBM per device.

v0:
```python
import math

import jax
import jax.numpy as jnp
from jax import lax
from jax.sharding import PartitionSpec as P

EPSILON = 1e-06
MASKED = -1e30
HIGH = lax.Precision.HIGHEST
TANH_COEFF = 0.7978845608028654
BLOCK_LIMIT = 512


def layer_norm(values):
    average = jnp.mean(values, axis=-1, keepdims=True)
    centred = values - average
    variance = jnp.mean(centred * centred, axis=-1, keepdims=True)
    return centred * lax.rsqrt(variance + EPSILON)


def gelu_tanh(values):
    return (
        0.5 * values * (1.0 + jnp.tanh(TANH_COEFF * (values + 0.044715 * values * values * values)))
    )


def silu_plain(values):
    return values / (1.0 + jnp.exp(-values))


def modulate(values, shift_term, scale_term):
    return layer_norm(values) * (1.0 + scale_term) + shift_term


def contract_rows(left_matrix, right_matrix):
    return lax.dot_general(
        left_matrix, right_matrix, (((0,), (0,)), ((), ())), preferred_element_type=jnp.float32
    )


def contract_rows_exact(left_matrix, right_matrix):
    return lax.dot_general(
        left_matrix,
        right_matrix,
        (((0,), (0,)), ((), ())),
        precision=HIGH,
        preferred_element_type=jnp.float32,
    )


def times_transposed(left_matrix, right_matrix):
    return lax.dot_general(
        left_matrix, right_matrix, (((1,), (1,)), ((), ())), preferred_element_type=jnp.float32
    )


def gather_weights(time_table, class_table, w_ada, w_qkv, w_out, w_fc1, w_fc2):
    return (
        lax.all_gather(time_table, "rows", axis=0, tiled=True),
        lax.all_gather(class_table, "rows", axis=0, tiled=True),
        lax.all_gather(w_ada, "rows", axis=1, tiled=True),
        lax.all_gather(w_qkv, "rows", axis=0, tiled=True),
        lax.all_gather(w_out, "rows", axis=0, tiled=True),
        lax.all_gather(w_fc1, "rows", axis=0, tiled=True),
        lax.all_gather(w_fc2, "rows", axis=0, tiled=True),
    )


def shards(
    patches,
    time_table,
    class_table,
    w_ada,
    b_ada,
    w_qkv,
    b_qv,
    w_out,
    b_out,
    w_fc1,
    b_fc1,
    w_fc2,
    b_fc2,
    image_lengths,
    segment_ids,
    bucket_ids,
    class_labels,
    cotangent,
):
    head_parts = lax.axis_size("heads")
    member = lax.axis_index("heads")
    tok_rows = patches.shape[0]
    model_width = patches.shape[1]
    seq_count = segment_ids.shape[0]
    seq_len = segment_ids.shape[1]
    slot_count = image_lengths.shape[1]
    image_count = seq_count * slot_count
    group_rows = tok_rows * head_parts
    head_local = b_qv.shape[0]
    head_size = b_qv.shape[1] // 2
    block_rows = min(BLOCK_LIMIT, seq_len)
    scale_factor = 1.0 / math.sqrt(head_size)
    full_time, full_class, ada_cols, qkv_cols, out_cols, fc1_cols, fc2_cols = gather_weights(
        time_table, class_table, w_ada, w_qkv, w_out, w_fc1, w_fc2
    )
    bucket_hot = (
        bucket_ids.reshape(image_count)[:, None]
        == jnp.arange(full_time.shape[0], dtype=jnp.int32)[None, :]
    ).astype(jnp.bfloat16)
    label_hot = (
        class_labels.reshape(image_count)[:, None]
        == jnp.arange(full_class.shape[0], dtype=jnp.int32)[None, :]
    ).astype(jnp.bfloat16)
    condition = jnp.dot(bucket_hot, full_time, preferred_element_type=jnp.float32) + jnp.dot(
        label_hot, full_class, preferred_element_type=jnp.float32
    )
    silu_value, silu_pull = jax.vjp(silu_plain, condition)
    silu_low = silu_value.astype(jnp.bfloat16)
    mods_part = jnp.dot(silu_low, ada_cols, preferred_element_type=jnp.float32)
    mods_all = lax.psum(mods_part, "heads") + b_ada.astype(jnp.float32)
    positions = member * tok_rows + jnp.arange(tok_rows, dtype=jnp.int32)
    own_segments = lax.dynamic_slice_in_dim(
        segment_ids.reshape(seq_count * seq_len), member * tok_rows, tok_rows
    )
    token_image = positions // seq_len * slot_count + own_segments
    token_hot = (token_image[:, None] == jnp.arange(image_count, dtype=jnp.int32)[None, :]).astype(
        jnp.float32
    )
    token_mods = [
        jnp.dot(
            token_hot,
            mods_all[:, part_index * model_width : (part_index + 1) * model_width],
            precision=HIGH,
        )
        for part_index in range(6)
    ]
    shift_attn, scale_attn, gate_attn, shift_mlp, scale_mlp, gate_mlp = token_mods
    inputs = patches.astype(jnp.float32)
    first_value, first_pull = jax.vjp(modulate, inputs, shift_attn, scale_attn)
    hidden_one = first_value.astype(jnp.bfloat16)
    rows_one = lax.all_gather(hidden_one, "heads", axis=0, tiled=True)
    zero_bias = jnp.zeros((head_local, head_size), b_qv.dtype)
    qkv_bias = (
        jnp.concatenate([b_qv[:, :head_size], zero_bias, b_qv[:, head_size:]], axis=1)
        .reshape(head_local * 3 * head_size)
        .astype(jnp.float32)
    )
    projected = (jnp.dot(rows_one, qkv_cols, preferred_element_type=jnp.float32) + qkv_bias).astype(
        jnp.bfloat16
    )
    seq_qkv = projected.reshape(seq_count, seq_len, head_local, 3, head_size)
    slot_ends = jnp.cumsum(image_lengths, axis=1)
    places = jnp.arange(seq_len, dtype=jnp.int32)
    image_of = jnp.sum((places[None, :, None] >= slot_ends[:, None, :]).astype(jnp.int32), axis=2)

    def block_scores(query_rows, key_rows, image_rows, image_cols):
        scores = (
            jnp.einsum("qhd,khd->hqk", query_rows, key_rows, preferred_element_type=jnp.float32)
            * scale_factor
        )
        return jnp.where((image_rows[:, None] == image_cols[None, :])[None], scores, MASKED)

    def attend_forward(pieces):
        seq_block, seq_image = pieces
        key_rows = seq_block[:, :, 1]
        value_rows = seq_block[:, :, 2]
        outputs = []
        totals = []
        for row_start in range(0, seq_len, block_rows):
            stop_row = row_start + block_rows
            query_rows = seq_block[row_start:stop_row, :, 0]
            scores = block_scores(query_rows, key_rows, seq_image[row_start:stop_row], seq_image)
            row_peak = jnp.max(scores, axis=2, keepdims=True)
            raised = jnp.exp(scores - row_peak)
            row_total = jnp.sum(raised, axis=2, keepdims=True)
            soft_low = (raised / row_total).astype(jnp.bfloat16)
            outputs.append(
                jnp.einsum(
                    "hqk,khd->qhd", soft_low, value_rows, preferred_element_type=jnp.float32
                ).astype(jnp.bfloat16)
            )
            totals.append((row_peak + jnp.log(row_total))[:, :, 0])
        return (jnp.concatenate(outputs, axis=0), jnp.concatenate(totals, axis=1))

    mixed, log_totals = lax.map(attend_forward, (seq_qkv, image_of))
    mixed_rows = mixed.reshape(group_rows, head_local * head_size)
    attn_out = lax.psum_scatter(
        times_transposed(
            lax.slice_in_dim(mixed_rows, 0, tok_rows * lax.axis_size("heads"), axis=0), out_cols
        ).astype(jnp.bfloat16),
        "heads",
        scatter_dimension=0,
        tiled=True,
    ).astype(jnp.float32) + b_out.astype(jnp.float32)
    after_attn = inputs + gate_attn * attn_out
    second_value, second_pull = jax.vjp(modulate, after_attn, shift_mlp, scale_mlp)
    hidden_two = second_value.astype(jnp.bfloat16)
    rows_two = lax.all_gather(hidden_two, "heads", axis=0, tiled=True)
    inner = jnp.dot(rows_two, fc1_cols, preferred_element_type=jnp.float32) + b_fc1.astype(
        jnp.float32
    )
    gelu_value, gelu_pull = jax.vjp(gelu_tanh, inner)
    active = gelu_value.astype(jnp.bfloat16)
    ffn_out = lax.psum_scatter(
        times_transposed(
            lax.slice_in_dim(active, 0, tok_rows * lax.axis_size("heads"), axis=0), fc2_cols
        ).astype(jnp.bfloat16),
        "heads",
        scatter_dimension=0,
        tiled=True,
    ).astype(jnp.float32) + b_fc2.astype(jnp.float32)
    block_out = (after_attn + gate_mlp * ffn_out).astype(jnp.bfloat16)
    anchored = lax.optimization_barrier(
        (time_table, class_table, w_ada, w_qkv, w_out, w_fc1, w_fc2, block_out)
    )
    regathered = gather_weights(
        anchored[0], anchored[1], anchored[2], anchored[3], anchored[4], anchored[5], anchored[6]
    )
    ada_back = regathered[2]
    qkv_back = regathered[3]
    out_back = regathered[4]
    fc1_back = regathered[5]
    fc2_back = regathered[6]
    upstream = cotangent.astype(jnp.float32)
    grad_ffn = (gate_mlp * upstream).astype(jnp.bfloat16)
    ffn_rows = lax.all_gather(grad_ffn, "heads", axis=0, tiled=True)
    grad_w_fc2 = contract_rows(ffn_rows, active)
    grad_b_fc2 = jnp.sum(ffn_rows, axis=0, dtype=jnp.float32)
    grad_active = jnp.dot(ffn_rows, fc2_back, preferred_element_type=jnp.float32)
    grad_inner = gelu_pull(grad_active)[0].astype(jnp.bfloat16)
    grad_w_fc1 = contract_rows(rows_two, grad_inner)
    grad_b_fc1 = jnp.sum(grad_inner, axis=0, dtype=jnp.float32)
    grad_hidden_two = lax.psum_scatter(
        times_transposed(
            lax.slice_in_dim(grad_inner, 0, tok_rows * lax.axis_size("heads"), axis=0), fc1_back
        ).astype(jnp.bfloat16),
        "heads",
        scatter_dimension=0,
        tiled=True,
    ).astype(jnp.float32)
    grad_after, grad_shift_mlp, grad_scale_mlp = second_pull(grad_hidden_two)
    grad_after = grad_after + upstream
    grad_gate_mlp = upstream * ffn_out
    grad_gate_attn = grad_after * attn_out
    grad_attn = (gate_attn * grad_after).astype(jnp.bfloat16)
    attn_rows_grad = lax.all_gather(grad_attn, "heads", axis=0, tiled=True)
    grad_w_out = contract_rows(attn_rows_grad, mixed_rows)
    grad_b_out = jnp.sum(attn_rows_grad, axis=0, dtype=jnp.float32)
    grad_mixed = jnp.dot(attn_rows_grad, out_back, preferred_element_type=jnp.float32).astype(
        jnp.bfloat16
    )
    grad_seq = grad_mixed.reshape(seq_count, seq_len, head_local, head_size)

    def attend_backward(pieces):
        seq_block, seq_image, seq_grad, seq_totals = pieces
        key_rows = seq_block[:, :, 1]
        value_rows = seq_block[:, :, 2]
        grad_keys = jnp.zeros(key_rows.shape, jnp.float32)
        grad_values = jnp.zeros(value_rows.shape, jnp.float32)
        grad_queries = []
        for row_start in range(0, seq_len, block_rows):
            stop_row = row_start + block_rows
            query_rows = seq_block[row_start:stop_row, :, 0]
            grad_rows = seq_grad[row_start:stop_row]
            scores = block_scores(query_rows, key_rows, seq_image[row_start:stop_row], seq_image)
            soft_probs = jnp.exp(scores - seq_totals[:, row_start:stop_row, None])
            grad_probs = jnp.einsum(
                "qhd,khd->hqk", grad_rows, value_rows, preferred_element_type=jnp.float32
            )
            inner_sum = jnp.sum(soft_probs * grad_probs, axis=2, keepdims=True)
            grad_scores = (soft_probs * (grad_probs - inner_sum)).astype(jnp.bfloat16)
            grad_queries.append(
                jnp.einsum(
                    "hqk,khd->qhd", grad_scores, key_rows, preferred_element_type=jnp.float32
                )
                * scale_factor
            )
            grad_keys = (
                grad_keys
                + jnp.einsum(
                    "hqk,qhd->khd", grad_scores, query_rows, preferred_element_type=jnp.float32
                )
                * scale_factor
            )
            grad_values = grad_values + jnp.einsum(
                "hqk,qhd->khd",
                soft_probs.astype(jnp.bfloat16),
                grad_rows,
                preferred_element_type=jnp.float32,
            )
        stacked = jnp.stack([jnp.concatenate(grad_queries, axis=0), grad_keys, grad_values], axis=2)
        return stacked.astype(jnp.bfloat16)

    grad_qkv = lax.map(attend_backward, (seq_qkv, image_of, grad_seq, log_totals)).reshape(
        group_rows, head_local * 3 * head_size
    )
    grad_w_qkv = contract_rows(rows_one, grad_qkv)
    bias_terms = jnp.sum(grad_qkv, axis=0, dtype=jnp.float32).reshape(head_local, 3, head_size)
    grad_b_qv = jnp.concatenate([bias_terms[:, 0], bias_terms[:, 2]], axis=1)
    grad_hidden_one = lax.psum_scatter(
        times_transposed(
            lax.slice_in_dim(grad_qkv, 0, tok_rows * lax.axis_size("heads"), axis=0), qkv_back
        ).astype(jnp.bfloat16),
        "heads",
        scatter_dimension=0,
        tiled=True,
    ).astype(jnp.float32)
    grad_inputs, grad_shift_attn, grad_scale_attn = first_pull(grad_hidden_one)
    grad_patches = grad_inputs + grad_after
    token_grads = (
        grad_shift_attn,
        grad_scale_attn,
        grad_gate_attn,
        grad_shift_mlp,
        grad_scale_mlp,
        grad_gate_mlp,
    )
    mods_grad_part = jnp.concatenate(
        [contract_rows_exact(token_hot, grad_term) for grad_term in token_grads], axis=1
    )
    grad_mods = lax.psum(mods_grad_part.astype(jnp.bfloat16), "heads")
    grad_w_ada = contract_rows(silu_low, grad_mods)
    grad_b_ada = jnp.sum(grad_mods, axis=0, dtype=jnp.float32)
    grad_silu = times_transposed(grad_mods, ada_back)
    grad_condition = silu_pull(grad_silu)[0]
    grad_time = contract_rows_exact(bucket_hot.astype(jnp.float32), grad_condition)
    grad_class = contract_rows_exact(label_hot.astype(jnp.float32), grad_condition)
    reduced = (
        lax.psum_scatter(grad_time, "rows", scatter_dimension=0, tiled=True),
        lax.psum_scatter(grad_class, "rows", scatter_dimension=0, tiled=True),
        lax.psum_scatter(grad_w_ada, "rows", scatter_dimension=1, tiled=True),
        lax.psum_scatter(grad_w_qkv, "rows", scatter_dimension=0, tiled=True),
        lax.psum_scatter(grad_w_out, "rows", scatter_dimension=0, tiled=True),
        lax.psum_scatter(grad_w_fc1, "rows", scatter_dimension=0, tiled=True),
        lax.psum_scatter(grad_w_fc2, "rows", scatter_dimension=0, tiled=True),
        lax.psum_scatter(grad_b_ada, "rows", scatter_dimension=0, tiled=True),
        lax.psum_scatter(grad_b_out, "rows", scatter_dimension=0, tiled=True),
        lax.psum_scatter(grad_b_fc2, "rows", scatter_dimension=0, tiled=True),
    )
    bias_pair = lax.psum((grad_b_qv, grad_b_fc1), "rows")
    return (
        block_out,
        grad_patches,
        reduced[0],
        reduced[1],
        reduced[2],
        reduced[7],
        reduced[3],
        bias_pair[0],
        reduced[4],
        reduced[8],
        reduced[5],
        bias_pair[1],
        reduced[6],
        reduced[9],
    )


def solution(mesh):
    placed = (
        P(("rows", "heads"), None),
        P("rows", "heads"),
        P("rows", "heads"),
        P("heads", "rows"),
        P(),
        P("rows", "heads"),
        P("heads", None),
        P("rows", "heads"),
        P(),
        P("rows", "heads"),
        P("heads"),
        P("rows", "heads"),
        P(),
        P("rows", None),
        P("rows", None),
        P("rows", None),
        P("rows", None),
        P(("rows", "heads"), None),
    )
    return jax.shard_map(
        shards,
        mesh=mesh,
        in_specs=placed,
        out_specs=(
            P(("rows", "heads"), None),
            P(("rows", "heads"), None),
            P("rows", "heads"),
            P("rows", "heads"),
            P("heads", "rows"),
            P("rows"),
            P("rows", "heads"),
            P("heads", None),
            P("rows", "heads"),
            P("rows"),
            P("rows", "heads"),
            P("heads"),
            P("rows", "heads"),
            P("rows"),
        ),
        check_vma=False,
    )
```

profile of v0, /device:TPU:0, one launch (start us, length us, event | category | flops | bytes accessed | tf_op | source)
XLA Modules:
  0.0 1549.1 jit_solution(7737884635386131951)
XLA Ops:
  8.0 32.3 %all_gather.48 = bf16[1024,288]{0,1:T(8,128)(2,1)S(1)} all-gather(bf16[128,288]{0,1:T(8,128)(2,1)} %param.19), channel_id=1, replica_groups=mesh['rows'=8,'heads'=4] {'rows'}, dimensions={0}, use_global_device_ids=true | all-gather | bytes 663552 | tf_op jit(solution)/shard_map/all_gather | solution.py:60
  41.2 32.8 %all_gather.49 = bf16[1024,288]{0,1:T(8,128)(2,1)S(1)} all-gather(bf16[128,288]{0,1:T(8,128)(2,1)} %param.20), channel_id=1, replica_groups=mesh['rows'=8,'heads'=4] {'rows'}, dimensions={0}, use_global_device_ids=true | all-gather | bytes 663552 | tf_op jit(solution)/shard_map/all_gather | solution.py:61
  74.2 23.8 %all-gather.35.cloned.1.call-done = bf16[8,864,288]{1,2,0:T(8,128)(2,1)} async-done(((bf16[1,864,288]{1,2,0:T(8,128)(2,1)}), bf16[8,864,288]{1,2,0:T(8,128)(2,1)}) %all-gather.35.cloned.1.call-update) | async-done | bytes 3981328 | tf_op jit(solution)/shard_map/all_gather | solution.py:62
  98.0 5.5 copy.50
  103.5 7.8 reshape.268
  111.4 3.5 fusion.92
  116.3 28.2 %all-reduce.6.cloned.1.call-done = f32[4,6912]{1,0:T(4,128)} async-done(((f32[4,6912]{1,0:T(4,128)}), f32[4,6912]{1,0:T(4,128)}) %all-reduce.6.cloned.1.call-update) | async-done | bytes 110608 | tf_op jit(solution)/shard_map/psum | solution.py:120
  150.2 34.3 %all_gather.53 = bf16[1152,288]{1,0:T(8,128)(2,1)S(1)} all-gather(bf16[144,288]{1,0:T(8,128)(2,1)S(1)} %copy-done.28), channel_id=1, replica_groups=mesh['rows'=8,'heads'=4] {'rows'}, dimensions={0}, use_global_device_ids=true | all-gather | bytes 746496 | tf_op jit(solution)/shard_map/all_gather | solution.py:64
  184.6 15.7 %all-gather.17.cloned.1.call-done = bf16[1152,864]{1,0:T(8,128)(2,1)} async-done(((bf16[144,864]{1,0:T(8,128)(2,1)}), bf16[1152,864]{1,0:T(8,128)(2,1)}) %all-gather.17.cloned.1.call-update) | async-done | bytes 1990672 | tf_op jit(solution)/shard_map/all_gather | solution.py:63
  200.3 25.6 %all-gather.15.cloned.1.call-done = bf16[1024,1152]{1,0:T(8,128)(2,1)} async-done(((bf16[256,1152]{1,0:T(8,128)(2,1)}), bf16[1024,1152]{1,0:T(8,128)(2,1)}) %all-gather.15.cloned.1.call-update) | async-done | bytes 2359312 | tf_op jit(solution)/shard_map/all_gather | solution.py:141
  225.9 4.8 add_convert_fusion
  230.7 1.9 fusion.102
  236.0 1.9 fusion.48
  243.2 1.9 fusion.47
  246.1 2.9 convolution_convert_fusion.1
  250.6 31.4 %reduce-scatter.14.cloned.1.call-done = bf16[256,1152]{1,0:T(8,128)(2,1)} async-done(((bf16[1024,1152]{1,0:T(8,128)(2,1)}), bf16[256,1152]{1,0:T(8,128)(2,1)}) %reduce-scatter.14.cloned.1.call-update) | async-done | bytes 589840 | tf_op jit(solution)/shard_map/reduce_scatter | solution.py:187
  282.0 2.9 fusion.98
  287.7 51.3 %all-gather.21.cloned.1.call-done = bf16[1152,1152]{1,0:T(8,128)(2,1)} async-done(((bf16[144,1152]{1,0:T(8,128)(2,1)}), bf16[1152,1152]{1,0:T(8,128)(2,1)}) %all-gather.21.cloned.1.call-update) | async-done | bytes 2654224 | tf_op jit(solution)/shard_map/all_gather | solution.py:65
  339.0 24.8 %all-gather.19.cloned.1.call-done = bf16[1024,1152]{1,0:T(8,128)(2,1)} async-done(((bf16[256,1152]{1,0:T(8,128)(2,1)}), bf16[1024,1152]{1,0:T(8,128)(2,1)}) %all-gather.19.cloned.1.call-update) | async-done | bytes 2359312 | tf_op jit(solution)/shard_map/all_gather | solution.py:198
  363.8 8.2 convolution_add_fusion
  372.0 49.0 %all-gather.23.cloned.1.call-done = bf16[1152,1152]{1,0:T(8,128)(2,1)} async-done(((bf16[144,1152]{1,0:T(8,128)(2,1)}), bf16[1152,1152]{1,0:T(8,128)(2,1)}) %all-gather.23.cloned.1.call-update) | async-done | bytes 2654224 | tf_op jit(solution)/shard_map/all_gather | solution.py:66
  421.0 8.7 convolution_convert_fusion.3
  431.1 30.2 %reduce-scatter.16.cloned.1.call-done = bf16[256,1152]{1,0:T(8,128)(2,1)} async-done(((bf16[1024,1152]{1,0:T(8,128)(2,1)}), bf16[256,1152]{1,0:T(8,128)(2,1)}) %reduce-scatter.16.cloned.1.call-update) | async-done | bytes 589840 | tf_op jit(solution)/shard_map/reduce_scatter | solution.py:204
  461.3 3.0 fusion.45
  466.1 22.4 %all-gather.25.cloned.1.call-done = bf16[1024,1152]{1,0:T(8,128)(2,1)} async-done(((bf16[256,1152]{1,0:T(8,128)(2,1)}), bf16[1024,1152]{1,0:T(8,128)(2,1)}) %all-gather.25.cloned.1.call-update) | async-done | bytes 2359312 | tf_op jit(solution)/shard_map/all_gather | solution.py:226
  488.5 57.2 %all-gather.27.cloned.1.call-done = bf16[1152,1152]{1,0:T(8,128)(2,1)} async-done(((bf16[144,1152]{1,0:T(8,128)(2,1)}), bf16[1152,1152]{1,0:T(8,128)(2,1)}) %all-gather.27.cloned.1.call-update) | async-done | bytes 2654224 | tf_op jit(solution)/shard_map/all_gather | solution.py:66
  545.7 10.3 convert_reduce_fusion.1
  556.0 45.3 %all-gather.29.cloned.1.call-done = bf16[1152,1152]{1,0:T(8,128)(2,1)} async-done(((bf16[144,1152]{1,0:T(8,128)(2,1)}), bf16[1152,1152]{1,0:T(8,128)(2,1)}) %all-gather.29.cloned.1.call-update) | async-done | bytes 2654224 | tf_op jit(solution)/shard_map/all_gather | solution.py:65
  601.3 7.4 convolution_convert_fusion.2
  608.8 31.5 %reduce-scatter.18.cloned.1.call-done = bf16[256,1152]{1,0:T(8,128)(2,1)} async-done(((bf16[1024,1152]{1,0:T(8,128)(2,1)}), bf16[256,1152]{1,0:T(8,128)(2,1)}) %reduce-scatter.18.cloned.1.call-update) | async-done | bytes 589840 | tf_op jit(solution)/shard_map/reduce_scatter | solution.py:233
  648.7 34.7 %all_gather.61 = bf16[1152,288]{1,0:T(8,128)(2,1)} all-gather(bf16[144,288]{1,0:T(8,128)(2,1)} %param.25), channel_id=1, replica_groups=mesh['rows'=8,'heads'=4] {'rows'}, dimensions={0}, use_global_device_ids=true | all-gather | bytes 746496 | tf_op jit(solution)/shard_map/all_gather | solution.py:64
  683.5 3.0 convolution_convert_fusion.10
  686.6 8.1 multiply_reduce_fusion.1
  695.5 4.7 multiply_convert_fusion.1
  700.8 4.3 multiply_reduce_fusion
  705.1 2.1 fusion.39
  707.2 4.4 multiply_convert_fusion
  720.8 11.6 all-gather.33.cloned.1.call-done
  732.4 6.4 convolution_convert_fusion
  739.7 30.7 %reduce-scatter.20.cloned.1.call-done = bf16[256,1152]{1,0:T(8,128)(2,1)} async-done(((bf16[1024,1152]{1,0:T(8,128)(2,1)}), bf16[256,1152]{1,0:T(8,128)(2,1)}) %reduce-scatter.20.cloned.1.call-update) | async-done | bytes 589840 | tf_op jit(solution)/shard_map/reduce_scatter | solution.py:300
  770.4 2.1 fusion.25
  772.5 2.5 fusion.24
  775.0 2.2 fusion.23
  780.7 12.0 psum.29
  792.7 5.6 convolution_bitcast_fusion
  798.3 8.7 fusion.94
  807.1 7.9 fusion.107
  816.1 4.4 fusion.106
  820.6 23.9 %all-gather.37.cloned.1.call-done = bf16[8,864,288]{1,2,0:T(8,128)(2,1)} async-done(((bf16[1,864,288]{1,2,0:T(8,128)(2,1)}), bf16[8,864,288]{1,2,0:T(8,128)(2,1)}) %all-gather.37.cloned.1.call-update) | async-done | bytes 3981328 | tf_op jit(solution)/shard_map/all_gather | solution.py:62
  844.5 5.6 copy.56
  850.1 7.9 reshape.270
  857.9 3.3 fusion.104
  864.9 6.9 fusion.105
  874.4 2.1 convert_reduce_fusion
  877.3 2.6 convert_reduce_fusion.2
  880.7 39.4 %all-reduce.3 = (f32[6912]{0:T(1024)}, f32[4,144]{1,0:T(4,128)}, f32[1152]{0:T(1024)}, f32[1152]{0:T(1024)}, f32[1152]{0:T(1024)}) all-reduce(f32[6912]{0:T(1024)} %convert_reduce_fusion.5, f32[4,144]{1,0:T(4,128)S(1)} %pad_maximum_fusion.1, f32[1152]{0:T(1024)} %convert_reduce_fusion.2, ...), channel_id=9, replica_groups=mesh['rows'=8,'heads'=4] {'rows'}, use_global_device_ids=true, to_apply=%region_26.27.clone | all-reduce | flops 10944 | bytes 87552
  928.7 99.1 %reduce-scatter.34.cloned.1.call-done = f32[864,288]{1,0:T(8,128)} async-done(((f32[6912,288]{1,0:T(8,128)}), f32[864,288]{1,0:T(8,128)}) %reduce-scatter.34.cloned.1.call-update) | async-done | bytes 995344
  1027.8 2.7 copy.58
  1030.5 105.1 %reduce-scatter.32.cloned.1.call-done = f32[144,1152]{1,0:T(8,128)} async-done(((f32[1152,1152]{1,0:T(8,128)}), f32[144,1152]{1,0:T(8,128)}) %reduce-scatter.32.cloned.1.call-update) | async-done | bytes 663568 | tf_op jit(solution)/shard_map/reduce_scatter | solution.py:335
  1135.6 108.2 %reduce-scatter.30.cloned.1.call-done = f32[144,1152]{1,0:T(8,128)} async-done(((f32[1152,1152]{1,0:T(8,128)}), f32[144,1152]{1,0:T(8,128)}) %reduce-scatter.30.cloned.1.call-update) | async-done | bytes 663568 | tf_op jit(solution)/shard_map/reduce_scatter | solution.py:334
  1243.8 70.2 %reduce-scatter.28.cloned.1.call-done = f32[144,288]{1,0:T(8,128)} async-done(((f32[1152,288]{1,0:T(8,128)}), f32[144,288]{1,0:T(8,128)}) %reduce-scatter.28.cloned.1.call-update) | async-done | bytes 165904 | tf_op jit(solution)/shard_map/reduce_scatter | solution.py:333
  1314.0 68.3 %reduce-scatter.24.cloned.1.call-done = f32[128,288]{0,1:T(8,128)} async-done(((f32[1024,288]{0,1:T(8,128)}), f32[128,288]{0,1:T(8,128)}) %reduce-scatter.24.cloned.1.call-update) | async-done | bytes 147472 | tf_op jit(solution)/shard_map/reduce_scatter | solution.py:330
  1382.3 68.5 %reduce-scatter.22.cloned.1.call-done = f32[128,288]{0,1:T(8,128)} async-done(((f32[1024,288]{0,1:T(8,128)}), f32[128,288]{0,1:T(8,128)}) %reduce-scatter.22.cloned.1.call-update) | async-done | bytes 147472 | tf_op jit(solution)/shard_map/reduce_scatter | solution.py:329
  1450.9 90.9 %reduce-scatter.26.cloned.1.call-done = f32[144,864]{1,0:T(8,128)} async-done(((f32[1152,864]{1,0:T(8,128)}), f32[144,864]{1,0:T(8,128)}) %reduce-scatter.26.cloned.1.call-update) | async-done | bytes 497680 | tf_op jit(solution)/shard_map/reduce_scatter | solution.py:332
  (235 shorter events, 65.5 us)
Async XLA Ops:
  7.2 108.5 %copy-start = (s32[1,1024]{1,0:T(1,128)S(1)}, s32[1,1024]{1,0:T(1,128)}, u32[]{:S(2)}) copy-start(s32[1,1024]{1,0:T(1,128)} %param.32) | copy-start | bytes 12292
  7.2 66.8 %copy-start.50 = (s32[1,4]{1,0:T(1,128)S(1)}, s32[1,4]{1,0:T(1,128)}, u32[]{:S(2)}) copy-start(s32[1,4]{1,0:T(1,128)} %param.34) | copy-start | bytes 52
  7.2 90.8 %all-gather.35.cloned.1.call-start = ((), (), s32[]{:S(2)}) async-start(), calls=%async_computation.32 | async-start | bytes 4644864 | tf_op jit(solution)/shard_map/all_gather | solution.py:62
  7.9 136.6 %all-reduce.6.cloned.1.call-start = ((), (), s32[]{:S(2)}) async-start(), calls=%async_computation.11 | async-start | bytes 221184 | tf_op jit(solution)/shard_map/psum | solution.py:120
  111.4 4.3 copy-start.43
  111.4 4.4 copy-start.4
  114.9 85.4 %all-gather.17.cloned.1.call-start = ((), (), s32[]{:S(2)}) async-start(), calls=%async_computation.13 | async-start | bytes 2322432 | tf_op jit(solution)/shard_map/all_gather | solution.py:63
  115.6 110.3 %all-gather.15.cloned.1.call-start = ((), (), s32[]{:S(2)}) async-start(), calls=%async_computation.12 | async-start | bytes 2949120 | tf_op jit(solution)/shard_map/all_gather | solution.py:141
  115.9 33.0 %copy-start.37 = (f32[256]{0:T(256)}, f32[256]{0:T(256)S(1)}, u32[]{:S(2)}) copy-start(f32[256]{0:T(256)S(1)} %broadcast_multiply_fusion.1) | copy-start | bytes 3076
  116.2 34.0 %copy-start.44 = (f32[256]{0:T(256)}, f32[256]{0:T(256)S(1)}, u32[]{:S(2)}) copy-start(f32[256]{0:T(256)S(1)} %fusion.43) | copy-start | bytes 3076
  116.2 32.7 %copy-start.53 = (s32[1,4]{1,0:T(1,128)S(1)}, s32[1,4]{1,0:T(1,128)}, u32[]{:S(2)}) copy-start(s32[1,4]{1,0:T(1,128)} %param.31) | copy-start | bytes 52
  116.2 33.0 %copy-start.49 = (bf16[4,144]{1,0:T(4,128)(2,1)S(1)}, bf16[4,144]{1,0:T(4,128)(2,1)}, u32[]{:S(2)}) copy-start(bf16[4,144]{1,0:T(4,128)(2,1)} %param.24) | copy-start | bytes 3460
  116.3 33.9 %copy-start.46 = (f32[256]{0:T(256)}, f32[256]{0:T(256)S(1)}, u32[]{:S(2)}) copy-start(f32[256]{0:T(256)S(1)} %fusion.89) | copy-start | bytes 3076
  145.5 139.8 %copy-start.27 = (f32[4,6912]{1,0:T(4,128)}, f32[4,6912]{1,0:T(4,128)S(1)}, u32[]{:S(2)}) copy-start(f32[4,6912]{1,0:T(4,128)S(1)} %broadcast_add_fusion) | copy-start | bytes 331780
  145.5 4.8 copy-start.28
  148.9 133.1 %reduce-scatter.14.cloned.1.call-start = ((), (), s32[]{:S(2)}) async-start(), calls=%async_computation.14 | async-start | bytes 2949120 | tf_op jit(solution)/shard_map/reduce_scatter | solution.py:187
  230.7 10.9 copy-start.11
  232.6 3.4 copy-start.33
  239.8 3.4 copy-start.3
  239.9 3.4 copy-start.35
  249.0 90.0 %all-gather.21.cloned.1.call-start = ((), (), s32[]{:S(2)}) async-start(), calls=%async_computation.16 | async-start | bytes 2985984 | tf_op jit(solution)/shard_map/all_gather | solution.py:65
  249.6 114.2 %all-gather.19.cloned.1.call-start = ((), (), s32[]{:S(2)}) async-start(), calls=%async_computation.15 | async-start | bytes 2949120 | tf_op jit(solution)/shard_map/all_gather | solution.py:198
  249.9 35.0 %copy-start.31 = (f32[1152]{0:T(1024)}, f32[1152]{0:T(1024)S(1)}, u32[]{:S(2)}) copy-start(f32[1152]{0:T(1024)S(1)} %convert_element_type.178) | copy-start | bytes 13828
  250.6 389.7 %copy-start.5 = (f32[256,1152]{1,0:T(8,128)}, f32[256,1152]{1,0:T(8,128)S(1)}, u32[]{:S(2)}) copy-start(f32[256,1152]{1,0:T(8,128)S(1)} %convolution_add_fusion.2) | copy-start | bytes 3538948
  285.2 86.8 %copy-start.45 = (f32[256]{0:T(256)}, f32[256]{0:T(256)S(1)}, u32[]{:S(2)}) copy-start(f32[256]{0:T(256)S(1)} %multiply_reduce_fusion.3) | copy-start | bytes 3076
  285.2 86.8 %copy-start.39 = (f32[256]{0:T(256)}, f32[256]{0:T(256)S(1)}, u32[]{:S(2)}) copy-start(f32[256]{0:T(256)S(1)} %fusion.90) | copy-start | bytes 3076
  286.9 134.1 %all-gather.23.cloned.1.call-start = ((), (), s32[]{:S(2)}) async-start(), calls=%async_computation.17 | async-start | bytes 2985984 | tf_op jit(solution)/shard_map/all_gather | solution.py:66
  287.7 173.6 %reduce-scatter.16.cloned.1.call-start = ((), (), s32[]{:S(2)}) async-start(), calls=%async_computation.18 | async-start | bytes 2949120 | tf_op jit(solution)/shard_map/reduce_scatter | solution.py:204
  429.7 31.6 %copy-start.8 = (bf16[256,1152]{1,0:T(8,128)(2,1)S(1)}, bf16[256,1152]{1,0:T(8,128)(2,1)}, u32[]{:S(2)}) copy-start(bf16[256,1152]{1,0:T(8,128)(2,1)} %param.35) | copy-start | bytes 1769476
  429.7 58.8 %all-gather.25.cloned.1.call-start = ((), (), s32[]{:S(2)}) async-start(), calls=%async_computation.19 | async-start | bytes 2949120 | tf_op jit(solution)/shard_map/all_gather | solution.py:226
  464.3 81.4 %all-gather.27.cloned.1.call-start = ((), (), s32[]{:S(2)}) async-start(), calls=%async_computation.20 | async-start | bytes 2985984 | tf_op jit(solution)/shard_map/all_gather | solution.py:66
  465.0 136.3 %all-gather.29.cloned.1.call-start = ((), (), s32[]{:S(2)}) async-start(), calls=%async_computation.21 | async-start | bytes 2985984 | tf_op jit(solution)/shard_map/all_gather | solution.py:65
  465.6 174.7 %reduce-scatter.18.cloned.1.call-start = ((), (), s32[]{:S(2)}) async-start(), calls=%async_computation.22 | async-start | bytes 2949120 | tf_op jit(solution)/shard_map/reduce_scatter | solution.py:233
  608.7 74.7 %all-gather.31.cloned.1.call-start = ((), (), s32[]{:S(2)}) async-start(), calls=%async_computation.23 | async-start | bytes 2949120 | tf_op jit(solution)/shard_map/all_gather | solution.py:246
  646.0 86.4 %all-gather.33.cloned.1.call-start = ((), (), s32[]{:S(2)}) async-start(), calls=%async_computation.24 | async-start | bytes 2322432 | tf_op jit(solution)/shard_map/all_gather | solution.py:63
  683.4 87.0 %reduce-scatter.20.cloned.1.call-start = ((), (), s32[]{:S(2)}) async-start(), calls=%async_computation.25 | async-start | bytes 2949120 | tf_op jit(solution)/shard_map/reduce_scatter | solution.py:300
  686.5 8.2 copy-start.16
  686.6 13.6 copy-start.18
  686.6 8.2 slice-start.2
  686.6 8.9 slice-start.3
  686.6 8.9 copy-start.29
  694.7 5.5 slice-start
  695.5 5.3 slice-start.1
  695.5 5.3 copy-start.30
  738.9 105.6 %all-gather.37.cloned.1.call-start = ((), (), s32[]{:S(2)}) async-start(), calls=%async_computation.33 | async-start | bytes 4644864 | tf_op jit(solution)/shard_map/all_gather | solution.py:62
  739.5 288.3 %reduce-scatter.34.cloned.1.call-start = ((), (), s32[]{:S(2)}) async-start(), calls=%async_computation.34 | async-start | bytes 11943936
  770.4 4.5 copy-start.21
  770.4 6.7 copy-start.10
  772.5 5.5 copy-start.40
  775.0 4.4 copy-start.20
  775.0 4.4 copy-start.32
  792.6 65.3 %copy-start.23 = (bf16[4,6912]{1,0:T(4,128)(2,1)}, bf16[4,6912]{1,0:T(4,128)(2,1)S(1)}, u32[]{:S(2)}) copy-start(bf16[4,6912]{1,0:T(4,128)(2,1)S(1)} %psum.29) | copy-start | bytes 165892
  798.3 337.3 %reduce-scatter.32.cloned.1.call-start = ((), (), s32[]{:S(2)}) async-start(), calls=%async_computation.31 | async-start | bytes 5971968 | tf_op jit(solution)/shard_map/reduce_scatter | solution.py:335
  807.1 436.7 %reduce-scatter.30.cloned.1.call-start = ((), (), s32[]{:S(2)}) async-start(), calls=%async_computation.30 | async-start | bytes 5971968 | tf_op jit(solution)/shard_map/reduce_scatter | solution.py:334
  815.1 498.9 %reduce-scatter.28.cloned.1.call-start = ((), (), s32[]{:S(2)}) async-start(), calls=%async_computation.29 | async-start | bytes 1990656 | tf_op jit(solution)/shard_map/reduce_scatter | solution.py:333
  820.5 561.8 %reduce-scatter.24.cloned.1.call-start = ((), (), s32[]{:S(2)}) async-start(), calls=%async_computation.27 | async-start | bytes 1327104 | tf_op jit(solution)/shard_map/reduce_scatter | solution.py:330
  857.9 5.1 copy-start.52
  863.0 587.9 %reduce-scatter.22.cloned.1.call-start = ((), (), s32[]{:S(2)}) async-start(), calls=%async_computation.26 | async-start | bytes 1327104 | tf_op jit(solution)/shard_map/reduce_scatter | solution.py:329
  864.9 677.0 %reduce-scatter.26.cloned.1.call-start = ((), (), s32[]{:S(2)}) async-start(), calls=%async_computation.28 | async-start | bytes 4644864 | tf_op jit(solution)/shard_map/reduce_scatter | solution.py:332
  874.4 5.6 copy-start.24
  874.4 49.7 %copy-start.7 = (f32[256,1152]{1,0:T(8,128)S(1)}, f32[256,1152]{1,0:T(8,128)}, u32[]{:S(2)}) copy-start(f32[256,1152]{1,0:T(8,128)} %copy-done.6) | copy-start | bytes 3538948
  874.4 49.7 %copy-start.38 = (f32[256]{0:T(256)S(1)}, f32[256]{0:T(256)}, u32[]{:S(2)}) copy-start(f32[256]{0:T(256)} %copy-done.37) | copy-start | bytes 3076
  920.0 6.2 copy-start.14
  927.4 614.4 %copy-start.1 = (s32[1,1024]{1,0:T(1,128)S(1)}, s32[1,1024]{1,0:T(1,128)}, u32[]{:S(2)}) copy-start(s32[1,1024]{1,0:T(1,128)} %param.32) | copy-start | bytes 12292
  (19 other events, 34.4 us)
Sparse Core Ops, SparseCore 0:
  10.2 87.7 all-gather.34
  115.0 29.4 all-reduce.5
  146.7 53.5 all-gather.16
  202.3 23.5 all-gather.14
  249.1 32.8 reduce-scatter.13
  284.0 54.9 all-gather.20
  341.1 22.6 all-gather.18
  366.0 54.9 all-gather.22
  429.9 31.3 reduce-scatter.15
  464.4 24.0 all-gather.24
  490.7 54.9 all-gather.26
  547.7 53.5 all-gather.28
  608.9 31.3 reduce-scatter.17
  646.2 24.0 all-gather.30
  683.5 48.8 all-gather.32
  739.0 31.3 reduce-scatter.19
  772.5 71.9 all-gather.36
  847.9 179.8 reduce-scatter.33
  1032.0 103.6 reduce-scatter.31
  1139.6 104.1 reduce-scatter.29
  1247.8 66.1 reduce-scatter.27
  1318.0 64.2 reduce-scatter.23
  1386.3 64.4 reduce-scatter.21
  1454.9 86.8 reduce-scatter.25
where the time goes:
time: 1560 us; the launch traced here: 1550 us
  waiting for transfers between devices  1120 us (72%)
  blocking collectives  185 us (12%)
  matrix products  147 us (9%)
  local copies, waits for them, and re-layouts  45.1 us (3%)
  other arithmetic  35.5 us (2%)
  between operations  16.9 us (1%)
    reduce_scatter x1, waiting for transfers between devices, shards(): lax.psum_scatter(grad_w_fc1, 'rows', scatter_dimension=0, tiled=True)  108 us
    all_gather x2, waiting for transfers between devices, gather_weights(): lax.all_gather(w_fc2, 'rows', axis=0, tiled=True)  106 us
    reduce_scatter x1, waiting for transfers between devices, shards(): lax.psum_scatter(grad_w_fc2, 'rows', scatter_dimension=0, tiled=True)  105 us
    unnamed x25, waiting for transfers between devices  104 us
    all_gather x2, waiting for transfers between devices, gather_weights(): lax.all_gather(w_fc1, 'rows', axis=0, tiled=True)  96.6 us
    reduce_scatter x1, waiting for transfers between devices, shards(): lax.psum_scatter(grad_w_qkv, 'rows', scatter_dimension=0, tiled=True)  90.9 us
    reduce_scatter x1, waiting for transfers between devices, shards(): lax.psum_scatter(grad_w_out, 'rows', scatter_dimension=0, tiled=True)  70.2 us
    all_gather x2, blocking collectives, gather_weights(): lax.all_gather(w_out, 'rows', axis=0, tiled=True)  69 us
  transfers between devices with their start and end apart: 24, of which 23 were waited for; matrix products, arithmetic and copies ran while one was open for 10% of the time, Pallas kernels for 0%

commit v1 on v0

--- a/solution.py
+++ b/solution.py
@@ -55,11 +55,8 @@
     )
 
 
-def gather_weights(time_table, class_table, w_ada, w_qkv, w_out, w_fc1, w_fc2):
+def gather_weights(w_qkv, w_out, w_fc1, w_fc2):
     return (
-        lax.all_gather(time_table, "rows", axis=0, tiled=True),
-        lax.all_gather(class_table, "rows", axis=0, tiled=True),
-        lax.all_gather(w_ada, "rows", axis=1, tiled=True),
         lax.all_gather(w_qkv, "rows", axis=0, tiled=True),
         lax.all_gather(w_out, "rows", axis=0, tiled=True),
         lax.all_gather(w_fc1, "rows", axis=0, tiled=True),
@@ -100,24 +97,34 @@
     head_size = b_qv.shape[1] // 2
     block_rows = min(BLOCK_LIMIT, seq_len)
     scale_factor = 1.0 / math.sqrt(head_size)
-    full_time, full_class, ada_cols, qkv_cols, out_cols, fc1_cols, fc2_cols = gather_weights(
-        time_table, class_table, w_ada, w_qkv, w_out, w_fc1, w_fc2
-    )
+    row_parts = lax.axis_size("rows")
+    table_rows = time_table.shape[0]
+    ada_width = w_ada.shape[1]
+    qkv_cols, out_cols, fc1_cols, fc2_cols = gather_weights(w_qkv, w_out, w_fc1, w_fc2)
+    ids_all = lax.all_gather(
+        jnp.concatenate([bucket_ids, class_labels], axis=1), "rows", axis=0, tiled=True
+    )
+    every_slot = row_parts * image_count
+    table_places = lax.axis_index("rows") * table_rows + jnp.arange(table_rows, dtype=jnp.int32)
     bucket_hot = (
-        bucket_ids.reshape(image_count)[:, None]
-        == jnp.arange(full_time.shape[0], dtype=jnp.int32)[None, :]
+        ids_all[:, :slot_count].reshape(every_slot)[:, None] == table_places[None, :]
     ).astype(jnp.bfloat16)
     label_hot = (
-        class_labels.reshape(image_count)[:, None]
-        == jnp.arange(full_class.shape[0], dtype=jnp.int32)[None, :]
+        ids_all[:, slot_count:].reshape(every_slot)[:, None] == table_places[None, :]
     ).astype(jnp.bfloat16)
-    condition = jnp.dot(bucket_hot, full_time, preferred_element_type=jnp.float32) + jnp.dot(
-        label_hot, full_class, preferred_element_type=jnp.float32
+    condition = lax.psum(
+        jnp.dot(bucket_hot, time_table, preferred_element_type=jnp.float32)
+        + jnp.dot(label_hot, class_table, preferred_element_type=jnp.float32),
+        "rows",
     )
     silu_value, silu_pull = jax.vjp(silu_plain, condition)
     silu_low = silu_value.astype(jnp.bfloat16)
-    mods_part = jnp.dot(silu_low, ada_cols, preferred_element_type=jnp.float32)
-    mods_all = lax.psum(mods_part, "heads") + b_ada.astype(jnp.float32)
+    mods_part = jnp.dot(silu_low, w_ada, preferred_element_type=jnp.float32)
+    mods_cols = lax.psum(mods_part, "heads").reshape(row_parts, image_count, ada_width)
+    mods_own = lax.all_to_all(mods_cols, "rows", split_axis=0, concat_axis=0, tiled=True)
+    mods_all = mods_own.transpose(1, 0, 2).reshape(
+        image_count, row_parts * ada_width
+    ) + b_ada.astype(jnp.float32)
     positions = member * tok_rows + jnp.arange(tok_rows, dtype=jnp.int32)
     own_segments = lax.dynamic_slice_in_dim(
         segment_ids.reshape(seq_count * seq_len), member * tok_rows, tok_rows
@@ -210,29 +217,18 @@
         tiled=True,
     ).astype(jnp.float32) + b_fc2.astype(jnp.float32)
     block_out = (after_attn + gate_mlp * ffn_out).astype(jnp.bfloat16)
-    anchored = lax.optimization_barrier(
-        (time_table, class_table, w_ada, w_qkv, w_out, w_fc1, w_fc2, block_out)
-    )
-    regathered = gather_weights(
-        anchored[0], anchored[1], anchored[2], anchored[3], anchored[4], anchored[5], anchored[6]
-    )
-    ada_back = regathered[2]
-    qkv_back = regathered[3]
-    out_back = regathered[4]
-    fc1_back = regathered[5]
-    fc2_back = regathered[6]
     upstream = cotangent.astype(jnp.float32)
     grad_ffn = (gate_mlp * upstream).astype(jnp.bfloat16)
     ffn_rows = lax.all_gather(grad_ffn, "heads", axis=0, tiled=True)
     grad_w_fc2 = contract_rows(ffn_rows, active)
     grad_b_fc2 = jnp.sum(ffn_rows, axis=0, dtype=jnp.float32)
-    grad_active = jnp.dot(ffn_rows, fc2_back, preferred_element_type=jnp.float32)
+    grad_active = jnp.dot(ffn_rows, fc2_cols, preferred_element_type=jnp.float32)
     grad_inner = gelu_pull(grad_active)[0].astype(jnp.bfloat16)
     grad_w_fc1 = contract_rows(rows_two, grad_inner)
     grad_b_fc1 = jnp.sum(grad_inner, axis=0, dtype=jnp.float32)
     grad_hidden_two = lax.psum_scatter(
         times_transposed(
-            lax.slice_in_dim(grad_inner, 0, tok_rows * lax.axis_size("heads"), axis=0), fc1_back
+            lax.slice_in_dim(grad_inner, 0, tok_rows * lax.axis_size("heads"), axis=0), fc1_cols
         ).astype(jnp.bfloat16),
         "heads",
         scatter_dimension=0,
@@ -246,7 +242,7 @@
     attn_rows_grad = lax.all_gather(grad_attn, "heads", axis=0, tiled=True)
     grad_w_out = contract_rows(attn_rows_grad, mixed_rows)
     grad_b_out = jnp.sum(attn_rows_grad, axis=0, dtype=jnp.float32)
-    grad_mixed = jnp.dot(attn_rows_grad, out_back, preferred_element_type=jnp.float32).astype(
+    grad_mixed = jnp.dot(attn_rows_grad, out_cols, preferred_element_type=jnp.float32).astype(
         jnp.bfloat16
     )
     grad_seq = grad_mixed.reshape(seq_count, seq_len, head_local, head_size)
@@ -299,7 +295,7 @@
     grad_b_qv = jnp.concatenate([bias_terms[:, 0], bias_terms[:, 2]], axis=1)
     grad_hidden_one = lax.psum_scatter(
         times_transposed(
-            lax.slice_in_dim(grad_qkv, 0, tok_rows * lax.axis_size("heads"), axis=0), qkv_back
+            lax.slice_in_dim(grad_qkv, 0, tok_rows * lax.axis_size("heads"), axis=0), qkv_cols
         ).astype(jnp.bfloat16),
         "heads",
         scatter_dimension=0,
@@ -319,40 +315,57 @@
         [contract_rows_exact(token_hot, grad_term) for grad_term in token_grads], axis=1
     )
     grad_mods = lax.psum(mods_grad_part.astype(jnp.bfloat16), "heads")
-    grad_w_ada = contract_rows(silu_low, grad_mods)
-    grad_b_ada = jnp.sum(grad_mods, axis=0, dtype=jnp.float32)
-    grad_silu = times_transposed(grad_mods, ada_back)
+    grad_cols = lax.all_to_all(
+        grad_mods.reshape(image_count, row_parts, ada_width).transpose(1, 0, 2),
+        "rows",
+        split_axis=0,
+        concat_axis=0,
+        tiled=True,
+    ).reshape(every_slot, ada_width)
+    grad_w_ada = contract_rows(silu_low, grad_cols)
+    grad_b_ada = jnp.sum(grad_cols, axis=0, dtype=jnp.float32)
+    grad_silu = lax.psum(times_transposed(grad_cols, w_ada), "rows")
     grad_condition = silu_pull(grad_silu)[0]
     grad_time = contract_rows_exact(bucket_hot.astype(jnp.float32), grad_condition)
     grad_class = contract_rows_exact(label_hot.astype(jnp.float32), grad_condition)
-    reduced = (
-        lax.psum_scatter(grad_time, "rows", scatter_dimension=0, tiled=True),
-        lax.psum_scatter(grad_class, "rows", scatter_dimension=0, tiled=True),
-        lax.psum_scatter(grad_w_ada, "rows", scatter_dimension=1, tiled=True),
-        lax.psum_scatter(grad_w_qkv, "rows", scatter_dimension=0, tiled=True),
-        lax.psum_scatter(grad_w_out, "rows", scatter_dimension=0, tiled=True),
-        lax.psum_scatter(grad_w_fc1, "rows", scatter_dimension=0, tiled=True),
-        lax.psum_scatter(grad_w_fc2, "rows", scatter_dimension=0, tiled=True),
-        lax.psum_scatter(grad_b_ada, "rows", scatter_dimension=0, tiled=True),
-        lax.psum_scatter(grad_b_out, "rows", scatter_dimension=0, tiled=True),
-        lax.psum_scatter(grad_b_fc2, "rows", scatter_dimension=0, tiled=True),
-    )
-    bias_pair = lax.psum((grad_b_qv, grad_b_fc1), "rows")
+
+    def row_reduced(partial):
+        return lax.psum_scatter(
+            partial.astype(jnp.bfloat16), "rows", scatter_dimension=0, tiled=True
+        ).astype(jnp.float32)
+
+    grad_w_qkv, grad_w_out, grad_w_fc1, grad_w_fc2 = (
+        row_reduced(grad_w_qkv),
+        row_reduced(grad_w_out),
+        row_reduced(grad_w_fc1),
+        row_reduced(grad_w_fc2),
+    )
+    bias_sizes = (grad_b_qv.size, grad_b_fc1.size, grad_b_out.size, grad_b_fc2.size)
+    bias_all = lax.psum(
+        jnp.concatenate([grad_b_qv.reshape(-1), grad_b_fc1, grad_b_out, grad_b_fc2]), "rows"
+    )
+    edges = [sum(bias_sizes[:step]) for step in range(5)]
+    bias_rows = model_width // row_parts
+    row_start = lax.axis_index("rows") * bias_rows
+    grad_b_qv = bias_all[edges[0] : edges[1]].reshape(grad_b_qv.shape)
+    grad_b_fc1 = bias_all[edges[1] : edges[2]]
+    grad_b_out = lax.dynamic_slice_in_dim(bias_all[edges[2] : edges[3]], row_start, bias_rows)
+    grad_b_fc2 = lax.dynamic_slice_in_dim(bias_all[edges[3] : edges[4]], row_start, bias_rows)
     return (
         block_out,
         grad_patches,
-        reduced[0],
-        reduced[1],
-        reduced[2],
-        reduced[7],
-        reduced[3],
-        bias_pair[0],
-        reduced[4],
-        reduced[8],
-        reduced[5],
-        bias_pair[1],
-        reduced[6],
-        reduced[9],
+        grad_time,
+        grad_class,
+        grad_w_ada,
+        grad_b_ada,
+        grad_w_qkv,
+        grad_b_qv,
+        grad_w_out,
+        grad_b_out,
+        grad_w_fc1,
+        grad_b_fc1,
+        grad_w_fc2,
+        grad_b_fc2,
     )
 
 

time: 1560 us -> 832 us (0.53)
  waiting for transfers between devices: 1120 us -> 480 us
  blocking collectives: 185 us -> 134 us
  local copies, waits for them, and re-layouts: 45.1 us -> 14.5 us
  matrix products: 147 us -> 127 us
    reduce_scatter x6 -> x4, waiting for transfers between devices: 511 us -> 200 us  [row_reduced(): lax.psum_scatter(partial.astype(jnp.bfloat16), 'rows', scatter_dimension=...]
    unnamed x25 -> x16, waiting for transfers between devices: 104 us -> 1.94 us
    all_gather x2 -> x1, waiting for transfers between devices: 96.6 us -> 15 us  [gather_weights(): lax.all_gather(w_fc1, 'rows', axis=0, tiled=True)]
    psum x0 -> x2, blocking collectives: none -> 67.5 us  [the longest x1 34.1 us: shards(): grad_silu = lax.psum(times_transposed(grad_cols, w_ada), 'rows')]
    all_gather x2 -> x1, waiting for transfers between devices: 106 us -> 57.1 us  [gather_weights(): lax.all_gather(w_fc2, 'rows', axis=0, tiled=True)]
    all_gather x2 -> x0, waiting for transfers between devices: 47.7 us -> none  [gather_weights(): lax.all_gather(w_ada, 'rows', axis=1, tiled=True)]
    all_gather x2 -> x1, blocking collectives: 65 us -> 22.3 us  [shards(): lax.all_gather(jnp.concatenate([bucket_ids, class_labels], axis=1), 'rows...]
    unnamed x1 -> x0, blocking collectives: 39.4 us -> none
  transfers between devices with their start and end apart: 24 -> 18, of which waited for: 23 -> 15; matrix products, arithmetic and copies ran while one was open for 10% -> 14% of each run, Pallas kernels for 0% -> 0%
where the time goes in v1:
time: 832 us; the launch traced here: 827 us
  waiting for transfers between devices  480 us (58%)
  blocking collectives  134 us (16%)
  matrix products  127 us (15%)
  other arithmetic  42 us (5%)
  between operations  16.6 us (2%)
  local copies, waits for them, and re-layouts  14.5 us (2%)
  starting transfers between devices  13 us (2%)
    reduce_scatter x4, waiting for transfers between devices, row_reduced(): lax.psum_scatter(partial.astype(jnp.bfloat16), 'rows', scatter_dimension=...  200 us
    all_gather x1, waiting for transfers between devices, gather_weights(): lax.all_gather(w_fc2, 'rows', axis=0, tiled=True)  57.1 us
    psum x1, blocking collectives, shards(): grad_silu = lax.psum(times_transposed(grad_cols, w_ada), 'rows')  34.1 us
    psum x1, blocking collectives, shards(): lax.psum(jnp.dot(bucket_hot, time_table, preferred_element_type=jnp.float...  33.4 us
    reduce_scatter x1, waiting for transfers between devices, shards(): lax.psum_scatter(times_transposed(lax.slice_in_dim(active, 0, tok_rows *...  33.2 us
    all_gather x1, blocking collectives, gather_weights(): lax.all_gather(w_out, 'rows', axis=0, tiled=True)  33 us
    reduce_scatter x1, waiting for transfers between devices, shards(): lax.psum_scatter(times_transposed(lax.slice_in_dim(grad_qkv, 0, tok_rows...  31.9 us
    reduce_scatter x1, waiting for transfers between devices, shards(): lax.psum_scatter(times_transposed(lax.slice_in_dim(mixed_rows, 0, tok_row...  29.6 us
  transfers between devices with their start and end apart: 18, of which 15 were waited for; matrix products, arithmetic and copies ran while one was open for 14% of the time, Pallas kernels for 0%

profile of v1, /device:TPU:0, one launch (start us, length us, event | category | flops | bytes accessed | tf_op | source)
XLA Modules:
  0.0 827.3 jit_solution(14502792928962573080)
XLA Ops:
  8.9 22.3 %all-gather = s32[8,1,8]{2,1,0:T(1,128)S(1)} all-gather(s32[1,1,8]{2,1,0:T(1,128)S(1)} %add_bitcast_fusion), channel_id=1, replica_groups=mesh['rows'=8,'heads'=4] {'rows'}, dimensions={0}, use_global_device_ids=true | all-gather | bytes 288 | tf_op jit(solution)/shard_map/all_gather | solution.py:104
  34.2 33.4 %psum.35 = f32[32,288]{1,0:T(8,128)S(1)} all-reduce(f32[32,288]{1,0:T(8,128)S(1)} %convolution_add_fusion.6), channel_id=1, replica_groups=mesh['rows'=8,'heads'=4] {'rows'}, use_global_device_ids=true, to_apply=%region_0.0 | all-reduce | flops 9216 | bytes 73728 | tf_op jit(solution)/shard_map/psum | solution.py:115
  72.1 25.7 %all-reduce.3.cloned.1.call-done = f32[8,4,864]{2,1,0:T(4,128)} async-done(((f32[8,4,864]{2,1,0:T(4,128)}), f32[8,4,864]{2,1,0:T(4,128)}) %all-reduce.3.cloned.1.call-update) | async-done | bytes 110608 | tf_op jit(solution)/shard_map/psum | solution.py:123
  97.8 5.5 all-to-all-start
  103.4 9.3 %all-to-all-done = f32[8,4,864]{2,1,0:T(4,128)S(1)} async-done(((f32[8,4,864]{2,1,0:T(4,128)}), f32[8,4,864]{2,1,0:T(4,128)S(1)}, u32[]{:S(2)}, u32[]{:S(2)}) %all-to-all-start) | async-done | bytes 110624 | tf_op jit(solution)/shard_map/all_to_all | solution.py:124
  113.6 1.7 fusion.18
  115.9 1.6 broadcast_compare_fusion.1
  117.5 33.0 %all_gather.30 = bf16[1152,288]{1,0:T(8,128)(2,1)S(1)} all-gather(bf16[144,288]{1,0:T(8,128)(2,1)S(1)} %copy-done.31), channel_id=1, replica_groups=mesh['rows'=8,'heads'=4] {'rows'}, dimensions={0}, use_global_device_ids=true | all-gather | bytes 746496 | tf_op jit(solution)/shard_map/all_gather | solution.py:61
  150.6 5.1 add_convert_fusion
  155.7 1.9 fusion.111
  157.6 1.9 fusion.1
  160.9 2.1 fusion.48
  163.1 1.9 fusion.112
  165.0 1.9 fusion
  166.9 1.5 copy-done.1
  168.4 2.1 fusion.47
  170.6 3.0 convolution_convert_fusion.3
  175.9 29.6 %reduce-scatter.9.cloned.1.call-done = bf16[256,1152]{1,0:T(8,128)(2,1)} async-done(((bf16[1024,1152]{1,0:T(8,128)(2,1)}), bf16[256,1152]{1,0:T(8,128)(2,1)}) %reduce-scatter.9.cloned.1.call-update) | async-done | bytes 589840 | tf_op jit(solution)/shard_map/reduce_scatter | solution.py:194
  205.5 3.0 fusion.105
  208.8 2.4 fusion.19
  211.3 3.0 fusion.45
  215.1 15.0 %all-gather.15.cloned.1.call-done = bf16[1152,1152]{1,0:T(8,128)(2,1)} async-done(((bf16[144,1152]{1,0:T(8,128)(2,1)}), bf16[1152,1152]{1,0:T(8,128)(2,1)}) %all-gather.15.cloned.1.call-update) | async-done | bytes 2654224 | tf_op jit(solution)/shard_map/all_gather | solution.py:62
  230.1 24.7 %all-gather.13.cloned.1.call-done = bf16[1024,1152]{1,0:T(8,128)(2,1)} async-done(((bf16[256,1152]{1,0:T(8,128)(2,1)}), bf16[1024,1152]{1,0:T(8,128)(2,1)}) %all-gather.13.cloned.1.call-update) | async-done | bytes 2359312 | tf_op jit(solution)/shard_map/all_gather | solution.py:205
  254.8 8.1 convolution_add_fusion
  262.9 18.0 %all-gather.19.cloned.1.call-done = bf16[1024,1152]{1,0:T(8,128)(2,1)} async-done(((bf16[256,1152]{1,0:T(8,128)(2,1)}), bf16[1024,1152]{1,0:T(8,128)(2,1)}) %all-gather.19.cloned.1.call-update) | async-done | bytes 2359312 | tf_op jit(solution)/shard_map/all_gather | solution.py:222
  280.9 57.1 %all-gather.17.cloned.1.call-done = bf16[1152,1152]{1,0:T(8,128)(2,1)} async-done(((bf16[144,1152]{1,0:T(8,128)(2,1)}), bf16[1152,1152]{1,0:T(8,128)(2,1)}) %all-gather.17.cloned.1.call-update) | async-done | bytes 2654224 | tf_op jit(solution)/shard_map/all_gather | solution.py:63
  338.0 9.2 %convert_reduce_fusion.2 = (f32[1152]{0:T(1024)S(1)}, bf16[1024,1152]{1,0:T(8,128)(2,1)S(1)}) fusion(f32[1024,1152]{1,0:T(8,128)} %convolution_add_fusion, bf16[1024,1152]{1,0:T(8,128)(2,1)} %all-gather.19.cloned.1.call-done, bf16[1152,1152]{1,0:T(8,128)(2,1)} %all-gather.17.cloned.1.call-done), kind=kOutput, calls=%fused_computation.30 | convolution fusion | flops 2748578816 | bytes 12096000 | tf_op jit(solution)/shard_map/dot_general | solution.py:225
  348.7 4.8 convolution_convert_fusion.4
  353.7 8.8 %convolution_convert_fusion.5 = bf16[1024,1152]{1,0:T(8,128)(2,1)} fusion(bf16[1152,1152]{1,0:T(8,128)(2,1)} %all-gather.17.cloned.1.call-done, f32[1024,1152]{1,0:T(8,128)} %convolution_add_fusion), kind=kOutput, calls=%fused_computation.42 | convolution fusion | flops 2729705472 | bytes 9732096 | tf_op jit(solution)/shard_map/dot_general | solution.py:53
  363.3 21.8 %reduce-scatter.13.cloned.1.call-done = bf16[256,1152]{1,0:T(8,128)(2,1)} async-done(((bf16[1024,1152]{1,0:T(8,128)(2,1)}), bf16[256,1152]{1,0:T(8,128)(2,1)}) %reduce-scatter.13.cloned.1.call-update) | async-done | bytes 589840 | tf_op jit(solution)/shard_map/reduce_scatter | solution.py:229
  387.0 33.2 %reduce-scatter.11.cloned.1.call-done = bf16[256,1152]{1,0:T(8,128)(2,1)} async-done(((bf16[1024,1152]{1,0:T(8,128)(2,1)}), bf16[256,1152]{1,0:T(8,128)(2,1)}) %reduce-scatter.11.cloned.1.call-update) | async-done | bytes 589840 | tf_op jit(solution)/shard_map/reduce_scatter | solution.py:211
  420.3 3.5 fusion.104
  424.9 7.1 convolution_convert_fusion.1
  432.2 8.3 %convolution_convert_fusion = bf16[1152,1152]{1,0:T(8,128)(2,1)} fusion(bf16[1024,1152]{1,0:T(8,128)(2,1)} %all-gather.19.cloned.1.call-done, f32[1024,1152]{1,0:T(8,128)} %convolution_add_fusion), kind=kOutput, calls=%fused_computation.12 | convolution fusion | flops 2729852928 | bytes 9732096 | tf_op jit(solution)/shard_map/dot_general | solution.py:37
  441.0 8.1 all-gather.21.cloned.1.call-done
  449.1 3.0 convolution_convert_fusion.14
  453.0 2.3 convolution_convert_fusion.7
  455.4 9.0 %multiply_reduce_fusion.1 = (f32[4,512]{1,0:T(4,128)S(1)}, f32[4,512,1024]{2,1,0:T(8,128)}) fusion(f32[4,512,1024]{2,1,0:T(8,128)} %copy-done.1, f32[4,512]{1,0:T(4,128)S(1)} %log_add_fusion.1, bf16[512,4,72]{0,2,1:T(8,128)(2,1)} %bitcast.131, bf16[1024,4,3,72]{0,3,2,1:T(8,128)(2,1)} %bitcast.125), kind=kOutput, calls=%fused_computation.4 | convolution fusion | flops 308279296 | bytes 17678336 | tf_op jit(solution)/shard_map/while/body/eval_jaxpr/qhd,khd->hqk/dot_general | solution.py:263
  464.4 4.7 multiply_convert_fusion.1
  469.0 2.2 fusion.39
  471.2 2.6 multiply_reduce_fusion
  473.8 1.8 multiply_convert_fusion
  475.6 2.1 fusion.40
  478.6 1.7 fusion.31
  480.3 2.5 fusion.10
  484.2 5.3 fusion.36
  492.2 4.0 convolution_convert_fusion.6
  496.2 6.5 convolution_convert_fusion.2
  502.7 2.1 convert_reduce_fusion
  504.8 1.9 convert_element_type.236
  506.7 70.9 %reduce-scatter.23.cloned.1.call-done = bf16[144,1152]{1,0:T(8,128)(2,1)} async-done(((bf16[1152,1152]{1,0:T(8,128)(2,1)}), bf16[144,1152]{1,0:T(8,128)(2,1)}) %reduce-scatter.23.cloned.1.call-update) | async-done | bytes 331792 | tf_op jit(solution)/shard_map/reduce_scatter | solution.py:333
  577.6 1.9 convert_element_type.238
  579.6 2.1 convert_reduce_fusion.1
  582.3 60.1 %reduce-scatter.19.cloned.1.call-done = bf16[144,288]{1,0:T(8,128)(2,1)} async-done(((bf16[1152,288]{1,0:T(8,128)(2,1)}), bf16[144,288]{1,0:T(8,128)(2,1)}) %reduce-scatter.19.cloned.1.call-update) | async-done | bytes 82960 | tf_op jit(solution)/shard_map/reduce_scatter | solution.py:333
  642.5 1.6 convert_element_type.234
  644.1 68.6 %reduce-scatter.17.cloned.1.call-done = bf16[144,864]{1,0:T(8,128)(2,1)} async-done(((bf16[1152,864]{1,0:T(8,128)(2,1)}), bf16[144,864]{1,0:T(8,128)(2,1)}) %reduce-scatter.17.cloned.1.call-update) | async-done | bytes 248848 | tf_op jit(solution)/shard_map/reduce_scatter | solution.py:333
  712.7 1.8 convert_element_type.228
  714.5 31.9 %reduce-scatter.15.cloned.1.call-done = bf16[256,1152]{1,0:T(8,128)(2,1)} async-done(((bf16[1024,1152]{1,0:T(8,128)(2,1)}), bf16[256,1152]{1,0:T(8,128)(2,1)}) %reduce-scatter.15.cloned.1.call-update) | async-done | bytes 589840 | tf_op jit(solution)/shard_map/reduce_scatter | solution.py:296
  746.3 1.9 fusion.44
  754.9 11.3 %psum.37 = bf16[8,4,864]{2,1,0:T(4,128)(2,1)} all-reduce(bf16[8,4,864]{2,1,0:T(4,128)(2,1)S(1)} %bitcast.140), channel_id=1, replica_groups=mesh['rows'=8,'heads'=4] {'heads'}, use_global_device_ids=true, to_apply=%region_22.23 | all-reduce | flops 27648 | bytes 110592 | tf_op jit(solution)/shard_map/psum | solution.py:317
  766.2 5.8 all-to-all-start.1
  772.0 2.6 add_add_fusion.2
  774.6 4.2 all-to-all-done.1
  779.1 34.1 %all-reduce = (f32[32,288]{1,0:T(8,128)S(1)}, f32[4032]{0:T(1024)S(1)}) all-reduce(f32[32,288]{1,0:T(8,128)S(1)} %fusion.113, f32[4032]{0:T(1024)S(1)} %copy-done.32), channel_id=1, replica_groups=mesh['rows'=8,'heads'=4] {'rows'}, use_global_device_ids=true, to_apply=%region_23.24 | all-reduce | flops 13248 | bytes 105984 | tf_op jit(solution)/shard_map/psum | solution.py:327
  (221 shorter events, 40.9 us)
Async XLA Ops:
  8.0 59.6 %copy-start = (bf16[288,864]{1,0:T(8,128)(2,1)S(1)}, bf16[288,864]{1,0:T(8,128)(2,1)}, u32[]{:S(2)}) copy-start(bf16[288,864]{1,0:T(8,128)(2,1)} %param.21) | copy-start | bytes 1492996
  8.0 63.7 %copy-start.3 = (bf16[256,1152]{1,0:T(8,128)(2,1)S(1)}, bf16[256,1152]{1,0:T(8,128)(2,1)}, u32[]{:S(2)}) copy-start(bf16[256,1152]{1,0:T(8,128)(2,1)} %param.18) | copy-start | bytes 1769476
  8.0 89.7 %all-reduce.3.cloned.1.call-start = ((), (), s32[]{:S(2)}) async-start(), calls=%async_computation.10 | async-start | bytes 229376 | tf_op jit(solution)/shard_map/psum | solution.py:123
  8.1 26.1 %copy-start.41 = (s32[128]{0:T(128)}, s32[128]{0:T(128)S(1)}, u32[]{:S(2)}) copy-start(s32[128]{0:T(128)S(1)} %iota_add_fusion) | copy-start | bytes 1540
  31.4 2.8 copy-start.43
  67.6 45.1 %copy-start.28 = (f32[32,288]{1,0:T(8,128)}, f32[32,288]{1,0:T(8,128)S(1)}, u32[]{:S(2)}) copy-start(f32[32,288]{1,0:T(8,128)S(1)} %psum.35) | copy-start | bytes 110596
  68.5 82.0 %all-gather.11.cloned.1.call-start = ((), (), s32[]{:S(2)}) async-start(), calls=%async_computation.12 | async-start | bytes 2322432 | tf_op jit(solution)/shard_map/all_gather | solution.py:60
  97.8 14.9 %all-to-all-start = ((f32[8,4,864]{2,1,0:T(4,128)}), f32[8,4,864]{2,1,0:T(4,128)S(1)}, u32[]{:S(2)}, u32[]{:S(2)}) async-start(f32[8,4,864]{2,1,0:T(4,128)} %all-reduce.3.cloned.1.call-done), calls=%async_computation | async-start | bytes 229376 | tf_op jit(solution)/shard_map/all_to_all | solution.py:124
  103.3 47.3 %all-gather.9.cloned.1.call-start = ((), (), s32[]{:S(2)}) async-start(), calls=%async_computation.11 | async-start | bytes 2949120 | tf_op jit(solution)/shard_map/all_gather | solution.py:148
  103.4 644.9 %copy-start.36 = (f32[256]{0:T(256)}, f32[256]{0:T(256)S(1)}, u32[]{:S(2)}) copy-start(f32[256]{0:T(256)S(1)} %fusion.96) | copy-start | bytes 3076
  112.7 2.6 copy-start.50
  112.7 2.9 copy-start.47
  112.9 4.7 copy-start.31
  113.6 36.9 %copy-start.4 = (f32[256,1152]{1,0:T(8,128)}, f32[256,1152]{1,0:T(8,128)S(1)}, u32[]{:S(2)}) copy-start(f32[256,1152]{1,0:T(8,128)S(1)} %convolution_add_fusion.4) | copy-start | bytes 3538948
  115.3 90.3 %reduce-scatter.9.cloned.1.call-start = ((), (), s32[]{:S(2)}) async-start(), calls=%async_computation.13 | async-start | bytes 2949120 | tf_op jit(solution)/shard_map/reduce_scatter | solution.py:194
  150.5 20.1 %copy-start.23 = (bf16[1152,288]{1,0:T(8,128)(2,1)}, bf16[1152,288]{1,0:T(8,128)(2,1)S(1)}, u32[]{:S(2)}) copy-start(bf16[1152,288]{1,0:T(8,128)(2,1)S(1)} %all_gather.30) | copy-start | bytes 1990660
  150.5 5.2 copy-start.27
  155.7 11.2 %copy-start.11 = (bf16[1024,864]{0,1:T(8,128)(2,1)}, bf16[1024,864]{0,1:T(8,128)(2,1)S(1)}, u32[]{:S(2)}) copy-start(bf16[1024,864]{0,1:T(8,128)(2,1)S(1)} %add_convert_fusion) | copy-start | bytes 5308420
  157.6 3.3 copy-start.2
  160.9 2.2 copy-start.26
  165.0 3.3 copy-start.1
  170.6 3.1 copy-start.24
  173.7 56.4 %all-gather.15.cloned.1.call-start = ((), (), s32[]{:S(2)}) async-start(), calls=%async_computation.15 | async-start | bytes 2985984 | tf_op jit(solution)/shard_map/all_gather | solution.py:62
  174.3 80.5 %all-gather.13.cloned.1.call-start = ((), (), s32[]{:S(2)}) async-start(), calls=%async_computation.14 | async-start | bytes 2949120 | tf_op jit(solution)/shard_map/all_gather | solution.py:205
  175.9 209.1 %copy-start.6 = (f32[256,1152]{1,0:T(8,128)}, f32[256,1152]{1,0:T(8,128)S(1)}, u32[]{:S(2)}) copy-start(f32[256,1152]{1,0:T(8,128)S(1)} %convolution_add_fusion.2) | copy-start | bytes 3538948
  211.2 3.9 copy-start.39
  211.3 69.6 %all-gather.19.cloned.1.call-start = ((), (), s32[]{:S(2)}) async-start(), calls=%async_computation.18 | async-start | bytes 2949120 | tf_op jit(solution)/shard_map/all_gather | solution.py:222
  214.3 123.7 %all-gather.17.cloned.1.call-start = ((), (), s32[]{:S(2)}) async-start(), calls=%async_computation.16 | async-start | bytes 2985984 | tf_op jit(solution)/shard_map/all_gather | solution.py:63
  215.1 170.0 %reduce-scatter.13.cloned.1.call-start = ((), (), s32[]{:S(2)}) async-start(), calls=%async_computation.19 | async-start | bytes 2949120 | tf_op jit(solution)/shard_map/reduce_scatter | solution.py:229
  338.0 10.7 %copy-start.48 = (bf16[1152,1152]{1,0:T(8,128)(2,1)S(1)}, bf16[1152,1152]{1,0:T(8,128)(2,1)}, u32[]{:S(2)}) copy-start(bf16[1152,1152]{1,0:T(8,128)(2,1)} %all-gather.15.cloned.1.call-done) | copy-start | bytes 7962628
  353.5 66.8 %reduce-scatter.11.cloned.1.call-start = ((), (), s32[]{:S(2)}) async-start(), calls=%async_computation.17 | async-start | bytes 2949120 | tf_op jit(solution)/shard_map/reduce_scatter | solution.py:211
  362.6 86.5 %all-gather.21.cloned.1.call-start = ((), (), s32[]{:S(2)}) async-start(), calls=%async_computation.20 | async-start | bytes 2949120 | tf_op jit(solution)/shard_map/all_gather | solution.py:242
  420.2 3.5 copy-start.7
  420.3 3.5 copy-start.15
  423.8 8.3 %copy-start.33 = (f32[256]{0:T(256)}, f32[256]{0:T(256)S(1)}, u32[]{:S(2)}) copy-start(f32[256]{0:T(256)S(1)} %negate_multiply_fusion.1) | copy-start | bytes 3076
  424.9 79.9 %reduce-scatter.21.cloned.1.call-start = ((), (), s32[]{:S(2)}) async-start(), calls=%async_computation.24 | async-start | bytes 2985984 | tf_op jit(solution)/shard_map/reduce_scatter | solution.py:333
  432.1 145.5 %reduce-scatter.23.cloned.1.call-start = ((), (), s32[]{:S(2)}) async-start(), calls=%async_computation.25 | async-start | bytes 2985984 | tf_op jit(solution)/shard_map/reduce_scatter | solution.py:333
  440.5 202.0 %reduce-scatter.19.cloned.1.call-start = ((), (), s32[]{:S(2)}) async-start(), calls=%async_computation.23 | async-start | bytes 995328 | tf_op jit(solution)/shard_map/reduce_scatter | solution.py:333
  449.1 3.9 copy-start.18
  449.1 3.9 copy-start.25
  455.3 9.0 %slice-start = ((s8[8388608]{0:T(1024)(128)(4,1)}), s8[4194304]{0:T(1024)(128)(4,1)S(1)}, s32[]{:S(2)}) async-start(s8[8388608]{0:T(1024)(128)(4,1)} %bitcast.117), calls=%async_computation.26 | async-start | bytes 8388608
  455.3 9.0 %slice-start.1 = ((s8[8388608]{0:T(1024)(128)(4,1)}), s8[4194304]{0:T(1024)(128)(4,1)S(1)}, s32[]{:S(2)}) async-start(s8[8388608]{0:T(1024)(128)(4,1)} %bitcast.117), calls=%async_computation.27 | async-start | bytes 8388608
  464.3 6.9 slice-start.2
  464.3 4.7 copy-start.12
  464.4 6.9 slice-start.3
  469.0 2.2 copy-start.16
  475.6 2.2 copy-start.13
  482.9 229.8 %reduce-scatter.17.cloned.1.call-start = ((), (), s32[]{:S(2)}) async-start(), calls=%async_computation.22 | async-start | bytes 2322432 | tf_op jit(solution)/shard_map/reduce_scatter | solution.py:333
  484.2 5.3 copy-start.20
  489.9 2.3 copy-start.49
  496.2 250.1 %reduce-scatter.15.cloned.1.call-start = ((), (), s32[]{:S(2)}) async-start(), calls=%async_computation.21 | async-start | bytes 2949120 | tf_op jit(solution)/shard_map/reduce_scatter | solution.py:296
  748.3 3.8 copy-start.8
  748.3 3.8 copy-start.19
  748.3 3.8 copy-start.34
  749.8 3.2 copy-start.10
  752.9 19.0 %copy-start.9 = (bf16[256,1152]{1,0:T(8,128)(2,1)S(1)}, bf16[256,1152]{1,0:T(8,128)(2,1)}, u32[]{:S(2)}) copy-start(bf16[256,1152]{1,0:T(8,128)(2,1)} %param.35) | copy-start | bytes 1769476
  752.9 19.0 %copy-start.35 = (f32[256]{0:T(256)S(1)}, f32[256]{0:T(256)}, u32[]{:S(2)}) copy-start(f32[256]{0:T(256)} %copy-done.33) | copy-start | bytes 3076
  753.0 19.0 %copy-start.37 = (f32[256]{0:T(256)S(1)}, f32[256]{0:T(256)}, u32[]{:S(2)}) copy-start(f32[256]{0:T(256)} %negate_multiply_fusion) | copy-start | bytes 3076
  766.2 12.6 %all-to-all-start.1 = ((bf16[8,4,864]{2,1,0:T(4,128)(2,1)}), bf16[8,4,864]{2,1,0:T(4,128)(2,1)S(1)}, u32[]{:S(2)}, u32[]{:S(2)}) async-start(bf16[8,4,864]{2,1,0:T(4,128)(2,1)} %psum.37), calls=%async_computation.5 | async-start | bytes 114688 | tf_op jit(solution)/shard_map/all_to_all | solution.py:318
  772.0 7.1 copy-start.32
  772.0 41.9 %copy-start.29 = (f32[32,288]{1,0:T(8,128)S(1)}, f32[32,288]{1,0:T(8,128)}, u32[]{:S(2)}) copy-start(f32[32,288]{1,0:T(8,128)} %copy-done.28) | copy-start | bytes 110596
  772.0 41.9 %copy-start.42 = (s32[128]{0:T(128)S(1)}, s32[128]{0:T(128)}, u32[]{:S(2)}) copy-start(s32[128]{0:T(128)} %copy-done.41) | copy-start | bytes 1540
  772.0 41.9 %copy-start.44 = (s32[32]{0:T(128)S(1)}, s32[32]{0:T(128)}, u32[]{:S(2)}) copy-start(s32[32]{0:T(128)} %copy-done.43) | copy-start | bytes 388
  772.0 42.9 %copy-start.46 = (s32[32]{0:T(128)S(1)}, s32[32]{0:T(128)}, u32[]{:S(2)}) copy-start(s32[32]{0:T(128)} %copy-done.45) | copy-start | bytes 388
  (10 other events, 13.0 us)
Sparse Core Ops, SparseCore 0:
  68.7 29.0 all-reduce.2
  173.8 31.6 reduce-scatter.8
  353.6 31.3 reduce-scatter.12
  387.4 32.8 reduce-scatter.10
  425.0 24.0 all-gather.20
Sparse Core Ops, SparseCore 1:
  71.2 48.7 all-gather.10
  121.9 22.5 all-gather.8
  176.3 53.7 all-gather.14
  232.3 22.5 all-gather.12
  257.0 23.9 all-gather.18
  283.1 54.8 all-gather.16
  432.2 72.1 reduce-scatter.20
  507.9 69.6 reduce-scatter.22
  581.4 61.0 reduce-scatter.18
  646.0 66.6 reduce-scatter.16
  715.1 31.2 reduce-scatter.14

commit v2 on v1

--- a/solution.py
+++ b/solution.py
@@ -1,8 +1,11 @@
+import functools
 import math
 
 import jax
 import jax.numpy as jnp
 from jax import lax
+from jax.experimental import pallas as pl
+from jax.experimental.pallas import tpu as pltpu
 from jax.sharding import PartitionSpec as P
 
 EPSILON = 1e-06
@@ -64,7 +67,7 @@
     )
 
 
-def shards(
+def shards_plain(
     patches,
     time_table,
     class_table,
@@ -369,6 +372,625 @@
     )
 
 
+MESH = pl.DeviceIdType.MESH
+ROW_PARTS = 8
+HEAD_PARTS = 4
+SLOT_ROWS = 8
+VMEM_SPEC = pl.BlockSpec(memory_space=pltpu.VMEM)
+ANY_SPEC = pl.BlockSpec(memory_space=pl.ANY)
+DMA = pltpu.SemaphoreType.DMA
+GRANT = 60 * 1024 * 1024
+
+
+def places():
+    row = lax.axis_index("rows")
+    member = lax.axis_index("heads")
+    sibling = member + 1 - 2 * lax.rem(member, 2)
+    partner = lax.rem(member + 2, HEAD_PARTS)
+    opposite = lax.rem(sibling + 2, HEAD_PARTS)
+    return row, member, sibling, partner, opposite
+
+
+def greet(row_steps, head_members):
+    barrier = pltpu.get_barrier_semaphore()
+    row = lax.axis_index("rows")
+    for step in row_steps:
+        pl.semaphore_signal(
+            barrier,
+            inc=1,
+            device_id={"rows": lax.rem(row + step, ROW_PARTS)},
+            device_id_type=MESH,
+        )
+    for other in head_members:
+        pl.semaphore_signal(barrier, inc=1, device_id={"heads": other}, device_id_type=MESH)
+    pl.semaphore_wait(barrier, len(row_steps) + len(head_members))
+
+
+def to_row(source, target, send, recv, row):
+    return pltpu.make_async_remote_copy(
+        src_ref=source,
+        dst_ref=target,
+        send_sem=send,
+        recv_sem=recv,
+        device_id={"rows": row},
+        device_id_type=MESH,
+    )
+
+
+def to_head(source, target, send, recv, member):
+    return pltpu.make_async_remote_copy(
+        src_ref=source,
+        dst_ref=target,
+        send_sem=send,
+        recv_sem=recv,
+        device_id={"heads": member},
+        device_id_type=MESH,
+    )
+
+
+class RowGather:
+    def __init__(self, shard, full, sends, recvs, local_sem, chunks):
+        self.row = lax.axis_index("rows")
+        self.level = self.row // 2
+        self.side = lax.rem(self.row, 2)
+        self.mate = self.row + 1 - 2 * self.side
+        size = shard.shape[0] // chunks
+        self.own = pltpu.make_async_copy(shard, full.at[self.row], local_sem)
+        self.straight = []
+        self.across = []
+        for chunk in range(chunks):
+            part = pl.ds(chunk * size, size)
+            straight = []
+            across = [
+                to_row(
+                    shard.at[part],
+                    full.at[self.row, part],
+                    sends.at[chunk, 3],
+                    recvs.at[chunk, 3],
+                    self.mate,
+                )
+            ]
+            for step in range(1, 4):
+                target = lax.rem(self.level + step, 4) * 2 + self.side
+                origin = lax.rem(self.level + 4 - step, 4) * 2 + self.side
+                straight.append(
+                    to_row(
+                        shard.at[part],
+                        full.at[self.row, part],
+                        sends.at[chunk, step - 1],
+                        recvs.at[chunk, step - 1],
+                        target,
+                    )
+                )
+                across.append(
+                    to_row(
+                        full.at[origin, part],
+                        full.at[origin, part],
+                        sends.at[chunk, 3 + step],
+                        recvs.at[chunk, 3 + step],
+                        self.mate,
+                    )
+                )
+            self.straight.append(straight)
+            self.across.append(across)
+
+    def start(self):
+        self.own.start()
+        for straight, across in zip(self.straight, self.across):
+            for copy in straight:
+                copy.start()
+            across[0].start()
+
+    def relay(self, chunk):
+        for step in range(3):
+            self.straight[chunk][step].wait_recv()
+            self.across[chunk][1 + step].start()
+
+    def finish(self):
+        self.own.wait()
+        for straight, across in zip(self.straight, self.across):
+            for copy in straight:
+                copy.wait_send()
+            for copy in across:
+                copy.wait()
+
+
+class HeadGather:
+    def __init__(self, block, full, sends, recvs, local_sem):
+        row, member, sibling, partner, opposite = places()
+        self.own = pltpu.make_async_copy(block, full.at[member], local_sem)
+        self.beside = to_head(block, full.at[member], sends.at[0], recvs.at[0], sibling)
+        self.across = to_head(block, full.at[member], sends.at[1], recvs.at[1], partner)
+        self.onward = to_head(
+            full.at[partner], full.at[partner], sends.at[2], recvs.at[2], sibling
+        )
+
+    def start(self):
+        self.across.start()
+        self.beside.start()
+        self.own.start()
+
+    def wait_sibling(self):
+        self.beside.wait_recv()
+
+    def wait_partner(self):
+        self.across.wait_recv()
+        self.onward.start()
+
+    def wait_opposite(self):
+        self.onward.wait_recv()
+
+    def finish(self):
+        self.own.wait()
+        self.beside.wait_send()
+        self.across.wait_send()
+        self.onward.wait_send()
+
+
+def front_kernel(
+    ids_ref,
+    time_ref,
+    class_ref,
+    ada_ref,
+    patches_ref,
+    qkv_ref,
+    out_ref,
+    qkv_full,
+    out_full,
+    patches_full,
+    cond_all,
+    mods_ref,
+    ids_all,
+    cond_part,
+    cond_in,
+    mods_part,
+    mods_in,
+    mods_sibling,
+    mods_pair,
+    mods_partner,
+    small_send,
+    small_recv,
+    pair_send,
+    pair_recv,
+    head_send,
+    head_recv,
+    qkv_send,
+    qkv_recv,
+    out_send,
+    out_recv,
+    local_sems,
+):
+    row, member, sibling, partner, opposite = places()
+    greet(range(1, ROW_PARTS), (sibling, partner))
+    others = [(step, lax.rem(row + step, ROW_PARTS)) for step in range(1, ROW_PARTS)]
+
+    def spread(stage, source_of, target):
+        copies = []
+        for step, other in others:
+            copy = to_row(
+                source_of(other),
+                target.at[row],
+                small_send.at[stage, step - 1],
+                small_recv.at[stage, step - 1],
+                other,
+            )
+            copy.start()
+            copies.append(copy)
+        return copies
+
+    def settle(copies):
+        for copy in copies:
+            copy.wait()
+
+    ids_copies = spread(0, lambda other: ids_ref, ids_all)
+    gather_qkv = RowGather(qkv_ref, qkv_full, qkv_send, qkv_recv, local_sems.at[0], 3)
+    gather_out = RowGather(out_ref, out_full, out_send, out_recv, local_sems.at[1], 1)
+    gather_patches = HeadGather(patches_ref, patches_full, head_send, head_recv, local_sems.at[2])
+    gather_qkv.start()
+    gather_out.start()
+    gather_patches.start()
+    ids_all[row] = ids_ref[...]
+    settle(ids_copies)
+    table_rows = time_ref.shape[0]
+    slots = ROW_PARTS * SLOT_ROWS
+    table_places = row * table_rows + lax.broadcasted_iota(jnp.int32, (slots, table_rows), 1)
+    bucket_hot = (
+        ids_all[:, 0:SLOT_ROWS].reshape(slots, table_rows) == table_places
+    ).astype(jnp.bfloat16)
+    label_hot = (
+        ids_all[:, SLOT_ROWS : 2 * SLOT_ROWS].reshape(slots, table_rows) == table_places
+    ).astype(jnp.bfloat16)
+    found = jnp.dot(bucket_hot, time_ref[...], preferred_element_type=jnp.float32) + jnp.dot(
+        label_hot, class_ref[...], preferred_element_type=jnp.float32
+    )
+    cond_part[...] = found.reshape(cond_part.shape)
+    copies = spread(1, lambda other: cond_part.at[other], cond_in)
+    cond_in[row] = cond_part[row]
+    settle(copies)
+    condition = jnp.sum(cond_in[...], axis=0)
+    cond_all[row] = condition
+    cond_part[row] = condition
+    copies = spread(2, lambda other: cond_part.at[row], cond_all)
+    settle(copies)
+    every = cond_all[...].reshape(slots, cond_all.shape[2])
+    silu_low = (every / (1.0 + jnp.exp(-every))).astype(jnp.bfloat16)
+    mods_part[...] = jnp.dot(
+        silu_low, ada_ref[...], preferred_element_type=jnp.float32
+    ).reshape(mods_part.shape)
+    copies = spread(3, lambda other: mods_part.at[other], mods_in)
+    mods_in[row] = mods_part[row]
+    gather_qkv.relay(0)
+    settle(copies)
+    beside = to_head(mods_in, mods_sibling, pair_send.at[0], pair_recv.at[0], sibling)
+    beside.start()
+    gather_patches.wait_sibling()
+    beside.wait()
+    mods_pair[...] = mods_in[...] + mods_sibling[...]
+    across = to_head(mods_pair, mods_partner, pair_send.at[1], pair_recv.at[1], partner)
+    across.start()
+    gather_patches.wait_partner()
+    gather_qkv.relay(1)
+    across.wait()
+    mods_ref[...] = mods_pair[...] + mods_partner[...]
+    gather_patches.wait_opposite()
+    gather_qkv.relay(2)
+    gather_out.relay(0)
+    gather_patches.finish()
+    gather_qkv.finish()
+    gather_out.finish()
+
+
+def front(ids, time_table, class_table, w_ada, patches, w_qkv, w_out):
+    depth, ada_width = w_ada.shape
+    shape = jax.ShapeDtypeStruct
+    slotted = (ROW_PARTS, SLOT_ROWS)
+    return pl.pallas_call(
+        front_kernel,
+        out_shape=(
+            shape((ROW_PARTS,) + w_qkv.shape, jnp.bfloat16),
+            shape((ROW_PARTS,) + w_out.shape, jnp.bfloat16),
+            shape((HEAD_PARTS,) + patches.shape, jnp.bfloat16),
+            shape(slotted + (depth,), jnp.float32),
+            shape(slotted + (ada_width,), jnp.float32),
+        ),
+        in_specs=[VMEM_SPEC] * 7,
+        out_specs=(ANY_SPEC, ANY_SPEC, ANY_SPEC, VMEM_SPEC, VMEM_SPEC),
+        scratch_shapes=[
+            pltpu.VMEM((ROW_PARTS,) + ids.shape, jnp.int32),
+            pltpu.VMEM(slotted + (depth,), jnp.float32),
+            pltpu.VMEM(slotted + (depth,), jnp.float32),
+            pltpu.VMEM(slotted + (ada_width,), jnp.float32),
+            pltpu.VMEM(slotted + (ada_width,), jnp.float32),
+            pltpu.VMEM(slotted + (ada_width,), jnp.float32),
+            pltpu.VMEM(slotted + (ada_width,), jnp.float32),
+            pltpu.VMEM(slotted + (ada_width,), jnp.float32),
+            DMA((4, 7)),
+            DMA((4, 7)),
+            DMA((2,)),
+            DMA((2,)),
+            DMA((3,)),
+            DMA((3,)),
+            DMA((3, 7)),
+            DMA((3, 7)),
+            DMA((1, 7)),
+            DMA((1, 7)),
+            DMA((3,)),
+        ],
+        compiler_params=pltpu.CompilerParams(
+            collective_id=0, has_side_effects=True, vmem_limit_bytes=GRANT
+        ),
+        name="front",
+    )(ids, time_table, class_table, w_ada, patches, w_qkv, w_out)
+
+
+def shards_linked(
+    patches,
+    time_table,
+    class_table,
+    w_ada,
+    b_ada,
+    w_qkv,
+    b_qv,
+    w_out,
+    b_out,
+    w_fc1,
+    b_fc1,
+    w_fc2,
+    b_fc2,
+    image_lengths,
+    segment_ids,
+    bucket_ids,
+    class_labels,
+    cotangent,
+):
+    head_parts = lax.axis_size("heads")
+    member = lax.axis_index("heads")
+    tok_rows = patches.shape[0]
+    model_width = patches.shape[1]
+    seq_count = segment_ids.shape[0]
+    seq_len = segment_ids.shape[1]
+    slot_count = image_lengths.shape[1]
+    image_count = seq_count * slot_count
+    group_rows = tok_rows * head_parts
+    head_local = b_qv.shape[0]
+    head_size = b_qv.shape[1] // 2
+    block_rows = min(BLOCK_LIMIT, seq_len)
+    scale_factor = 1.0 / math.sqrt(head_size)
+    row_parts = lax.axis_size("rows")
+    table_rows = time_table.shape[0]
+    ada_width = w_ada.shape[1]
+    fc1_cols = lax.all_gather(w_fc1, "rows", axis=0, tiled=True)
+    fc2_cols = lax.all_gather(w_fc2, "rows", axis=0, tiled=True)
+    every_slot = row_parts * SLOT_ROWS
+    slot_pad = jnp.full((SLOT_ROWS - slot_count,), -1, jnp.int32)
+    ids = jnp.broadcast_to(
+        jnp.concatenate([bucket_ids[0], slot_pad, class_labels[0], slot_pad])[:, None],
+        (2 * SLOT_ROWS, table_rows),
+    )
+    qkv_full, out_full, patches_full, condition, mods = front(
+        ids, time_table, class_table, w_ada, patches, w_qkv, w_out
+    )
+    qkv_cols = qkv_full.reshape(model_width, w_qkv.shape[1])
+    out_cols = out_full.reshape(model_width, w_out.shape[1])
+    condition = condition.reshape(every_slot, condition.shape[2])
+    silu_value, silu_pull = jax.vjp(silu_plain, condition)
+    silu_low = silu_value.astype(jnp.bfloat16)
+    mods_all = mods[:, :slot_count].transpose(1, 0, 2).reshape(
+        slot_count, row_parts * ada_width
+    ) + b_ada.astype(jnp.float32)
+    row_segments = segment_ids[0][:, None]
+
+    def by_token(part_index, segments):
+        vectors = mods_all[:, part_index * model_width : (part_index + 1) * model_width]
+        chosen = vectors[slot_count - 1][None, :]
+        for slot in range(slot_count - 2, -1, -1):
+            chosen = jnp.where(segments == slot, vectors[slot][None, :], chosen)
+        return chosen
+
+    own_segments = lax.dynamic_slice_in_dim(segment_ids[0], member * tok_rows, tok_rows)[:, None]
+    token_hot = (own_segments == jnp.arange(slot_count, dtype=jnp.int32)[None, :]).astype(
+        jnp.float32
+    )
+    shift_attn, scale_attn, gate_attn, shift_mlp, scale_mlp, gate_mlp = (
+        by_token(part_index, own_segments) for part_index in range(6)
+    )
+    inputs = patches.astype(jnp.float32)
+    _, first_pull = jax.vjp(modulate, inputs, shift_attn, scale_attn)
+    rows_one = modulate(
+        patches_full.reshape(group_rows, model_width).astype(jnp.float32),
+        by_token(0, row_segments),
+        by_token(1, row_segments),
+    ).astype(jnp.bfloat16)
+    zero_bias = jnp.zeros((head_local, head_size), b_qv.dtype)
+    qkv_bias = (
+        jnp.concatenate([b_qv[:, :head_size], zero_bias, b_qv[:, head_size:]], axis=1)
+        .reshape(head_local * 3 * head_size)
+        .astype(jnp.float32)
+    )
+    projected = (jnp.dot(rows_one, qkv_cols, preferred_element_type=jnp.float32) + qkv_bias).astype(
+        jnp.bfloat16
+    )
+    seq_qkv = projected.reshape(seq_count, seq_len, head_local, 3, head_size)
+    slot_ends = jnp.cumsum(image_lengths, axis=1)
+    places = jnp.arange(seq_len, dtype=jnp.int32)
+    image_of = jnp.sum((places[None, :, None] >= slot_ends[:, None, :]).astype(jnp.int32), axis=2)
+
+    def block_scores(query_rows, key_rows, image_rows, image_cols):
+        scores = (
+            jnp.einsum("qhd,khd->hqk", query_rows, key_rows, preferred_element_type=jnp.float32)
+            * scale_factor
+        )
+        return jnp.where((image_rows[:, None] == image_cols[None, :])[None], scores, MASKED)
+
+    def attend_forward(pieces):
+        seq_block, seq_image = pieces
+        key_rows = seq_block[:, :, 1]
+        value_rows = seq_block[:, :, 2]
+        outputs = []
+        totals = []
+        for row_start in range(0, seq_len, block_rows):
+            stop_row = row_start + block_rows
+            query_rows = seq_block[row_start:stop_row, :, 0]
+            scores = block_scores(query_rows, key_rows, seq_image[row_start:stop_row], seq_image)
+            row_peak = jnp.max(scores, axis=2, keepdims=True)
+            raised = jnp.exp(scores - row_peak)
+            row_total = jnp.sum(raised, axis=2, keepdims=True)
+            soft_low = (raised / row_total).astype(jnp.bfloat16)
+            outputs.append(
+                jnp.einsum(
+                    "hqk,khd->qhd", soft_low, value_rows, preferred_element_type=jnp.float32
+                ).astype(jnp.bfloat16)
+            )
+            totals.append((row_peak + jnp.log(row_total))[:, :, 0])
+        return (jnp.concatenate(outputs, axis=0), jnp.concatenate(totals, axis=1))
+
+    mixed, log_totals = lax.map(attend_forward, (seq_qkv, image_of))
+    mixed_rows = mixed.reshape(group_rows, head_local * head_size)
+    attn_out = lax.psum_scatter(
+        times_transposed(
+            lax.slice_in_dim(mixed_rows, 0, tok_rows * lax.axis_size("heads"), axis=0), out_cols
+        ).astype(jnp.bfloat16),
+        "heads",
+        scatter_dimension=0,
+        tiled=True,
+    ).astype(jnp.float32) + b_out.astype(jnp.float32)
+    after_attn = inputs + gate_attn * attn_out
+    second_value, second_pull = jax.vjp(modulate, after_attn, shift_mlp, scale_mlp)
+    hidden_two = second_value.astype(jnp.bfloat16)
+    rows_two = lax.all_gather(hidden_two, "heads", axis=0, tiled=True)
+    inner = jnp.dot(rows_two, fc1_cols, preferred_element_type=jnp.float32) + b_fc1.astype(
+        jnp.float32
+    )
+    gelu_value, gelu_pull = jax.vjp(gelu_tanh, inner)
+    active = gelu_value.astype(jnp.bfloat16)
+    ffn_out = lax.psum_scatter(
+        times_transposed(
+            lax.slice_in_dim(active, 0, tok_rows * lax.axis_size("heads"), axis=0), fc2_cols
+        ).astype(jnp.bfloat16),
+        "heads",
+        scatter_dimension=0,
+        tiled=True,
+    ).astype(jnp.float32) + b_fc2.astype(jnp.float32)
+    block_out = (after_attn + gate_mlp * ffn_out).astype(jnp.bfloat16)
+    upstream = cotangent.astype(jnp.float32)
+    grad_ffn = (gate_mlp * upstream).astype(jnp.bfloat16)
+    ffn_rows = lax.all_gather(grad_ffn, "heads", axis=0, tiled=True)
+    grad_w_fc2 = contract_rows(ffn_rows, active)
+    grad_b_fc2 = jnp.sum(ffn_rows, axis=0, dtype=jnp.float32)
+    grad_active = jnp.dot(ffn_rows, fc2_cols, preferred_element_type=jnp.float32)
+    grad_inner = gelu_pull(grad_active)[0].astype(jnp.bfloat16)
+    grad_w_fc1 = contract_rows(rows_two, grad_inner)
+    grad_b_fc1 = jnp.sum(grad_inner, axis=0, dtype=jnp.float32)
+    grad_hidden_two = lax.psum_scatter(
+        times_transposed(
+            lax.slice_in_dim(grad_inner, 0, tok_rows * lax.axis_size("heads"), axis=0), fc1_cols
+        ).astype(jnp.bfloat16),
+        "heads",
+        scatter_dimension=0,
+        tiled=True,
+    ).astype(jnp.float32)
+    grad_after, grad_shift_mlp, grad_scale_mlp = second_pull(grad_hidden_two)
+    grad_after = grad_after + upstream
+    grad_gate_mlp = upstream * ffn_out
+    grad_gate_attn = grad_after * attn_out
+    grad_attn = (gate_attn * grad_after).astype(jnp.bfloat16)
+    attn_rows_grad = lax.all_gather(grad_attn, "heads", axis=0, tiled=True)
+    grad_w_out = contract_rows(attn_rows_grad, mixed_rows)
+    grad_b_out = jnp.sum(attn_rows_grad, axis=0, dtype=jnp.float32)
+    grad_mixed = jnp.dot(attn_rows_grad, out_cols, preferred_element_type=jnp.float32).astype(
+        jnp.bfloat16
+    )
+    grad_seq = grad_mixed.reshape(seq_count, seq_len, head_local, head_size)
+
+    def attend_backward(pieces):
+        seq_block, seq_image, seq_grad, seq_totals = pieces
+        key_rows = seq_block[:, :, 1]
+        value_rows = seq_block[:, :, 2]
+        grad_keys = jnp.zeros(key_rows.shape, jnp.float32)
+        grad_values = jnp.zeros(value_rows.shape, jnp.float32)
+        grad_queries = []
+        for row_start in range(0, seq_len, block_rows):
+            stop_row = row_start + block_rows
+            query_rows = seq_block[row_start:stop_row, :, 0]
+            grad_rows = seq_grad[row_start:stop_row]
+            scores = block_scores(query_rows, key_rows, seq_image[row_start:stop_row], seq_image)
+            soft_probs = jnp.exp(scores - seq_totals[:, row_start:stop_row, None])
+            grad_probs = jnp.einsum(
+                "qhd,khd->hqk", grad_rows, value_rows, preferred_element_type=jnp.float32
+            )
+            inner_sum = jnp.sum(soft_probs * grad_probs, axis=2, keepdims=True)
+            grad_scores = (soft_probs * (grad_probs - inner_sum)).astype(jnp.bfloat16)
+            grad_queries.append(
+                jnp.einsum(
+                    "hqk,khd->qhd", grad_scores, key_rows, preferred_element_type=jnp.float32
+                )
+                * scale_factor
+            )
+            grad_keys = (
+                grad_keys
+                + jnp.einsum(
+                    "hqk,qhd->khd", grad_scores, query_rows, preferred_element_type=jnp.float32
+                )
+                * scale_factor
+            )
+            grad_values = grad_values + jnp.einsum(
+                "hqk,qhd->khd",
+                soft_probs.astype(jnp.bfloat16),
+                grad_rows,
+                preferred_element_type=jnp.float32,
+            )
+        stacked = jnp.stack([jnp.concatenate(grad_queries, axis=0), grad_keys, grad_values], axis=2)
+        return stacked.astype(jnp.bfloat16)
+
+    grad_qkv = lax.map(attend_backward, (seq_qkv, image_of, grad_seq, log_totals)).reshape(
+        group_rows, head_local * 3 * head_size
+    )
+    grad_w_qkv = contract_rows(rows_one, grad_qkv)
+    bias_terms = jnp.sum(grad_qkv, axis=0, dtype=jnp.float32).reshape(head_local, 3, head_size)
+    grad_b_qv = jnp.concatenate([bias_terms[:, 0], bias_terms[:, 2]], axis=1)
+    grad_hidden_one = lax.psum_scatter(
+        times_transposed(
+            lax.slice_in_dim(grad_qkv, 0, tok_rows * lax.axis_size("heads"), axis=0), qkv_cols
+        ).astype(jnp.bfloat16),
+        "heads",
+        scatter_dimension=0,
+        tiled=True,
+    ).astype(jnp.float32)
+    grad_inputs, grad_shift_attn, grad_scale_attn = first_pull(grad_hidden_one)
+    grad_patches = grad_inputs + grad_after
+    token_grads = (
+        grad_shift_attn,
+        grad_scale_attn,
+        grad_gate_attn,
+        grad_shift_mlp,
+        grad_scale_mlp,
+        grad_gate_mlp,
+    )
+    mods_grad_part = jnp.concatenate(
+        [contract_rows_exact(token_hot, grad_term) for grad_term in token_grads], axis=1
+    )
+    grad_mods = lax.psum(mods_grad_part.astype(jnp.bfloat16), "heads")
+    grad_cols = lax.all_to_all(
+        jnp.pad(
+            grad_mods.reshape(slot_count, row_parts, ada_width).transpose(1, 0, 2),
+            ((0, 0), (0, SLOT_ROWS - slot_count), (0, 0)),
+        ),
+        "rows",
+        split_axis=0,
+        concat_axis=0,
+        tiled=True,
+    ).reshape(every_slot, ada_width)
+    grad_w_ada = contract_rows(silu_low, grad_cols)
+    grad_b_ada = jnp.sum(grad_cols, axis=0, dtype=jnp.float32)
+    grad_silu = lax.psum(times_transposed(grad_cols, w_ada), "rows")
+    grad_condition = silu_pull(grad_silu)[0]
+    ids_all = lax.all_gather(ids[:, 0], "rows", axis=0)
+    table_places = lax.axis_index("rows") * table_rows + jnp.arange(table_rows, dtype=jnp.int32)
+    bucket_hot = ids_all[:, :SLOT_ROWS].reshape(every_slot)[:, None] == table_places[None, :]
+    label_hot = ids_all[:, SLOT_ROWS:].reshape(every_slot)[:, None] == table_places[None, :]
+    grad_time = contract_rows_exact(bucket_hot.astype(jnp.float32), grad_condition)
+    grad_class = contract_rows_exact(label_hot.astype(jnp.float32), grad_condition)
+
+    def row_reduced(partial):
+        return lax.psum_scatter(
+            partial.astype(jnp.bfloat16), "rows", scatter_dimension=0, tiled=True
+        ).astype(jnp.float32)
+
+    grad_w_qkv, grad_w_out, grad_w_fc1, grad_w_fc2 = (
+        row_reduced(grad_w_qkv),
+        row_reduced(grad_w_out),
+        row_reduced(grad_w_fc1),
+        row_reduced(grad_w_fc2),
+    )
+    bias_sizes = (grad_b_qv.size, grad_b_fc1.size, grad_b_out.size, grad_b_fc2.size)
+    bias_all = lax.psum(
+        jnp.concatenate([grad_b_qv.reshape(-1), grad_b_fc1, grad_b_out, grad_b_fc2]), "rows"
+    )
+    edges = [sum(bias_sizes[:step]) for step in range(5)]
+    bias_rows = model_width // row_parts
+    row_start = lax.axis_index("rows") * bias_rows
+    grad_b_qv = bias_all[edges[0] : edges[1]].reshape(grad_b_qv.shape)
+    grad_b_fc1 = bias_all[edges[1] : edges[2]]
+    grad_b_out = lax.dynamic_slice_in_dim(bias_all[edges[2] : edges[3]], row_start, bias_rows)
+    grad_b_fc2 = lax.dynamic_slice_in_dim(bias_all[edges[3] : edges[4]], row_start, bias_rows)
+    return (
+        block_out,
+        grad_patches,
+        grad_time,
+        grad_class,
+        grad_w_ada,
+        grad_b_ada,
+        grad_w_qkv,
+        grad_b_qv,
+        grad_w_out,
+        grad_b_out,
+        grad_w_fc1,
+        grad_b_fc1,
+        grad_w_fc2,
+        grad_b_fc2,
+    )
+
+
 def solution(mesh):
     placed = (
         P(("rows", "heads"), None),
@@ -390,8 +1012,9 @@
         P("rows", None),
         P(("rows", "heads"), None),
     )
+    linked = mesh.shape["rows"] == ROW_PARTS and mesh.shape["heads"] == HEAD_PARTS
     return jax.shard_map(
-        shards,
+        shards_linked if linked else shards_plain,
         mesh=mesh,
         in_specs=placed,
         out_specs=(

time: 832 us -> 828 us (level)
  Pallas kernels: 0 us -> 78.8 us
  blocking collectives: 134 us -> 57.4 us
  waiting for transfers between devices: 480 us -> 448 us
  other arithmetic: 42 us -> 66.3 us
  local copies, waits for them, and re-layouts: 14.5 us -> 29.7 us
  matrix products: 127 us -> 118 us
    pallas_call x0 -> x1, Pallas kernels: none -> 78.8 us  [front(): pl.pallas_call(front_kernel, out_shape=(shape((ROW_PARTS,) + w_qkv.shape,...]
    reduce_scatter x4, waiting for transfers between devices: 200 us -> 139 us  [row_reduced(): lax.psum_scatter(partial.astype(jnp.bfloat16), 'rows', scatter_dimension=...]
    all_gather x2 -> x0, blocking collectives: 55.2 us -> none  [the longest x1 33 us: gather_weights(): lax.all_gather(w_out, 'rows', axis=0, tiled=True)]
    psum x1, waiting for transfers between devices: 25.7 us -> 63.5 us  [shards_linked(): grad_silu = lax.psum(times_transposed(grad_cols, w_ada), 'rows')]
    psum x3 -> x2, blocking collectives: 78.8 us -> 46.3 us  [the longest x1 35.6 us: shards_linked(): lax.psum(jnp.concatenate([grad_b_qv.reshape(-1), grad_b_fc1, grad_b_out,...]
    dot_general x13 -> x4, matrix products: 39.9 us -> 23.4 us  [the longest x1 9.82 us: shards_linked(): jnp.dot(ffn_rows, fc2_cols, preferred_element_type=jnp.float32)]
    convert_element_type x6 -> x8, other arithmetic: 1.9 us -> 15.7 us  [the longest x1 9.1 us: shards_linked(): rows_one = modulate(patches_full.reshape(group_rows, model_width).astype(...]
    unnamed x0 -> x1, blocking collectives: none -> 11.1 us
  transfers between devices with their start and end apart: 18 -> 15, of which waited for: 15 -> 14; matrix products, arithmetic and copies ran while one was open for 14% -> 15% of each run, Pallas kernels for 0% -> 0%
where the time goes in v2:
time: 828 us; the launch traced here: 823 us
  waiting for transfers between devices  448 us (54%)
  matrix products  118 us (14%)
  Pallas kernels  78.8 us (10%)
  other arithmetic  66.3 us (8%)
  blocking collectives  57.4 us (7%)
  local copies, waits for them, and re-layouts  29.7 us (4%)
  between operations  17.1 us (2%)
    reduce_scatter x4, waiting for transfers between devices, row_reduced(): lax.psum_scatter(partial.astype(jnp.bfloat16), 'rows', scatter_dimension=...  139 us
    pallas_call x1, Pallas kernels, front(): pl.pallas_call(front_kernel, out_shape=(shape((ROW_PARTS,) + w_qkv.shape,...  78.8 us
    psum x1, waiting for transfers between devices, shards_linked(): grad_silu = lax.psum(times_transposed(grad_cols, w_ada), 'rows')  63.5 us
    all_gather x1, waiting for transfers between devices, shards_linked(): fc2_cols = lax.all_gather(w_fc2, 'rows', axis=0, tiled=True)  48.9 us
    psum x1, blocking collectives, shards_linked(): lax.psum(jnp.concatenate([grad_b_qv.reshape(-1), grad_b_fc1, grad_b_out,...  35.6 us
    reduce_scatter x1, waiting for transfers between devices, shards_linked(): lax.psum_scatter(times_transposed(lax.slice_in_dim(active, 0, tok_rows *...  33.1 us
    reduce_scatter x1, waiting for transfers between devices, shards_linked(): lax.psum_scatter(times_transposed(lax.slice_in_dim(grad_qkv, 0, tok_rows...  32.1 us
    reduce_scatter x1, waiting for transfers between devices, shards_linked(): lax.psum_scatter(times_transposed(lax.slice_in_dim(mixed_rows, 0, tok_row...  31.1 us
  transfers between devices with their start and end apart: 15, of which 14 were waited for; matrix products, arithmetic and copies ran while one was open for 15% of the time, Pallas kernels for 0%

profile of v2, /device:TPU:0, one launch (start us, length us, event | category | flops | bytes accessed | tf_op | source)
XLA Modules:
  0.0 822.9 jit_solution(17234838805519083516)
XLA Ops:
  15.5 78.8 %front.1 = (bf16[8,144,864]{2,1,0:T(8,128)(2,1)}, bf16[8,144,288]{2,1,0:T(8,128)(2,1)}, bf16[4,256,1152]{2,1,0:T(8,128)(2,1)}, f32[8,8,288]{2,1,0:T(8,128)}, f32[8,8,864]{2,1,0:T(8,128)}) custom-call(s32[16,128]{1,0:T(8,128)} %broadcast_in_dim.423.ids_ref, bf16[128,288]{1,0:T(8,128)(2,1)} %copy.59.time_ref, bf16[128,288]{1,0:T(8,128)(2,1)} %copy.60.class_ref, ...), custom_call_target="tpu_custom_call" | custom-call | tf_op jit(solution)/shard_map/front/pallas_call | solution.py:647
  96.8 2.0 convert_reduce_fusion
  100.4 9.1 %fusion.9 = bf16[4,256,1152]{2,1,0:T(8,128)(2,1)S(1)} fusion(bf16[4,256,1152]{2,1,0:T(8,128)(2,1)S(1)} %copy-done.2, f32[1152]{0:T(1024)S(1)} %get-tuple-element.71, f32[1152]{0:T(1024)S(1)} %get-tuple-element.72, f32[1152]{0:T(1024)S(1)} %get-tuple-element.73, f32[1152]{0:T(1024)S(1)} %get-tuple-element.74, f32[1152]{0:T(1024)S(1)} %get-tuple-element.75, ...), kind=kLoop, calls=%fused_computation.29 | loop fusion | flops 15335424 | bytes 4766720 | tf_op jit(solution)/shard_map/convert_element_type | solution.py:763
  109.5 2.5 add_convert_fusion
  112.0 1.9 fusion.105
  113.9 1.9 fusion.1
  117.1 2.1 fusion.58
  119.3 1.9 fusion.106
  121.2 1.9 fusion
  124.4 2.7 fusion.57
  128.0 3.0 convolution_convert_fusion.3
  131.8 31.1 %reduce-scatter.9.cloned.1.call-done = bf16[256,1152]{1,0:T(8,128)(2,1)} async-done(((bf16[1024,1152]{1,0:T(8,128)(2,1)}), bf16[256,1152]{1,0:T(8,128)(2,1)}) %reduce-scatter.9.cloned.1.call-update) | async-done | bytes 589840 | tf_op jit(solution)/shard_map/reduce_scatter | solution.py:809
  162.9 3.7 fusion.99
  166.9 2.8 add_convert_fusion.2
  171.1 16.3 %all-gather.9.cloned.1.call-done = bf16[1152,1152]{1,0:T(8,128)(2,1)} async-done(((bf16[144,1152]{1,0:T(8,128)(2,1)}), bf16[1152,1152]{1,0:T(8,128)(2,1)}) %all-gather.9.cloned.1.call-update) | async-done | bytes 2654224 | tf_op jit(solution)/shard_map/all_gather | solution.py:722
  187.4 24.5 %all-gather.7.cloned.1.call-done = bf16[1024,1152]{1,0:T(8,128)(2,1)} async-done(((bf16[256,1152]{1,0:T(8,128)(2,1)}), bf16[1024,1152]{1,0:T(8,128)(2,1)}) %all-gather.7.cloned.1.call-update) | async-done | bytes 2359312 | tf_op jit(solution)/shard_map/all_gather | solution.py:820
  211.9 8.1 convolution_add_fusion
  220.0 48.9 %all-gather.11.cloned.1.call-done = bf16[1152,1152]{1,0:T(8,128)(2,1)} async-done(((bf16[144,1152]{1,0:T(8,128)(2,1)}), bf16[1152,1152]{1,0:T(8,128)(2,1)}) %all-gather.11.cloned.1.call-update) | async-done | bytes 2654224 | tf_op jit(solution)/shard_map/all_gather | solution.py:723
  268.9 24.7 %all-gather.13.cloned.1.call-done = bf16[1024,1152]{1,0:T(8,128)(2,1)} async-done(((bf16[256,1152]{1,0:T(8,128)(2,1)}), bf16[1024,1152]{1,0:T(8,128)(2,1)}) %all-gather.13.cloned.1.call-update) | async-done | bytes 2359312 | tf_op jit(solution)/shard_map/all_gather | solution.py:837
  293.6 9.8 %convert_reduce_fusion.3 = (f32[1152]{0:T(1024)}, bf16[1024,1152]{1,0:T(8,128)(2,1)S(1)}) fusion(f32[1024,1152]{1,0:T(8,128)} %convolution_add_fusion, bf16[1024,1152]{1,0:T(8,128)(2,1)} %all-gather.13.cloned.1.call-done, bf16[1152,1152]{1,0:T(8,128)(2,1)} %all-gather.11.cloned.1.call-done), kind=kOutput, calls=%fused_computation.38 | convolution fusion | flops 2748578816 | bytes 12096000 | tf_op jit(solution)/shard_map/dot_general | solution.py:840
  304.8 4.8 convolution_convert_fusion.4
  309.8 8.8 %convolution_convert_fusion.5 = bf16[1024,1152]{1,0:T(8,128)(2,1)} fusion(bf16[1152,1152]{1,0:T(8,128)(2,1)} %all-gather.11.cloned.1.call-done, f32[1024,1152]{1,0:T(8,128)} %convolution_add_fusion), kind=kOutput, calls=%fused_computation.50 | convolution fusion | flops 2729705472 | bytes 9732096 | tf_op jit(solution)/shard_map/dot_general | solution.py:56
  319.9 22.6 %reduce-scatter.13.cloned.1.call-done = bf16[256,1152]{1,0:T(8,128)(2,1)} async-done(((bf16[1024,1152]{1,0:T(8,128)(2,1)}), bf16[256,1152]{1,0:T(8,128)(2,1)}) %reduce-scatter.13.cloned.1.call-update) | async-done | bytes 589840 | tf_op jit(solution)/shard_map/reduce_scatter | solution.py:844
  344.8 33.1 %reduce-scatter.11.cloned.1.call-done = bf16[256,1152]{1,0:T(8,128)(2,1)} async-done(((bf16[1024,1152]{1,0:T(8,128)(2,1)}), bf16[256,1152]{1,0:T(8,128)(2,1)}) %reduce-scatter.11.cloned.1.call-update) | async-done | bytes 589840 | tf_op jit(solution)/shard_map/reduce_scatter | solution.py:826
  377.9 3.1 fusion.98
  381.7 2.4 multiply_convert_fusion.3
  384.1 7.2 convolution_convert_fusion.1
  393.5 8.0 convolution_convert_fusion
  401.8 6.5 all-gather.15.cloned.1.call-done
  408.3 3.0 convolution_convert_fusion.14
  412.2 2.3 convolution_convert_fusion.7
  414.5 9.0 %multiply_reduce_fusion.1 = (f32[4,512]{1,0:T(4,128)S(1)}, f32[4,512,1024]{2,1,0:T(8,128)}) fusion(f32[4,512,1024]{2,1,0:T(8,128)} %copy-done, f32[4,512]{1,0:T(4,128)S(1)} %log_add_fusion.1, bf16[512,4,72]{0,2,1:T(8,128)(2,1)} %bitcast.153, bf16[1024,4,3,72]{0,3,2,1:T(8,128)(2,1)} %bitcast.147), kind=kOutput, calls=%fused_computation.4 | convolution fusion | flops 308279296 | bytes 17678336 | tf_op jit(solution)/shard_map/while/body/eval_jaxpr/qhd,khd->hqk/dot_general | solution.py:878
  423.6 4.6 multiply_convert_fusion.1
  428.2 2.2 fusion.56
  430.4 2.6 multiply_reduce_fusion
  433.0 1.8 multiply_convert_fusion
  434.7 2.1 fusion.55
  437.7 1.7 fusion.42
  439.4 2.5 fusion.16
  443.6 5.5 fusion.43
  452.3 3.9 convolution_convert_fusion.6
  456.4 6.4 convolution_convert_fusion.2
  463.4 11.1 %all-reduce.1 = s32[128]{0:T(128)S(1)} all-reduce(s32[128]{0:T(128)S(1)} %copy-done.75), channel_id=2, replica_groups=mesh['rows'=8,'heads'=4] {'rows'}, use_global_device_ids=true, to_apply=%add.1 | all-reduce | flops 128 | bytes 1024
  477.0 2.7 convert_reduce_fusion.1
  479.7 1.9 convert_element_type.257
  481.6 55.8 %reduce-scatter.23.cloned.1.call-done = bf16[144,1152]{1,0:T(8,128)(2,1)} async-done(((bf16[1152,1152]{1,0:T(8,128)(2,1)}), bf16[144,1152]{1,0:T(8,128)(2,1)}) %reduce-scatter.23.cloned.1.call-update) | async-done | bytes 331792 | tf_op jit(solution)/shard_map/reduce_scatter | solution.py:955
  537.3 1.9 convert_element_type.259
  541.9 2.6 convert_reduce_fusion.2
  546.0 35.6 %psum.23 = f32[4032]{0:T(1024)} all-reduce(f32[4032]{0:T(1024)} %concatenate.33), channel_id=1, replica_groups=mesh['rows'=8,'heads'=4] {'rows'}, use_global_device_ids=true, to_apply=%region_30.31 | all-reduce | flops 4032 | bytes 32256 | tf_op jit(solution)/shard_map/psum | solution.py:966
  586.9 15.3 %reduce-scatter.19.cloned.1.call-done = bf16[144,288]{1,0:T(8,128)(2,1)} async-done(((bf16[1152,288]{1,0:T(8,128)(2,1)}), bf16[144,288]{1,0:T(8,128)(2,1)}) %reduce-scatter.19.cloned.1.call-update) | async-done | bytes 82960 | tf_op jit(solution)/shard_map/reduce_scatter | solution.py:955
  603.8 68.4 %reduce-scatter.17.cloned.1.call-done = bf16[144,864]{1,0:T(8,128)(2,1)} async-done(((bf16[1152,864]{1,0:T(8,128)(2,1)}), bf16[144,864]{1,0:T(8,128)(2,1)}) %reduce-scatter.17.cloned.1.call-update) | async-done | bytes 248848 | tf_op jit(solution)/shard_map/reduce_scatter | solution.py:955
  672.2 1.8 convert_element_type.249
  674.0 32.1 %reduce-scatter.15.cloned.1.call-done = bf16[256,1152]{1,0:T(8,128)(2,1)} async-done(((bf16[1024,1152]{1,0:T(8,128)(2,1)}), bf16[256,1152]{1,0:T(8,128)(2,1)}) %reduce-scatter.15.cloned.1.call-update) | async-done | bytes 589840 | tf_op jit(solution)/shard_map/reduce_scatter | solution.py:911
  706.1 1.9 fusion.50
  708.6 2.0 fusion.29
  710.6 2.4 fusion.28
  719.0 10.7 %psum.21 = bf16[8,4,864]{2,1,0:T(4,128)(2,1)S(1)} all-reduce(bf16[8,4,864]{2,1,0:T(4,128)(2,1)S(1)} %bitcast.163), channel_id=1, replica_groups=mesh['rows'=8,'heads'=4] {'heads'}, use_global_device_ids=true, to_apply=%region_22.23 | all-reduce | flops 27648 | bytes 110592 | tf_op jit(solution)/shard_map/psum | solution.py:932
  730.4 5.8 all-to-all-start
  736.2 1.9 fusion.97
  738.1 2.0 add_add_fusion.2
  740.1 3.3 all-to-all-done
  743.5 1.8 fusion.70
  745.3 2.3 convolution_bitcast_fusion
  749.1 63.5 %all-reduce.4.cloned.1.call-done = f32[64,288]{1,0:T(8,128)} async-done(((f32[64,288]{1,0:T(8,128)}), f32[64,288]{1,0:T(8,128)}) %all-reduce.4.cloned.1.call-update) | async-done | bytes 73744 | tf_op jit(solution)/shard_map/psum | solution.py:945
  (271 shorter events, 57.3 us)
Async XLA Ops:
  8.0 88.0 %copy-start.73 = (s32[1,4]{1,0:T(1,128)S(1)}, s32[1,4]{1,0:T(1,128)}, u32[]{:S(2)}) copy-start(s32[1,4]{1,0:T(1,128)} %param.31) | copy-start | bytes 52
  8.0 88.3 %copy-start.69 = (bf16[4,144]{1,0:T(4,128)(2,1)S(1)}, bf16[4,144]{1,0:T(4,128)(2,1)}, u32[]{:S(2)}) copy-start(bf16[4,144]{1,0:T(4,128)(2,1)} %param.24) | copy-start | bytes 3460
  8.0 88.6 %copy-start.60 = (s32[1,1024]{1,0:T(1,128)S(1)}, s32[1,1024]{1,0:T(1,128)}, u32[]{:S(2)}) copy-start(s32[1,1024]{1,0:T(1,128)} %param.32) | copy-start | bytes 12292
  8.0 154.8 %reduce-scatter.9.cloned.1.call-start = ((), (), s32[]{:S(2)}) async-start(), calls=%async_computation.9 | async-start | bytes 2949120 | tf_op jit(solution)/shard_map/reduce_scatter | solution.py:809
  94.3 4.5 copy-start.2
  95.7 4.6 copy-start.21
  95.7 67.1 %copy-start.33 = (f32[1152]{0:T(1024)}, f32[1152]{0:T(1024)S(1)}, u32[]{:S(2)}) copy-start(f32[1152]{0:T(1024)S(1)} %get-tuple-element.78) | copy-start | bytes 13828
  95.7 67.1 %copy-start.34 = (f32[1152]{0:T(1024)}, f32[1152]{0:T(1024)S(1)}, u32[]{:S(2)}) copy-start(f32[1152]{0:T(1024)S(1)} %get-tuple-element.80) | copy-start | bytes 13828
  95.7 67.1 %copy-start.35 = (f32[1152]{0:T(1024)}, f32[1152]{0:T(1024)S(1)}, u32[]{:S(2)}) copy-start(f32[1152]{0:T(1024)S(1)} %get-tuple-element.81) | copy-start | bytes 13828
  95.7 67.1 %copy-start.36 = (f32[1152]{0:T(1024)}, f32[1152]{0:T(1024)S(1)}, u32[]{:S(2)}) copy-start(f32[1152]{0:T(1024)S(1)} %get-tuple-element.82) | copy-start | bytes 13828
  96.0 66.8 %copy-start.37 = (f32[1152]{0:T(1024)}, f32[1152]{0:T(1024)S(1)}, u32[]{:S(2)}) copy-start(f32[1152]{0:T(1024)S(1)} %get-tuple-element.59) | copy-start | bytes 13828
  96.0 66.8 %copy-start.38 = (f32[1152]{0:T(1024)}, f32[1152]{0:T(1024)S(1)}, u32[]{:S(2)}) copy-start(f32[1152]{0:T(1024)S(1)} %get-tuple-element.68) | copy-start | bytes 13828
  96.1 66.8 %copy-start.39 = (f32[1152]{0:T(1024)}, f32[1152]{0:T(1024)S(1)}, u32[]{:S(2)}) copy-start(f32[1152]{0:T(1024)S(1)} %get-tuple-element.69) | copy-start | bytes 13828
  96.1 66.8 %copy-start.40 = (f32[1152]{0:T(1024)}, f32[1152]{0:T(1024)S(1)}, u32[]{:S(2)}) copy-start(f32[1152]{0:T(1024)S(1)} %get-tuple-element.70) | copy-start | bytes 13828
  96.1 246.5 %copy-start.27 = (f32[1152]{0:T(1024)}, f32[1152]{0:T(1024)S(1)}, u32[]{:S(2)}) copy-start(f32[1152]{0:T(1024)S(1)} %get-tuple-element.66) | copy-start | bytes 13828
  96.1 246.5 %copy-start.28 = (f32[1152]{0:T(1024)}, f32[1152]{0:T(1024)S(1)}, u32[]{:S(2)}) copy-start(f32[1152]{0:T(1024)S(1)} %get-tuple-element.67) | copy-start | bytes 13828
  100.3 9.1 %copy-start.71 = (bf16[8,144,864]{2,1,0:T(8,128)(2,1)S(1)}, bf16[8,144,864]{2,1,0:T(8,128)(2,1)}, u32[]{:S(2)}) copy-start(bf16[8,144,864]{2,1,0:T(8,128)(2,1)} %get-tuple-element.54) | copy-start | bytes 5971972
  112.0 11.0 %copy-start.6 = (bf16[1024,864]{0,1:T(8,128)(2,1)}, bf16[1024,864]{0,1:T(8,128)(2,1)S(1)}, u32[]{:S(2)}) copy-start(bf16[1024,864]{0,1:T(8,128)(2,1)S(1)} %add_convert_fusion) | copy-start | bytes 5308420
  131.0 31.9 %copy-start.3 = (bf16[256,1152]{1,0:T(8,128)(2,1)S(1)}, bf16[256,1152]{1,0:T(8,128)(2,1)}, u32[]{:S(2)}) copy-start(bf16[256,1152]{1,0:T(8,128)(2,1)} %param.35) | copy-start | bytes 1769476
  131.0 31.9 %copy-start.4 = (bf16[256,1152]{1,0:T(8,128)(2,1)S(1)}, bf16[256,1152]{1,0:T(8,128)(2,1)}, u32[]{:S(2)}) copy-start(bf16[256,1152]{1,0:T(8,128)(2,1)} %patches_ref.1) | copy-start | bytes 1769476
  131.0 56.4 %all-gather.9.cloned.1.call-start = ((), (), s32[]{:S(2)}) async-start(), calls=%async_computation.11 | async-start | bytes 2985984 | tf_op jit(solution)/shard_map/all_gather | solution.py:722
  131.6 80.3 %all-gather.7.cloned.1.call-start = ((), (), s32[]{:S(2)}) async-start(), calls=%async_computation.10 | async-start | bytes 2949120 | tf_op jit(solution)/shard_map/all_gather | solution.py:820
  131.7 35.2 %copy-start.30 = (f32[1152]{0:T(1024)}, f32[1152]{0:T(1024)S(1)}, u32[]{:S(2)}) copy-start(f32[1152]{0:T(1024)S(1)} %convert_element_type.224) | copy-start | bytes 13828
  131.7 35.2 %copy-start.41 = (s32[1,256]{1,0:T(1,128)}, s32[1,256]{1,0:T(1,128)S(1)}, u32[]{:S(2)}) copy-start(s32[1,256]{1,0:T(1,128)S(1)} %constant_dynamic-slice_fusion) | copy-start | bytes 3076
  131.8 210.8 %copy-start.45 = (pred[256]{0:T(512)(128)(4,1)}, pred[256]{0:T(512)(128)(4,1)S(1)}, u32[]{:S(2)}) copy-start(pred[256]{0:T(512)(128)(4,1)S(1)} %get-tuple-element.118) | copy-start | bytes 772
  131.8 210.8 %copy-start.47 = (pred[256]{0:T(512)(128)(4,1)}, pred[256]{0:T(512)(128)(4,1)S(1)}, u32[]{:S(2)}) copy-start(pred[256]{0:T(512)(128)(4,1)S(1)} %get-tuple-element.119) | copy-start | bytes 772
  131.8 210.8 %copy-start.49 = (pred[256]{0:T(512)(128)(4,1)}, pred[256]{0:T(512)(128)(4,1)S(1)}, u32[]{:S(2)}) copy-start(pred[256]{0:T(512)(128)(4,1)S(1)} %get-tuple-element.120) | copy-start | bytes 772
  166.6 4.5 copy-start.63
  166.6 176.0 %copy-start.43 = (f32[256]{0:T(256)}, f32[256]{0:T(256)S(1)}, u32[]{:S(2)}) copy-start(f32[256]{0:T(256)S(1)} %broadcast_multiply_fusion.2) | copy-start | bytes 3076
  166.9 53.1 %copy-start.58 = (f32[256]{0:T(256)}, f32[256]{0:T(256)S(1)}, u32[]{:S(2)}) copy-start(f32[256]{0:T(256)S(1)} %fusion.92) | copy-start | bytes 3076
  169.7 99.1 %all-gather.11.cloned.1.call-start = ((), (), s32[]{:S(2)}) async-start(), calls=%async_computation.12 | async-start | bytes 2985984 | tf_op jit(solution)/shard_map/all_gather | solution.py:723
  170.3 123.2 %all-gather.13.cloned.1.call-start = ((), (), s32[]{:S(2)}) async-start(), calls=%async_computation.14 | async-start | bytes 2949120 | tf_op jit(solution)/shard_map/all_gather | solution.py:837
  171.1 171.5 %reduce-scatter.13.cloned.1.call-start = ((), (), s32[]{:S(2)}) async-start(), calls=%async_computation.15 | async-start | bytes 2949120 | tf_op jit(solution)/shard_map/reduce_scatter | solution.py:844
  293.6 11.2 %copy-start.70 = (bf16[1152,1152]{1,0:T(8,128)(2,1)S(1)}, bf16[1152,1152]{1,0:T(8,128)(2,1)}, u32[]{:S(2)}) copy-start(bf16[1152,1152]{1,0:T(8,128)(2,1)} %all-gather.9.cloned.1.call-done) | copy-start | bytes 7962628
  309.6 68.4 %reduce-scatter.11.cloned.1.call-start = ((), (), s32[]{:S(2)}) async-start(), calls=%async_computation.13 | async-start | bytes 2949120 | tf_op jit(solution)/shard_map/reduce_scatter | solution.py:826
  318.7 89.6 %all-gather.15.cloned.1.call-start = ((), (), s32[]{:S(2)}) async-start(), calls=%async_computation.16 | async-start | bytes 2949120 | tf_op jit(solution)/shard_map/all_gather | solution.py:857
  384.1 95.6 %reduce-scatter.21.cloned.1.call-start = ((), (), s32[]{:S(2)}) async-start(), calls=%async_computation.21 | async-start | bytes 2985984 | tf_op jit(solution)/shard_map/reduce_scatter | solution.py:955
  391.4 145.9 %reduce-scatter.23.cloned.1.call-start = ((), (), s32[]{:S(2)}) async-start(), calls=%async_computation.22 | async-start | bytes 2985984 | tf_op jit(solution)/shard_map/reduce_scatter | solution.py:955
  401.5 200.7 %reduce-scatter.19.cloned.1.call-start = ((), (), s32[]{:S(2)}) async-start(), calls=%async_computation.20 | async-start | bytes 995328 | tf_op jit(solution)/shard_map/reduce_scatter | solution.py:955
  414.5 9.0 %slice-start = ((s8[8388608]{0:T(1024)(128)(4,1)}), s8[4194304]{0:T(1024)(128)(4,1)S(1)}, s32[]{:S(2)}) async-start(s8[8388608]{0:T(1024)(128)(4,1)} %bitcast.139), calls=%async_computation.23 | async-start | bytes 8388608
  414.5 9.0 %slice-start.1 = ((s8[8388608]{0:T(1024)(128)(4,1)}), s8[4194304]{0:T(1024)(128)(4,1)S(1)}, s32[]{:S(2)}) async-start(s8[8388608]{0:T(1024)(128)(4,1)} %bitcast.139), calls=%async_computation.24 | async-start | bytes 8388608
  423.5 6.8 slice-start.2
  423.5 4.6 copy-start.7
  423.5 6.8 slice-start.3
  442.0 230.2 %reduce-scatter.17.cloned.1.call-start = ((), (), s32[]{:S(2)}) async-start(), calls=%async_computation.19 | async-start | bytes 2322432 | tf_op jit(solution)/shard_map/reduce_scatter | solution.py:955
  443.6 5.5 copy-start.15
  456.3 249.8 %reduce-scatter.15.cloned.1.call-start = ((), (), s32[]{:S(2)}) async-start(), calls=%async_computation.17 | async-start | bytes 2949120 | tf_op jit(solution)/shard_map/reduce_scatter | solution.py:911
  462.8 13.7 %copy-start.65 = (f32[256]{0:T(256)S(1)}, f32[256]{0:T(256)}, u32[]{:S(2)}) copy-start(f32[256]{0:T(256)} %get-tuple-element.101) | copy-start | bytes 3076
  481.5 224.5 %copy-start.22 = (f32[1152]{0:T(1024)S(1)}, f32[1152]{0:T(1024)}, u32[]{:S(2)}) copy-start(f32[1152]{0:T(1024)} %copy-done.21) | copy-start | bytes 13828
  481.5 224.5 %copy-start.24 = (f32[1152]{0:T(1024)S(1)}, f32[1152]{0:T(1024)}, u32[]{:S(2)}) copy-start(f32[1152]{0:T(1024)} %copy-done.23) | copy-start | bytes 13828
  706.1 6.9 copy-start.14
  706.1 6.9 copy-start.31
  706.1 6.9 copy-start.42
  706.1 6.9 copy-start.57
  708.0 6.4 copy-start.5
  710.6 4.8 copy-start.44
  710.6 4.8 copy-start.59
  730.4 13.1 %all-to-all-start = ((bf16[8,8,864]{2,1,0:T(8,128)(2,1)}), bf16[8,8,864]{2,1,0:T(8,128)(2,1)}, u32[]{:S(2)}, u32[]{:S(2)}) async-start(bf16[8,8,864]{2,1,0:T(8,128)(2,1)} %pad.4), calls=%async_computation.4 | async-start | bytes 229376 | tf_op jit(solution)/shard_map/all_to_all | solution.py:933
  736.1 76.5 %all-reduce.4.cloned.1.call-start = ((), (), s32[]{:S(2)}) async-start(), calls=%async_computation.18 | async-start | bytes 196608 | tf_op jit(solution)/shard_map/psum | solution.py:945
  738.1 5.4 copy-start.17
  740.1 72.6 %copy-start.29 = (f32[8,8,288]{2,1,0:T(8,128)S(1)}, f32[8,8,288]{2,1,0:T(8,128)}, u32[]{:S(2)}) copy-start(f32[8,8,288]{2,1,0:T(8,128)} %get-tuple-element.56) | copy-start | bytes 221188
  740.1 73.5 %copy-start.66 = (s32[128]{0:T(128)S(1)}, s32[128]{0:T(128)}, u32[]{:S(2)}) copy-start(s32[128]{0:T(128)} %iota_add_fusion) | copy-start | bytes 1540
  740.1 73.5 %copy-start.67 = (s32[64]{0:T(128)S(1)}, s32[64]{0:T(128)}, u32[]{:S(2)}) copy-start(s32[64]{0:T(128)} %eq.208) | copy-start | bytes 772
  740.1 74.5 %copy-start.68 = (s32[64]{0:T(128)S(1)}, s32[64]{0:T(128)}, u32[]{:S(2)}) copy-start(s32[64]{0:T(128)} %eq.201) | copy-start | bytes 772
  (32 other events, 80.8 us)
Sparse Core Ops, SparseCore 0:
  131.2 31.6 reduce-scatter.8
  309.7 32.8 reduce-scatter.12
  345.1 32.8 reduce-scatter.10
  384.2 24.0 all-gather.14
Sparse Core Ops, SparseCore 1:
  133.7 53.7 all-gather.8
  189.4 22.5 all-gather.6
  214.0 54.8 all-gather.10
  271.0 22.5 all-gather.12
  391.5 71.5 reduce-scatter.20
  466.7 70.5 reduce-scatter.22
  541.2 61.0 reduce-scatter.18
  605.6 66.5 reduce-scatter.16
  674.6 31.4 reduce-scatter.14
  745.4 67.2 all-reduce.3

commit v3 on v2

--- a/solution.py
+++ b/solution.py
@@ -652,11 +652,11 @@
             shape((HEAD_PARTS,) + patches.shape, jnp.bfloat16),
             shape(slotted + (depth,), jnp.float32),
             shape(slotted + (ada_width,), jnp.float32),
+            shape((ROW_PARTS,) + ids.shape, jnp.int32),
         ),
         in_specs=[VMEM_SPEC] * 7,
-        out_specs=(ANY_SPEC, ANY_SPEC, ANY_SPEC, VMEM_SPEC, VMEM_SPEC),
+        out_specs=(ANY_SPEC, ANY_SPEC, ANY_SPEC, VMEM_SPEC, VMEM_SPEC, VMEM_SPEC),
         scratch_shapes=[
-            pltpu.VMEM((ROW_PARTS,) + ids.shape, jnp.int32),
             pltpu.VMEM(slotted + (depth,), jnp.float32),
             pltpu.VMEM(slotted + (depth,), jnp.float32),
             pltpu.VMEM(slotted + (ada_width,), jnp.float32),
@@ -681,6 +681,417 @@
         ),
         name="front",
     )(ids, time_table, class_table, w_ada, patches, w_qkv, w_out)
+
+
+class HeadReduce:
+    def __init__(self, partial, beside_in, pair, across_in, sends, recvs):
+        row, member, sibling, partner, opposite = places()
+        self.member = member
+        self.partner = partner
+        self.partial = partial
+        self.beside_in = beside_in
+        self.pair = pair
+        self.across_in = across_in
+        self.first = to_head(
+            partial.at[opposite], beside_in.at[1], sends.at[0], recvs.at[0], sibling
+        )
+        self.second = to_head(
+            partial.at[sibling], beside_in.at[0], sends.at[1], recvs.at[1], sibling
+        )
+        self.across = to_head(pair, across_in, sends.at[2], recvs.at[2], partner)
+
+    def start(self):
+        self.first.start()
+        self.second.start()
+
+    def send_pair(self):
+        self.first.wait_recv()
+        self.pair[...] = (
+            self.partial[self.partner].astype(jnp.float32)
+            + self.beside_in[1].astype(jnp.float32)
+        ).astype(jnp.bfloat16)
+        self.across.start()
+
+    def settle(self):
+        self.second.wait_recv()
+        self.across.wait_recv()
+
+    def rows(self, part):
+        return (
+            self.partial[self.member, part].astype(jnp.float32)
+            + self.beside_in[0, part].astype(jnp.float32)
+            + self.across_in[part].astype(jnp.float32)
+        )
+
+    def finish(self):
+        self.first.wait_send()
+        self.second.wait_send()
+        self.across.wait_send()
+
+
+class RowReduce:
+    def __init__(self, partial, mate_in, pair, straight_in, total, part, sends, recvs):
+        row = lax.axis_index("rows")
+        self.level = row // 2
+        self.side = lax.rem(row, 2)
+        mate = row + 1 - 2 * self.side
+        self.partial = partial
+        self.mate_in = mate_in
+        self.pair = pair
+        self.straight_in = straight_in
+        self.total = total
+        self.part = part
+        self.beside = to_row(
+            partial.at[:, 1 - self.side, part],
+            mate_in.at[:, part],
+            sends.at[0],
+            recvs.at[0],
+            mate,
+        )
+        self.straight = []
+        for step in range(1, 4):
+            target = lax.rem(self.level + step, 4)
+            self.straight.append(
+                to_row(
+                    pair.at[target, part],
+                    straight_in.at[step - 1, part],
+                    sends.at[step],
+                    recvs.at[step],
+                    target * 2 + self.side,
+                )
+            )
+
+    def start(self):
+        self.beside.start()
+
+    def send_pair(self):
+        self.beside.wait_recv()
+
+        def one(level, carry):
+            self.pair[level, self.part] = (
+                self.partial[level, self.side, self.part].astype(jnp.float32)
+                + self.mate_in[level, self.part].astype(jnp.float32)
+            ).astype(jnp.bfloat16)
+            return carry
+
+        lax.fori_loop(0, 4, one, 0)
+        for copy in self.straight:
+            copy.start()
+
+    def finish(self):
+        for copy in self.straight:
+            copy.wait_recv()
+        self.total[self.part] = (
+            self.pair[self.level, self.part].astype(jnp.float32)
+            + self.straight_in[0, self.part].astype(jnp.float32)
+            + self.straight_in[1, self.part].astype(jnp.float32)
+            + self.straight_in[2, self.part].astype(jnp.float32)
+        )
+        self.beside.wait_send()
+        for copy in self.straight:
+            copy.wait_send()
+
+
+BACK_CHUNKS = (3, 3, 3, 1)
+
+
+def back_kernel(
+    hidden_ref,
+    fc2_part,
+    fc1_part,
+    qkv_part,
+    out_part,
+    bias_ref,
+    patches_ref,
+    after_ref,
+    scale_ref,
+    hot_ref,
+    sums_ref,
+    silu_ref,
+    slope_ref,
+    bucket_ref,
+    label_ref,
+    ada_ref,
+    patches_grad,
+    time_grad,
+    class_grad,
+    ada_grad,
+    ada_bias,
+    fc2_grad,
+    fc1_grad,
+    qkv_grad,
+    out_grad,
+    bias_sum,
+    beside_in,
+    pair_rows,
+    across_in,
+    fc2_mate,
+    fc2_pair,
+    fc2_straight,
+    fc1_mate,
+    fc1_pair,
+    fc1_straight,
+    qkv_mate,
+    qkv_pair,
+    qkv_straight,
+    out_mate,
+    out_pair,
+    out_straight,
+    slot_sums,
+    mods_own,
+    mods_sibling,
+    mods_pair,
+    mods_partner,
+    mods_low,
+    mods_cols,
+    bias_all,
+    silu_part,
+    silu_in,
+    silu_all,
+    small_send,
+    small_recv,
+    pair_send,
+    pair_recv,
+    head_send,
+    head_recv,
+    weight_send,
+    weight_recv,
+):
+    row, member, sibling, partner, opposite = places()
+    greet(range(1, ROW_PARTS), (sibling, partner))
+    others = [(step, lax.rem(row + step, ROW_PARTS)) for step in range(1, ROW_PARTS)]
+
+    def spread(stage, source_of, target):
+        copies = []
+        for step, other in others:
+            copy = to_row(
+                source_of(other),
+                target.at[row],
+                small_send.at[stage, step - 1],
+                small_recv.at[stage, step - 1],
+                other,
+            )
+            copy.start()
+            copies.append(copy)
+        return copies
+
+    def settle(copies):
+        for copy in copies:
+            copy.wait()
+
+    reduce_rows = HeadReduce(hidden_ref, beside_in, pair_rows, across_in, head_send, head_recv)
+    reduce_rows.start()
+    units = []
+    for partial, mate, pair, straight, total, chunks in (
+        (fc2_part, fc2_mate, fc2_pair, fc2_straight, fc2_grad, BACK_CHUNKS[0]),
+        (fc1_part, fc1_mate, fc1_pair, fc1_straight, fc1_grad, BACK_CHUNKS[1]),
+        (qkv_part, qkv_mate, qkv_pair, qkv_straight, qkv_grad, BACK_CHUNKS[2]),
+        (out_part, out_mate, out_pair, out_straight, out_grad, BACK_CHUNKS[3]),
+    ):
+        size = total.shape[0] // chunks
+        for chunk in range(chunks):
+            place = len(units)
+            units.append(
+                RowReduce(
+                    partial,
+                    mate,
+                    pair,
+                    straight,
+                    total,
+                    pl.ds(chunk * size, size),
+                    weight_send.at[place],
+                    weight_recv.at[place],
+                )
+            )
+
+    units[0].start()
+    units[1].start()
+
+    def advance(place):
+        units[place].send_pair()
+        if place + 2 < len(units):
+            units[place + 2].start()
+        if place > 0:
+            units[place - 1].finish()
+
+    reduce_rows.send_pair()
+    advance(0)
+    reduce_rows.settle()
+    tok_rows = patches_ref.shape[0]
+    model_width = patches_ref.shape[1]
+    parts_count = 6
+    slot_sums[...] = jnp.zeros_like(slot_sums)
+
+    def rows_back(block, carry):
+        part = pl.ds(pl.multiple_of(block * 128, 128), 128)
+        grad = reduce_rows.rows(part)
+        values = patches_ref[part].astype(jnp.float32)
+        centred = values - jnp.mean(values, axis=1, keepdims=True)
+        factor = lax.rsqrt(jnp.mean(centred * centred, axis=1, keepdims=True) + EPSILON)
+        normed = centred * factor
+        weighted = grad * scale_ref[part]
+        patches_grad[part] = after_ref[part] + factor * (
+            weighted
+            - jnp.mean(weighted, axis=1, keepdims=True)
+            - normed * jnp.mean(weighted * normed, axis=1, keepdims=True)
+        )
+        hot = hot_ref[:, part]
+        slot_sums[0] += jnp.dot(hot, grad, precision=HIGH, preferred_element_type=jnp.float32)
+        slot_sums[1] += jnp.dot(
+            hot, grad * normed, precision=HIGH, preferred_element_type=jnp.float32
+        )
+        return carry
+
+    lax.fori_loop(0, tok_rows // 128, rows_back, 0)
+    ada_width = ada_ref.shape[1]
+    fine = ada_width // 3
+    for unit in range(3 * ROW_PARTS):
+        part_index, within = divmod(unit * fine, model_width)
+        source = (
+            slot_sums[part_index, :, within : within + fine]
+            if part_index < 2
+            else sums_ref[part_index - 2, :, within : within + fine]
+        )
+        mods_own[unit // 3, :, unit % 3 * fine : (unit % 3 + 1) * fine] = source
+    beside = to_head(mods_own, mods_sibling, pair_send.at[0], pair_recv.at[0], sibling)
+    beside.start()
+    advance(1)
+    beside.wait()
+    mods_pair[...] = mods_own[...] + mods_sibling[...]
+    across = to_head(mods_pair, mods_partner, pair_send.at[1], pair_recv.at[1], partner)
+    across.start()
+    across.wait()
+    mods_low[...] = (
+        (mods_pair[...] + mods_partner[...]).astype(jnp.bfloat16).astype(jnp.float32)
+    )
+    copies = spread(0, lambda other: mods_low.at[other], mods_cols)
+    bias_copies = spread(1, lambda other: bias_ref, bias_all)
+    mods_cols[row] = mods_low[row]
+    bias_all[row] = bias_ref[...]
+    advance(2)
+    advance(3)
+    settle(copies)
+    slots = ROW_PARTS * SLOT_ROWS
+    cols = mods_cols[...].reshape(slots, ada_width)
+    low = cols.astype(jnp.bfloat16)
+    ada_grad[...] = jnp.dot(silu_ref[...], low, preferred_element_type=jnp.float32)
+    ada_bias[...] = jnp.broadcast_to(jnp.sum(cols, axis=0, keepdims=True), ada_bias.shape)
+    silu_part[...] = times_transposed(low, ada_ref[...]).reshape(silu_part.shape)
+    copies = spread(2, lambda other: silu_part.at[other], silu_in)
+    silu_in[row] = silu_part[row]
+    settle(bias_copies)
+    bias_sum[...] = jnp.sum(bias_all[...], axis=0)
+    advance(4)
+    advance(5)
+    settle(copies)
+    summed = jnp.sum(silu_in[...], axis=0)
+    silu_all[row] = summed
+    silu_part[row] = summed
+    copies = spread(3, lambda other: silu_part.at[row], silu_all)
+    advance(6)
+    advance(7)
+    settle(copies)
+    grad_condition = silu_all[...].reshape(slots, silu_all.shape[2]) * slope_ref[...]
+    time_grad[...] = jnp.dot(
+        bucket_ref[...], grad_condition, precision=HIGH, preferred_element_type=jnp.float32
+    )
+    class_grad[...] = jnp.dot(
+        label_ref[...], grad_condition, precision=HIGH, preferred_element_type=jnp.float32
+    )
+    advance(8)
+    advance(9)
+    units[9].finish()
+    reduce_rows.finish()
+
+
+def back(
+    hidden,
+    grad_w_fc2,
+    grad_w_fc1,
+    grad_w_qkv,
+    grad_w_out,
+    biases,
+    patches,
+    grad_after,
+    scales,
+    hot,
+    sums,
+    silu_columns,
+    slopes,
+    buckets,
+    labels,
+    w_ada,
+):
+    shape = jax.ShapeDtypeStruct
+    tok_rows, model_width = patches.shape
+    depth, ada_width = w_ada.shape
+    table_rows = buckets.shape[0]
+    weights = (grad_w_fc2, grad_w_fc1, grad_w_qkv, grad_w_out)
+    totals = [shape(weight.shape[2:], jnp.float32) for weight in weights]
+    landing = []
+    for weight in weights:
+        size = weight.shape[2:]
+        landing += [
+            pltpu.VMEM((4,) + size, jnp.bfloat16),
+            pltpu.VMEM((4,) + size, jnp.bfloat16),
+            pltpu.VMEM((3,) + size, jnp.bfloat16),
+        ]
+    slotted = (ROW_PARTS, SLOT_ROWS)
+    wide = pltpu.VMEM(slotted + (ada_width,), jnp.float32)
+    narrow = pltpu.VMEM(slotted + (depth,), jnp.float32)
+    unit_count = sum(BACK_CHUNKS)
+    return pl.pallas_call(
+        back_kernel,
+        out_shape=[
+            shape((tok_rows, model_width), jnp.float32),
+            shape((table_rows, depth), jnp.float32),
+            shape((table_rows, depth), jnp.float32),
+            shape((depth, ada_width), jnp.float32),
+            shape((SLOT_ROWS, ada_width), jnp.float32),
+        ]
+        + totals
+        + [shape(biases.shape, jnp.float32)],
+        in_specs=[VMEM_SPEC] * 16,
+        out_specs=[VMEM_SPEC] * 10,
+        scratch_shapes=[
+            pltpu.VMEM((2, tok_rows, model_width), jnp.bfloat16),
+            pltpu.VMEM((tok_rows, model_width), jnp.bfloat16),
+            pltpu.VMEM((tok_rows, model_width), jnp.bfloat16),
+        ]
+        + landing
+        + [pltpu.VMEM((2, SLOT_ROWS, model_width), jnp.float32)]
+        + [wide] * 6
+        + [pltpu.VMEM((ROW_PARTS,) + biases.shape, jnp.float32)]
+        + [narrow] * 3
+        + [
+            DMA((4, 7)),
+            DMA((4, 7)),
+            DMA((2,)),
+            DMA((2,)),
+            DMA((3,)),
+            DMA((3,)),
+            DMA((unit_count, 4)),
+            DMA((unit_count, 4)),
+        ],
+        compiler_params=pltpu.CompilerParams(
+            collective_id=1, has_side_effects=True, vmem_limit_bytes=GRANT
+        ),
+        name="back",
+    )(
+        hidden,
+        *weights,
+        biases,
+        patches,
+        grad_after,
+        scales,
+        hot,
+        sums,
+        silu_columns,
+        slopes,
+        buckets,
+        labels,
+        w_ada,
+    )
 
 
 def shards_linked(
@@ -727,7 +1138,7 @@
         jnp.concatenate([bucket_ids[0], slot_pad, class_labels[0], slot_pad])[:, None],
         (2 * SLOT_ROWS, table_rows),
     )
-    qkv_full, out_full, patches_full, condition, mods = front(
+    qkv_full, out_full, patches_full, condition, mods, ids_all = front(
         ids, time_table, class_table, w_ada, patches, w_qkv, w_out
     )
     qkv_cols = qkv_full.reshape(model_width, w_qkv.shape[1])
@@ -748,14 +1159,13 @@
         return chosen
 
     own_segments = lax.dynamic_slice_in_dim(segment_ids[0], member * tok_rows, tok_rows)[:, None]
-    token_hot = (own_segments == jnp.arange(slot_count, dtype=jnp.int32)[None, :]).astype(
+    token_hot = (own_segments == jnp.arange(SLOT_ROWS, dtype=jnp.int32)[None, :]).astype(
         jnp.float32
     )
     shift_attn, scale_attn, gate_attn, shift_mlp, scale_mlp, gate_mlp = (
         by_token(part_index, own_segments) for part_index in range(6)
     )
     inputs = patches.astype(jnp.float32)
-    _, first_pull = jax.vjp(modulate, inputs, shift_attn, scale_attn)
     rows_one = modulate(
         patches_full.reshape(group_rows, model_width).astype(jnp.float32),
         by_token(0, row_segments),
@@ -908,64 +1318,59 @@
     grad_w_qkv = contract_rows(rows_one, grad_qkv)
     bias_terms = jnp.sum(grad_qkv, axis=0, dtype=jnp.float32).reshape(head_local, 3, head_size)
     grad_b_qv = jnp.concatenate([bias_terms[:, 0], bias_terms[:, 2]], axis=1)
-    grad_hidden_one = lax.psum_scatter(
-        times_transposed(
-            lax.slice_in_dim(grad_qkv, 0, tok_rows * lax.axis_size("heads"), axis=0), qkv_cols
-        ).astype(jnp.bfloat16),
-        "heads",
-        scatter_dimension=0,
-        tiled=True,
-    ).astype(jnp.float32)
-    grad_inputs, grad_shift_attn, grad_scale_attn = first_pull(grad_hidden_one)
-    grad_patches = grad_inputs + grad_after
-    token_grads = (
-        grad_shift_attn,
-        grad_scale_attn,
-        grad_gate_attn,
-        grad_shift_mlp,
-        grad_scale_mlp,
-        grad_gate_mlp,
-    )
-    mods_grad_part = jnp.concatenate(
-        [contract_rows_exact(token_hot, grad_term) for grad_term in token_grads], axis=1
-    )
-    grad_mods = lax.psum(mods_grad_part.astype(jnp.bfloat16), "heads")
-    grad_cols = lax.all_to_all(
-        jnp.pad(
-            grad_mods.reshape(slot_count, row_parts, ada_width).transpose(1, 0, 2),
-            ((0, 0), (0, SLOT_ROWS - slot_count), (0, 0)),
-        ),
-        "rows",
-        split_axis=0,
-        concat_axis=0,
-        tiled=True,
-    ).reshape(every_slot, ada_width)
-    grad_w_ada = contract_rows(silu_low, grad_cols)
-    grad_b_ada = jnp.sum(grad_cols, axis=0, dtype=jnp.float32)
-    grad_silu = lax.psum(times_transposed(grad_cols, w_ada), "rows")
-    grad_condition = silu_pull(grad_silu)[0]
-    ids_all = lax.all_gather(ids[:, 0], "rows", axis=0)
+    grad_hidden_one = times_transposed(grad_qkv, qkv_cols).astype(jnp.bfloat16)
+    sums = jnp.stack(
+        [
+            contract_rows_exact(token_hot, grad_term)
+            for grad_term in (grad_gate_attn, grad_shift_mlp, grad_scale_mlp, grad_gate_mlp)
+        ]
+    )
+    all_ids = ids_all[:, :, 0]
     table_places = lax.axis_index("rows") * table_rows + jnp.arange(table_rows, dtype=jnp.int32)
-    bucket_hot = ids_all[:, :SLOT_ROWS].reshape(every_slot)[:, None] == table_places[None, :]
-    label_hot = ids_all[:, SLOT_ROWS:].reshape(every_slot)[:, None] == table_places[None, :]
-    grad_time = contract_rows_exact(bucket_hot.astype(jnp.float32), grad_condition)
-    grad_class = contract_rows_exact(label_hot.astype(jnp.float32), grad_condition)
-
-    def row_reduced(partial):
-        return lax.psum_scatter(
-            partial.astype(jnp.bfloat16), "rows", scatter_dimension=0, tiled=True
-        ).astype(jnp.float32)
-
-    grad_w_qkv, grad_w_out, grad_w_fc1, grad_w_fc2 = (
-        row_reduced(grad_w_qkv),
-        row_reduced(grad_w_out),
-        row_reduced(grad_w_fc1),
-        row_reduced(grad_w_fc2),
-    )
+    bucket_hot = table_places[:, None] == all_ids[:, :SLOT_ROWS].reshape(every_slot)[None, :]
+    label_hot = table_places[:, None] == all_ids[:, SLOT_ROWS:].reshape(every_slot)[None, :]
+    bias_flat = jnp.concatenate([grad_b_qv.reshape(-1), grad_b_fc1, grad_b_out, grad_b_fc2])
+    bias_size = bias_flat.size
+    bias_tiles = -(-bias_size // 1024) * 8
+    biases = jnp.pad(bias_flat, (0, bias_tiles * 128 - bias_size)).reshape(bias_tiles, 128)
+
+    def by_row(partial):
+        return partial.astype(jnp.bfloat16).reshape(
+            4, 2, partial.shape[0] // ROW_PARTS, partial.shape[1]
+        )
+
+    (
+        grad_patches,
+        grad_time,
+        grad_class,
+        grad_w_ada,
+        grad_b_ada,
+        grad_w_fc2,
+        grad_w_fc1,
+        grad_w_qkv,
+        grad_w_out,
+        bias_all,
+    ) = back(
+        grad_hidden_one.reshape(HEAD_PARTS, tok_rows, model_width),
+        by_row(grad_w_fc2),
+        by_row(grad_w_fc1),
+        by_row(grad_w_qkv),
+        by_row(grad_w_out),
+        biases,
+        patches,
+        grad_after,
+        1.0 + scale_attn,
+        token_hot.T,
+        sums,
+        silu_low.T,
+        silu_pull(jnp.ones_like(condition))[0],
+        bucket_hot.astype(jnp.float32),
+        label_hot.astype(jnp.float32),
+        w_ada,
+    )
+    grad_b_ada = grad_b_ada[0]
+    bias_all = bias_all.reshape(-1)
     bias_sizes = (grad_b_qv.size, grad_b_fc1.size, grad_b_out.size, grad_b_fc2.size)
-    bias_all = lax.psum(
-        jnp.concatenate([grad_b_qv.reshape(-1), grad_b_fc1, grad_b_out, grad_b_fc2]), "rows"
-    )
     edges = [sum(bias_sizes[:step]) for step in range(5)]
     bias_rows = model_width // row_parts
     row_start = lax.axis_index("rows") * bias_rows

time: 828 us -> 597 us (0.72)
  waiting for transfers between devices: 448 us -> 210 us
  Pallas kernels: 78.8 us -> 202 us
  blocking collectives: 57.4 us -> 0 us
  matrix products: 118 us -> 88 us
  other arithmetic: 66.3 us -> 39 us
    reduce_scatter x5 -> x0, waiting for transfers between devices: 172 us -> none  [the longest x4 139 us: row_reduced(): lax.psum_scatter(partial.astype(jnp.bfloat16), 'rows', scatter_dimension=...]
    pallas_call x0 -> x1, Pallas kernels: none -> 123 us  [back(): pl.pallas_call(back_kernel, out_shape=[shape((tok_rows, model_width), jnp...]
    psum x1 -> x0, waiting for transfers between devices: 63.5 us -> none  [shards_linked(): grad_silu = lax.psum(times_transposed(grad_cols, w_ada), 'rows')]
    psum x2 -> x0, blocking collectives: 46.3 us -> none  [the longest x1 35.6 us: shards_linked(): lax.psum(jnp.concatenate([grad_b_qv.reshape(-1), grad_b_fc1, grad_b_out,...]
    unnamed x1 -> x0, blocking collectives: 11.1 us -> none
    dot_general x8 -> x4, matrix products: 11.3 us -> 2.35 us  [contract_rows_exact(): lax.dot_general(left_matrix, right_matrix, (((0,), (0,)), ((), ())), prec...]
    convert_element_type x5 -> x2, other arithmetic: 9.86 us -> 1.33 us  [the longest x1 0.73 us: shards_linked(): label_hot.astype(jnp.float32)]
    dot_general x5 -> x4, matrix products: 23.8 us -> 16.2 us  [contract_rows(): lax.dot_general(left_matrix, right_matrix, (((0,), (0,)), ((), ())), pref...]
  transfers between devices with their start and end apart: 15 -> 8, of which waited for: 14 -> 8; matrix products, arithmetic and copies ran while one was open for 15% -> 7% of each run, Pallas kernels for 0% -> 0%
where the time goes in v3:
time: 597 us; the launch traced here: 593 us
  waiting for transfers between devices  210 us (35%)
  Pallas kernels  202 us (34%)
  matrix products  88 us (15%)
  other arithmetic  39 us (7%)
  local copies, waits for them, and re-layouts  36.9 us (6%)
  between operations  16.4 us (3%)
    pallas_call x1, Pallas kernels, back(): pl.pallas_call(back_kernel, out_shape=[shape((tok_rows, model_width), jnp...  123 us
    pallas_call x1, Pallas kernels, front(): pl.pallas_call(front_kernel, out_shape=(shape((ROW_PARTS,) + w_qkv.shape,...  78.8 us
    all_gather x1, waiting for transfers between devices, shards_linked(): fc2_cols = lax.all_gather(w_fc2, 'rows', axis=0, tiled=True)  48.9 us
    reduce_scatter x1, waiting for transfers between devices, shards_linked(): lax.psum_scatter(times_transposed(lax.slice_in_dim(active, 0, tok_rows *...  33.7 us
    reduce_scatter x1, waiting for transfers between devices, shards_linked(): lax.psum_scatter(times_transposed(lax.slice_in_dim(mixed_rows, 0, tok_row...  31.1 us
    all_gather x1, waiting for transfers between devices, shards_linked(): ffn_rows = lax.all_gather(grad_ffn, 'heads', axis=0, tiled=True)  24.7 us
    all_gather x1, waiting for transfers between devices, shards_linked(): rows_two = lax.all_gather(hidden_two, 'heads', axis=0, tiled=True)  24.5 us
    unnamed x98, local copies, waits for them, and re-layouts  21.4 us
  transfers between devices with their start and end apart: 8, of which 8 were waited for; matrix products, arithmetic and copies ran while one was open for 7% of the time, Pallas kernels for 0%

profile of v3, /device:TPU:0, one launch (start us, length us, event | category | flops | bytes accessed | tf_op | source)
XLA Modules:
  0.0 593.1 jit_solution(3292333065397555969)
XLA Ops:
  8.8 1.6 copy.84.time_ref
  10.4 1.6 copy.85.class_ref
  13.5 78.8 %front.1 = (bf16[8,144,864]{2,1,0:T(8,128)(2,1)}, bf16[8,144,288]{2,1,0:T(8,128)(2,1)}, bf16[4,256,1152]{2,1,0:T(8,128)(2,1)}, f32[8,8,288]{2,1,0:T(8,128)}, f32...) custom-call(s32[16,128]{1,0:T(8,128)} %broadcast_in_dim.415.ids_ref, bf16[128,288]{1,0:T(8,128)(2,1)} %copy.84.time_ref, ...), custom_call_target="tpu_custom_call" | custom-call | tf_op jit(solution)/shard_map/front/pallas_call | solution.py:647
  92.3 1.1 slice_bitcast_fusion.16
  94.6 2.0 convert_reduce_fusion
  98.2 9.0 %fusion.9 = bf16[4,256,1152]{2,1,0:T(8,128)(2,1)S(1)} fusion(bf16[4,256,1152]{2,1,0:T(8,128)(2,1)S(1)} %copy-done.2, f32[1152]{0:T(1024)S(1)} %get-tuple-element.161, f32[1152]{0:T(1024)S(1)} %get-tuple-element.162, f32[1152]{0:T(1024)S(1)} %get-tuple-element.163, f32[1152]{0:T(1024)S(1)} %get-tuple-element.164, f32[1152]{0:T(1024)S(1)} %get-tuple-element.165, ...), kind=kLoop, calls=%fused_computation.29 | loop fusion | flops 15335424 | bytes 4766720 | tf_op jit(solution)/shard_map/convert_element_type | solution.py:1173
  107.2 2.5 add_convert_fusion
  109.7 1.9 fusion.76
  111.7 1.9 fusion.1
  113.5 1.4 copy-done
  114.9 2.1 fusion.45
  117.0 1.9 fusion.77
  119.0 1.9 fusion
  120.8 1.3 copy-done.1
  122.2 2.6 fusion.44
  125.6 3.0 convolution_convert_fusion.3
  129.3 31.1 %reduce-scatter.4.cloned.1.call-done = bf16[256,1152]{1,0:T(8,128)(2,1)} async-done(((bf16[1024,1152]{1,0:T(8,128)(2,1)}), bf16[256,1152]{1,0:T(8,128)(2,1)}) %reduce-scatter.4.cloned.1.call-update) | async-done | bytes 589840 | tf_op jit(solution)/shard_map/reduce_scatter | solution.py:1219
  160.4 2.8 fusion.70
  163.5 2.1 select_add_fusion
  166.9 18.0 %all-gather.8.cloned.1.call-done = bf16[1152,1152]{1,0:T(8,128)(2,1)} async-done(((bf16[144,1152]{1,0:T(8,128)(2,1)}), bf16[1152,1152]{1,0:T(8,128)(2,1)}) %all-gather.8.cloned.1.call-update) | async-done | bytes 2654224 | tf_op jit(solution)/shard_map/all_gather | solution.py:1133
  185.0 24.5 %all-gather.6.cloned.1.call-done = bf16[1024,1152]{1,0:T(8,128)(2,1)} async-done(((bf16[256,1152]{1,0:T(8,128)(2,1)}), bf16[1024,1152]{1,0:T(8,128)(2,1)}) %all-gather.6.cloned.1.call-update) | async-done | bytes 2359312 | tf_op jit(solution)/shard_map/all_gather | solution.py:1230
  209.5 8.1 %convolution_add_fusion = f32[1024,1152]{1,0:T(8,128)} fusion(bf16[1024,1152]{1,0:T(8,128)(2,1)} %all-gather.6.cloned.1.call-done, bf16[1152,1152]{1,0:T(8,128)(2,1)} %all-gather.8.cloned.1.call-done, f32[1152]{0:T(1024)S(1)} %convert_element_type.212), kind=kOutput, calls=%fused_computation.40 | convolution fusion | flops 2719088640 | bytes 9736704 | tf_op jit(solution)/shard_map/dot_general | solution.py:1231
  217.6 48.9 %all-gather.10.cloned.1.call-done = bf16[1152,1152]{1,0:T(8,128)(2,1)} async-done(((bf16[144,1152]{1,0:T(8,128)(2,1)}), bf16[1152,1152]{1,0:T(8,128)(2,1)}) %all-gather.10.cloned.1.call-update) | async-done | bytes 2654224 | tf_op jit(solution)/shard_map/all_gather | solution.py:1134
  266.4 24.7 %all-gather.12.cloned.1.call-done = bf16[1024,1152]{1,0:T(8,128)(2,1)} async-done(((bf16[256,1152]{1,0:T(8,128)(2,1)}), bf16[1024,1152]{1,0:T(8,128)(2,1)}) %all-gather.12.cloned.1.call-update) | async-done | bytes 2359312 | tf_op jit(solution)/shard_map/all_gather | solution.py:1247
  291.1 9.2 %convert_reduce_fusion.3 = (f32[1152]{0:T(1024)S(1)}, bf16[1024,1152]{1,0:T(8,128)(2,1)S(1)}) fusion(f32[1024,1152]{1,0:T(8,128)} %convolution_add_fusion, bf16[1024,1152]{1,0:T(8,128)(2,1)} %all-gather.12.cloned.1.call-done, bf16[1152,1152]{1,0:T(8,128)(2,1)} %all-gather.10.cloned.1.call-done), kind=kOutput, calls=%fused_computation.38 | convolution fusion | flops 2748578816 | bytes 12096000 | tf_op jit(solution)/shard_map/dot_general | solution.py:1250
  300.4 1.4 copy-done.37
  301.7 4.8 convolution_convert_fusion.4
  306.6 8.8 %convolution_convert_fusion.5 = bf16[1024,1152]{1,0:T(8,128)(2,1)} fusion(bf16[1152,1152]{1,0:T(8,128)(2,1)} %all-gather.10.cloned.1.call-done, f32[1024,1152]{1,0:T(8,128)} %convolution_add_fusion), kind=kOutput, calls=%fused_computation.50 | convolution fusion | flops 2729705472 | bytes 9732096 | tf_op jit(solution)/shard_map/dot_general | solution.py:56
  318.2 21.3 %reduce-scatter.8.cloned.1.call-done = bf16[256,1152]{1,0:T(8,128)(2,1)} async-done(((bf16[1024,1152]{1,0:T(8,128)(2,1)}), bf16[256,1152]{1,0:T(8,128)(2,1)}) %reduce-scatter.8.cloned.1.call-update) | async-done | bytes 589840 | tf_op jit(solution)/shard_map/reduce_scatter | solution.py:1254
  339.6 1.6 multiply_reduce_fusion.2
  341.2 33.7 %reduce-scatter.6.cloned.1.call-done = bf16[256,1152]{1,0:T(8,128)(2,1)} async-done(((bf16[1024,1152]{1,0:T(8,128)(2,1)}), bf16[256,1152]{1,0:T(8,128)(2,1)}) %reduce-scatter.6.cloned.1.call-update) | async-done | bytes 589840 | tf_op jit(solution)/shard_map/reduce_scatter | solution.py:1236
  374.9 3.1 fusion.69
  378.0 1.7 multiply_convert_fusion.3
  381.1 2.2 convert_reduce_fusion.1
  383.3 6.6 %convolution_convert_fusion = bf16[1152,1152]{1,0:T(8,128)(2,1)} fusion(bf16[1024,1152]{1,0:T(8,128)(2,1)S(1)} %copy-done.32, bf16[1024,1152]{1,0:T(8,128)(2,1)} %copy-done.37), kind=kOutput, calls=%fused_computation.12 | convolution fusion | flops 2719236096 | bytes 7372800 | tf_op jit(solution)/shard_map/dot_general | solution.py:40
  390.0 4.9 convolution_convert_fusion.1
  397.9 6.0 %all-gather.14.cloned.1.call-done = bf16[1024,1152]{1,0:T(8,128)(2,1)} async-done(((bf16[256,1152]{1,0:T(8,128)(2,1)}), bf16[1024,1152]{1,0:T(8,128)(2,1)}) %all-gather.14.cloned.1.call-update) | async-done | bytes 2359312 | tf_op jit(solution)/shard_map/all_gather | solution.py:1267
  403.9 3.1 convolution_convert_fusion.8
  407.1 5.1 multiply_reduce_fusion.1
  412.1 1.0 slice-done.3
  413.2 1.7 multiply_convert_fusion.1
  414.9 2.6 fusion.43
  417.5 0.9 fusion.54
  418.4 1.7 fusion.16
  420.2 2.6 multiply_reduce_fusion
  422.8 1.8 fusion.33
  424.5 1.7 multiply_convert_fusion
  426.3 1.4 fusion.42
  427.7 0.9 fusion.32
  429.2 1.5 copy-done.13
  430.7 3.7 convolution_convert_fusion.6
  434.4 4.5 convolution_convert_fusion.2
  438.9 0.9 convolution_convert_fusion.7
  439.9 1.2 copy.93
  442.4 4.1 copy.92
  446.5 123.5 %back.1 = (f32[256,1152]{1,0:T(8,128)}, f32[128,288]{1,0:T(8,128)}, f32[128,288]{1,0:T(8,128)}, f32[288,864]{1,0:T(8,128)}, f32[8,864]{1,0:T(8,128)}, /*index=5*...) custom-call(bf16[4,256,1152]{2,1,0:T(8,128)(2,1)} %bitcast.172, ...), custom_call_target="tpu_custom_call" | custom-call | tf_op jit(solution)/shard_map/back/pallas_call | solution.py:1043
  570.7 1.5 fusion.72
  572.2 1.4 slice_reduce_fusion.25
  575.5 1.7 copy.97
  577.2 1.8 copy.98
  579.0 2.4 copy.109
  581.4 1.0 copy.110
  583.8 0.8 copy.113
  584.7 0.8 copy.114
  (170 shorter events, 21.3 us)
Async XLA Ops:
  8.0 85.9 %copy-start.30 = (bf16[4,144]{1,0:T(4,128)(2,1)S(1)}, bf16[4,144]{1,0:T(4,128)(2,1)}, u32[]{:S(2)}) copy-start(bf16[4,144]{1,0:T(4,128)(2,1)} %param.24) | copy-start | bytes 3460
  8.0 86.2 %copy-start.26 = (s32[1,1024]{1,0:T(1,128)S(1)}, s32[1,1024]{1,0:T(1,128)}, u32[]{:S(2)}) copy-start(s32[1,1024]{1,0:T(1,128)} %param.32) | copy-start | bytes 12292
  8.0 86.3 %copy-start.36 = (s32[1,4]{1,0:T(1,128)S(1)}, s32[1,4]{1,0:T(1,128)}, u32[]{:S(2)}) copy-start(s32[1,4]{1,0:T(1,128)} %param.31) | copy-start | bytes 52
  8.0 152.3 %reduce-scatter.4.cloned.1.call-start = ((), (), s32[]{:S(2)}) async-start(), calls=%async_computation.3 | async-start | bytes 2949120 | tf_op jit(solution)/shard_map/reduce_scatter | solution.py:1219
  92.3 4.4 copy-start.2
  98.1 9.0 %copy-start.33 = (bf16[8,144,864]{2,1,0:T(8,128)(2,1)S(1)}, bf16[8,144,864]{2,1,0:T(8,128)(2,1)}, u32[]{:S(2)}) copy-start(bf16[8,144,864]{2,1,0:T(8,128)(2,1)} %get-tuple-element.65) | copy-start | bytes 5971972
  107.2 2.6 copy-start.12
  109.7 11.1 %copy-start.5 = (bf16[1024,864]{0,1:T(8,128)(2,1)}, bf16[1024,864]{0,1:T(8,128)(2,1)S(1)}, u32[]{:S(2)}) copy-start(bf16[1024,864]{0,1:T(8,128)(2,1)S(1)} %add_convert_fusion) | copy-start | bytes 5308420
  111.7 3.2 copy-start
  118.9 3.2 copy-start.1
  122.2 3.5 copy-start.35
  124.8 0.8 copy-start.20
  128.6 0.7 copy-start.27
  128.6 31.8 %copy-start.8 = (bf16[256,1152]{1,0:T(8,128)(2,1)S(1)}, bf16[256,1152]{1,0:T(8,128)(2,1)}, u32[]{:S(2)}) copy-start(bf16[256,1152]{1,0:T(8,128)(2,1)} %patches_ref.3) | copy-start | bytes 1769476
  128.6 31.8 %copy-start.9 = (bf16[256,1152]{1,0:T(8,128)(2,1)S(1)}, bf16[256,1152]{1,0:T(8,128)(2,1)}, u32[]{:S(2)}) copy-start(bf16[256,1152]{1,0:T(8,128)(2,1)} %param.35) | copy-start | bytes 1769476
  128.6 56.4 %all-gather.8.cloned.1.call-start = ((), (), s32[]{:S(2)}) async-start(), calls=%async_computation.5 | async-start | bytes 2985984 | tf_op jit(solution)/shard_map/all_gather | solution.py:1133
  129.2 80.3 %all-gather.6.cloned.1.call-start = ((), (), s32[]{:S(2)}) async-start(), calls=%async_computation.4 | async-start | bytes 2949120 | tf_op jit(solution)/shard_map/all_gather | solution.py:1230
  163.4 3.5 copy-start.28
  165.5 100.9 %all-gather.10.cloned.1.call-start = ((), (), s32[]{:S(2)}) async-start(), calls=%async_computation.6 | async-start | bytes 2985984 | tf_op jit(solution)/shard_map/all_gather | solution.py:1134
  166.1 125.0 %all-gather.12.cloned.1.call-start = ((), (), s32[]{:S(2)}) async-start(), calls=%async_computation.8 | async-start | bytes 2949120 | tf_op jit(solution)/shard_map/all_gather | solution.py:1247
  166.9 172.7 %reduce-scatter.8.cloned.1.call-start = ((), (), s32[]{:S(2)}) async-start(), calls=%async_computation.9 | async-start | bytes 2949120 | tf_op jit(solution)/shard_map/reduce_scatter | solution.py:1254
  291.1 10.6 %copy-start.31 = (bf16[1152,1152]{1,0:T(8,128)(2,1)S(1)}, bf16[1152,1152]{1,0:T(8,128)(2,1)}, u32[]{:S(2)}) copy-start(bf16[1152,1152]{1,0:T(8,128)(2,1)} %all-gather.8.cloned.1.call-done) | copy-start | bytes 7962628
  300.3 1.4 copy-start.37
  306.6 68.4 %reduce-scatter.6.cloned.1.call-start = ((), (), s32[]{:S(2)}) async-start(), calls=%async_computation.7 | async-start | bytes 2949120 | tf_op jit(solution)/shard_map/reduce_scatter | solution.py:1236
  315.4 0.7 copy-start.29
  315.5 0.9 copy-start.25
  315.5 1.3 copy-start.24
  315.5 88.4 %all-gather.14.cloned.1.call-start = ((), (), s32[]{:S(2)}) async-start(), calls=%async_computation.10 | async-start | bytes 2949120 | tf_op jit(solution)/shard_map/all_gather | solution.py:1267
  341.2 36.8 %copy-start.10 = (bf16[256,1152]{1,0:T(8,128)(2,1)S(1)}, bf16[256,1152]{1,0:T(8,128)(2,1)}, u32[]{:S(2)}) copy-start(bf16[256,1152]{1,0:T(8,128)(2,1)} %param.35) | copy-start | bytes 1769476
  379.7 16.2 %copy-start.3 = (f32[256,1152]{1,0:T(8,128)}, f32[256,1152]{1,0:T(8,128)S(1)}, u32[]{:S(2)}) copy-start(f32[256,1152]{1,0:T(8,128)S(1)} %get-tuple-element.181.after_ref) | copy-start | bytes 3538948
  379.7 3.6 copy-start.32
  381.1 8.9 %slice-start.4 = ((s8[4718592]{0:T(1024)(128)(4,1)}), s8[4194304]{0:T(1024)(128)(4,1)S(1)}, s32[]{:S(2)}) async-start(s8[4718592]{0:T(1024)(128)(4,1)} %bitcast.197), calls=%async_computation.15 | async-start | bytes 8388608
  383.3 6.7 %copy-start.14 = (bf16[1024,1152]{1,0:T(8,128)(2,1)S(1)}, bf16[1024,1152]{1,0:T(8,128)(2,1)}, u32[]{:S(2)}) copy-start(bf16[1024,1152]{1,0:T(8,128)(2,1)} %all-gather.12.cloned.1.call-done) | copy-start | bytes 7077892
  383.3 6.7 %slice-start.5 = ((s8[4718592]{0:T(1024)(128)(4,1)}), s8[524288]{0:T(1024)(128)(4,1)S(1)}, s32[]{:S(2)}) async-start(s8[4718592]{0:T(1024)(128)(4,1)} %bitcast.197), calls=%async_computation.16 | async-start | bytes 1048576
  390.0 4.9 copy-start.4
  390.0 5.2 copy-start.16
  390.0 5.9 copy-start.11
  407.0 5.1 slice-start.2
  407.1 6.1 %slice-start.3 = ((s8[8388608]{0:T(1024)(128)(4,1)}), s8[4194304]{0:T(1024)(128)(4,1)S(1)}, s32[]{:S(2)}) async-start(s8[8388608]{0:T(1024)(128)(4,1)} %bitcast.152), calls=%async_computation.14 | async-start | bytes 8388608
  412.1 6.3 %slice-start = ((s8[8388608]{0:T(1024)(128)(4,1)}), s8[4194304]{0:T(1024)(128)(4,1)S(1)}, s32[]{:S(2)}) async-start(s8[8388608]{0:T(1024)(128)(4,1)} %bitcast.150), calls=%async_computation.11 | async-start | bytes 8388608
  413.2 5.3 slice-start.1
  414.9 2.6 copy-start.6
  424.5 1.8 copy-start.7
  429.0 1.7 copy-start.13
  430.7 3.7 copy-start.34
  434.4 4.5 copy-start.15
  434.4 4.5 copy-start.21
  570.0 11.4 %copy-start.17 = (f32[288,864]{1,0:T(8,128)S(1)}, f32[288,864]{1,0:T(8,128)}, u32[]{:S(2)}) copy-start(f32[288,864]{1,0:T(8,128)} %get-tuple-element.238) | copy-start | bytes 2985988
  577.2 5.1 copy-start.22
  579.0 4.2 copy-start.23
  581.4 2.4 copy-start.19
  581.4 3.3 copy-start.18
Sparse Core Ops, SparseCore 0:
  128.7 31.6 reduce-scatter.3
  306.7 32.8 reduce-scatter.7
  342.1 32.8 reduce-scatter.5
  379.8 24.0 all-gather.13
Sparse Core Ops, SparseCore 1:
  131.3 53.7 all-gather.7
  187.0 22.5 all-gather.5
  211.5 54.8 all-gather.9
  268.6 22.5 all-gather.11

commit v4 on v3

--- a/solution.py
+++ b/solution.py
@@ -474,12 +474,10 @@
             self.straight.append(straight)
             self.across.append(across)
 
-    def start(self):
-        self.own.start()
-        for straight, across in zip(self.straight, self.across):
-            for copy in straight:
-                copy.start()
-            across[0].start()
+    def start(self, chunk):
+        for copy in self.straight[chunk]:
+            copy.start()
+        self.across[chunk][0].start()
 
     def relay(self, chunk):
         for step in range(3):
@@ -498,7 +496,11 @@
 class HeadGather:
     def __init__(self, block, full, sends, recvs, local_sem):
         row, member, sibling, partner, opposite = places()
-        self.own = pltpu.make_async_copy(block, full.at[member], local_sem)
+        self.own = None
+        if block is None:
+            block = full.at[member]
+        else:
+            self.own = pltpu.make_async_copy(block, full.at[member], local_sem)
         self.beside = to_head(block, full.at[member], sends.at[0], recvs.at[0], sibling)
         self.across = to_head(block, full.at[member], sends.at[1], recvs.at[1], partner)
         self.onward = to_head(
@@ -508,7 +510,8 @@
     def start(self):
         self.across.start()
         self.beside.start()
-        self.own.start()
+        if self.own is not None:
+            self.own.start()
 
     def wait_sibling(self):
         self.beside.wait_recv()
@@ -521,7 +524,8 @@
         self.onward.wait_recv()
 
     def finish(self):
-        self.own.wait()
+        if self.own is not None:
+            self.own.wait()
         self.beside.wait_send()
         self.across.wait_send()
         self.onward.wait_send()
@@ -533,11 +537,15 @@
     class_ref,
     ada_ref,
     patches_ref,
+    cotangent_ref,
     qkv_ref,
     out_ref,
+    fc1_ref,
     qkv_full,
     out_full,
+    fc1_full,
     patches_full,
+    cotangent_full,
     cond_all,
     mods_ref,
     ids_all,
@@ -558,6 +566,8 @@
     qkv_recv,
     out_send,
     out_recv,
+    fc1_send,
+    fc1_recv,
     local_sems,
 ):
     row, member, sibling, partner, opposite = places()
@@ -585,10 +595,18 @@
     ids_copies = spread(0, lambda other: ids_ref, ids_all)
     gather_qkv = RowGather(qkv_ref, qkv_full, qkv_send, qkv_recv, local_sems.at[0], 3)
     gather_out = RowGather(out_ref, out_full, out_send, out_recv, local_sems.at[1], 1)
-    gather_patches = HeadGather(patches_ref, patches_full, head_send, head_recv, local_sems.at[2])
-    gather_qkv.start()
-    gather_out.start()
+    gather_fc1 = RowGather(fc1_ref, fc1_full, fc1_send, fc1_recv, local_sems.at[2], 3)
+    gather_patches = HeadGather(
+        patches_ref, patches_full, head_send.at[0], head_recv.at[0], local_sems.at[3]
+    )
+    gather_cotangent = HeadGather(
+        cotangent_ref, cotangent_full, head_send.at[1], head_recv.at[1], local_sems.at[4]
+    )
     gather_patches.start()
+    gather_qkv.own.start()
+    gather_out.own.start()
+    gather_fc1.own.start()
+    gather_qkv.start(0)
     ids_all[row] = ids_ref[...]
     settle(ids_copies)
     table_rows = time_ref.shape[0]
@@ -605,12 +623,14 @@
     )
     cond_part[...] = found.reshape(cond_part.shape)
     copies = spread(1, lambda other: cond_part.at[other], cond_in)
+    gather_qkv.start(1)
     cond_in[row] = cond_part[row]
     settle(copies)
     condition = jnp.sum(cond_in[...], axis=0)
     cond_all[row] = condition
     cond_part[row] = condition
     copies = spread(2, lambda other: cond_part.at[row], cond_all)
+    gather_qkv.relay(0)
     settle(copies)
     every = cond_all[...].reshape(slots, cond_all.shape[2])
     silu_low = (every / (1.0 + jnp.exp(-every))).astype(jnp.bfloat16)
@@ -618,9 +638,11 @@
         silu_low, ada_ref[...], preferred_element_type=jnp.float32
     ).reshape(mods_part.shape)
     copies = spread(3, lambda other: mods_part.at[other], mods_in)
+    gather_qkv.start(2)
     mods_in[row] = mods_part[row]
-    gather_qkv.relay(0)
+    gather_qkv.relay(1)
     settle(copies)
+    gather_out.start(0)
     beside = to_head(mods_in, mods_sibling, pair_send.at[0], pair_recv.at[0], sibling)
     beside.start()
     gather_patches.wait_sibling()
@@ -629,58 +651,70 @@
     across = to_head(mods_pair, mods_partner, pair_send.at[1], pair_recv.at[1], partner)
     across.start()
     gather_patches.wait_partner()
-    gather_qkv.relay(1)
+    gather_cotangent.start()
+    gather_fc1.start(0)
+    gather_qkv.relay(2)
     across.wait()
     mods_ref[...] = mods_pair[...] + mods_partner[...]
     gather_patches.wait_opposite()
-    gather_qkv.relay(2)
+    gather_fc1.start(1)
     gather_out.relay(0)
+    gather_fc1.start(2)
+    gather_fc1.relay(0)
+    gather_cotangent.wait_sibling()
+    gather_cotangent.wait_partner()
+    gather_fc1.relay(1)
+    gather_cotangent.wait_opposite()
+    gather_fc1.relay(2)
     gather_patches.finish()
+    gather_cotangent.finish()
     gather_qkv.finish()
     gather_out.finish()
-
-
-def front(ids, time_table, class_table, w_ada, patches, w_qkv, w_out):
+    gather_fc1.finish()
+
+
+def front(ids, time_table, class_table, w_ada, patches, cotangent, w_qkv, w_out, w_fc1):
     depth, ada_width = w_ada.shape
     shape = jax.ShapeDtypeStruct
     slotted = (ROW_PARTS, SLOT_ROWS)
+    wide = pltpu.VMEM(slotted + (ada_width,), jnp.float32)
+    narrow = pltpu.VMEM(slotted + (depth,), jnp.float32)
     return pl.pallas_call(
         front_kernel,
         out_shape=(
             shape((ROW_PARTS,) + w_qkv.shape, jnp.bfloat16),
             shape((ROW_PARTS,) + w_out.shape, jnp.bfloat16),
+            shape((ROW_PARTS,) + w_fc1.shape, jnp.bfloat16),
+            shape((HEAD_PARTS,) + patches.shape, jnp.bfloat16),
             shape((HEAD_PARTS,) + patches.shape, jnp.bfloat16),
             shape(slotted + (depth,), jnp.float32),
             shape(slotted + (ada_width,), jnp.float32),
             shape((ROW_PARTS,) + ids.shape, jnp.int32),
         ),
-        in_specs=[VMEM_SPEC] * 7,
-        out_specs=(ANY_SPEC, ANY_SPEC, ANY_SPEC, VMEM_SPEC, VMEM_SPEC, VMEM_SPEC),
-        scratch_shapes=[
-            pltpu.VMEM(slotted + (depth,), jnp.float32),
-            pltpu.VMEM(slotted + (depth,), jnp.float32),
-            pltpu.VMEM(slotted + (ada_width,), jnp.float32),
-            pltpu.VMEM(slotted + (ada_width,), jnp.float32),
-            pltpu.VMEM(slotted + (ada_width,), jnp.float32),
-            pltpu.VMEM(slotted + (ada_width,), jnp.float32),
-            pltpu.VMEM(slotted + (ada_width,), jnp.float32),
+        in_specs=[VMEM_SPEC] * 9,
+        out_specs=[ANY_SPEC] * 5 + [VMEM_SPEC] * 3,
+        scratch_shapes=[narrow] * 2
+        + [wide] * 5
+        + [
             DMA((4, 7)),
             DMA((4, 7)),
             DMA((2,)),
             DMA((2,)),
-            DMA((3,)),
-            DMA((3,)),
+            DMA((2, 3)),
+            DMA((2, 3)),
             DMA((3, 7)),
             DMA((3, 7)),
             DMA((1, 7)),
             DMA((1, 7)),
-            DMA((3,)),
+            DMA((3, 7)),
+            DMA((3, 7)),
+            DMA((5,)),
         ],
         compiler_params=pltpu.CompilerParams(
             collective_id=0, has_side_effects=True, vmem_limit_bytes=GRANT
         ),
         name="front",
-    )(ids, time_table, class_table, w_ada, patches, w_qkv, w_out)
+    )(ids, time_table, class_table, w_ada, patches, cotangent, w_qkv, w_out, w_fc1)
 
 
 class HeadReduce:
@@ -730,31 +764,26 @@
 
 
 class RowReduce:
-    def __init__(self, partial, mate_in, pair, straight_in, total, part, sends, recvs):
+    def __init__(self, partial, chunk, buffers, total, sends, recvs):
         row = lax.axis_index("rows")
         self.level = row // 2
         self.side = lax.rem(row, 2)
         mate = row + 1 - 2 * self.side
         self.partial = partial
-        self.mate_in = mate_in
-        self.pair = pair
-        self.straight_in = straight_in
+        self.mate_in, self.pair, self.straight_in = buffers
         self.total = total
-        self.part = part
+        size = total.shape[0]
+        self.part = pl.ds(chunk * size, size)
         self.beside = to_row(
-            partial.at[:, 1 - self.side, part],
-            mate_in.at[:, part],
-            sends.at[0],
-            recvs.at[0],
-            mate,
+            partial.at[:, 1 - self.side, self.part], self.mate_in, sends.at[0], recvs.at[0], mate
         )
         self.straight = []
         for step in range(1, 4):
             target = lax.rem(self.level + step, 4)
             self.straight.append(
                 to_row(
-                    pair.at[target, part],
-                    straight_in.at[step - 1, part],
+                    self.pair.at[target],
+                    self.straight_in.at[step - 1],
                     sends.at[step],
                     recvs.at[step],
                     target * 2 + self.side,
@@ -768,9 +797,9 @@
         self.beside.wait_recv()
 
         def one(level, carry):
-            self.pair[level, self.part] = (
+            self.pair[level] = (
                 self.partial[level, self.side, self.part].astype(jnp.float32)
-                + self.mate_in[level, self.part].astype(jnp.float32)
+                + self.mate_in[level].astype(jnp.float32)
             ).astype(jnp.bfloat16)
             return carry
 
@@ -781,23 +810,504 @@
     def finish(self):
         for copy in self.straight:
             copy.wait_recv()
-        self.total[self.part] = (
-            self.pair[self.level, self.part].astype(jnp.float32)
-            + self.straight_in[0, self.part].astype(jnp.float32)
-            + self.straight_in[1, self.part].astype(jnp.float32)
-            + self.straight_in[2, self.part].astype(jnp.float32)
+        self.total[...] = (
+            self.pair[self.level].astype(jnp.float32)
+            + self.straight_in[0].astype(jnp.float32)
+            + self.straight_in[1].astype(jnp.float32)
+            + self.straight_in[2].astype(jnp.float32)
         )
         self.beside.wait_send()
         for copy in self.straight:
             copy.wait_send()
 
 
-BACK_CHUNKS = (3, 3, 3, 1)
+class Reduces:
+    def __init__(self, jobs, buffers, sends, recvs):
+        self.units = [
+            RowReduce(
+                partial,
+                chunk,
+                buffers[3 * place : 3 * place + 3],
+                total,
+                sends.at[place],
+                recvs.at[place],
+            )
+            for place, (partial, chunk, total) in enumerate(jobs)
+        ]
+        self.done = 0
+
+    def start(self):
+        for unit in self.units[:2]:
+            unit.start()
+
+    def advance(self):
+        place = self.done
+        self.done += 1
+        self.units[place].send_pair()
+        if place + 2 < len(self.units):
+            self.units[place + 2].start()
+        if place > 0:
+            self.units[place - 1].finish()
+
+    def finish(self):
+        while self.done < len(self.units):
+            self.advance()
+        self.units[-1].finish()
+
+
+def reduce_scratch(sizes):
+    landing = []
+    for rows, columns in sizes:
+        landing += [
+            pltpu.VMEM((4, rows, columns), jnp.bfloat16),
+            pltpu.VMEM((4, rows, columns), jnp.bfloat16),
+            pltpu.VMEM((3, rows, columns), jnp.bfloat16),
+        ]
+    return landing + [DMA((len(sizes), 4)), DMA((len(sizes), 4))]
+
+
+def picked(vectors, part_index, segments, width):
+    wide = jnp.broadcast_to(segments, (segments.shape[0], width))
+    slot_count = vectors.shape[1]
+    chosen = vectors[part_index, slot_count - 1 : slot_count]
+    for slot in range(slot_count - 2, -1, -1):
+        chosen = jnp.where(wide == slot, vectors[part_index, slot : slot + 1], chosen)
+    return chosen
+
+
+def centre_rows(values):
+    centred = values - jnp.mean(values, axis=1, keepdims=True)
+    factor = lax.rsqrt(jnp.mean(centred * centred, axis=1, keepdims=True) + EPSILON)
+    return centred * factor, factor
+
+
+def middle_kernel(
+    mixed_ref,
+    out_ref,
+    fc1_ref,
+    fc2_ref,
+    cotangent_ref,
+    patches_ref,
+    segments_ref,
+    hot_ref,
+    vectors_ref,
+    bias_ref,
+    ffn_rows,
+    hidden_rows,
+    active_rows,
+    inner_grad,
+    ffn_part,
+    after_ref,
+    after_grad,
+    attn_grad,
+    slot_sums,
+    inner_bias,
+    fc2_part,
+    fc1_part,
+    fc2_head,
+    fc2_neck,
+    fc2_full,
+    active_grad,
+    first_part,
+    second_part,
+    first_beside,
+    second_beside,
+    first_pair,
+    second_pair,
+    first_across,
+    second_across,
+    attn_out,
+    gather_send,
+    gather_recv,
+    reduce_send,
+    reduce_recv,
+    fc2_send,
+    fc2_recv,
+    local_sem,
+    *reducing,
+):
+    row, member, sibling, partner, opposite = places()
+    greet(range(1, ROW_PARTS), (sibling, partner))
+    tok_rows, model_width = patches_ref.shape
+    gather_fc2 = RowGather(fc2_ref, fc2_full, fc2_send, fc2_recv, local_sem, 3)
+    gather_fc2.own.start()
+    gather_fc2.start(0)
+    gather_fc2.start(1)
+    first = HeadReduce(
+        first_part, first_beside, first_pair, first_across, reduce_send.at[0], reduce_recv.at[0]
+    )
+    second = HeadReduce(
+        second_part,
+        second_beside,
+        second_pair,
+        second_across,
+        reduce_send.at[1],
+        reduce_recv.at[1],
+    )
+    gather_hidden = HeadGather(None, hidden_rows, gather_send.at[0], gather_recv.at[0], None)
+    gather_grad = HeadGather(None, attn_grad, gather_send.at[1], gather_recv.at[1], None)
+
+    def project(block):
+        first_part[block] = times_transposed(mixed_ref[block], out_ref[...]).astype(jnp.bfloat16)
+
+    project(opposite)
+    first.first.start()
+    project(partner)
+    first.send_pair()
+    project(sibling)
+    first.second.start()
+    project(member)
+
+    def scale_cotangent(block, carry):
+        index = block // 2
+        part = pl.ds(pl.multiple_of(lax.rem(block, 2) * 128, 128), 128)
+        ffn_rows[index, part] = (
+            picked(vectors_ref, 5, segments_ref[index, part], model_width)
+            * cotangent_ref[index, part].astype(jnp.float32)
+        ).astype(jnp.bfloat16)
+        return carry
+
+    lax.fori_loop(0, 2 * HEAD_PARTS, scale_cotangent, 0)
+    gather_fc2.relay(0)
+    gather_fc2.start(2)
+    first.settle()
+
+    def second_norm(block, carry):
+        part = pl.ds(pl.multiple_of(block * 128, 128), 128)
+        segments = segments_ref[member, part]
+        out = first.rows(part) + bias_ref[0:1]
+        after = patches_ref[part].astype(jnp.float32) + (
+            picked(vectors_ref, 2, segments, model_width) * out
+        )
+        attn_out[part] = out
+        after_ref[part] = after
+        normed, _ = centre_rows(after)
+        hidden_rows[member, part] = (
+            normed * (1.0 + picked(vectors_ref, 4, segments, model_width))
+            + picked(vectors_ref, 3, segments, model_width)
+        ).astype(jnp.bfloat16)
+        return carry
+
+    lax.fori_loop(0, tok_rows // 128, second_norm, 0)
+    gather_hidden.start()
+    gather_fc2.relay(1)
+    gather_fc2.relay(2)
+    gather_fc2.finish()
+    fc2 = fc2_full.reshape(fc1_ref.shape)
+
+    def through_fc2(block, carry):
+        active_grad[block] = jnp.dot(
+            ffn_rows[block], fc2[...], preferred_element_type=jnp.float32
+        )
+        return carry
+
+    lax.fori_loop(0, HEAD_PARTS, through_fc2, 0)
+    inner_bias[...] = jnp.zeros_like(inner_bias)
+
+    def feed(block, carry):
+        inner = jnp.dot(
+            hidden_rows[block], fc1_ref[...], preferred_element_type=jnp.float32
+        ) + bias_ref[1:2]
+        square = inner * inner
+        bent = jnp.tanh(TANH_COEFF * (inner + 0.044715 * square * inner))
+        half = 0.5 * (1.0 + bent)
+        active_rows[block] = (inner * half).astype(jnp.bfloat16)
+        slope = half + 0.5 * inner * (1.0 - bent * bent) * (
+            TANH_COEFF * (1.0 + 3.0 * 0.044715 * square)
+        )
+        grad = (active_grad[block] * slope).astype(jnp.bfloat16)
+        inner_grad[block] = grad
+        inner_bias[...] += jnp.sum(
+            grad.astype(jnp.float32).reshape(tok_rows // 8, 8, inner.shape[1]), axis=0
+        )
+        return carry
+
+    def return_fc1(block, carry):
+        second_part[block] = times_transposed(inner_grad[block], fc1_ref[...]).astype(jnp.bfloat16)
+        return carry
+
+    direction = sibling - member
+    gather_hidden.wait_sibling()
+    lax.fori_loop(0, 2, lambda step, carry: feed(member + step * direction, carry), 0)
+    gather_hidden.wait_partner()
+    gather_hidden.wait_opposite()
+
+    def feed_far(step, carry):
+        block = opposite - step * direction
+        feed(block, carry)
+        return return_fc1(block, carry)
+
+    lax.fori_loop(0, 2, feed_far, 0)
+    second.first.start()
+    second.send_pair()
+    lax.fori_loop(0, 2, lambda step, carry: return_fc1(sibling - step * direction, carry), 0)
+    second.second.start()
+
+    def forward_fc2(block, carry):
+        ffn_part[block] = times_transposed(active_rows[block], fc2[...]).astype(jnp.bfloat16)
+        return carry
+
+    def weight_grad(left, right, target):
+        height = HEAD_PARTS * tok_rows
+        grad = contract_rows(
+            left[...].reshape(height, left.shape[2]), right[...].reshape(height, right.shape[2])
+        )
+        target[...] = grad.astype(jnp.bfloat16).reshape(target.shape)
+
+    weight_grad(ffn_rows, active_rows, fc2_part)
+    reduces = Reduces(
+        ((fc2_part, 0, fc2_head), (fc2_part, 1, fc2_neck)),
+        reducing[:-2],
+        reducing[-2],
+        reducing[-1],
+    )
+    reduces.start()
+    lax.fori_loop(0, HEAD_PARTS, forward_fc2, 0)
+    slot_sums[...] = jnp.zeros_like(slot_sums)
+    second.settle()
+
+    def second_back(block, carry):
+        part = pl.ds(pl.multiple_of(block * 128, 128), 128)
+        segments = segments_ref[member, part]
+        grad = second.rows(part)
+        normed, factor = centre_rows(after_ref[part])
+        weighted = grad * (1.0 + picked(vectors_ref, 4, segments, model_width))
+        total = cotangent_ref[member, part].astype(jnp.float32) + factor * (
+            weighted
+            - jnp.mean(weighted, axis=1, keepdims=True)
+            - normed * jnp.mean(weighted * normed, axis=1, keepdims=True)
+        )
+        after_grad[part] = total
+        attn_grad[member, part] = (
+            picked(vectors_ref, 2, segments, model_width) * total
+        ).astype(jnp.bfloat16)
+        hot = hot_ref[:, part]
+        for index, term in enumerate((total * attn_out[part], grad, grad * normed)):
+            slot_sums[index] += jnp.dot(
+                hot, term, precision=HIGH, preferred_element_type=jnp.float32
+            )
+        return carry
+
+    lax.fori_loop(0, tok_rows // 128, second_back, 0)
+    gather_grad.start()
+    weight_grad(hidden_rows, inner_grad, fc1_part)
+    reduces.advance()
+    gather_grad.wait_sibling()
+    gather_grad.wait_partner()
+    gather_grad.wait_opposite()
+    reduces.finish()
+    gather_hidden.finish()
+    gather_grad.finish()
+    first.finish()
+    second.finish()
+
+
+def middle(mixed, w_out, w_fc1, w_fc2, cotangent, patches, segments, hot, vectors, biases):
+    shape = jax.ShapeDtypeStruct
+    tok_rows, model_width = patches.shape
+    hidden_width = w_fc1.shape[1]
+    width_part = w_fc2.shape[0]
+    rows_low = shape((HEAD_PARTS, tok_rows, model_width), jnp.bfloat16)
+    wide_low = shape((HEAD_PARTS, tok_rows, hidden_width), jnp.bfloat16)
+    own = shape((tok_rows, model_width), jnp.float32)
+    own_low = pltpu.VMEM((tok_rows, model_width), jnp.bfloat16)
+    group_low = pltpu.VMEM((HEAD_PARTS, tok_rows, model_width), jnp.bfloat16)
+    pair_low = pltpu.VMEM((2, tok_rows, model_width), jnp.bfloat16)
+    return pl.pallas_call(
+        middle_kernel,
+        out_shape=[
+            rows_low,
+            rows_low,
+            wide_low,
+            wide_low,
+            rows_low,
+            own,
+            own,
+            rows_low,
+            shape((3, SLOT_ROWS, model_width), jnp.float32),
+            shape((8, hidden_width), jnp.float32),
+            shape((4, 2, width_part, hidden_width), jnp.bfloat16),
+            shape((4, 2, width_part, hidden_width), jnp.bfloat16),
+            shape((width_part // 3, hidden_width), jnp.float32),
+            shape((width_part // 3, hidden_width), jnp.float32),
+        ],
+        in_specs=[VMEM_SPEC] * 10,
+        out_specs=[VMEM_SPEC] * 14,
+        scratch_shapes=[
+            pltpu.VMEM((ROW_PARTS,) + w_fc2.shape, jnp.bfloat16),
+            pltpu.VMEM((HEAD_PARTS, tok_rows, hidden_width), jnp.float32),
+            group_low,
+            group_low,
+            pair_low,
+            pair_low,
+            own_low,
+            own_low,
+            own_low,
+            own_low,
+            pltpu.VMEM((tok_rows, model_width), jnp.float32),
+            DMA((2, 3)),
+            DMA((2, 3)),
+            DMA((2, 3)),
+            DMA((2, 3)),
+            DMA((3, 7)),
+            DMA((3, 7)),
+            DMA(()),
+        ]
+        + reduce_scratch([(width_part // 3, hidden_width)] * 2),
+        compiler_params=pltpu.CompilerParams(
+            collective_id=2, has_side_effects=True, vmem_limit_bytes=GRANT
+        ),
+        name="middle",
+    )(mixed, w_out, w_fc1, w_fc2, cotangent, patches, segments, hot, vectors, biases)
+
+
+HEAD_LANES = 128
+
+
+def attend_back_kernel(
+    projected_ref,
+    grad_ref,
+    out_ref,
+    totals_ref,
+    keys_image,
+    rows_image,
+    fc2_part,
+    fc1_part,
+    qkv_grad,
+    fc2_tail,
+    fc1_head,
+    fc1_neck,
+    parts,
+    mixed_grad,
+    key_columns,
+    grad_queries,
+    grad_keys,
+    grad_values,
+    bias,
+    packed,
+    *reducing,
+):
+    greet(range(1, ROW_PARTS), ())
+    reduces = Reduces(
+        ((fc2_part, 2, fc2_tail), (fc1_part, 0, fc1_head), (fc1_part, 1, fc1_neck)),
+        reducing[:-2],
+        reducing[-2],
+        reducing[-1],
+    )
+    reduces.start()
+    blocks, tok_rows, width = projected_ref.shape
+    head_local = totals_ref.shape[0]
+    head_size = width // (3 * head_local)
+    scale_factor = 1.0 / math.sqrt(head_size)
+    parts[...] = jnp.zeros_like(parts)
+    mixed_grad[...] = jnp.zeros_like(mixed_grad)
+
+    def unpack(block, carry):
+        rows = pl.ds(pl.multiple_of(block * tok_rows, tok_rows), tok_rows)
+        packed[...] = projected_ref[block].astype(jnp.float32)
+        for part in range(3 * head_local):
+            parts[part, rows, 0:head_size] = packed[
+                :, part * head_size : (part + 1) * head_size
+            ].astype(jnp.bfloat16)
+        packed[:, 0 : head_local * head_size] = jnp.dot(
+            grad_ref[block], out_ref[...], preferred_element_type=jnp.float32
+        )
+        for head in range(head_local):
+            mixed_grad[head, rows, 0:head_size] = packed[
+                :, head * head_size : (head + 1) * head_size
+            ].astype(jnp.bfloat16)
+        return carry
+
+    lax.fori_loop(0, blocks, unpack, 0)
+
+    def turn(head, carry):
+        key_columns[head] = parts[3 * head + 1].astype(jnp.float32).T.astype(jnp.bfloat16)
+        return carry
+
+    lax.fori_loop(0, head_local, turn, 0)
+    grad_keys[...] = jnp.zeros_like(grad_keys)
+    grad_values[...] = jnp.zeros_like(grad_values)
+    seq_len = blocks * tok_rows
+
+    for block in range(blocks):
+        rows = pl.ds(block * tok_rows, tok_rows)
+        same = jnp.broadcast_to(keys_image[...], (seq_len, tok_rows)) == jnp.broadcast_to(
+            rows_image[block], (seq_len, tok_rows)
+        )
+        bias[...] = jnp.where(same, 0.0, MASKED)
+
+        def one_head(head, carry):
+            query = parts[3 * head, rows]
+            grad = mixed_grad[head, rows]
+            scores = times_transposed(parts[3 * head + 1], query) * scale_factor + bias[...]
+            probs = jnp.exp(scores - totals_ref[head, block])
+            grad_probs = times_transposed(parts[3 * head + 2], grad)
+            inner = jnp.sum(probs * grad_probs, axis=0, keepdims=True)
+            grad_scores = (probs * (grad_probs - inner)).astype(jnp.bfloat16)
+            grad_values[head] += jnp.dot(
+                probs.astype(jnp.bfloat16), grad, preferred_element_type=jnp.float32
+            )
+            grad_keys[head] += jnp.dot(grad_scores, query, preferred_element_type=jnp.float32)
+            grad_queries[head, rows] = jnp.dot(
+                key_columns[head], grad_scores, preferred_element_type=jnp.float32
+            ).T
+            return carry
+
+        lax.fori_loop(0, head_local, one_head, 0)
+        if block > 0:
+            reduces.advance()
+
+    def pack(block, carry):
+        rows = pl.ds(pl.multiple_of(block * tok_rows, tok_rows), tok_rows)
+        for head in range(head_local):
+            for place, (grads, factor) in enumerate(
+                ((grad_queries, scale_factor), (grad_keys, scale_factor), (grad_values, None))
+            ):
+                start = (3 * head + place) * head_size
+                term = grads[head, rows, 0:head_size]
+                packed[:, start : start + head_size] = term if factor is None else term * factor
+        qkv_grad[block] = packed[...].astype(jnp.bfloat16)
+        return carry
+
+    lax.fori_loop(0, blocks, pack, 0)
+    reduces.finish()
+
+
+def attend_back(
+    projected, grad, w_out, totals, keys_image, rows_image, grad_w_fc2, grad_w_fc1
+):
+    shape = jax.ShapeDtypeStruct
+    blocks, tok_rows, width = projected.shape
+    head_local = totals.shape[0]
+    seq_len = blocks * tok_rows
+    width_part, hidden_width = grad_w_fc2.shape[2:]
+    third = (width_part // 3, hidden_width)
+    wide = pltpu.VMEM((head_local, seq_len, HEAD_LANES), jnp.float32)
+    return pl.pallas_call(
+        attend_back_kernel,
+        out_shape=[shape(projected.shape, jnp.bfloat16)] + [shape(third, jnp.float32)] * 3,
+        in_specs=[VMEM_SPEC] * 8,
+        out_specs=[VMEM_SPEC] * 4,
+        scratch_shapes=[
+            pltpu.VMEM((3 * head_local, seq_len, HEAD_LANES), jnp.bfloat16),
+            pltpu.VMEM((head_local, seq_len, HEAD_LANES), jnp.bfloat16),
+            pltpu.VMEM((head_local, HEAD_LANES, seq_len), jnp.bfloat16),
+            wide,
+            wide,
+            wide,
+            pltpu.VMEM((seq_len, tok_rows), jnp.float32),
+            pltpu.VMEM((tok_rows, width), jnp.float32),
+        ]
+        + reduce_scratch([third] * 3),
+        compiler_params=pltpu.CompilerParams(
+            collective_id=3, has_side_effects=True, vmem_limit_bytes=GRANT
+        ),
+        name="attend_back",
+    )(projected, grad, w_out, totals, keys_image, rows_image, grad_w_fc2, grad_w_fc1)
 
 
 def back_kernel(
     hidden_ref,
-    fc2_part,
     fc1_part,
     qkv_part,
     out_part,
@@ -812,31 +1322,29 @@
     bucket_ref,
     label_ref,
     ada_ref,
+    ffn_ref,
+    block_ref,
+    gate_ref,
+    cotangent_ref,
+    ffn_bias,
+    block_out,
     patches_grad,
     time_grad,
     class_grad,
     ada_grad,
     ada_bias,
-    fc2_grad,
-    fc1_grad,
-    qkv_grad,
+    fc1_tail,
+    qkv_head,
+    qkv_neck,
+    qkv_tail,
     out_grad,
     bias_sum,
     beside_in,
     pair_rows,
     across_in,
-    fc2_mate,
-    fc2_pair,
-    fc2_straight,
-    fc1_mate,
-    fc1_pair,
-    fc1_straight,
-    qkv_mate,
-    qkv_pair,
-    qkv_straight,
-    out_mate,
-    out_pair,
-    out_straight,
+    ffn_beside,
+    ffn_pair,
+    ffn_across,
     slot_sums,
     mods_own,
     mods_sibling,
@@ -854,8 +1362,7 @@
     pair_recv,
     head_send,
     head_recv,
-    weight_send,
-    weight_recv,
+    *reducing,
 ):
     row, member, sibling, partner, opposite = places()
     greet(range(1, ROW_PARTS), (sibling, partner))
@@ -879,56 +1386,39 @@
         for copy in copies:
             copy.wait()
 
-    reduce_rows = HeadReduce(hidden_ref, beside_in, pair_rows, across_in, head_send, head_recv)
+    reduce_rows = HeadReduce(
+        hidden_ref, beside_in, pair_rows, across_in, head_send.at[0], head_recv.at[0]
+    )
+    reduce_ffn = HeadReduce(
+        ffn_ref, ffn_beside, ffn_pair, ffn_across, head_send.at[1], head_recv.at[1]
+    )
     reduce_rows.start()
-    units = []
-    for partial, mate, pair, straight, total, chunks in (
-        (fc2_part, fc2_mate, fc2_pair, fc2_straight, fc2_grad, BACK_CHUNKS[0]),
-        (fc1_part, fc1_mate, fc1_pair, fc1_straight, fc1_grad, BACK_CHUNKS[1]),
-        (qkv_part, qkv_mate, qkv_pair, qkv_straight, qkv_grad, BACK_CHUNKS[2]),
-        (out_part, out_mate, out_pair, out_straight, out_grad, BACK_CHUNKS[3]),
-    ):
-        size = total.shape[0] // chunks
-        for chunk in range(chunks):
-            place = len(units)
-            units.append(
-                RowReduce(
-                    partial,
-                    mate,
-                    pair,
-                    straight,
-                    total,
-                    pl.ds(chunk * size, size),
-                    weight_send.at[place],
-                    weight_recv.at[place],
-                )
-            )
-
-    units[0].start()
-    units[1].start()
-
-    def advance(place):
-        units[place].send_pair()
-        if place + 2 < len(units):
-            units[place + 2].start()
-        if place > 0:
-            units[place - 1].finish()
-
+    reduce_ffn.start()
+    reduces = Reduces(
+        (
+            (fc1_part, 2, fc1_tail),
+            (qkv_part, 0, qkv_head),
+            (qkv_part, 1, qkv_neck),
+            (qkv_part, 2, qkv_tail),
+            (out_part, 0, out_grad),
+        ),
+        reducing[:-2],
+        reducing[-2],
+        reducing[-1],
+    )
+    reduces.start()
     reduce_rows.send_pair()
-    advance(0)
+    reduce_ffn.send_pair()
+    reduces.advance()
     reduce_rows.settle()
     tok_rows = patches_ref.shape[0]
     model_width = patches_ref.shape[1]
-    parts_count = 6
     slot_sums[...] = jnp.zeros_like(slot_sums)
 
     def rows_back(block, carry):
         part = pl.ds(pl.multiple_of(block * 128, 128), 128)
         grad = reduce_rows.rows(part)
-        values = patches_ref[part].astype(jnp.float32)
-        centred = values - jnp.mean(values, axis=1, keepdims=True)
-        factor = lax.rsqrt(jnp.mean(centred * centred, axis=1, keepdims=True) + EPSILON)
-        normed = centred * factor
+        normed, factor = centre_rows(patches_ref[part].astype(jnp.float32))
         weighted = grad * scale_ref[part]
         patches_grad[part] = after_ref[part] + factor * (
             weighted
@@ -943,19 +1433,36 @@
         return carry
 
     lax.fori_loop(0, tok_rows // 128, rows_back, 0)
+    reduce_ffn.settle()
+
+    def rows_out(block, carry):
+        part = pl.ds(pl.multiple_of(block * 128, 128), 128)
+        ffn = reduce_ffn.rows(part) + ffn_bias[0:1]
+        block_out[part] = (block_ref[part] + gate_ref[part] * ffn).astype(jnp.bfloat16)
+        slot_sums[2] += jnp.dot(
+            hot_ref[:, part],
+            cotangent_ref[part].astype(jnp.float32) * ffn,
+            precision=HIGH,
+            preferred_element_type=jnp.float32,
+        )
+        return carry
+
+    lax.fori_loop(0, tok_rows // 128, rows_out, 0)
     ada_width = ada_ref.shape[1]
     fine = ada_width // 3
     for unit in range(3 * ROW_PARTS):
         part_index, within = divmod(unit * fine, model_width)
-        source = (
-            slot_sums[part_index, :, within : within + fine]
-            if part_index < 2
-            else sums_ref[part_index - 2, :, within : within + fine]
-        )
+        span = slice(within, within + fine)
+        if part_index < 2:
+            source = slot_sums[part_index, :, span]
+        elif part_index == 5:
+            source = slot_sums[2, :, span]
+        else:
+            source = sums_ref[part_index - 2, :, span]
         mods_own[unit // 3, :, unit % 3 * fine : (unit % 3 + 1) * fine] = source
     beside = to_head(mods_own, mods_sibling, pair_send.at[0], pair_recv.at[0], sibling)
     beside.start()
-    advance(1)
+    reduces.advance()
     beside.wait()
     mods_pair[...] = mods_own[...] + mods_sibling[...]
     across = to_head(mods_pair, mods_partner, pair_send.at[1], pair_recv.at[1], partner)
@@ -968,8 +1475,6 @@
     bias_copies = spread(1, lambda other: bias_ref, bias_all)
     mods_cols[row] = mods_low[row]
     bias_all[row] = bias_ref[...]
-    advance(2)
-    advance(3)
     settle(copies)
     slots = ROW_PARTS * SLOT_ROWS
     cols = mods_cols[...].reshape(slots, ada_width)
@@ -981,15 +1486,13 @@
     silu_in[row] = silu_part[row]
     settle(bias_copies)
     bias_sum[...] = jnp.sum(bias_all[...], axis=0)
-    advance(4)
-    advance(5)
+    reduces.advance()
     settle(copies)
     summed = jnp.sum(silu_in[...], axis=0)
     silu_all[row] = summed
     silu_part[row] = summed
     copies = spread(3, lambda other: silu_part.at[row], silu_all)
-    advance(6)
-    advance(7)
+    reduces.advance()
     settle(copies)
     grad_condition = silu_all[...].reshape(slots, silu_all.shape[2]) * slope_ref[...]
     time_grad[...] = jnp.dot(
@@ -998,15 +1501,13 @@
     class_grad[...] = jnp.dot(
         label_ref[...], grad_condition, precision=HIGH, preferred_element_type=jnp.float32
     )
-    advance(8)
-    advance(9)
-    units[9].finish()
+    reduces.finish()
     reduce_rows.finish()
+    reduce_ffn.finish()
 
 
 def back(
     hidden,
-    grad_w_fc2,
     grad_w_fc1,
     grad_w_qkv,
     grad_w_out,
@@ -1021,28 +1522,27 @@
     buckets,
     labels,
     w_ada,
+    ffn,
+    after,
+    gates,
+    cotangent,
+    ffn_bias,
 ):
     shape = jax.ShapeDtypeStruct
     tok_rows, model_width = patches.shape
     depth, ada_width = w_ada.shape
     table_rows = buckets.shape[0]
-    weights = (grad_w_fc2, grad_w_fc1, grad_w_qkv, grad_w_out)
-    totals = [shape(weight.shape[2:], jnp.float32) for weight in weights]
-    landing = []
-    for weight in weights:
-        size = weight.shape[2:]
-        landing += [
-            pltpu.VMEM((4,) + size, jnp.bfloat16),
-            pltpu.VMEM((4,) + size, jnp.bfloat16),
-            pltpu.VMEM((3,) + size, jnp.bfloat16),
-        ]
+    weights = (grad_w_fc1, grad_w_qkv, grad_w_out)
+    thirds = [(weight.shape[2] // 3, weight.shape[3]) for weight in (grad_w_fc1, grad_w_qkv)]
+    sizes = [thirds[0]] + [thirds[1]] * 3 + [grad_w_out.shape[2:]]
+    totals = [shape(size, jnp.float32) for size in sizes]
     slotted = (ROW_PARTS, SLOT_ROWS)
     wide = pltpu.VMEM(slotted + (ada_width,), jnp.float32)
     narrow = pltpu.VMEM(slotted + (depth,), jnp.float32)
-    unit_count = sum(BACK_CHUNKS)
     return pl.pallas_call(
         back_kernel,
         out_shape=[
+            shape((tok_rows, model_width), jnp.bfloat16),
             shape((tok_rows, model_width), jnp.float32),
             shape((table_rows, depth), jnp.float32),
             shape((table_rows, depth), jnp.float32),
@@ -1051,15 +1551,15 @@
         ]
         + totals
         + [shape(biases.shape, jnp.float32)],
-        in_specs=[VMEM_SPEC] * 16,
-        out_specs=[VMEM_SPEC] * 10,
+        in_specs=[VMEM_SPEC] * 20,
+        out_specs=[VMEM_SPEC] * 12,
         scratch_shapes=[
             pltpu.VMEM((2, tok_rows, model_width), jnp.bfloat16),
             pltpu.VMEM((tok_rows, model_width), jnp.bfloat16),
             pltpu.VMEM((tok_rows, model_width), jnp.bfloat16),
         ]
-        + landing
-        + [pltpu.VMEM((2, SLOT_ROWS, model_width), jnp.float32)]
+        * 2
+        + [pltpu.VMEM((3, SLOT_ROWS, model_width), jnp.float32)]
         + [wide] * 6
         + [pltpu.VMEM((ROW_PARTS,) + biases.shape, jnp.float32)]
         + [narrow] * 3
@@ -1068,11 +1568,10 @@
             DMA((4, 7)),
             DMA((2,)),
             DMA((2,)),
-            DMA((3,)),
-            DMA((3,)),
-            DMA((unit_count, 4)),
-            DMA((unit_count, 4)),
-        ],
+            DMA((2, 3)),
+            DMA((2, 3)),
+        ]
+        + reduce_scratch(sizes),
         compiler_params=pltpu.CompilerParams(
             collective_id=1, has_side_effects=True, vmem_limit_bytes=GRANT
         ),
@@ -1091,6 +1590,11 @@
         buckets,
         labels,
         w_ada,
+        ffn,
+        after,
+        gates,
+        cotangent,
+        ffn_bias,
     )
 
 
@@ -1130,19 +1634,25 @@
     row_parts = lax.axis_size("rows")
     table_rows = time_table.shape[0]
     ada_width = w_ada.shape[1]
-    fc1_cols = lax.all_gather(w_fc1, "rows", axis=0, tiled=True)
-    fc2_cols = lax.all_gather(w_fc2, "rows", axis=0, tiled=True)
     every_slot = row_parts * SLOT_ROWS
     slot_pad = jnp.full((SLOT_ROWS - slot_count,), -1, jnp.int32)
     ids = jnp.broadcast_to(
         jnp.concatenate([bucket_ids[0], slot_pad, class_labels[0], slot_pad])[:, None],
         (2 * SLOT_ROWS, table_rows),
     )
-    qkv_full, out_full, patches_full, condition, mods, ids_all = front(
-        ids, time_table, class_table, w_ada, patches, w_qkv, w_out
-    )
+    (
+        qkv_full,
+        out_full,
+        fc1_full,
+        patches_full,
+        cotangent_full,
+        condition,
+        mods,
+        ids_all,
+    ) = front(ids, time_table, class_table, w_ada, patches, cotangent, w_qkv, w_out, w_fc1)
     qkv_cols = qkv_full.reshape(model_width, w_qkv.shape[1])
     out_cols = out_full.reshape(model_width, w_out.shape[1])
+    fc1_cols = fc1_full.reshape(model_width, w_fc1.shape[1])
     condition = condition.reshape(every_slot, condition.shape[2])
     silu_value, silu_pull = jax.vjp(silu_plain, condition)
     silu_low = silu_value.astype(jnp.bfloat16)
@@ -1162,10 +1672,8 @@
     token_hot = (own_segments == jnp.arange(SLOT_ROWS, dtype=jnp.int32)[None, :]).astype(
         jnp.float32
     )
-    shift_attn, scale_attn, gate_attn, shift_mlp, scale_mlp, gate_mlp = (
-        by_token(part_index, own_segments) for part_index in range(6)
-    )
-    inputs = patches.astype(jnp.float32)
+    scale_attn = by_token(1, own_segments)
+    gate_mlp = by_token(5, own_segments)
     rows_one = modulate(
         patches_full.reshape(group_rows, model_width).astype(jnp.float32),
         by_token(0, row_segments),
@@ -1216,115 +1724,54 @@
 
     mixed, log_totals = lax.map(attend_forward, (seq_qkv, image_of))
     mixed_rows = mixed.reshape(group_rows, head_local * head_size)
-    attn_out = lax.psum_scatter(
-        times_transposed(
-            lax.slice_in_dim(mixed_rows, 0, tok_rows * lax.axis_size("heads"), axis=0), out_cols
-        ).astype(jnp.bfloat16),
-        "heads",
-        scatter_dimension=0,
-        tiled=True,
-    ).astype(jnp.float32) + b_out.astype(jnp.float32)
-    after_attn = inputs + gate_attn * attn_out
-    second_value, second_pull = jax.vjp(modulate, after_attn, shift_mlp, scale_mlp)
-    hidden_two = second_value.astype(jnp.bfloat16)
-    rows_two = lax.all_gather(hidden_two, "heads", axis=0, tiled=True)
-    inner = jnp.dot(rows_two, fc1_cols, preferred_element_type=jnp.float32) + b_fc1.astype(
-        jnp.float32
-    )
-    gelu_value, gelu_pull = jax.vjp(gelu_tanh, inner)
-    active = gelu_value.astype(jnp.bfloat16)
-    ffn_out = lax.psum_scatter(
-        times_transposed(
-            lax.slice_in_dim(active, 0, tok_rows * lax.axis_size("heads"), axis=0), fc2_cols
-        ).astype(jnp.bfloat16),
-        "heads",
-        scatter_dimension=0,
-        tiled=True,
-    ).astype(jnp.float32) + b_fc2.astype(jnp.float32)
-    block_out = (after_attn + gate_mlp * ffn_out).astype(jnp.bfloat16)
-    upstream = cotangent.astype(jnp.float32)
-    grad_ffn = (gate_mlp * upstream).astype(jnp.bfloat16)
-    ffn_rows = lax.all_gather(grad_ffn, "heads", axis=0, tiled=True)
-    grad_w_fc2 = contract_rows(ffn_rows, active)
+    (
+        ffn_rows,
+        rows_two,
+        active,
+        grad_inner,
+        ffn_part,
+        after_attn,
+        grad_after,
+        attn_rows_grad,
+        sums,
+        inner_bias,
+        grad_w_fc2,
+        grad_w_fc1,
+        fc2_head,
+        fc2_neck,
+    ) = middle(
+        mixed_rows.reshape(head_parts, tok_rows, mixed_rows.shape[1]),
+        out_cols,
+        fc1_cols,
+        w_fc2,
+        cotangent_full,
+        patches,
+        segment_ids.reshape(head_parts, tok_rows, 1),
+        token_hot.T,
+        mods_all.reshape(slot_count, 6, model_width).transpose(1, 0, 2),
+        jnp.stack([b_out, b_fc1]).astype(jnp.float32),
+    )
+    ffn_rows = ffn_rows.reshape(group_rows, model_width)
     grad_b_fc2 = jnp.sum(ffn_rows, axis=0, dtype=jnp.float32)
-    grad_active = jnp.dot(ffn_rows, fc2_cols, preferred_element_type=jnp.float32)
-    grad_inner = gelu_pull(grad_active)[0].astype(jnp.bfloat16)
-    grad_w_fc1 = contract_rows(rows_two, grad_inner)
-    grad_b_fc1 = jnp.sum(grad_inner, axis=0, dtype=jnp.float32)
-    grad_hidden_two = lax.psum_scatter(
-        times_transposed(
-            lax.slice_in_dim(grad_inner, 0, tok_rows * lax.axis_size("heads"), axis=0), fc1_cols
-        ).astype(jnp.bfloat16),
-        "heads",
-        scatter_dimension=0,
-        tiled=True,
-    ).astype(jnp.float32)
-    grad_after, grad_shift_mlp, grad_scale_mlp = second_pull(grad_hidden_two)
-    grad_after = grad_after + upstream
-    grad_gate_mlp = upstream * ffn_out
-    grad_gate_attn = grad_after * attn_out
-    grad_attn = (gate_attn * grad_after).astype(jnp.bfloat16)
-    attn_rows_grad = lax.all_gather(grad_attn, "heads", axis=0, tiled=True)
+    grad_b_fc1 = jnp.sum(inner_bias, axis=0)
+    grad_qkv, fc2_tail, fc1_head, fc1_neck = attend_back(
+        projected.reshape(head_parts, tok_rows, projected.shape[1]),
+        attn_rows_grad,
+        out_cols,
+        log_totals.reshape(head_local, head_parts, 1, tok_rows),
+        image_of.reshape(seq_len, 1),
+        image_of.reshape(head_parts, 1, tok_rows),
+        grad_w_fc2,
+        grad_w_fc1,
+    )
+    grad_qkv = grad_qkv.reshape(group_rows, head_local * 3 * head_size)
+    attn_rows_grad = attn_rows_grad.reshape(group_rows, model_width)
     grad_w_out = contract_rows(attn_rows_grad, mixed_rows)
     grad_b_out = jnp.sum(attn_rows_grad, axis=0, dtype=jnp.float32)
-    grad_mixed = jnp.dot(attn_rows_grad, out_cols, preferred_element_type=jnp.float32).astype(
-        jnp.bfloat16
-    )
-    grad_seq = grad_mixed.reshape(seq_count, seq_len, head_local, head_size)
-
-    def attend_backward(pieces):
-        seq_block, seq_image, seq_grad, seq_totals = pieces
-        key_rows = seq_block[:, :, 1]
-        value_rows = seq_block[:, :, 2]
-        grad_keys = jnp.zeros(key_rows.shape, jnp.float32)
-        grad_values = jnp.zeros(value_rows.shape, jnp.float32)
-        grad_queries = []
-        for row_start in range(0, seq_len, block_rows):
-            stop_row = row_start + block_rows
-            query_rows = seq_block[row_start:stop_row, :, 0]
-            grad_rows = seq_grad[row_start:stop_row]
-            scores = block_scores(query_rows, key_rows, seq_image[row_start:stop_row], seq_image)
-            soft_probs = jnp.exp(scores - seq_totals[:, row_start:stop_row, None])
-            grad_probs = jnp.einsum(
-                "qhd,khd->hqk", grad_rows, value_rows, preferred_element_type=jnp.float32
-            )
-            inner_sum = jnp.sum(soft_probs * grad_probs, axis=2, keepdims=True)
-            grad_scores = (soft_probs * (grad_probs - inner_sum)).astype(jnp.bfloat16)
-            grad_queries.append(
-                jnp.einsum(
-                    "hqk,khd->qhd", grad_scores, key_rows, preferred_element_type=jnp.float32
-                )
-                * scale_factor
-            )
-            grad_keys = (
-                grad_keys
-                + jnp.einsum(
-                    "hqk,qhd->khd", grad_scores, query_rows, preferred_element_type=jnp.float32
-                )
-                * scale_factor
-            )
-            grad_values = grad_values + jnp.einsum(
-                "hqk,qhd->khd",
-                soft_probs.astype(jnp.bfloat16),
-                grad_rows,
-                preferred_element_type=jnp.float32,
-            )
-        stacked = jnp.stack([jnp.concatenate(grad_queries, axis=0), grad_keys, grad_values], axis=2)
-        return stacked.astype(jnp.bfloat16)
-
-    grad_qkv = lax.map(attend_backward, (seq_qkv, image_of, grad_seq, log_totals)).reshape(
-        group_rows, head_local * 3 * head_size
-    )
     grad_w_qkv = contract_rows(rows_one, grad_qkv)
     bias_terms = jnp.sum(grad_qkv, axis=0, dtype=jnp.float32).reshape(head_local, 3, head_size)
     grad_b_qv = jnp.concatenate([bias_terms[:, 0], bias_terms[:, 2]], axis=1)
     grad_hidden_one = times_transposed(grad_qkv, qkv_cols).astype(jnp.bfloat16)
-    sums = jnp.stack(
-        [
-            contract_rows_exact(token_hot, grad_term)
-            for grad_term in (grad_gate_attn, grad_shift_mlp, grad_scale_mlp, grad_gate_mlp)
-        ]
-    )
     all_ids = ids_all[:, :, 0]
     table_places = lax.axis_index("rows") * table_rows + jnp.arange(table_rows, dtype=jnp.int32)
     bucket_hot = table_places[:, None] == all_ids[:, :SLOT_ROWS].reshape(every_slot)[None, :]
@@ -1340,20 +1787,21 @@
         )
 
     (
+        block_out,
         grad_patches,
         grad_time,
         grad_class,
         grad_w_ada,
         grad_b_ada,
-        grad_w_fc2,
-        grad_w_fc1,
-        grad_w_qkv,
+        fc1_tail,
+        qkv_head,
+        qkv_neck,
+        qkv_tail,
         grad_w_out,
         bias_all,
     ) = back(
         grad_hidden_one.reshape(HEAD_PARTS, tok_rows, model_width),
-        by_row(grad_w_fc2),
-        by_row(grad_w_fc1),
+        grad_w_fc1,
         by_row(grad_w_qkv),
         by_row(grad_w_out),
         biases,
@@ -1367,7 +1815,15 @@
         bucket_hot.astype(jnp.float32),
         label_hot.astype(jnp.float32),
         w_ada,
-    )
+        ffn_part,
+        after_attn,
+        gate_mlp,
+        cotangent,
+        b_fc2.astype(jnp.float32)[None, :],
+    )
+    grad_w_fc2 = jnp.concatenate([fc2_head, fc2_neck, fc2_tail], axis=0)
+    grad_w_fc1 = jnp.concatenate([fc1_head, fc1_neck, fc1_tail], axis=0)
+    grad_w_qkv = jnp.concatenate([qkv_head, qkv_neck, qkv_tail], axis=0)
     grad_b_ada = grad_b_ada[0]
     bias_all = bias_all.reshape(-1)
     bias_sizes = (grad_b_qv.size, grad_b_fc1.size, grad_b_out.size, grad_b_fc2.size)

time: 597 us -> 444 us (0.74)
  waiting for transfers between devices: 210 us -> 0 us
  Pallas kernels: 202 us -> 343 us
  matrix products: 88 us -> 29.6 us
  between operations: 16.4 us -> 1.36 us
    pallas_call x0 -> x2, Pallas kernels: none -> 163 us  [the longest x1 112 us: middle(): pl.pallas_call(middle_kernel, out_shape=[rows_low, rows_low, wide_low, wi...]
    all_gather x5 -> x0, waiting for transfers between devices: 122 us -> none  [the longest x1 48.9 us: shards_linked(): fc2_cols = lax.all_gather(w_fc2, 'rows', axis=0, tiled=True)]
    reduce_scatter x3 -> x0, waiting for transfers between devices: 86.1 us -> none  [the longest x1 33.7 us: shards_linked(): lax.psum_scatter(times_transposed(lax.slice_in_dim(active, 0, tok_rows *...]
    dot_general x15 -> x0, matrix products: 39.7 us -> none  [the longest x1 9.23 us: shards_linked(): jnp.dot(ffn_rows, fc2_cols, preferred_element_type=jnp.float32)]
    pallas_call x1, Pallas kernels: 123 us -> 91.1 us  [back(): pl.pallas_call(back_kernel, out_shape=[shape((tok_rows, model_width), jnp...]
    dot_general x4 -> x1, matrix products: 21.1 us -> 6.43 us  [times_transposed(): lax.dot_general(left_matrix, right_matrix, (((1,), (1,)), ((), ())), pref...]
    unnamed x98 -> x63, local copies, waits for them, and re-layouts: 21.4 us -> 10.5 us
    pallas_call x1, Pallas kernels: 78.8 us -> 88.7 us  [front(): pl.pallas_call(front_kernel, out_shape=(shape((ROW_PARTS,) + w_qkv.shape,...]
  transfers between devices with their start and end apart: 8 -> 0, of which waited for: 8 -> 0; matrix products, arithmetic and copies ran while one was open for 7% -> 0% of each run, Pallas kernels for 0% -> 0%
where the time goes in v4:
time: 444 us; the launch traced here: 441 us
  Pallas kernels  343 us (77%)
  other arithmetic  36 us (8%)
  local copies, waits for them, and re-layouts  31.1 us (7%)
  matrix products  29.6 us (7%)
    pallas_call x1, Pallas kernels, middle(): pl.pallas_call(middle_kernel, out_shape=[rows_low, rows_low, wide_low, wi...  112 us
    pallas_call x1, Pallas kernels, back(): pl.pallas_call(back_kernel, out_shape=[shape((tok_rows, model_width), jnp...  91.1 us
    pallas_call x1, Pallas kernels, front(): pl.pallas_call(front_kernel, out_shape=(shape((ROW_PARTS,) + w_qkv.shape,...  88.7 us
    pallas_call x1, Pallas kernels, attend_back(): pl.pallas_call(attend_back_kernel, out_shape=[shape(projected.shape, jnp....  50.8 us
    unnamed x63, local copies, waits for them, and re-layouts  10.5 us
    convert_element_type x1, other arithmetic, shards_linked(): rows_one = modulate(patches_full.reshape(group_rows, model_width).astype(...  9.68 us

profile of v4, /device:TPU:0, one launch (start us, length us, event | category | flops | bytes accessed | tf_op | source)
XLA Modules:
  0.0 440.7 jit_solution(12741984748015169592)
XLA Ops:
  0.7 1.6 copy.87.time_ref
  2.3 1.6 copy.88.class_ref
  3.9 0.7 pad_add_fusion
  4.7 0.7 broadcast_in_dim.257.ids_ref
  5.3 88.7 %front.1 = (bf16[8,144,864]{2,1,0:T(8,128)(2,1)}, bf16[8,144,288]{2,1,0:T(8,128)(2,1)}, bf16[8,144,1152]{2,1,0:T(8,128)(2,1)}, bf16[4,256,1152]{2,1,0:T(8,128)(2...) custom-call(s32[16,128]{1,0:T(8,128)} %broadcast_in_dim.257.ids_ref, ...), custom_call_target="tpu_custom_call" | custom-call | tf_op jit(solution)/shard_map/front/pallas_call | solution.py:682
  94.1 1.1 slice_bitcast_fusion.10
  95.2 0.1 reshape.523
  95.4 0.1 slice_reduce_fusion.4
  95.6 2.1 convert_reduce_fusion
  97.6 0.8 fusion.6
  98.5 9.7 %fusion.9 = bf16[4,256,1152]{2,1,0:T(8,128)(2,1)} fusion(bf16[4,256,1152]{2,1,0:T(8,128)(2,1)S(1)} %copy-done, f32[1152]{0:T(1024)S(1)} %get-tuple-element.159, f32[1152]{0:T(1024)S(1)} %get-tuple-element.160, f32[1152]{0:T(1024)S(1)} %get-tuple-element.161, f32[1152]{0:T(1024)S(1)} %get-tuple-element.162, f32[1152]{0:T(1024)S(1)} %get-tuple-element.163, ...), kind=kLoop, calls=%fused_computation.17 | loop fusion | flops 15335424 | bytes 4766720 | tf_op jit(solution)/shard_map/convert_element_type | solution.py:1681
  108.5 4.8 %add_convert_fusion = bf16[1024,864]{0,1:T(8,128)(2,1)S(1)} fusion(bf16[1024,1152]{1,0:T(8,128)(2,1)} %bitcast.110, bf16[1152,864]{1,0:T(8,128)(2,1)} %bitcast.131, f32[864]{0:T(1024)S(1)} %reshape.544), kind=kOutput, calls=%fused_computation.25 | convolution fusion | flops 2040201216 | bytes 6122880 | tf_op jit(solution)/shard_map/dot_general | solution.py:1688
  113.4 0.2 reduce_window_sum.11
  113.6 0.7 broadcast_compare_fusion.1
  114.3 1.9 fusion.1
  116.2 1.9 fusion
  118.0 1.4 copy-done.2
  119.4 4.7 %fusion.2 = (f32[4,512]{1,0:T(4,128)S(1)}, f32[4,512]{1,0:T(4,128)S(1)}) fusion(f32[4,512,1024]{2,1,0:T(8,128)S(1)} %get-tuple-element.195, f32[4,512]{1,0:T(4,128)S(1)} %get-tuple-element.194, pred[512,1024]{1,0:T(8,128)(4,1)S(1)} %get-tuple-element.179, f32[4,512]{1,0:T(4,128)S(1)} %get-tuple-element.192, f32[4,512,1024]{2,1,0:T(8,128)S(1)} %get-tuple-element.193, ...), kind=kLoop, calls=%fused_computation.8 | loop fusion | flops 16773120 | bytes 17858560 | tf_op jit(solution)/shard_map/while/body/eval_jaxpr/reduce_sum | solution.py:1715
  124.2 0.6 pad_maximum_fusion.4.totals_ref
  124.8 5.6 %fusion.14 = bf16[512,4,72]{0,2,1:T(8,128)(2,1)S(1)} fusion(f32[4,512,1024]{2,1,0:T(8,128)} %copy-done.4, f32[4,512]{1,0:T(4,128)S(1)} %get-tuple-element.196, f32[4,512]{1,0:T(4,128)S(1)} %get-tuple-element.194, pred[512,1024]{1,0:T(8,128)(4,1)S(1)} %get-tuple-element.179, bf16[1024,4,3,72]{0,3,2,1:T(8,128)(2,1)S(1)} %bitcast.115), kind=kOutput, calls=%fused_computation.31 | convolution fusion | flops 312623104 | bytes 9814016 | tf_op jit(solution)/shard_map/while/body/eval_jaxpr/hqk,khd->qhd/dot_general | solution.py:1718
  130.4 0.3 copy-done.3
  130.6 2.6 fusion.15
  133.3 0.4 reshape_reshape.3
  133.7 1.4 copy.97.mixed_ref
  135.1 0.6 fusion.26.hot_ref
  135.9 0.7 fusion.18.vectors_ref
  136.6 0.5 broadcast.323
  137.1 0.7 reduce.43
  137.8 1.1 reshape.547.segments_ref
  138.9 0.6 maximum_convert_fusion.bias_ref
  139.6 112.0 %middle.1 = (bf16[4,256,1152]{2,1,0:T(8,128)(2,1)}, bf16[4,256,1152]{2,1,0:T(8,128)(2,1)}, bf16[4,256,1152]{2,1,0:T(8,128)(2,1)}, bf16[4,256,1152]{2,1,0:T(8,128...) custom-call(bf16[4,256,288]{2,1,0:T(8,128)(2,1)} %copy.97.mixed_ref,, ...), custom_call_target="tpu_custom_call" | custom-call | tf_op jit(solution)/shard_map/middle/pallas_call | solution.py:1116
  251.5 2.5 copy.90
  254.0 1.0 copy.99.keys_image
  255.1 50.8 %attend_back.1 = (bf16[4,256,864]{2,1,0:T(8,128)(2,1)}, f32[48,1152]{1,0:T(8,128)}, f32[48,1152]{1,0:T(8,128)}, f32[48,1152]{1,0:T(8,128)}) custom-call(bf16[4,256,864]{2,1,0:T(8,128)(2,1)} %bitcast.104, bf16[4,256,1152]{2,1,0:T(8,128)(2,1)} %get-tuple-element.70.grad_ref, bf16[1152,288]{1,0:T(8,128)(2,1)} %bitcast.106, ...), custom_call_target="tpu_custom_call" | custom-call | tf_op jit(solution)/shard_map/attend_back/pallas_call | solution.py:1286
  305.9 1.8 pad_maximum_fusion.1
  307.7 2.0 convert_reduce_fusion.3
  310.0 2.1 convert_reduce_fusion.1
  312.0 0.4 convert_reduce_fusion.2
  312.5 0.6 pad_bitcast_fusion.bias_ref
  313.1 1.8 convolution_convert_fusion.1
  314.9 2.3 copy.102
  317.2 4.7 %bitcast_convert_fusion = bf16[1152,864]{0,1:T(8,128)(2,1)S(1)} fusion(bf16[4,256,1152]{2,1,0:T(8,128)(2,1)} %fusion.9, bf16[4,256,864]{2,1,0:T(8,128)(2,1)} %get-tuple-element.73), kind=kOutput, calls=%fused_computation.22 | convolution fusion | flops 2039427072 | bytes 6119424 | tf_op jit(solution)/shard_map/dot_general | solution.py:40
  321.9 2.7 copy.101
  324.6 6.4 %convolution_convert_fusion = bf16[1024,1152]{1,0:T(8,128)(2,1)} fusion(bf16[1024,864]{1,0:T(8,128)(2,1)} %bitcast.112, bf16[1152,864]{1,0:T(8,128)(2,1)} %bitcast.132), kind=kOutput, calls=%fused_computation.23 | convolution fusion | flops 2039611392 | bytes 6119424 | tf_op jit(solution)/shard_map/dot_general | solution.py:56
  331.1 2.1 select_select_fusion
  333.1 0.2 slice_reduce_fusion
  333.6 0.7 compare_convert_fusion
  334.3 0.7 fusion.24
  335.0 0.7 copy.106.silu_ref
  335.8 0.6 reshape.545.ffn_bias
  336.4 91.1 %back.1 = (bf16[256,1152]{1,0:T(8,128)(2,1)}, f32[256,1152]{1,0:T(8,128)}, f32[128,288]{1,0:T(8,128)}, f32[128,288]{1,0:T(8,128)}, f32[288,864]{1,0:T(8,128)}, /...) custom-call(bf16[4,256,1152]{2,1,0:T(8,128)(2,1)} %bitcast.109, ...), custom_call_target="tpu_custom_call" | custom-call | tf_op jit(solution)/shard_map/back/pallas_call | solution.py:1542
  427.6 2.0 pad_maximum_fusion
  429.6 1.9 pad_maximum_fusion.3
  431.5 0.8 copy.107
  432.2 0.8 copy.108
  433.0 0.7 fusion.31
  433.7 0.6 dynamic_slice.16
  434.3 0.6 dynamic_slice.17
  435.0 0.7 reshape.543
  435.6 1.4 slice_reduce_fusion.13
  437.0 0.8 copy.122
  437.8 1.0 copy.123
  438.8 1.0 copy.124
  439.8 0.7 copy.125
  (91 shorter events, 1.5 us)
Async XLA Ops:
  0.6 94.7 %copy-start.18 = (bf16[6912]{0:T(1024)(128)(2,1)S(1)}, bf16[6912]{0:T(1024)(128)(2,1)}, u32[]{:S(2)}) copy-start(bf16[6912]{0:T(1024)(128)(2,1)} %param.22) | copy-start | bytes 41476
  94.1 3.6 copy-start
  95.6 2.9 copy-start.21
  98.5 9.7 %copy-start.25 = (bf16[4,144]{1,0:T(4,128)(2,1)S(1)}, bf16[4,144]{1,0:T(4,128)(2,1)}, u32[]{:S(2)}) copy-start(bf16[4,144]{1,0:T(4,128)(2,1)} %param.24) | copy-start | bytes 3460
  108.5 4.8 %copy-start.26 = (s32[1,4]{1,0:T(1,128)S(1)}, s32[1,4]{1,0:T(1,128)}, u32[]{:S(2)}) copy-start(s32[1,4]{1,0:T(1,128)} %param.31) | copy-start | bytes 52
  113.6 140.4 %copy-start.15 = (s32[1024]{0:T(1024)}, s32[1024]{0:T(1024)S(1)}, u32[]{:S(2)}) copy-start(s32[1024]{0:T(1024)S(1)} %convert_reduce_fusion.4) | copy-start | bytes 12292
  116.2 3.2 copy-start.2
  118.0 6.1 %copy-start.4 = (f32[4,512,1024]{2,1,0:T(8,128)}, f32[4,512,1024]{2,1,0:T(8,128)S(1)}, u32[]{:S(2)}) copy-start(f32[4,512,1024]{2,1,0:T(8,128)S(1)} %get-tuple-element.195) | copy-start | bytes 25165828
  124.8 5.8 %copy-start.3 = (f32[4,512,1024]{2,1,0:T(8,128)S(1)}, f32[4,512,1024]{2,1,0:T(8,128)}, u32[]{:S(2)}) copy-start(f32[4,512,1024]{2,1,0:T(8,128)} %copy-done.2) | copy-start | bytes 25165828
  133.2 5.7 %copy-start.22 = (bf16[1152]{0:T(1024)(128)(2,1)S(1)}, bf16[1152]{0:T(1024)(128)(2,1)}, u32[]{:S(2)}) copy-start(bf16[1152]{0:T(1024)(128)(2,1)} %param.28) | copy-start | bytes 6916
  133.2 5.7 %copy-start.23 = (bf16[1152]{0:T(1024)(128)(2,1)S(1)}, bf16[1152]{0:T(1024)(128)(2,1)}, u32[]{:S(2)}) copy-start(bf16[1152]{0:T(1024)(128)(2,1)} %param.26) | copy-start | bytes 6916
  255.1 50.8 %copy-start.11 = (f32[48,1152]{1,0:T(8,128)S(1)}, f32[48,1152]{1,0:T(8,128)}, u32[]{:S(2)}) copy-start(f32[48,1152]{1,0:T(8,128)} %get-tuple-element.96) | copy-start | bytes 663556
  255.1 50.8 %copy-start.12 = (f32[48,1152]{1,0:T(8,128)S(1)}, f32[48,1152]{1,0:T(8,128)}, u32[]{:S(2)}) copy-start(f32[48,1152]{1,0:T(8,128)} %get-tuple-element.97) | copy-start | bytes 663556
  307.7 4.3 copy-start.1
  310.0 2.5 copy-start.20
  331.0 2.1 copy-start.17
  331.0 3.3 copy-start.16
  331.0 4.7 %copy-start.24 = (bf16[1152]{0:T(1024)(128)(2,1)S(1)}, bf16[1152]{0:T(1024)(128)(2,1)}, u32[]{:S(2)}) copy-start(bf16[1152]{0:T(1024)(128)(2,1)} %param.30) | copy-start | bytes 6916
  336.4 91.2 %copy-start.9 = (f32[48,1152]{1,0:T(8,128)S(1)}, f32[48,1152]{1,0:T(8,128)}, u32[]{:S(2)}) copy-start(f32[48,1152]{1,0:T(8,128)} %get-tuple-element.93) | copy-start | bytes 663556
  336.4 91.2 %copy-start.10 = (f32[48,1152]{1,0:T(8,128)S(1)}, f32[48,1152]{1,0:T(8,128)}, u32[]{:S(2)}) copy-start(f32[48,1152]{1,0:T(8,128)} %get-tuple-element.94) | copy-start | bytes 663556
  427.5 3.9 copy-start.14
  427.5 4.7 %copy-start.13 = (f32[128,288]{1,0:T(8,128)S(1)}, f32[128,288]{1,0:T(8,128)}, u32[]{:S(2)}) copy-start(f32[128,288]{1,0:T(8,128)} %get-tuple-element.144) | copy-start | bytes 442372
  427.5 5.5 %copy-start.19 = (f32[32,128]{1,0:T(8,128)S(1)}, f32[32,128]{1,0:T(8,128)}, u32[]{:S(2)}) copy-start(f32[32,128]{1,0:T(8,128)} %get-tuple-element.91) | copy-start | bytes 49156
  427.6 9.4 %copy-start.7 = (bf16[256,1152]{1,0:T(8,128)(2,1)S(1)}, bf16[256,1152]{1,0:T(8,128)(2,1)}, u32[]{:S(2)}) copy-start(bf16[256,1152]{1,0:T(8,128)(2,1)} %get-tuple-element.212) | copy-start | bytes 1769476
  427.6 10.2 %copy-start.5 = (f32[256,1152]{1,0:T(8,128)S(1)}, f32[256,1152]{1,0:T(8,128)}, u32[]{:S(2)}) copy-start(f32[256,1152]{1,0:T(8,128)} %get-tuple-element.213) | copy-start | bytes 3538948
  431.5 7.4 %copy-start.6 = (f32[288,864]{1,0:T(8,128)S(1)}, f32[288,864]{1,0:T(8,128)}, u32[]{:S(2)}) copy-start(f32[288,864]{1,0:T(8,128)} %get-tuple-element.216) | copy-start | bytes 2985988
  437.8 2.0 copy-start.8

commit v5 on v4

--- a/solution.py
+++ b/solution.py
@@ -821,38 +821,19 @@
             copy.wait_send()
 
 
-class Reduces:
-    def __init__(self, jobs, buffers, sends, recvs):
-        self.units = [
-            RowReduce(
-                partial,
-                chunk,
-                buffers[3 * place : 3 * place + 3],
-                total,
-                sends.at[place],
-                recvs.at[place],
-            )
-            for place, (partial, chunk, total) in enumerate(jobs)
-        ]
-        self.done = 0
-
-    def start(self):
-        for unit in self.units[:2]:
-            unit.start()
-
-    def advance(self):
-        place = self.done
-        self.done += 1
-        self.units[place].send_pair()
-        if place + 2 < len(self.units):
-            self.units[place + 2].start()
-        if place > 0:
-            self.units[place - 1].finish()
-
-    def finish(self):
-        while self.done < len(self.units):
-            self.advance()
-        self.units[-1].finish()
+def row_reduces(jobs, reducing):
+    buffers, sends, recvs = reducing[:-2], reducing[-2], reducing[-1]
+    return [
+        RowReduce(
+            partial,
+            chunk,
+            buffers[3 * place : 3 * place + 3],
+            total,
+            sends.at[place],
+            recvs.at[place],
+        )
+        for place, (partial, chunk, total) in enumerate(jobs)
+    ]
 
 
 def reduce_scratch(sizes):
@@ -879,6 +860,23 @@
     centred = values - jnp.mean(values, axis=1, keepdims=True)
     factor = lax.rsqrt(jnp.mean(centred * centred, axis=1, keepdims=True) + EPSILON)
     return centred * factor, factor
+
+
+def weight_grad(left, right, target):
+    blocks, tok_rows, depth = left.shape
+    height = blocks * tok_rows
+    flat = target.reshape(depth, target.shape[3])
+    third = depth // 3
+
+    def some(step, carry):
+        columns = pl.ds(pl.multiple_of(step * third, 128), third)
+        flat[columns] = contract_rows(
+            left[:, :, columns].reshape(height, third),
+            right[...].reshape(height, right.shape[2]),
+        ).astype(jnp.bfloat16)
+        return carry
+
+    lax.fori_loop(0, 3, some, 0)
 
 
 def middle_kernel(
@@ -901,11 +899,14 @@
     after_grad,
     attn_grad,
     slot_sums,
-    inner_bias,
-    fc2_part,
+    bias_sums,
+    fc2_rest,
     fc1_part,
     fc2_head,
     fc2_neck,
+    fc2_part,
+    inner_bias,
+    ffn_bias,
     fc2_full,
     active_grad,
     first_part,
@@ -961,12 +962,15 @@
     def scale_cotangent(block, carry):
         index = block // 2
         part = pl.ds(pl.multiple_of(lax.rem(block, 2) * 128, 128), 128)
-        ffn_rows[index, part] = (
+        grad = (
             picked(vectors_ref, 5, segments_ref[index, part], model_width)
             * cotangent_ref[index, part].astype(jnp.float32)
         ).astype(jnp.bfloat16)
+        ffn_rows[index, part] = grad
+        ffn_bias[...] += jnp.sum(grad.astype(jnp.float32).reshape(16, 8, model_width), axis=0)
         return carry
 
+    ffn_bias[...] = jnp.zeros_like(ffn_bias)
     lax.fori_loop(0, 2 * HEAD_PARTS, scale_cotangent, 0)
     gather_fc2.relay(0)
     gather_fc2.start(2)
@@ -1047,21 +1051,12 @@
         ffn_part[block] = times_transposed(active_rows[block], fc2[...]).astype(jnp.bfloat16)
         return carry
 
-    def weight_grad(left, right, target):
-        height = HEAD_PARTS * tok_rows
-        grad = contract_rows(
-            left[...].reshape(height, left.shape[2]), right[...].reshape(height, right.shape[2])
-        )
-        target[...] = grad.astype(jnp.bfloat16).reshape(target.shape)
-
     weight_grad(ffn_rows, active_rows, fc2_part)
-    reduces = Reduces(
-        ((fc2_part, 0, fc2_head), (fc2_part, 1, fc2_neck)),
-        reducing[:-2],
-        reducing[-2],
-        reducing[-1],
-    )
-    reduces.start()
+    third = fc2_rest.shape[2]
+    fc2_rest[...] = fc2_part[:, :, 2 * third : 3 * third]
+    reduces = row_reduces(((fc2_part, 0, fc2_head), (fc2_part, 1, fc2_neck)), reducing)
+    for unit in reduces:
+        unit.start()
     lax.fori_loop(0, HEAD_PARTS, forward_fc2, 0)
     slot_sums[...] = jnp.zeros_like(slot_sums)
     second.settle()
@@ -1091,11 +1086,16 @@
     lax.fori_loop(0, tok_rows // 128, second_back, 0)
     gather_grad.start()
     weight_grad(hidden_rows, inner_grad, fc1_part)
-    reduces.advance()
+    reduces[0].send_pair()
+    bias_sums[...] = jnp.zeros_like(bias_sums)
+    bias_sums[0:1] = jnp.sum(inner_bias[...], axis=0, keepdims=True)
+    bias_sums[1:2] = jnp.sum(ffn_bias[...], axis=0, keepdims=True)
     gather_grad.wait_sibling()
     gather_grad.wait_partner()
     gather_grad.wait_opposite()
-    reduces.finish()
+    reduces[1].send_pair()
+    for unit in reduces:
+        unit.finish()
     gather_hidden.finish()
     gather_grad.finish()
     first.finish()
@@ -1126,7 +1126,7 @@
             rows_low,
             shape((3, SLOT_ROWS, model_width), jnp.float32),
             shape((8, hidden_width), jnp.float32),
-            shape((4, 2, width_part, hidden_width), jnp.bfloat16),
+            shape((4, 2, width_part // 3, hidden_width), jnp.bfloat16),
             shape((4, 2, width_part, hidden_width), jnp.bfloat16),
             shape((width_part // 3, hidden_width), jnp.float32),
             shape((width_part // 3, hidden_width), jnp.float32),
@@ -1134,6 +1134,9 @@
         in_specs=[VMEM_SPEC] * 10,
         out_specs=[VMEM_SPEC] * 14,
         scratch_shapes=[
+            pltpu.VMEM((4, 2, width_part, hidden_width), jnp.bfloat16),
+            pltpu.VMEM((8, hidden_width), jnp.float32),
+            pltpu.VMEM((8, model_width), jnp.float32),
             pltpu.VMEM((ROW_PARTS,) + w_fc2.shape, jnp.bfloat16),
             pltpu.VMEM((HEAD_PARTS, tok_rows, hidden_width), jnp.float32),
             group_low,
@@ -1164,7 +1167,7 @@
 HEAD_LANES = 128
 
 
-def attend_back_kernel(
+def rear_kernel(
     projected_ref,
     grad_ref,
     out_ref,
@@ -1173,148 +1176,14 @@
     rows_image,
     fc2_part,
     fc1_part,
-    qkv_grad,
-    fc2_tail,
-    fc1_head,
-    fc1_neck,
-    parts,
-    mixed_grad,
-    key_columns,
-    grad_queries,
-    grad_keys,
-    grad_values,
-    bias,
-    packed,
-    *reducing,
-):
-    greet(range(1, ROW_PARTS), ())
-    reduces = Reduces(
-        ((fc2_part, 2, fc2_tail), (fc1_part, 0, fc1_head), (fc1_part, 1, fc1_neck)),
-        reducing[:-2],
-        reducing[-2],
-        reducing[-1],
-    )
-    reduces.start()
-    blocks, tok_rows, width = projected_ref.shape
-    head_local = totals_ref.shape[0]
-    head_size = width // (3 * head_local)
-    scale_factor = 1.0 / math.sqrt(head_size)
-    parts[...] = jnp.zeros_like(parts)
-    mixed_grad[...] = jnp.zeros_like(mixed_grad)
-
-    def unpack(block, carry):
-        rows = pl.ds(pl.multiple_of(block * tok_rows, tok_rows), tok_rows)
-        packed[...] = projected_ref[block].astype(jnp.float32)
-        for part in range(3 * head_local):
-            parts[part, rows, 0:head_size] = packed[
-                :, part * head_size : (part + 1) * head_size
-            ].astype(jnp.bfloat16)
-        packed[:, 0 : head_local * head_size] = jnp.dot(
-            grad_ref[block], out_ref[...], preferred_element_type=jnp.float32
-        )
-        for head in range(head_local):
-            mixed_grad[head, rows, 0:head_size] = packed[
-                :, head * head_size : (head + 1) * head_size
-            ].astype(jnp.bfloat16)
-        return carry
-
-    lax.fori_loop(0, blocks, unpack, 0)
-
-    def turn(head, carry):
-        key_columns[head] = parts[3 * head + 1].astype(jnp.float32).T.astype(jnp.bfloat16)
-        return carry
-
-    lax.fori_loop(0, head_local, turn, 0)
-    grad_keys[...] = jnp.zeros_like(grad_keys)
-    grad_values[...] = jnp.zeros_like(grad_values)
-    seq_len = blocks * tok_rows
-
-    for block in range(blocks):
-        rows = pl.ds(block * tok_rows, tok_rows)
-        same = jnp.broadcast_to(keys_image[...], (seq_len, tok_rows)) == jnp.broadcast_to(
-            rows_image[block], (seq_len, tok_rows)
-        )
-        bias[...] = jnp.where(same, 0.0, MASKED)
-
-        def one_head(head, carry):
-            query = parts[3 * head, rows]
-            grad = mixed_grad[head, rows]
-            scores = times_transposed(parts[3 * head + 1], query) * scale_factor + bias[...]
-            probs = jnp.exp(scores - totals_ref[head, block])
-            grad_probs = times_transposed(parts[3 * head + 2], grad)
-            inner = jnp.sum(probs * grad_probs, axis=0, keepdims=True)
-            grad_scores = (probs * (grad_probs - inner)).astype(jnp.bfloat16)
-            grad_values[head] += jnp.dot(
-                probs.astype(jnp.bfloat16), grad, preferred_element_type=jnp.float32
-            )
-            grad_keys[head] += jnp.dot(grad_scores, query, preferred_element_type=jnp.float32)
-            grad_queries[head, rows] = jnp.dot(
-                key_columns[head], grad_scores, preferred_element_type=jnp.float32
-            ).T
-            return carry
-
-        lax.fori_loop(0, head_local, one_head, 0)
-        if block > 0:
-            reduces.advance()
-
-    def pack(block, carry):
-        rows = pl.ds(pl.multiple_of(block * tok_rows, tok_rows), tok_rows)
-        for head in range(head_local):
-            for place, (grads, factor) in enumerate(
-                ((grad_queries, scale_factor), (grad_keys, scale_factor), (grad_values, None))
-            ):
-                start = (3 * head + place) * head_size
-                term = grads[head, rows, 0:head_size]
-                packed[:, start : start + head_size] = term if factor is None else term * factor
-        qkv_grad[block] = packed[...].astype(jnp.bfloat16)
-        return carry
-
-    lax.fori_loop(0, blocks, pack, 0)
-    reduces.finish()
-
-
-def attend_back(
-    projected, grad, w_out, totals, keys_image, rows_image, grad_w_fc2, grad_w_fc1
-):
-    shape = jax.ShapeDtypeStruct
-    blocks, tok_rows, width = projected.shape
-    head_local = totals.shape[0]
-    seq_len = blocks * tok_rows
-    width_part, hidden_width = grad_w_fc2.shape[2:]
-    third = (width_part // 3, hidden_width)
-    wide = pltpu.VMEM((head_local, seq_len, HEAD_LANES), jnp.float32)
-    return pl.pallas_call(
-        attend_back_kernel,
-        out_shape=[shape(projected.shape, jnp.bfloat16)] + [shape(third, jnp.float32)] * 3,
-        in_specs=[VMEM_SPEC] * 8,
-        out_specs=[VMEM_SPEC] * 4,
-        scratch_shapes=[
-            pltpu.VMEM((3 * head_local, seq_len, HEAD_LANES), jnp.bfloat16),
-            pltpu.VMEM((head_local, seq_len, HEAD_LANES), jnp.bfloat16),
-            pltpu.VMEM((head_local, HEAD_LANES, seq_len), jnp.bfloat16),
-            wide,
-            wide,
-            wide,
-            pltpu.VMEM((seq_len, tok_rows), jnp.float32),
-            pltpu.VMEM((tok_rows, width), jnp.float32),
-        ]
-        + reduce_scratch([third] * 3),
-        compiler_params=pltpu.CompilerParams(
-            collective_id=3, has_side_effects=True, vmem_limit_bytes=GRANT
-        ),
-        name="attend_back",
-    )(projected, grad, w_out, totals, keys_image, rows_image, grad_w_fc2, grad_w_fc1)
-
-
-def back_kernel(
-    hidden_ref,
-    fc1_part,
-    qkv_part,
-    out_part,
+    hidden_rows,
+    qkv_ref,
+    mixed_ref,
     bias_ref,
     patches_ref,
     after_ref,
-    scale_ref,
+    vectors_ref,
+    segments_ref,
     hot_ref,
     sums_ref,
     silu_ref,
@@ -1324,7 +1193,6 @@
     ada_ref,
     ffn_ref,
     block_ref,
-    gate_ref,
     cotangent_ref,
     ffn_bias,
     block_out,
@@ -1333,12 +1201,23 @@
     class_grad,
     ada_grad,
     ada_bias,
-    fc1_tail,
-    qkv_head,
-    qkv_neck,
-    qkv_tail,
+    fc2_tail,
+    fc1_grad,
+    qkv_grad,
     out_grad,
     bias_sum,
+    parts,
+    mixed_grad,
+    key_columns,
+    grad_keys,
+    grad_values,
+    bias,
+    packed,
+    packed_grad,
+    hidden_part,
+    qkv_part,
+    out_part,
+    bias_own,
     beside_in,
     pair_rows,
     across_in,
@@ -1350,7 +1229,6 @@
     mods_sibling,
     mods_pair,
     mods_partner,
-    mods_low,
     mods_cols,
     bias_all,
     silu_part,
@@ -1386,59 +1264,153 @@
         for copy in copies:
             copy.wait()
 
+    third = fc2_tail.shape[0]
+    units = row_reduces(
+        [(fc2_part, 0, fc2_tail)]
+        + [(fc1_part, chunk, fc1_grad.at[pl.ds(chunk * third, third)]) for chunk in range(3)]
+        + [(out_part, 0, out_grad)]
+        + [(qkv_part, chunk, qkv_grad.at[pl.ds(chunk * third, third)]) for chunk in range(3)],
+        reducing,
+    )
     reduce_rows = HeadReduce(
-        hidden_ref, beside_in, pair_rows, across_in, head_send.at[0], head_recv.at[0]
+        hidden_part, beside_in, pair_rows, across_in, head_send.at[0], head_recv.at[0]
     )
     reduce_ffn = HeadReduce(
         ffn_ref, ffn_beside, ffn_pair, ffn_across, head_send.at[1], head_recv.at[1]
     )
-    reduce_rows.start()
+    for unit in units[:3]:
+        unit.start()
     reduce_ffn.start()
-    reduces = Reduces(
-        (
-            (fc1_part, 2, fc1_tail),
-            (qkv_part, 0, qkv_head),
-            (qkv_part, 1, qkv_neck),
-            (qkv_part, 2, qkv_tail),
-            (out_part, 0, out_grad),
-        ),
-        reducing[:-2],
-        reducing[-2],
-        reducing[-1],
-    )
-    reduces.start()
+    reduce_ffn.send_pair()
+    blocks, tok_rows, width = projected_ref.shape
+    model_width = patches_ref.shape[1]
+    head_local = totals_ref.shape[0]
+    head_size = width // (3 * head_local)
+    scale_factor = 1.0 / math.sqrt(head_size)
+    seq_len = blocks * tok_rows
+    parts[...] = jnp.zeros_like(parts)
+    mixed_grad[...] = jnp.zeros_like(mixed_grad)
+    bias_own[...] = jnp.zeros_like(bias_own)
+
+    def unpack(block, carry):
+        rows = pl.ds(pl.multiple_of(block * tok_rows, tok_rows), tok_rows)
+        packed[...] = projected_ref[block].astype(jnp.float32)
+        for part in range(3 * head_local):
+            parts[part, rows, 0:head_size] = packed[
+                :, part * head_size : (part + 1) * head_size
+            ].astype(jnp.bfloat16)
+        packed[:, 0 : head_local * head_size] = jnp.dot(
+            grad_ref[block], out_ref[...], preferred_element_type=jnp.float32
+        )
+        for head in range(head_local):
+            mixed_grad[head, rows, 0:head_size] = packed[
+                :, head * head_size : (head + 1) * head_size
+            ].astype(jnp.bfloat16)
+        bias_own[0] += jnp.sum(
+            grad_ref[block].astype(jnp.float32).reshape(tok_rows // 8, 8, model_width), axis=0
+        )
+        return carry
+
+    lax.fori_loop(0, blocks, unpack, 0)
+
+    def turn(head, carry):
+        key_columns[head] = parts[3 * head + 1].astype(jnp.float32).T.astype(jnp.bfloat16)
+        return carry
+
+    lax.fori_loop(0, head_local, turn, 0)
+    grad_keys[...] = jnp.zeros_like(grad_keys)
+    grad_values[...] = jnp.zeros_like(grad_values)
+    weight_grad(grad_ref, mixed_ref, out_part)
+
+    for block in range(blocks):
+        rows = pl.ds(block * tok_rows, tok_rows)
+        same = jnp.broadcast_to(keys_image[...], (seq_len, tok_rows)) == jnp.broadcast_to(
+            rows_image[block], (seq_len, tok_rows)
+        )
+        bias[...] = jnp.where(same, 0.0, MASKED)
+
+        def one_head(head, carry):
+            query = parts[3 * head, rows]
+            grad = mixed_grad[head, rows]
+            scores = times_transposed(parts[3 * head + 1], query) * scale_factor + bias[...]
+            probs = jnp.exp(scores - totals_ref[head, block])
+            grad_probs = times_transposed(parts[3 * head + 2], grad)
+            inner = jnp.sum(probs * grad_probs, axis=0, keepdims=True)
+            grad_scores = (probs * (grad_probs - inner)).astype(jnp.bfloat16)
+            grad_values[head] += jnp.dot(
+                probs.astype(jnp.bfloat16), grad, preferred_element_type=jnp.float32
+            )
+            grad_keys[head] += jnp.dot(grad_scores, query, preferred_element_type=jnp.float32)
+            lanes = pl.ds(pl.multiple_of(head * HEAD_LANES, HEAD_LANES), HEAD_LANES)
+            hidden_part[block, :, lanes] = (
+                jnp.dot(key_columns[head], grad_scores, preferred_element_type=jnp.float32).T
+                * scale_factor
+            ).astype(jnp.bfloat16)
+            return carry
+
+        lax.fori_loop(0, head_local, one_head, 0)
+        units[block].send_pair()
+        if block < 2:
+            units[block + 3].start()
+
+    def pack(block, carry):
+        rows = pl.ds(pl.multiple_of(block * tok_rows, tok_rows), tok_rows)
+        for head in range(head_local):
+            lane = head * HEAD_LANES
+            terms = (
+                hidden_part[block, :, lane : lane + head_size].astype(jnp.float32),
+                grad_keys[head, rows, 0:head_size] * scale_factor,
+                grad_values[head, rows, 0:head_size],
+            )
+            for place, term in enumerate(terms):
+                start = (3 * head + place) * head_size
+                packed[:, start : start + head_size] = term
+        low = packed[...].astype(jnp.bfloat16)
+        packed_grad[block] = low
+        bias_own[1, :, 0:width] += jnp.sum(
+            low.astype(jnp.float32).reshape(tok_rows // 8, 8, width), axis=0
+        )
+        return carry
+
+    lax.fori_loop(0, blocks, pack, 0)
+    direction = sibling - member
+
+    def project_back(block):
+        hidden_part[block] = times_transposed(packed_grad[block], qkv_ref[...]).astype(
+            jnp.bfloat16
+        )
+
+    def far(step, carry):
+        project_back(opposite - step * direction)
+        return carry
+
+    def near(step, carry):
+        project_back(sibling - step * direction)
+        return carry
+
+    lax.fori_loop(0, 2, far, 0)
+    reduce_rows.first.start()
     reduce_rows.send_pair()
-    reduce_ffn.send_pair()
-    reduces.advance()
-    reduce_rows.settle()
-    tok_rows = patches_ref.shape[0]
-    model_width = patches_ref.shape[1]
+    lax.fori_loop(0, 2, near, 0)
+    reduce_rows.second.start()
+    weight_grad(hidden_rows, packed_grad, qkv_part)
+    for unit in units[5:]:
+        unit.start()
+    bias_own[2] = jnp.zeros_like(bias_own[2])
+    bias_own[2] = bias_ref[...]
+    bias_own[2, 2:3] = jnp.sum(bias_own[0], axis=0, keepdims=True)
+    bias_own[2, 3:4] = jnp.sum(bias_own[1], axis=0, keepdims=True)
+    bias_copies = spread(1, lambda other: bias_own.at[2], bias_all)
+    bias_all[row] = bias_own[2]
+    units[4].send_pair()
     slot_sums[...] = jnp.zeros_like(slot_sums)
-
-    def rows_back(block, carry):
-        part = pl.ds(pl.multiple_of(block * 128, 128), 128)
-        grad = reduce_rows.rows(part)
-        normed, factor = centre_rows(patches_ref[part].astype(jnp.float32))
-        weighted = grad * scale_ref[part]
-        patches_grad[part] = after_ref[part] + factor * (
-            weighted
-            - jnp.mean(weighted, axis=1, keepdims=True)
-            - normed * jnp.mean(weighted * normed, axis=1, keepdims=True)
-        )
-        hot = hot_ref[:, part]
-        slot_sums[0] += jnp.dot(hot, grad, precision=HIGH, preferred_element_type=jnp.float32)
-        slot_sums[1] += jnp.dot(
-            hot, grad * normed, precision=HIGH, preferred_element_type=jnp.float32
-        )
-        return carry
-
-    lax.fori_loop(0, tok_rows // 128, rows_back, 0)
     reduce_ffn.settle()
 
     def rows_out(block, carry):
         part = pl.ds(pl.multiple_of(block * 128, 128), 128)
         ffn = reduce_ffn.rows(part) + ffn_bias[0:1]
-        block_out[part] = (block_ref[part] + gate_ref[part] * ffn).astype(jnp.bfloat16)
+        gate = picked(vectors_ref, 5, segments_ref[member, part], model_width)
+        block_out[part] = (block_ref[part] + gate * ffn).astype(jnp.bfloat16)
         slot_sums[2] += jnp.dot(
             hot_ref[:, part],
             cotangent_ref[part].astype(jnp.float32) * ffn,
@@ -1448,6 +1420,29 @@
         return carry
 
     lax.fori_loop(0, tok_rows // 128, rows_out, 0)
+    units[0].finish()
+    units[1].finish()
+    units[5].send_pair()
+    reduce_rows.settle()
+
+    def rows_back(block, carry):
+        part = pl.ds(pl.multiple_of(block * 128, 128), 128)
+        grad = reduce_rows.rows(part)
+        normed, factor = centre_rows(patches_ref[part].astype(jnp.float32))
+        weighted = grad * (1.0 + picked(vectors_ref, 1, segments_ref[member, part], model_width))
+        patches_grad[part] = after_ref[part] + factor * (
+            weighted
+            - jnp.mean(weighted, axis=1, keepdims=True)
+            - normed * jnp.mean(weighted * normed, axis=1, keepdims=True)
+        )
+        hot = hot_ref[:, part]
+        slot_sums[0] += jnp.dot(hot, grad, precision=HIGH, preferred_element_type=jnp.float32)
+        slot_sums[1] += jnp.dot(
+            hot, grad * normed, precision=HIGH, preferred_element_type=jnp.float32
+        )
+        return carry
+
+    lax.fori_loop(0, tok_rows // 128, rows_back, 0)
     ada_width = ada_ref.shape[1]
     fine = ada_width // 3
     for unit in range(3 * ROW_PARTS):
@@ -1462,37 +1457,40 @@
         mods_own[unit // 3, :, unit % 3 * fine : (unit % 3 + 1) * fine] = source
     beside = to_head(mods_own, mods_sibling, pair_send.at[0], pair_recv.at[0], sibling)
     beside.start()
-    reduces.advance()
+    units[6].send_pair()
     beside.wait()
     mods_pair[...] = mods_own[...] + mods_sibling[...]
     across = to_head(mods_pair, mods_partner, pair_send.at[1], pair_recv.at[1], partner)
     across.start()
+    units[2].finish()
+    units[3].finish()
+    settle(bias_copies)
+    bias_sum[...] = jnp.sum(bias_all[...], axis=0)
     across.wait()
-    mods_low[...] = (
+    mods_own[...] = (
         (mods_pair[...] + mods_partner[...]).astype(jnp.bfloat16).astype(jnp.float32)
     )
-    copies = spread(0, lambda other: mods_low.at[other], mods_cols)
-    bias_copies = spread(1, lambda other: bias_ref, bias_all)
-    mods_cols[row] = mods_low[row]
-    bias_all[row] = bias_ref[...]
+    copies = spread(0, lambda other: mods_own.at[other], mods_cols)
+    mods_cols[row] = mods_own[row]
+    units[7].send_pair()
+    units[4].finish()
     settle(copies)
     slots = ROW_PARTS * SLOT_ROWS
     cols = mods_cols[...].reshape(slots, ada_width)
     low = cols.astype(jnp.bfloat16)
-    ada_grad[...] = jnp.dot(silu_ref[...], low, preferred_element_type=jnp.float32)
-    ada_bias[...] = jnp.broadcast_to(jnp.sum(cols, axis=0, keepdims=True), ada_bias.shape)
     silu_part[...] = times_transposed(low, ada_ref[...]).reshape(silu_part.shape)
     copies = spread(2, lambda other: silu_part.at[other], silu_in)
     silu_in[row] = silu_part[row]
-    settle(bias_copies)
-    bias_sum[...] = jnp.sum(bias_all[...], axis=0)
-    reduces.advance()
+    ada_grad[...] = jnp.dot(silu_ref[...], low, preferred_element_type=jnp.float32)
+    ada_bias[...] = jnp.broadcast_to(jnp.sum(cols, axis=0, keepdims=True), ada_bias.shape)
     settle(copies)
     summed = jnp.sum(silu_in[...], axis=0)
     silu_all[row] = summed
     silu_part[row] = summed
     copies = spread(3, lambda other: silu_part.at[row], silu_all)
-    reduces.advance()
+    units[5].finish()
+    units[6].finish()
+    units[7].finish()
     settle(copies)
     grad_condition = silu_all[...].reshape(slots, silu_all.shape[2]) * slope_ref[...]
     time_grad[...] = jnp.dot(
@@ -1501,67 +1499,73 @@
     class_grad[...] = jnp.dot(
         label_ref[...], grad_condition, precision=HIGH, preferred_element_type=jnp.float32
     )
-    reduces.finish()
     reduce_rows.finish()
     reduce_ffn.finish()
 
 
-def back(
-    hidden,
-    grad_w_fc1,
-    grad_w_qkv,
-    grad_w_out,
-    biases,
-    patches,
-    grad_after,
-    scales,
-    hot,
-    sums,
-    silu_columns,
-    slopes,
-    buckets,
-    labels,
-    w_ada,
-    ffn,
-    after,
-    gates,
-    cotangent,
-    ffn_bias,
-):
+def rear(*args):
     shape = jax.ShapeDtypeStruct
-    tok_rows, model_width = patches.shape
+    projected, w_out, totals, grad_w_fc2, w_qkv, biases, patches, buckets, w_ada = (
+        args[place] for place in (0, 2, 3, 6, 9, 11, 12, 20, 22)
+    )
+    blocks, tok_rows, width = projected.shape
+    head_local = totals.shape[0]
+    seq_len = blocks * tok_rows
+    model_width = patches.shape[1]
+    third, hidden_width = grad_w_fc2.shape[2:]
+    width_part = 3 * third
+    out_width = w_out.shape[1]
     depth, ada_width = w_ada.shape
     table_rows = buckets.shape[0]
-    weights = (grad_w_fc1, grad_w_qkv, grad_w_out)
-    thirds = [(weight.shape[2] // 3, weight.shape[3]) for weight in (grad_w_fc1, grad_w_qkv)]
-    sizes = [thirds[0]] + [thirds[1]] * 3 + [grad_w_out.shape[2:]]
-    totals = [shape(size, jnp.float32) for size in sizes]
+    low = jnp.bfloat16
+    full = jnp.float32
+    heads_wide = pltpu.VMEM((head_local, seq_len, HEAD_LANES), full)
     slotted = (ROW_PARTS, SLOT_ROWS)
-    wide = pltpu.VMEM(slotted + (ada_width,), jnp.float32)
-    narrow = pltpu.VMEM(slotted + (depth,), jnp.float32)
+    wide = pltpu.VMEM(slotted + (ada_width,), full)
+    narrow = pltpu.VMEM(slotted + (depth,), full)
+    sizes = (
+        [(third, hidden_width)] * 4 + [(width_part, out_width)] + [(third, width)] * 3
+    )
     return pl.pallas_call(
-        back_kernel,
+        rear_kernel,
         out_shape=[
-            shape((tok_rows, model_width), jnp.bfloat16),
-            shape((tok_rows, model_width), jnp.float32),
-            shape((table_rows, depth), jnp.float32),
-            shape((table_rows, depth), jnp.float32),
-            shape((depth, ada_width), jnp.float32),
-            shape((SLOT_ROWS, ada_width), jnp.float32),
+            shape((tok_rows, model_width), low),
+            shape((tok_rows, model_width), full),
+            shape((table_rows, depth), full),
+            shape((table_rows, depth), full),
+            shape((depth, ada_width), full),
+            shape((SLOT_ROWS, ada_width), full),
+            shape((third, hidden_width), full),
+            shape((width_part, hidden_width), full),
+            shape((width_part, width), full),
+            shape((width_part, out_width), full),
+            shape(biases.shape, full),
+        ],
+        in_specs=[VMEM_SPEC] * 27,
+        out_specs=[VMEM_SPEC] * 11,
+        scratch_shapes=[
+            pltpu.VMEM((3 * head_local, seq_len, HEAD_LANES), low),
+            pltpu.VMEM((head_local, seq_len, HEAD_LANES), low),
+            pltpu.VMEM((head_local, HEAD_LANES, seq_len), low),
+            heads_wide,
+            heads_wide,
+            pltpu.VMEM((seq_len, tok_rows), full),
+            pltpu.VMEM((tok_rows, width), full),
+            pltpu.VMEM((blocks, tok_rows, width), low),
+            pltpu.VMEM((blocks, tok_rows, model_width), low),
+            pltpu.VMEM((4, 2, width_part, width), low),
+            pltpu.VMEM((4, 2, width_part, out_width), low),
+            pltpu.VMEM((3,) + biases.shape, full),
         ]
-        + totals
-        + [shape(biases.shape, jnp.float32)],
-        in_specs=[VMEM_SPEC] * 20,
-        out_specs=[VMEM_SPEC] * 12,
-        scratch_shapes=[
-            pltpu.VMEM((2, tok_rows, model_width), jnp.bfloat16),
-            pltpu.VMEM((tok_rows, model_width), jnp.bfloat16),
-            pltpu.VMEM((tok_rows, model_width), jnp.bfloat16),
+        + [
+            pltpu.VMEM((2, tok_rows, model_width), low),
+            pltpu.VMEM((tok_rows, model_width), low),
+            pltpu.VMEM((tok_rows, model_width), low),
         ]
         * 2
-        + [pltpu.VMEM((3, SLOT_ROWS, model_width), jnp.float32)]
-        + [wide] * 6
-        + [pltpu.VMEM((ROW_PARTS,) + biases.shape, jnp.float32)]
+        + [pltpu.VMEM((3, SLOT_ROWS, model_width), full)]
+        + [wide] * 5
+        + [pltpu.VMEM((ROW_PARTS,) + biases.shape, full)]
         + [narrow] * 3
         + [
             DMA((4, 7)),
@@ -1573,29 +1577,10 @@
         ]
         + reduce_scratch(sizes),
         compiler_params=pltpu.CompilerParams(
-            collective_id=1, has_side_effects=True, vmem_limit_bytes=GRANT
+            collective_id=1, has_side_effects=True, vmem_limit_bytes=67_000_000
         ),
-        name="back",
-    )(
-        hidden,
-        *weights,
-        biases,
-        patches,
-        grad_after,
-        scales,
-        hot,
-        sums,
-        silu_columns,
-        slopes,
-        buckets,
-        labels,
-        w_ada,
-        ffn,
-        after,
-        gates,
-        cotangent,
-        ffn_bias,
-    )
+        name="rear",
+    )(*args)
 
 
 def shards_linked(
@@ -1672,8 +1657,6 @@
     token_hot = (own_segments == jnp.arange(SLOT_ROWS, dtype=jnp.int32)[None, :]).astype(
         jnp.float32
     )
-    scale_attn = by_token(1, own_segments)
-    gate_mlp = by_token(5, own_segments)
     rows_one = modulate(
         patches_full.reshape(group_rows, model_width).astype(jnp.float32),
         by_token(0, row_segments),
@@ -1723,7 +1706,9 @@
         return (jnp.concatenate(outputs, axis=0), jnp.concatenate(totals, axis=1))
 
     mixed, log_totals = lax.map(attend_forward, (seq_qkv, image_of))
-    mixed_rows = mixed.reshape(group_rows, head_local * head_size)
+    mixed_rows = mixed.reshape(head_parts, tok_rows, head_local * head_size)
+    vectors = mods_all.reshape(slot_count, 6, model_width).transpose(1, 0, 2)
+    segments = segment_ids.reshape(head_parts, tok_rows, 1)
     (
         ffn_rows,
         rows_two,
@@ -1734,27 +1719,40 @@
         grad_after,
         attn_rows_grad,
         sums,
-        inner_bias,
+        bias_sums,
         grad_w_fc2,
         grad_w_fc1,
         fc2_head,
         fc2_neck,
     ) = middle(
-        mixed_rows.reshape(head_parts, tok_rows, mixed_rows.shape[1]),
+        mixed_rows,
         out_cols,
         fc1_cols,
         w_fc2,
         cotangent_full,
         patches,
-        segment_ids.reshape(head_parts, tok_rows, 1),
+        segments,
         token_hot.T,
-        mods_all.reshape(slot_count, 6, model_width).transpose(1, 0, 2),
+        vectors,
         jnp.stack([b_out, b_fc1]).astype(jnp.float32),
     )
-    ffn_rows = ffn_rows.reshape(group_rows, model_width)
-    grad_b_fc2 = jnp.sum(ffn_rows, axis=0, dtype=jnp.float32)
-    grad_b_fc1 = jnp.sum(inner_bias, axis=0)
-    grad_qkv, fc2_tail, fc1_head, fc1_neck = attend_back(
+    all_ids = ids_all[:, :, 0]
+    table_places = lax.axis_index("rows") * table_rows + jnp.arange(table_rows, dtype=jnp.int32)
+    bucket_hot = table_places[:, None] == all_ids[:, :SLOT_ROWS].reshape(every_slot)[None, :]
+    label_hot = table_places[:, None] == all_ids[:, SLOT_ROWS:].reshape(every_slot)[None, :]
+    (
+        block_out,
+        grad_patches,
+        grad_time,
+        grad_class,
+        grad_w_ada,
+        grad_b_ada,
+        fc2_tail,
+        grad_w_fc1,
+        grad_w_qkv,
+        grad_w_out,
+        bias_all,
+    ) = rear(
         projected.reshape(head_parts, tok_rows, projected.shape[1]),
         attn_rows_grad,
         out_cols,
@@ -1763,51 +1761,14 @@
         image_of.reshape(head_parts, 1, tok_rows),
         grad_w_fc2,
         grad_w_fc1,
-    )
-    grad_qkv = grad_qkv.reshape(group_rows, head_local * 3 * head_size)
-    attn_rows_grad = attn_rows_grad.reshape(group_rows, model_width)
-    grad_w_out = contract_rows(attn_rows_grad, mixed_rows)
-    grad_b_out = jnp.sum(attn_rows_grad, axis=0, dtype=jnp.float32)
-    grad_w_qkv = contract_rows(rows_one, grad_qkv)
-    bias_terms = jnp.sum(grad_qkv, axis=0, dtype=jnp.float32).reshape(head_local, 3, head_size)
-    grad_b_qv = jnp.concatenate([bias_terms[:, 0], bias_terms[:, 2]], axis=1)
-    grad_hidden_one = times_transposed(grad_qkv, qkv_cols).astype(jnp.bfloat16)
-    all_ids = ids_all[:, :, 0]
-    table_places = lax.axis_index("rows") * table_rows + jnp.arange(table_rows, dtype=jnp.int32)
-    bucket_hot = table_places[:, None] == all_ids[:, :SLOT_ROWS].reshape(every_slot)[None, :]
-    label_hot = table_places[:, None] == all_ids[:, SLOT_ROWS:].reshape(every_slot)[None, :]
-    bias_flat = jnp.concatenate([grad_b_qv.reshape(-1), grad_b_fc1, grad_b_out, grad_b_fc2])
-    bias_size = bias_flat.size
-    bias_tiles = -(-bias_size // 1024) * 8
-    biases = jnp.pad(bias_flat, (0, bias_tiles * 128 - bias_size)).reshape(bias_tiles, 128)
-
-    def by_row(partial):
-        return partial.astype(jnp.bfloat16).reshape(
-            4, 2, partial.shape[0] // ROW_PARTS, partial.shape[1]
-        )
-
-    (
-        block_out,
-        grad_patches,
-        grad_time,
-        grad_class,
-        grad_w_ada,
-        grad_b_ada,
-        fc1_tail,
-        qkv_head,
-        qkv_neck,
-        qkv_tail,
-        grad_w_out,
-        bias_all,
-    ) = back(
-        grad_hidden_one.reshape(HEAD_PARTS, tok_rows, model_width),
-        grad_w_fc1,
-        by_row(grad_w_qkv),
-        by_row(grad_w_out),
-        biases,
+        rows_one.reshape(head_parts, tok_rows, model_width),
+        qkv_cols,
+        mixed_rows,
+        bias_sums,
         patches,
         grad_after,
-        1.0 + scale_attn,
+        vectors,
+        segments,
         token_hot.T,
         sums,
         silu_low.T,
@@ -1817,23 +1778,18 @@
         w_ada,
         ffn_part,
         after_attn,
-        gate_mlp,
         cotangent,
         b_fc2.astype(jnp.float32)[None, :],
     )
     grad_w_fc2 = jnp.concatenate([fc2_head, fc2_neck, fc2_tail], axis=0)
-    grad_w_fc1 = jnp.concatenate([fc1_head, fc1_neck, fc1_tail], axis=0)
-    grad_w_qkv = jnp.concatenate([qkv_head, qkv_neck, qkv_tail], axis=0)
     grad_b_ada = grad_b_ada[0]
-    bias_all = bias_all.reshape(-1)
-    bias_sizes = (grad_b_qv.size, grad_b_fc1.size, grad_b_out.size, grad_b_fc2.size)
-    edges = [sum(bias_sizes[:step]) for step in range(5)]
     bias_rows = model_width // row_parts
     row_start = lax.axis_index("rows") * bias_rows
-    grad_b_qv = bias_all[edges[0] : edges[1]].reshape(grad_b_qv.shape)
-    grad_b_fc1 = bias_all[edges[1] : edges[2]]
-    grad_b_out = lax.dynamic_slice_in_dim(bias_all[edges[2] : edges[3]], row_start, bias_rows)
-    grad_b_fc2 = lax.dynamic_slice_in_dim(bias_all[edges[3] : edges[4]], row_start, bias_rows)
+    grad_b_fc1 = bias_all[0]
+    grad_b_fc2 = lax.dynamic_slice_in_dim(bias_all[1], row_start, bias_rows)
+    grad_b_out = lax.dynamic_slice_in_dim(bias_all[2], row_start, bias_rows)
+    bias_terms = bias_all[3, : head_local * 3 * head_size].reshape(head_local, 3, head_size)
+    grad_b_qv = jnp.concatenate([bias_terms[:, 0], bias_terms[:, 2]], axis=1)
     return (
         block_out,
         grad_patches,

time: 444 us -> 399 us (0.90)
  Pallas kernels: 343 us -> 319 us
  matrix products: 29.6 us -> 16.7 us
  other arithmetic: 36 us -> 28.4 us
    pallas_call x2 -> x1, Pallas kernels: 142 us -> 119 us  [rear(): pl.pallas_call(rear_kernel, out_shape=[shape((tok_rows, model_width), low...]
    dot_general x3 -> x0, matrix products: 12.9 us -> none  [the longest x2 6.47 us: contract_rows(): lax.dot_general(left_matrix, right_matrix, (((0,), (0,)), ((), ())), pref...]
    unnamed x63 -> x49, local copies, waits for them, and re-layouts: 10.5 us -> 16.5 us
    convert_element_type x2 -> x0, local copies, waits for them, and re-layouts: 4.99 us -> none  [by_row(): partial.astype(jnp.bfloat16)]
    reduce_sum x4 -> x0, other arithmetic: 4.45 us -> none  [the longest x1 2.06 us: shards_linked(): grad_b_fc2 = jnp.sum(ffn_rows, axis=0, dtype=jnp.float32)]
where the time goes in v5:
time: 399 us; the launch traced here: 396 us
  Pallas kernels  319 us (80%)
  local copies, waits for them, and re-layouts  31.2 us (8%)
  other arithmetic  28.4 us (7%)
  matrix products  16.7 us (4%)
    pallas_call x1, Pallas kernels, rear(): pl.pallas_call(rear_kernel, out_shape=[shape((tok_rows, model_width), low...  119 us
    pallas_call x1, Pallas kernels, middle(): pl.pallas_call(middle_kernel, out_shape=[rows_low, rows_low, wide_low, wi...  111 us
    pallas_call x1, Pallas kernels, front(): pl.pallas_call(front_kernel, out_shape=(shape((ROW_PARTS,) + w_qkv.shape,...  88.8 us
    unnamed x49, local copies, waits for them, and re-layouts  16.5 us
    convert_element_type x1, other arithmetic, shards_linked(): rows_one = modulate(patches_full.reshape(group_rows, model_width).astype(...  9.69 us
    dot_general x2, matrix products, attend_forward(): jnp.einsum('hqk,khd->qhd', soft_low, value_rows, preferred_element_type=j...  8.14 us

profile of v5, /device:TPU:0, one launch (start us, length us, event | category | flops | bytes accessed | tf_op | source)
XLA Modules:
  0.0 396.2 jit_solution(9316300192682933300)
XLA Ops:
  0.7 1.6 copy.83.time_ref
  2.3 1.6 copy.84.class_ref
  3.9 0.7 pad_add_fusion
  4.7 0.7 broadcast_in_dim.170.ids_ref
  5.4 88.8 %front.1 = (bf16[8,144,864]{2,1,0:T(8,128)(2,1)}, bf16[8,144,288]{2,1,0:T(8,128)(2,1)}, bf16[8,144,1152]{2,1,0:T(8,128)(2,1)}, bf16[4,256,1152]{2,1,0:T(8,128)(2...) custom-call(s32[16,128]{1,0:T(8,128)} %broadcast_in_dim.170.ids_ref, ...), custom_call_target="tpu_custom_call" | custom-call | tf_op jit(solution)/shard_map/front/pallas_call | solution.py:682
  94.1 2.2 convert_reduce_fusion
  96.4 2.4 fusion.6
  98.9 0.1 reshape.472
  99.0 0.1 slice_reduce_fusion.8
  99.3 9.7 %fusion.9.hidden_rows = bf16[4,256,1152]{2,1,0:T(8,128)(2,1)} fusion(bf16[4,256,1152]{2,1,0:T(8,128)(2,1)S(1)} %copy-done, f32[1152]{0:T(1024)S(1)} %get-tuple-element.144, f32[1152]{0:T(1024)S(1)} %get-tuple-element.145, f32[1152]{0:T(1024)S(1)} %get-tuple-element.146, f32[1152]{0:T(1024)S(1)} %get-tuple-element.147, f32[1152]{0:T(1024)S(1)} %get-tuple-element.148, ...), kind=kLoop, calls=%fused_computation.17 | loop fusion | flops 15335424 | bytes 4766720 | tf_op jit(solution)/shard_map/convert_element_type | solution.py:1664
  108.9 0.1 fusion.35
  109.0 0.1 pad.12.clone
  109.1 0.1 maximum_convert_fusion.1
  109.2 0.1 reshape.483
  109.3 4.8 %add_convert_fusion = bf16[1024,864]{0,1:T(8,128)(2,1)S(1)} fusion(bf16[1024,1152]{1,0:T(8,128)(2,1)} %bitcast.87, bf16[1152,864]{1,0:T(8,128)(2,1)} %bitcast.92, f32[864]{0:T(1024)S(1)} %reshape.483), kind=kOutput, calls=%fused_computation.20 | convolution fusion | flops 2040201216 | bytes 6122880 | tf_op jit(solution)/shard_map/dot_general | solution.py:1671
  114.1 0.2 reduce_window_sum.11
  114.3 0.1 convert_reduce_fusion.1
  114.4 0.7 broadcast_compare_fusion.1
  115.0 1.9 fusion.1
  116.9 1.9 fusion
  118.8 1.5 copy-done.1
  120.2 4.7 %fusion.2 = (f32[4,512]{1,0:T(4,128)S(1)}, f32[4,512]{1,0:T(4,128)S(1)}) fusion(f32[4,512,1024]{2,1,0:T(8,128)S(1)} %get-tuple-element.174, f32[4,512]{1,0:T(4,128)S(1)} %get-tuple-element.173, pred[512,1024]{1,0:T(8,128)(4,1)S(1)} %get-tuple-element.163, f32[4,512]{1,0:T(4,128)S(1)} %get-tuple-element.171, f32[4,512,1024]{2,1,0:T(8,128)S(1)} %get-tuple-element.172, ...), kind=kLoop, calls=%fused_computation.8 | loop fusion | flops 16773120 | bytes 17858560 | tf_op jit(solution)/shard_map/while/body/eval_jaxpr/reduce_sum | solution.py:1698
  125.0 0.6 pad_maximum_fusion.2.totals_ref
  125.6 5.6 %fusion.14 = bf16[512,4,72]{0,2,1:T(8,128)(2,1)S(1)} fusion(f32[4,512,1024]{2,1,0:T(8,128)} %copy-done.3, f32[4,512]{1,0:T(4,128)S(1)} %get-tuple-element.175, f32[4,512]{1,0:T(4,128)S(1)} %get-tuple-element.173, pred[512,1024]{1,0:T(8,128)(4,1)S(1)} %get-tuple-element.163, bf16[1024,4,3,72]{0,3,2,1:T(8,128)(2,1)S(1)} %bitcast.96), kind=kOutput, calls=%fused_computation.23 | convolution fusion | flops 312623104 | bytes 9814016 | tf_op jit(solution)/shard_map/while/body/eval_jaxpr/hqk,khd->qhd/dot_general | solution.py:1701
  131.2 0.3 copy-done.2
  131.5 2.6 fusion.15
  134.1 0.1 pad_maximum_fusion.1
  134.1 0.4 reshape.475
  134.6 1.4 copy.93.mixed_ref
  136.0 0.6 fusion.26.hot_ref
  136.6 0.1 reshape.479
  136.7 0.7 fusion.18.vectors_ref
  137.4 0.5 broadcast.289
  137.9 0.7 reduce.36
  138.6 1.1 reshape.485.segments_ref
  139.8 0.6 maximum_convert_fusion.bias_ref
  140.4 111.2 %middle.1 = (bf16[4,256,1152]{2,1,0:T(8,128)(2,1)}, bf16[4,256,1152]{2,1,0:T(8,128)(2,1)}, bf16[4,256,1152]{2,1,0:T(8,128)(2,1)}, bf16[4,256,1152]{2,1,0:T(8,128...) custom-call(bf16[4,256,288]{2,1,0:T(8,128)(2,1)} %copy.93.mixed_ref,, ...), custom_call_target="tpu_custom_call" | custom-call | tf_op jit(solution)/shard_map/middle/pallas_call | solution.py:1116
  251.6 2.5 copy.86
  254.1 0.2 slice_reduce_fusion
  254.3 0.1 fusion.33
  254.4 0.1 eq.145
  254.5 0.1 eq.148
  254.6 0.7 compare_convert_fusion
  255.3 0.7 fusion.24
  256.0 0.7 copy.100.silu_ref
  256.8 1.0 copy.97.keys_image
  257.8 0.6 reshape.484.ffn_bias
  258.4 118.7 %rear.1 = (bf16[256,1152]{1,0:T(8,128)(2,1)}, f32[256,1152]{1,0:T(8,128)}, f32[128,288]{1,0:T(8,128)}, f32[128,288]{1,0:T(8,128)}, f32[288,864]{1,0:T(8,128)}, /...) custom-call(bf16[4,256,864]{2,1,0:T(8,128)(2,1)} %bitcast.88, ...), custom_call_target="tpu_custom_call" | custom-call | tf_op jit(solution)/shard_map/rear/pallas_call | solution.py:1529
  377.2 2.2 pad_maximum_fusion
  379.4 0.8 slice_reduce_fusion.10
  380.1 0.1 reshape_squeeze.3
  380.2 0.7 pad_maximum_fusion.3
  380.9 1.7 copy.102
  382.6 1.7 copy.103
  384.3 1.5 fusion.31
  385.8 0.6 constant_dynamic-slice_fusion.1
  386.4 0.6 constant_dynamic-slice_fusion
  387.1 1.4 slice_reduce_fusion.11
  388.4 1.9 copy.118
  390.3 2.4 copy.119
  392.7 1.0 copy.120
  393.7 0.8 copy.121
  394.5 0.7 copy.122
  395.2 0.8 copy.123
  (59 shorter events, 0.4 us)
Async XLA Ops:
  0.6 98.3 %copy-start.12 = (bf16[6912]{0:T(1024)(128)(2,1)S(1)}, bf16[6912]{0:T(1024)(128)(2,1)}, u32[]{:S(2)}) copy-start(bf16[6912]{0:T(1024)(128)(2,1)} %param.22) | copy-start | bytes 41476
  0.7 98.5 %copy-start.13 = (s32[1,1024]{1,0:T(1,128)S(1)}, s32[1,1024]{1,0:T(1,128)}, u32[]{:S(2)}) copy-start(s32[1,1024]{1,0:T(1,128)} %param.32) | copy-start | bytes 12292
  94.1 4.7 %copy-start.11 = (f32[8,8,864]{2,1,0:T(8,128)S(1)}, f32[8,8,864]{2,1,0:T(8,128)}, u32[]{:S(2)}) copy-start(f32[8,8,864]{2,1,0:T(8,128)} %get-tuple-element.59) | copy-start | bytes 663556
  94.1 5.1 %copy-start = (bf16[4,256,1152]{2,1,0:T(8,128)(2,1)S(1)}, bf16[4,256,1152]{2,1,0:T(8,128)(2,1)}, u32[]{:S(2)}) copy-start(bf16[4,256,1152]{2,1,0:T(8,128)(2,1)} %get-tuple-element.58) | copy-start | bytes 7077892
  96.3 12.6 %copy-start.17 = (bf16[4,144]{1,0:T(4,128)(2,1)S(1)}, bf16[4,144]{1,0:T(4,128)(2,1)}, u32[]{:S(2)}) copy-start(bf16[4,144]{1,0:T(4,128)(2,1)} %param.24) | copy-start | bytes 3460
  109.3 4.8 %copy-start.18 = (s32[1,4]{1,0:T(1,128)S(1)}, s32[1,4]{1,0:T(1,128)}, u32[]{:S(2)}) copy-start(s32[1,4]{1,0:T(1,128)} %param.31) | copy-start | bytes 52
  114.3 142.4 %copy-start.8 = (s32[1024]{0:T(1024)}, s32[1024]{0:T(1024)S(1)}, u32[]{:S(2)}) copy-start(s32[1024]{0:T(1024)S(1)} %convert_reduce_fusion.1) | copy-start | bytes 12292
  116.9 3.3 copy-start.1
  118.7 6.2 %copy-start.3 = (f32[4,512,1024]{2,1,0:T(8,128)}, f32[4,512,1024]{2,1,0:T(8,128)S(1)}, u32[]{:S(2)}) copy-start(f32[4,512,1024]{2,1,0:T(8,128)S(1)} %get-tuple-element.174) | copy-start | bytes 25165828
  125.6 5.8 %copy-start.2 = (f32[4,512,1024]{2,1,0:T(8,128)S(1)}, f32[4,512,1024]{2,1,0:T(8,128)}, u32[]{:S(2)}) copy-start(f32[4,512,1024]{2,1,0:T(8,128)} %copy-done.1) | copy-start | bytes 25165828
  134.0 5.7 %copy-start.14 = (bf16[1152]{0:T(1024)(128)(2,1)S(1)}, bf16[1152]{0:T(1024)(128)(2,1)}, u32[]{:S(2)}) copy-start(bf16[1152]{0:T(1024)(128)(2,1)} %param.28) | copy-start | bytes 6916
  134.0 5.7 %copy-start.15 = (bf16[1152]{0:T(1024)(128)(2,1)S(1)}, bf16[1152]{0:T(1024)(128)(2,1)}, u32[]{:S(2)}) copy-start(bf16[1152]{0:T(1024)(128)(2,1)} %param.26) | copy-start | bytes 6916
  140.4 113.8 %copy-start.10 = (s32[8,16,128]{2,1,0:T(8,128)S(1)}, s32[8,16,128]{2,1,0:T(8,128)}, u32[]{:S(2)}) copy-start(s32[8,16,128]{2,1,0:T(8,128)} %get-tuple-element.71) | copy-start | bytes 196612
  140.4 115.0 %copy-start.9 = (f32[8,8,288]{2,1,0:T(8,128)S(1)}, f32[8,8,288]{2,1,0:T(8,128)}, u32[]{:S(2)}) copy-start(f32[8,8,288]{2,1,0:T(8,128)} %get-tuple-element.70) | copy-start | bytes 221188
  140.4 117.4 %copy-start.16 = (bf16[1152]{0:T(1024)(128)(2,1)S(1)}, bf16[1152]{0:T(1024)(128)(2,1)}, u32[]{:S(2)}) copy-start(bf16[1152]{0:T(1024)(128)(2,1)} %param.30) | copy-start | bytes 6916
  377.2 15.6 %copy-start.4 = (f32[288,864]{1,0:T(8,128)S(1)}, f32[288,864]{1,0:T(8,128)}, u32[]{:S(2)}) copy-start(f32[288,864]{1,0:T(8,128)} %get-tuple-element.195) | copy-start | bytes 2985988
  377.2 16.5 %copy-start.6 = (f32[144,864]{1,0:T(8,128)S(1)}, f32[144,864]{1,0:T(8,128)}, u32[]{:S(2)}) copy-start(f32[144,864]{1,0:T(8,128)} %get-tuple-element.197) | copy-start | bytes 1492996
  377.2 17.3 %copy-start.7 = (f32[144,288]{1,0:T(8,128)S(1)}, f32[144,288]{1,0:T(8,128)}, u32[]{:S(2)}) copy-start(f32[144,288]{1,0:T(8,128)} %get-tuple-element.199) | copy-start | bytes 497668
  377.2 18.0 %copy-start.5 = (f32[144,1152]{1,0:T(8,128)S(1)}, f32[144,1152]{1,0:T(8,128)}, u32[]{:S(2)}) copy-start(f32[144,1152]{1,0:T(8,128)} %get-tuple-element.201) | copy-start | bytes 1990660

commit v6 on v5

--- a/solution.py
+++ b/solution.py
@@ -537,15 +537,9 @@
     class_ref,
     ada_ref,
     patches_ref,
-    cotangent_ref,
     qkv_ref,
-    out_ref,
-    fc1_ref,
     qkv_full,
-    out_full,
-    fc1_full,
     patches_full,
-    cotangent_full,
     cond_all,
     mods_ref,
     ids_all,
@@ -564,10 +558,6 @@
     head_recv,
     qkv_send,
     qkv_recv,
-    out_send,
-    out_recv,
-    fc1_send,
-    fc1_recv,
     local_sems,
 ):
     row, member, sibling, partner, opposite = places()
@@ -594,18 +584,9 @@
 
     ids_copies = spread(0, lambda other: ids_ref, ids_all)
     gather_qkv = RowGather(qkv_ref, qkv_full, qkv_send, qkv_recv, local_sems.at[0], 3)
-    gather_out = RowGather(out_ref, out_full, out_send, out_recv, local_sems.at[1], 1)
-    gather_fc1 = RowGather(fc1_ref, fc1_full, fc1_send, fc1_recv, local_sems.at[2], 3)
-    gather_patches = HeadGather(
-        patches_ref, patches_full, head_send.at[0], head_recv.at[0], local_sems.at[3]
-    )
-    gather_cotangent = HeadGather(
-        cotangent_ref, cotangent_full, head_send.at[1], head_recv.at[1], local_sems.at[4]
-    )
+    gather_patches = HeadGather(patches_ref, patches_full, head_send, head_recv, local_sems.at[1])
     gather_patches.start()
     gather_qkv.own.start()
-    gather_out.own.start()
-    gather_fc1.own.start()
     gather_qkv.start(0)
     ids_all[row] = ids_ref[...]
     settle(ids_copies)
@@ -642,7 +623,6 @@
     mods_in[row] = mods_part[row]
     gather_qkv.relay(1)
     settle(copies)
-    gather_out.start(0)
     beside = to_head(mods_in, mods_sibling, pair_send.at[0], pair_recv.at[0], sibling)
     beside.start()
     gather_patches.wait_sibling()
@@ -651,29 +631,15 @@
     across = to_head(mods_pair, mods_partner, pair_send.at[1], pair_recv.at[1], partner)
     across.start()
     gather_patches.wait_partner()
-    gather_cotangent.start()
-    gather_fc1.start(0)
     gather_qkv.relay(2)
     across.wait()
     mods_ref[...] = mods_pair[...] + mods_partner[...]
     gather_patches.wait_opposite()
-    gather_fc1.start(1)
-    gather_out.relay(0)
-    gather_fc1.start(2)
-    gather_fc1.relay(0)
-    gather_cotangent.wait_sibling()
-    gather_cotangent.wait_partner()
-    gather_fc1.relay(1)
-    gather_cotangent.wait_opposite()
-    gather_fc1.relay(2)
     gather_patches.finish()
-    gather_cotangent.finish()
     gather_qkv.finish()
-    gather_out.finish()
-    gather_fc1.finish()
-
-
-def front(ids, time_table, class_table, w_ada, patches, cotangent, w_qkv, w_out, w_fc1):
+
+
+def front(ids, time_table, class_table, w_ada, patches, w_qkv):
     depth, ada_width = w_ada.shape
     shape = jax.ShapeDtypeStruct
     slotted = (ROW_PARTS, SLOT_ROWS)
@@ -683,16 +649,13 @@
         front_kernel,
         out_shape=(
             shape((ROW_PARTS,) + w_qkv.shape, jnp.bfloat16),
-            shape((ROW_PARTS,) + w_out.shape, jnp.bfloat16),
-            shape((ROW_PARTS,) + w_fc1.shape, jnp.bfloat16),
-            shape((HEAD_PARTS,) + patches.shape, jnp.bfloat16),
             shape((HEAD_PARTS,) + patches.shape, jnp.bfloat16),
             shape(slotted + (depth,), jnp.float32),
             shape(slotted + (ada_width,), jnp.float32),
             shape((ROW_PARTS,) + ids.shape, jnp.int32),
         ),
-        in_specs=[VMEM_SPEC] * 9,
-        out_specs=[ANY_SPEC] * 5 + [VMEM_SPEC] * 3,
+        in_specs=[VMEM_SPEC] * 6,
+        out_specs=[ANY_SPEC] * 2 + [VMEM_SPEC] * 3,
         scratch_shapes=[narrow] * 2
         + [wide] * 5
         + [
@@ -700,21 +663,17 @@
             DMA((4, 7)),
             DMA((2,)),
             DMA((2,)),
-            DMA((2, 3)),
-            DMA((2, 3)),
+            DMA((3,)),
+            DMA((3,)),
             DMA((3, 7)),
             DMA((3, 7)),
-            DMA((1, 7)),
-            DMA((1, 7)),
-            DMA((3, 7)),
-            DMA((3, 7)),
-            DMA((5,)),
+            DMA((2,)),
         ],
         compiler_params=pltpu.CompilerParams(
             collective_id=0, has_side_effects=True, vmem_limit_bytes=GRANT
         ),
         name="front",
-    )(ids, time_table, class_table, w_ada, patches, cotangent, w_qkv, w_out, w_fc1)
+    )(ids, time_table, class_table, w_ada, patches, w_qkv)
 
 
 class HeadReduce:
@@ -879,22 +838,27 @@
     lax.fori_loop(0, 3, some, 0)
 
 
-def middle_kernel(
-    mixed_ref,
-    out_ref,
-    fc1_ref,
-    fc2_ref,
+def core_kernel(
+    patches_full,
+    qkv_ref,
+    out_shard,
+    fc1_shard,
+    fc2_shard,
     cotangent_ref,
     patches_ref,
     segments_ref,
+    keys_image,
+    rows_image,
     hot_ref,
     vectors_ref,
     bias_ref,
-    ffn_rows,
-    hidden_rows,
+    qkv_bias,
+    normed_rows,
+    parts,
+    totals_out,
+    mixed,
+    out_w,
     active_rows,
-    inner_grad,
-    ffn_part,
     after_ref,
     after_grad,
     attn_grad,
@@ -904,82 +868,195 @@
     fc1_part,
     fc2_head,
     fc2_neck,
+    ffn_rows,
+    hidden_rows,
+    inner_grad,
     fc2_part,
     inner_bias,
     ffn_bias,
+    out_full,
+    fc1_full,
     fc2_full,
     active_grad,
-    first_part,
-    second_part,
-    first_beside,
-    second_beside,
-    first_pair,
-    second_pair,
-    first_across,
-    second_across,
+    value_columns,
+    head_mixed,
+    bias,
+    group_part,
+    beside_in,
+    pair_rows,
+    across_in,
     attn_out,
     gather_send,
     gather_recv,
     reduce_send,
     reduce_recv,
+    out_send,
+    out_recv,
+    fc1_send,
+    fc1_recv,
     fc2_send,
     fc2_recv,
-    local_sem,
+    local_sems,
     *reducing,
 ):
     row, member, sibling, partner, opposite = places()
+    direction = sibling - member
     greet(range(1, ROW_PARTS), (sibling, partner))
     tok_rows, model_width = patches_ref.shape
-    gather_fc2 = RowGather(fc2_ref, fc2_full, fc2_send, fc2_recv, local_sem, 3)
+    blocks = normed_rows.shape[0]
+    seq_len = blocks * tok_rows
+    width = qkv_ref.shape[1]
+    head_local = totals_out.shape[0]
+    head_size = width // (3 * head_local)
+    scale_factor = 1.0 / math.sqrt(head_size)
+    loads = [
+        pltpu.make_async_copy(patches_full.at[block], normed_rows.at[block], local_sems.at[block])
+        for block in range(blocks)
+    ]
+    for load in loads:
+        load.start()
+    gather_out = RowGather(out_shard, out_full, out_send, out_recv, local_sems.at[4], 1)
+    gather_fc1 = RowGather(fc1_shard, fc1_full, fc1_send, fc1_recv, local_sems.at[5], 3)
+    gather_fc2 = RowGather(fc2_shard, fc2_full, fc2_send, fc2_recv, local_sems.at[6], 3)
+    gather_cotangent = HeadGather(
+        cotangent_ref, ffn_rows, gather_send.at[2], gather_recv.at[2], local_sems.at[7]
+    )
+    gather_out.own.start()
+    gather_out.start(0)
+    gather_fc1.own.start()
+    gather_fc1.start(0)
     gather_fc2.own.start()
-    gather_fc2.start(0)
-    gather_fc2.start(1)
-    first = HeadReduce(
-        first_part, first_beside, first_pair, first_across, reduce_send.at[0], reduce_recv.at[0]
-    )
-    second = HeadReduce(
-        second_part,
-        second_beside,
-        second_pair,
-        second_across,
-        reduce_send.at[1],
-        reduce_recv.at[1],
+    gather_cotangent.start()
+    reduce_attn = HeadReduce(
+        group_part, beside_in, pair_rows, across_in, reduce_send.at[0], reduce_recv.at[0]
+    )
+    reduce_hidden = HeadReduce(
+        group_part, beside_in, pair_rows, across_in, reduce_send.at[1], reduce_recv.at[1]
     )
     gather_hidden = HeadGather(None, hidden_rows, gather_send.at[0], gather_recv.at[0], None)
     gather_grad = HeadGather(None, attn_grad, gather_send.at[1], gather_recv.at[1], None)
+    parts[...] = jnp.zeros_like(parts)
+    for load in loads:
+        load.wait()
+
+    def first_norm(step, carry):
+        block = step // 2
+        part = pl.ds(pl.multiple_of(lax.rem(step, 2) * 128, 128), 128)
+        segments = segments_ref[block, part]
+        normed, _ = centre_rows(normed_rows[block, part].astype(jnp.float32))
+        normed_rows[block, part] = (
+            normed * (1.0 + picked(vectors_ref, 1, segments, model_width))
+            + picked(vectors_ref, 0, segments, model_width)
+        ).astype(jnp.bfloat16)
+        return carry
+
+    lax.fori_loop(0, 2 * blocks, first_norm, 0)
+    gather_out.relay(0)
+    gather_fc1.start(1)
+
+    def project_in(block, carry):
+        rows = pl.ds(pl.multiple_of(block * tok_rows, tok_rows), tok_rows)
+        active_grad[0, :, 0:width] = (
+            jnp.dot(normed_rows[block], qkv_ref[...], preferred_element_type=jnp.float32)
+            + qkv_bias[...]
+        )
+        for part in range(3 * head_local):
+            parts[part, rows, 0:head_size] = active_grad[
+                0, :, part * head_size : (part + 1) * head_size
+            ].astype(jnp.bfloat16)
+        return carry
+
+    lax.fori_loop(0, blocks, project_in, 0)
+    gather_fc1.relay(0)
+    gather_fc1.start(2)
+
+    def turn(head, carry):
+        value_columns[head] = parts[3 * head + 2].astype(jnp.float32).T.astype(jnp.bfloat16)
+        return carry
+
+    lax.fori_loop(0, head_local, turn, 0)
+
+    def attend(block):
+        rows = pl.ds(pl.multiple_of(block * tok_rows, tok_rows), tok_rows)
+        same = jnp.broadcast_to(keys_image[...], (seq_len, tok_rows)) == jnp.broadcast_to(
+            rows_image[block], (seq_len, tok_rows)
+        )
+        bias[...] = jnp.where(same, 0.0, MASKED)
+
+        def one_head(head, carry):
+            scores = (
+                times_transposed(parts[3 * head + 1], parts[3 * head, rows]) * scale_factor
+                + bias[...]
+            )
+            peak = jnp.max(scores, axis=0, keepdims=True)
+            raised = jnp.exp(scores - peak)
+            total = jnp.sum(raised, axis=0, keepdims=True)
+            totals_out[head, block] = peak + jnp.log(total)
+            head_mixed[head] = jnp.dot(
+                value_columns[head],
+                (raised * (1.0 / total)).astype(jnp.bfloat16),
+                preferred_element_type=jnp.float32,
+            ).T
+            return carry
+
+        lax.fori_loop(0, head_local, one_head, 0)
+        for head in range(head_local):
+            active_grad[1, :, head * head_size : (head + 1) * head_size] = head_mixed[
+                head, :, 0:head_size
+            ]
+        mixed[block] = active_grad[1, :, 0 : head_local * head_size].astype(jnp.bfloat16)
+
+    def attend_pair(base, factor):
+        def one(step, carry):
+            attend(base + step * factor)
+            return carry
+
+        lax.fori_loop(0, 2, one, 0)
 
     def project(block):
-        first_part[block] = times_transposed(mixed_ref[block], out_ref[...]).astype(jnp.bfloat16)
-
+        group_part[block] = times_transposed(mixed[block], out_w[...]).astype(jnp.bfloat16)
+
+    attend_pair(opposite, -direction)
+    gather_out.finish()
+    out_w[...] = out_full[...].reshape(out_w.shape)
     project(opposite)
-    first.first.start()
+    reduce_attn.first.start()
     project(partner)
-    first.send_pair()
+    reduce_attn.send_pair()
+    gather_fc1.relay(1)
+    gather_fc2.start(0)
+    attend_pair(sibling, -direction)
+    gather_fc1.relay(2)
+    gather_fc2.start(1)
     project(sibling)
-    first.second.start()
+    reduce_attn.second.start()
     project(member)
-
-    def scale_cotangent(block, carry):
-        index = block // 2
-        part = pl.ds(pl.multiple_of(lax.rem(block, 2) * 128, 128), 128)
+    gather_cotangent.wait_sibling()
+    gather_cotangent.wait_partner()
+    gather_cotangent.wait_opposite()
+    gather_cotangent.finish()
+
+    def scale_cotangent(step, carry):
+        block = step // 2
+        part = pl.ds(pl.multiple_of(lax.rem(step, 2) * 128, 128), 128)
         grad = (
-            picked(vectors_ref, 5, segments_ref[index, part], model_width)
-            * cotangent_ref[index, part].astype(jnp.float32)
+            picked(vectors_ref, 5, segments_ref[block, part], model_width)
+            * ffn_rows[block, part].astype(jnp.float32)
         ).astype(jnp.bfloat16)
-        ffn_rows[index, part] = grad
+        ffn_rows[block, part] = grad
         ffn_bias[...] += jnp.sum(grad.astype(jnp.float32).reshape(16, 8, model_width), axis=0)
         return carry
 
     ffn_bias[...] = jnp.zeros_like(ffn_bias)
-    lax.fori_loop(0, 2 * HEAD_PARTS, scale_cotangent, 0)
+    lax.fori_loop(0, 2 * blocks, scale_cotangent, 0)
     gather_fc2.relay(0)
     gather_fc2.start(2)
-    first.settle()
+    reduce_attn.settle()
 
     def second_norm(block, carry):
         part = pl.ds(pl.multiple_of(block * 128, 128), 128)
         segments = segments_ref[member, part]
-        out = first.rows(part) + bias_ref[0:1]
+        out = reduce_attn.rows(part) + bias_ref[0:1]
         after = patches_ref[part].astype(jnp.float32) + (
             picked(vectors_ref, 2, segments, model_width) * out
         )
@@ -994,10 +1071,14 @@
 
     lax.fori_loop(0, tok_rows // 128, second_norm, 0)
     gather_hidden.start()
+    reduce_attn.finish()
     gather_fc2.relay(1)
     gather_fc2.relay(2)
+    gather_fc1.finish()
     gather_fc2.finish()
-    fc2 = fc2_full.reshape(fc1_ref.shape)
+    hidden_width = active_rows.shape[2]
+    fc1 = fc1_full.reshape(model_width, hidden_width)
+    fc2 = fc2_full.reshape(model_width, hidden_width)
 
     def through_fc2(block, carry):
         active_grad[block] = jnp.dot(
@@ -1010,7 +1091,7 @@
 
     def feed(block, carry):
         inner = jnp.dot(
-            hidden_rows[block], fc1_ref[...], preferred_element_type=jnp.float32
+            hidden_rows[block], fc1[...], preferred_element_type=jnp.float32
         ) + bias_ref[1:2]
         square = inner * inner
         bent = jnp.tanh(TANH_COEFF * (inner + 0.044715 * square * inner))
@@ -1027,10 +1108,9 @@
         return carry
 
     def return_fc1(block, carry):
-        second_part[block] = times_transposed(inner_grad[block], fc1_ref[...]).astype(jnp.bfloat16)
+        group_part[block] = times_transposed(inner_grad[block], fc1[...]).astype(jnp.bfloat16)
         return carry
 
-    direction = sibling - member
     gather_hidden.wait_sibling()
     lax.fori_loop(0, 2, lambda step, carry: feed(member + step * direction, carry), 0)
     gather_hidden.wait_partner()
@@ -1042,13 +1122,13 @@
         return return_fc1(block, carry)
 
     lax.fori_loop(0, 2, feed_far, 0)
-    second.first.start()
-    second.send_pair()
+    reduce_hidden.first.start()
+    reduce_hidden.send_pair()
     lax.fori_loop(0, 2, lambda step, carry: return_fc1(sibling - step * direction, carry), 0)
-    second.second.start()
+    reduce_hidden.second.start()
 
     def forward_fc2(block, carry):
-        ffn_part[block] = times_transposed(active_rows[block], fc2[...]).astype(jnp.bfloat16)
+        active_rows[block] = times_transposed(active_rows[block], fc2[...]).astype(jnp.bfloat16)
         return carry
 
     weight_grad(ffn_rows, active_rows, fc2_part)
@@ -1059,15 +1139,15 @@
         unit.start()
     lax.fori_loop(0, HEAD_PARTS, forward_fc2, 0)
     slot_sums[...] = jnp.zeros_like(slot_sums)
-    second.settle()
+    reduce_hidden.settle()
 
     def second_back(block, carry):
         part = pl.ds(pl.multiple_of(block * 128, 128), 128)
         segments = segments_ref[member, part]
-        grad = second.rows(part)
+        grad = reduce_hidden.rows(part)
         normed, factor = centre_rows(after_ref[part])
         weighted = grad * (1.0 + picked(vectors_ref, 4, segments, model_width))
-        total = cotangent_ref[member, part].astype(jnp.float32) + factor * (
+        total = cotangent_ref[part].astype(jnp.float32) + factor * (
             weighted
             - jnp.mean(weighted, axis=1, keepdims=True)
             - normed * jnp.mean(weighted * normed, axis=1, keepdims=True)
@@ -1098,77 +1178,91 @@
         unit.finish()
     gather_hidden.finish()
     gather_grad.finish()
-    first.finish()
-    second.finish()
-
-
-def middle(mixed, w_out, w_fc1, w_fc2, cotangent, patches, segments, hot, vectors, biases):
+    reduce_hidden.finish()
+
+
+def core(head_size, *args):
     shape = jax.ShapeDtypeStruct
-    tok_rows, model_width = patches.shape
-    hidden_width = w_fc1.shape[1]
-    width_part = w_fc2.shape[0]
-    rows_low = shape((HEAD_PARTS, tok_rows, model_width), jnp.bfloat16)
-    wide_low = shape((HEAD_PARTS, tok_rows, hidden_width), jnp.bfloat16)
-    own = shape((tok_rows, model_width), jnp.float32)
-    own_low = pltpu.VMEM((tok_rows, model_width), jnp.bfloat16)
-    group_low = pltpu.VMEM((HEAD_PARTS, tok_rows, model_width), jnp.bfloat16)
-    pair_low = pltpu.VMEM((2, tok_rows, model_width), jnp.bfloat16)
+    patches_full, w_qkv, out_shard, fc1_shard = args[:4]
+    blocks, tok_rows, model_width = patches_full.shape
+    seq_len = blocks * tok_rows
+    out_width = out_shard.shape[1]
+    width_part, hidden_width = fc1_shard.shape
+    third = width_part // 3
+    head_local = out_width // head_size
+    low = jnp.bfloat16
+    full = jnp.float32
+    rows_low = shape((blocks, tok_rows, model_width), low)
+    own = shape((tok_rows, model_width), full)
+    own_low = pltpu.VMEM((tok_rows, model_width), low)
+    group_low = pltpu.VMEM((blocks, tok_rows, model_width), low)
+    hidden_low = pltpu.VMEM((blocks, tok_rows, hidden_width), low)
+    part_low = (4, 2, width_part, hidden_width)
     return pl.pallas_call(
-        middle_kernel,
+        core_kernel,
         out_shape=[
             rows_low,
-            rows_low,
-            wide_low,
-            wide_low,
+            shape((3 * head_local, seq_len, HEAD_LANES), low),
+            shape((head_local, blocks, 1, tok_rows), full),
+            shape((blocks, tok_rows, out_width), low),
+            shape((model_width, out_width), low),
             rows_low,
             own,
             own,
             rows_low,
-            shape((3, SLOT_ROWS, model_width), jnp.float32),
-            shape((8, hidden_width), jnp.float32),
-            shape((4, 2, width_part // 3, hidden_width), jnp.bfloat16),
-            shape((4, 2, width_part, hidden_width), jnp.bfloat16),
-            shape((width_part // 3, hidden_width), jnp.float32),
-            shape((width_part // 3, hidden_width), jnp.float32),
+            shape((3, SLOT_ROWS, model_width), full),
+            shape((8, hidden_width), full),
+            shape((4, 2, third, hidden_width), low),
+            shape(part_low, low),
+            shape((third, hidden_width), full),
+            shape((third, hidden_width), full),
         ],
-        in_specs=[VMEM_SPEC] * 10,
-        out_specs=[VMEM_SPEC] * 14,
+        in_specs=[ANY_SPEC] + [VMEM_SPEC] * 13,
+        out_specs=[VMEM_SPEC] * 15,
         scratch_shapes=[
-            pltpu.VMEM((4, 2, width_part, hidden_width), jnp.bfloat16),
-            pltpu.VMEM((8, hidden_width), jnp.float32),
-            pltpu.VMEM((8, model_width), jnp.float32),
-            pltpu.VMEM((ROW_PARTS,) + w_fc2.shape, jnp.bfloat16),
-            pltpu.VMEM((HEAD_PARTS, tok_rows, hidden_width), jnp.float32),
             group_low,
             group_low,
-            pair_low,
-            pair_low,
+            hidden_low,
+            pltpu.VMEM(part_low, low),
+            pltpu.VMEM((8, hidden_width), full),
+            pltpu.VMEM((8, model_width), full),
+            pltpu.VMEM((ROW_PARTS,) + out_shard.shape, low),
+            pltpu.VMEM((ROW_PARTS,) + fc1_shard.shape, low),
+            pltpu.VMEM((ROW_PARTS,) + fc1_shard.shape, low),
+            pltpu.VMEM((blocks, tok_rows, hidden_width), full),
+            pltpu.VMEM((head_local, HEAD_LANES, seq_len), low),
+            pltpu.VMEM((head_local, tok_rows, HEAD_LANES), full),
+            pltpu.VMEM((seq_len, tok_rows), full),
+            group_low,
+            pltpu.VMEM((2, tok_rows, model_width), low),
             own_low,
             own_low,
-            own_low,
-            own_low,
-            pltpu.VMEM((tok_rows, model_width), jnp.float32),
+            pltpu.VMEM((tok_rows, model_width), full),
+            DMA((3, 3)),
+            DMA((3, 3)),
             DMA((2, 3)),
             DMA((2, 3)),
-            DMA((2, 3)),
-            DMA((2, 3)),
+            DMA((1, 7)),
+            DMA((1, 7)),
             DMA((3, 7)),
             DMA((3, 7)),
-            DMA(()),
+            DMA((3, 7)),
+            DMA((3, 7)),
+            DMA((8,)),
         ]
-        + reduce_scratch([(width_part // 3, hidden_width)] * 2),
+        + reduce_scratch([(third, hidden_width)] * 2),
         compiler_params=pltpu.CompilerParams(
-            collective_id=2, has_side_effects=True, vmem_limit_bytes=GRANT
+            collective_id=2, has_side_effects=True, vmem_limit_bytes=67_000_000
         ),
-        name="middle",
-    )(mixed, w_out, w_fc1, w_fc2, cotangent, patches, segments, hot, vectors, biases)
+        name="core",
+    )(*args)
 
 
 HEAD_LANES = 128
 
 
 def rear_kernel(
-    projected_ref,
+    parts,
     grad_ref,
     out_ref,
     totals_ref,
@@ -1206,7 +1300,6 @@
     qkv_grad,
     out_grad,
     bias_sum,
-    parts,
     mixed_grad,
     key_columns,
     grad_keys,
@@ -1282,23 +1375,17 @@
         unit.start()
     reduce_ffn.start()
     reduce_ffn.send_pair()
-    blocks, tok_rows, width = projected_ref.shape
-    model_width = patches_ref.shape[1]
+    blocks, tok_rows, model_width = grad_ref.shape
+    width = qkv_ref.shape[1]
     head_local = totals_ref.shape[0]
     head_size = width // (3 * head_local)
     scale_factor = 1.0 / math.sqrt(head_size)
     seq_len = blocks * tok_rows
-    parts[...] = jnp.zeros_like(parts)
     mixed_grad[...] = jnp.zeros_like(mixed_grad)
     bias_own[...] = jnp.zeros_like(bias_own)
 
     def unpack(block, carry):
         rows = pl.ds(pl.multiple_of(block * tok_rows, tok_rows), tok_rows)
-        packed[...] = projected_ref[block].astype(jnp.float32)
-        for part in range(3 * head_local):
-            parts[part, rows, 0:head_size] = packed[
-                :, part * head_size : (part + 1) * head_size
-            ].astype(jnp.bfloat16)
         packed[:, 0 : head_local * head_size] = jnp.dot(
             grad_ref[block], out_ref[...], preferred_element_type=jnp.float32
         )
@@ -1505,13 +1592,13 @@
 
 def rear(*args):
     shape = jax.ShapeDtypeStruct
-    projected, w_out, totals, grad_w_fc2, w_qkv, biases, patches, buckets, w_ada = (
-        args[place] for place in (0, 2, 3, 6, 9, 11, 12, 20, 22)
-    )
-    blocks, tok_rows, width = projected.shape
+    grads, w_out, totals, grad_w_fc2, w_qkv, biases, buckets, w_ada = (
+        args[place] for place in (1, 2, 3, 6, 9, 11, 20, 22)
+    )
+    blocks, tok_rows, model_width = grads.shape
+    width = w_qkv.shape[1]
     head_local = totals.shape[0]
     seq_len = blocks * tok_rows
-    model_width = patches.shape[1]
     third, hidden_width = grad_w_fc2.shape[2:]
     width_part = 3 * third
     out_width = w_out.shape[1]
@@ -1544,7 +1631,6 @@
         in_specs=[VMEM_SPEC] * 27,
         out_specs=[VMEM_SPEC] * 11,
         scratch_shapes=[
-            pltpu.VMEM((3 * head_local, seq_len, HEAD_LANES), low),
             pltpu.VMEM((head_local, seq_len, HEAD_LANES), low),
             pltpu.VMEM((head_local, HEAD_LANES, seq_len), low),
             heads_wide,
@@ -1625,95 +1711,40 @@
         jnp.concatenate([bucket_ids[0], slot_pad, class_labels[0], slot_pad])[:, None],
         (2 * SLOT_ROWS, table_rows),
     )
-    (
-        qkv_full,
-        out_full,
-        fc1_full,
-        patches_full,
-        cotangent_full,
-        condition,
-        mods,
-        ids_all,
-    ) = front(ids, time_table, class_table, w_ada, patches, cotangent, w_qkv, w_out, w_fc1)
+    qkv_full, patches_full, condition, mods, ids_all = front(
+        ids, time_table, class_table, w_ada, patches, w_qkv
+    )
     qkv_cols = qkv_full.reshape(model_width, w_qkv.shape[1])
-    out_cols = out_full.reshape(model_width, w_out.shape[1])
-    fc1_cols = fc1_full.reshape(model_width, w_fc1.shape[1])
     condition = condition.reshape(every_slot, condition.shape[2])
     silu_value, silu_pull = jax.vjp(silu_plain, condition)
     silu_low = silu_value.astype(jnp.bfloat16)
     mods_all = mods[:, :slot_count].transpose(1, 0, 2).reshape(
         slot_count, row_parts * ada_width
     ) + b_ada.astype(jnp.float32)
-    row_segments = segment_ids[0][:, None]
-
-    def by_token(part_index, segments):
-        vectors = mods_all[:, part_index * model_width : (part_index + 1) * model_width]
-        chosen = vectors[slot_count - 1][None, :]
-        for slot in range(slot_count - 2, -1, -1):
-            chosen = jnp.where(segments == slot, vectors[slot][None, :], chosen)
-        return chosen
-
     own_segments = lax.dynamic_slice_in_dim(segment_ids[0], member * tok_rows, tok_rows)[:, None]
     token_hot = (own_segments == jnp.arange(SLOT_ROWS, dtype=jnp.int32)[None, :]).astype(
         jnp.float32
     )
-    rows_one = modulate(
-        patches_full.reshape(group_rows, model_width).astype(jnp.float32),
-        by_token(0, row_segments),
-        by_token(1, row_segments),
-    ).astype(jnp.bfloat16)
     zero_bias = jnp.zeros((head_local, head_size), b_qv.dtype)
     qkv_bias = (
         jnp.concatenate([b_qv[:, :head_size], zero_bias, b_qv[:, head_size:]], axis=1)
         .reshape(head_local * 3 * head_size)
         .astype(jnp.float32)
     )
-    projected = (jnp.dot(rows_one, qkv_cols, preferred_element_type=jnp.float32) + qkv_bias).astype(
-        jnp.bfloat16
-    )
-    seq_qkv = projected.reshape(seq_count, seq_len, head_local, 3, head_size)
     slot_ends = jnp.cumsum(image_lengths, axis=1)
     places = jnp.arange(seq_len, dtype=jnp.int32)
     image_of = jnp.sum((places[None, :, None] >= slot_ends[:, None, :]).astype(jnp.int32), axis=2)
 
-    def block_scores(query_rows, key_rows, image_rows, image_cols):
-        scores = (
-            jnp.einsum("qhd,khd->hqk", query_rows, key_rows, preferred_element_type=jnp.float32)
-            * scale_factor
-        )
-        return jnp.where((image_rows[:, None] == image_cols[None, :])[None], scores, MASKED)
-
-    def attend_forward(pieces):
-        seq_block, seq_image = pieces
-        key_rows = seq_block[:, :, 1]
-        value_rows = seq_block[:, :, 2]
-        outputs = []
-        totals = []
-        for row_start in range(0, seq_len, block_rows):
-            stop_row = row_start + block_rows
-            query_rows = seq_block[row_start:stop_row, :, 0]
-            scores = block_scores(query_rows, key_rows, seq_image[row_start:stop_row], seq_image)
-            row_peak = jnp.max(scores, axis=2, keepdims=True)
-            raised = jnp.exp(scores - row_peak)
-            row_total = jnp.sum(raised, axis=2, keepdims=True)
-            soft_low = (raised / row_total).astype(jnp.bfloat16)
-            outputs.append(
-                jnp.einsum(
-                    "hqk,khd->qhd", soft_low, value_rows, preferred_element_type=jnp.float32
-                ).astype(jnp.bfloat16)
-            )
-            totals.append((row_peak + jnp.log(row_total))[:, :, 0])
-        return (jnp.concatenate(outputs, axis=0), jnp.concatenate(totals, axis=1))
-
-    mixed, log_totals = lax.map(attend_forward, (seq_qkv, image_of))
-    mixed_rows = mixed.reshape(head_parts, tok_rows, head_local * head_size)
     vectors = mods_all.reshape(slot_count, 6, model_width).transpose(1, 0, 2)
     segments = segment_ids.reshape(head_parts, tok_rows, 1)
+    keys_image = image_of.reshape(seq_len, 1)
+    rows_image = image_of.reshape(head_parts, 1, tok_rows)
     (
-        ffn_rows,
-        rows_two,
-        active,
-        grad_inner,
+        rows_one,
+        parts,
+        totals,
+        mixed_rows,
+        out_cols,
         ffn_part,
         after_attn,
         grad_after,
@@ -1724,17 +1755,22 @@
         grad_w_fc1,
         fc2_head,
         fc2_neck,
-    ) = middle(
-        mixed_rows,
-        out_cols,
-        fc1_cols,
+    ) = core(
+        head_size,
+        patches_full,
+        qkv_cols,
+        w_out,
+        w_fc1,
         w_fc2,
-        cotangent_full,
+        cotangent,
         patches,
         segments,
+        keys_image,
+        rows_image,
         token_hot.T,
         vectors,
         jnp.stack([b_out, b_fc1]).astype(jnp.float32),
+        qkv_bias[None, :],
     )
     all_ids = ids_all[:, :, 0]
     table_places = lax.axis_index("rows") * table_rows + jnp.arange(table_rows, dtype=jnp.int32)
@@ -1753,15 +1789,15 @@
         grad_w_out,
         bias_all,
     ) = rear(
-        projected.reshape(head_parts, tok_rows, projected.shape[1]),
+        parts,
         attn_rows_grad,
         out_cols,
-        log_totals.reshape(head_local, head_parts, 1, tok_rows),
-        image_of.reshape(seq_len, 1),
-        image_of.reshape(head_parts, 1, tok_rows),
+        totals,
+        keys_image,
+        rows_image,
         grad_w_fc2,
         grad_w_fc1,
-        rows_one.reshape(head_parts, tok_rows, model_width),
+        rows_one,
         qkv_cols,
         mixed_rows,
         bias_sums,

time: 399 us -> 362 us (0.907)
  other arithmetic: 28.4 us -> 10.1 us
  matrix products: 16.7 us -> 0 us
    pallas_call x1, Pallas kernels: 111 us -> 156 us  [core(): pl.pallas_call(core_kernel, out_shape=[rows_low, shape((3 * head_local, s...]
    pallas_call x1, Pallas kernels: 88.8 us -> 48.6 us  [front(): pl.pallas_call(front_kernel, out_shape=(shape((ROW_PARTS,) + w_qkv.shape,...]
    dot_general x5 -> x0, matrix products: 16.7 us -> none  [the longest x2 8.14 us: attend_forward(): jnp.einsum('hqk,khd->qhd', soft_low, value_rows, preferred_element_type=j...]
    convert_element_type x2 -> x0, other arithmetic: 9.69 us -> none  [the longest x1 9.69 us: shards_linked(): rows_one = modulate(patches_full.reshape(group_rows, model_width).astype(...]
    reduce_sum x3 -> x0, other arithmetic: 9.32 us -> none  [the longest x1 4.69 us: attend_forward(): row_total = jnp.sum(raised, axis=2, keepdims=True)]
    unnamed x49 -> x25, local copies, waits for them, and re-layouts: 16.5 us -> 12.3 us
where the time goes in v6:
time: 362 us; the launch traced here: 361 us
  Pallas kernels  322 us (89%)
  local copies, waits for them, and re-layouts  27.6 us (8%)
  other arithmetic  10.1 us (3%)
    pallas_call x1, Pallas kernels, core(): pl.pallas_call(core_kernel, out_shape=[rows_low, shape((3 * head_local, s...  156 us
    pallas_call x1, Pallas kernels, rear(): pl.pallas_call(rear_kernel, out_shape=[shape((tok_rows, model_width), low...  118 us
    pallas_call x1, Pallas kernels, front(): pl.pallas_call(front_kernel, out_shape=(shape((ROW_PARTS,) + w_qkv.shape,...  48.6 us
    unnamed x25, local copies, waits for them, and re-layouts  12.3 us

profile of v6, /device:TPU:0, one launch (start us, length us, event | category | flops | bytes accessed | tf_op | source)
XLA Modules:
  0.0 360.9 jit_solution(462193220957031520)
XLA Ops:
  0.7 0.8 reduce_window_sum.11
  1.5 0.7 constant_dynamic-slice_fusion.2
  2.2 0.7 pad_add_fusion
  2.9 0.1 pad.6.clone
  3.0 0.8 fusion.12
  3.8 0.1 maximum_convert_fusion.1
  3.9 0.7 reshape.136.qkv_bias
  4.6 0.1 convert_reduce_fusion
  4.7 0.0 copy-start.6
  4.7 0.5 broadcast.55
  5.2 1.3 reduce.12
  6.5 0.7 stack.9
  7.2 0.7 stack.10
  7.9 0.6 maximum_convert_fusion.bias_ref
  8.5 1.3 reshape.137.ffn_bias
  9.8 0.6 fusion.8.hot_ref
  10.4 0.7 broadcast_in_dim.8.ids_ref
  11.1 0.7 reshape.135
  11.8 1.6 copy.63.time_ref
  13.5 1.6 copy.64.class_ref
  15.1 1.1 reshape.138.segments_ref
  16.2 1.0 copy.68.keys_image
  17.3 48.6 %front.1 = (bf16[8,144,864]{2,1,0:T(8,128)(2,1)}, bf16[4,256,1152]{2,1,0:T(8,128)(2,1)}, f32[8,8,288]{2,1,0:T(8,128)}, f32[8,8,864]{2,1,0:T(8,128)}, s32[8,16,128]{2,1,0:T(8,128)}) custom-call(s32[16,128]{1,0:T(8,128)} %broadcast_in_dim.8.ids_ref, bf16[128,288]{1,0:T(8,128)(2,1)} %copy.63.time_ref, bf16[128,288]{1,0:T(8,128)(2,1)} %copy.64.class_ref, ...), custom_call_target="tpu_custom_call" | custom-call | tf_op jit(solution)/shard_map/front/pallas_call | solution.py:648
  65.9 1.0 slice_reduce_fusion
  67.0 0.1 fusion.11
  67.0 0.1 eq.52
  67.1 0.1 eq.49
  67.2 1.0 slice_bitcast_fusion
  68.2 0.1 reshape.133
  68.3 0.7 fusion.vectors_ref
  69.0 0.7 compare_convert_fusion
  69.7 1.6 fusion.6
  71.3 0.7 copy.73.silu_ref
  72.1 0.0 copy-done.6
  72.1 155.8 %core.1 = (bf16[4,256,1152]{2,1,0:T(8,128)(2,1)}, bf16[12,1024,128]{2,1,0:T(8,128)(2,1)}, f32[4,4,1,256]{3,2,1,0:T(1,128)}, bf16[4,256,288]{2,1,0:T(8,128)(2,1)}...) custom-call(bf16[4,256,1152]{2,1,0:T(8,128)(2,1)} %get-tuple-element, ...), custom_call_target="tpu_custom_call" | custom-call | tf_op jit(solution)/shard_map/core/pallas_call | solution.py:1201
  227.9 117.9 %rear.1 = (bf16[256,1152]{1,0:T(8,128)(2,1)}, f32[256,1152]{1,0:T(8,128)}, f32[128,288]{1,0:T(8,128)}, f32[128,288]{1,0:T(8,128)}, f32[288,864]{1,0:T(8,128)}, /...) custom-call(bf16[12,1024,128]{2,1,0:T(8,128)(2,1)} %get-tuple-elemen, ...), custom_call_target="tpu_custom_call" | custom-call | tf_op jit(solution)/shard_map/rear/pallas_call | solution.py:1616
  345.8 0.0 copy-start.3
  345.8 0.0 copy-start
  345.8 1.5 slice_reduce_fusion.2
  347.3 1.5 fusion.9
  348.8 0.6 constant_dynamic-slice_fusion
  349.5 0.1 reshape_squeeze.3
  349.6 0.7 pad_maximum_fusion.1
  350.2 1.7 copy.75
  351.9 1.7 copy.76
  353.6 0.0 copy-start.1
  353.6 2.1 pad_maximum_fusion
  355.7 0.0 copy-done.3
  355.7 0.8 copy.87
  356.5 0.0 copy-done
  356.6 0.0 copy-start.4
  356.6 0.0 copy-start.5
  356.6 1.0 copy.88
  357.6 0.0 copy-done.1
  357.6 0.0 copy-start.2
  357.6 1.0 copy.89
  358.5 0.0 copy-done.4
  358.5 0.8 copy.90
  359.3 0.0 copy-done.5
  359.3 0.7 copy.91
  360.0 0.0 copy-done.2
  360.0 0.8 copy.92
  (5 shorter events, 0.0 us)
Async XLA Ops:
  4.7 67.4 %copy-start.6 = (s32[1024]{0:T(1024)}, s32[1024]{0:T(1024)S(1)}, u32[]{:S(2)}) copy-start(s32[1024]{0:T(1024)S(1)} %convert_reduce_fusion) | copy-start | bytes 12292
  345.8 9.9 %copy-start.3 = (bf16[256,1152]{1,0:T(8,128)(2,1)S(1)}, bf16[256,1152]{1,0:T(8,128)(2,1)}, u32[]{:S(2)}) copy-start(bf16[256,1152]{1,0:T(8,128)(2,1)} %get-tuple-element.163) | copy-start | bytes 1769476
  345.8 10.8 %copy-start = (f32[256,1152]{1,0:T(8,128)S(1)}, f32[256,1152]{1,0:T(8,128)}, u32[]{:S(2)}) copy-start(f32[256,1152]{1,0:T(8,128)} %get-tuple-element.164) | copy-start | bytes 3538948
  353.6 4.0 %copy-start.1 = (f32[288,864]{1,0:T(8,128)S(1)}, f32[288,864]{1,0:T(8,128)}, u32[]{:S(2)}) copy-start(f32[288,864]{1,0:T(8,128)} %get-tuple-element.167) | copy-start | bytes 2985988
  356.6 2.0 copy-start.4
  356.6 2.8 copy-start.5
  357.6 2.4 copy-start.2

commit v7 on v6

--- a/solution.py
+++ b/solution.py
@@ -532,7 +532,8 @@
 
 
 def front_kernel(
-    ids_ref,
+    bucket_ref,
+    label_ref,
     time_ref,
     class_ref,
     ada_ref,
@@ -543,6 +544,7 @@
     cond_all,
     mods_ref,
     ids_all,
+    ids_own,
     cond_part,
     cond_in,
     mods_part,
@@ -582,25 +584,25 @@
         for copy in copies:
             copy.wait()
 
-    ids_copies = spread(0, lambda other: ids_ref, ids_all)
+    table_rows = time_ref.shape[1]
+    slots = ROW_PARTS * SLOT_ROWS
+    ids_own[...] = jnp.full_like(ids_own, -1)
+    for start, chosen in ((0, bucket_ref), (SLOT_ROWS, label_ref)):
+        for slot in range(chosen.shape[1]):
+            ids_own[start + slot : start + slot + 1] = jnp.broadcast_to(
+                chosen[0:1, slot : slot + 1], (1, table_rows)
+            )
+    ids_copies = spread(0, lambda other: ids_own, ids_all)
     gather_qkv = RowGather(qkv_ref, qkv_full, qkv_send, qkv_recv, local_sems.at[0], 3)
     gather_patches = HeadGather(patches_ref, patches_full, head_send, head_recv, local_sems.at[1])
     gather_patches.start()
     gather_qkv.own.start()
     gather_qkv.start(0)
-    ids_all[row] = ids_ref[...]
+    ids_all[row] = ids_own[...]
     settle(ids_copies)
-    table_rows = time_ref.shape[0]
-    slots = ROW_PARTS * SLOT_ROWS
-    table_places = row * table_rows + lax.broadcasted_iota(jnp.int32, (slots, table_rows), 1)
-    bucket_hot = (
-        ids_all[:, 0:SLOT_ROWS].reshape(slots, table_rows) == table_places
-    ).astype(jnp.bfloat16)
-    label_hot = (
-        ids_all[:, SLOT_ROWS : 2 * SLOT_ROWS].reshape(slots, table_rows) == table_places
-    ).astype(jnp.bfloat16)
-    found = jnp.dot(bucket_hot, time_ref[...], preferred_element_type=jnp.float32) + jnp.dot(
-        label_hot, class_ref[...], preferred_element_type=jnp.float32
+    bucket_hot, label_hot = (hot.astype(jnp.bfloat16) for hot in table_hots(ids_all, table_rows))
+    found = times_transposed(bucket_hot, time_ref[...]) + times_transposed(
+        label_hot, class_ref[...]
     )
     cond_part[...] = found.reshape(cond_part.shape)
     copies = spread(1, lambda other: cond_part.at[other], cond_in)
@@ -639,7 +641,7 @@
     gather_qkv.finish()
 
 
-def front(ids, time_table, class_table, w_ada, patches, w_qkv):
+def front(bucket_ids, class_labels, time_columns, class_columns, w_ada, patches, w_qkv):
     depth, ada_width = w_ada.shape
     shape = jax.ShapeDtypeStruct
     slotted = (ROW_PARTS, SLOT_ROWS)
@@ -652,11 +654,12 @@
             shape((HEAD_PARTS,) + patches.shape, jnp.bfloat16),
             shape(slotted + (depth,), jnp.float32),
             shape(slotted + (ada_width,), jnp.float32),
-            shape((ROW_PARTS,) + ids.shape, jnp.int32),
+            shape((ROW_PARTS, 2 * SLOT_ROWS, time_columns.shape[1]), jnp.int32),
         ),
-        in_specs=[VMEM_SPEC] * 6,
+        in_specs=[VMEM_SPEC] * 7,
         out_specs=[ANY_SPEC] * 2 + [VMEM_SPEC] * 3,
-        scratch_shapes=[narrow] * 2
+        scratch_shapes=[pltpu.VMEM((2 * SLOT_ROWS, time_columns.shape[1]), jnp.int32)]
+        + [narrow] * 2
         + [wide] * 5
         + [
             DMA((4, 7)),
@@ -673,7 +676,7 @@
             collective_id=0, has_side_effects=True, vmem_limit_bytes=GRANT
         ),
         name="front",
-    )(ids, time_table, class_table, w_ada, patches, w_qkv)
+    )(bucket_ids, class_labels, time_columns, class_columns, w_ada, patches, w_qkv)
 
 
 class HeadReduce:
@@ -807,12 +810,29 @@
 
 
 def picked(vectors, part_index, segments, width):
-    wide = jnp.broadcast_to(segments, (segments.shape[0], width))
+    wide = jnp.concatenate([segments] * (width // segments.shape[1]), axis=1)
     slot_count = vectors.shape[1]
     chosen = vectors[part_index, slot_count - 1 : slot_count]
     for slot in range(slot_count - 2, -1, -1):
         chosen = jnp.where(wide == slot, vectors[part_index, slot : slot + 1], chosen)
     return chosen
+
+
+def slot_hot(segment_row, start):
+    chosen = segment_row[:, pl.ds(pl.multiple_of(start, 128), 128)]
+    slots = lax.broadcasted_iota(jnp.int32, (SLOT_ROWS, 128), 0)
+    return (jnp.broadcast_to(chosen, slots.shape) == slots).astype(jnp.float32)
+
+
+def table_hots(ids_all, table_rows):
+    slots = ROW_PARTS * SLOT_ROWS
+    table_places = lax.axis_index("rows") * table_rows + lax.broadcasted_iota(
+        jnp.int32, (slots, table_rows), 1
+    )
+    return [
+        ids_all[:, start : start + SLOT_ROWS].reshape(slots, table_rows) == table_places
+        for start in (0, SLOT_ROWS)
+    ]
 
 
 def centre_rows(values):
@@ -846,13 +866,13 @@
     fc2_shard,
     cotangent_ref,
     patches_ref,
+    segment_row,
+    mods_ref,
+    ada_bias,
+    bias_ref,
+    value_bias,
     segments_ref,
-    keys_image,
-    rows_image,
-    hot_ref,
     vectors_ref,
-    bias_ref,
-    qkv_bias,
     normed_rows,
     parts,
     totals_out,
@@ -868,6 +888,7 @@
     fc1_part,
     fc2_head,
     fc2_neck,
+    qkv_bias,
     ffn_rows,
     hidden_rows,
     inner_grad,
@@ -924,8 +945,10 @@
     gather_out.own.start()
     gather_out.start(0)
     gather_fc1.own.start()
-    gather_fc1.start(0)
     gather_fc2.own.start()
+    for gather in (gather_fc1, gather_fc2):
+        for chunk in range(3):
+            gather.start(chunk)
     gather_cotangent.start()
     reduce_attn = HeadReduce(
         group_part, beside_in, pair_rows, across_in, reduce_send.at[0], reduce_recv.at[0]
@@ -936,13 +959,33 @@
     gather_hidden = HeadGather(None, hidden_rows, gather_send.at[0], gather_recv.at[0], None)
     gather_grad = HeadGather(None, attn_grad, gather_send.at[1], gather_recv.at[1], None)
     parts[...] = jnp.zeros_like(parts)
+    segments_ref[...] = (
+        jnp.broadcast_to(segment_row[...].astype(jnp.float32), (128, seq_len))
+        .T.astype(jnp.int32)
+    )
+    slot_count = vectors_ref.shape[1]
+    fine = mods_ref.shape[2] // 3
+    for unit in range(3 * ROW_PARTS):
+        part_index, within = divmod(unit * fine, model_width)
+        span = slice(within, within + fine)
+        vectors_ref[part_index, :, span] = mods_ref[
+            unit // 3, 0:slot_count, unit % 3 * fine : (unit % 3 + 1) * fine
+        ]
+    for part_index in range(6):
+        vectors_ref[part_index] += ada_bias[part_index : part_index + 1]
+    qkv_bias[...] = jnp.zeros_like(qkv_bias)
+    for head in range(head_local):
+        for place in (0, 2):
+            start = (3 * head + place) * head_size
+            taken = slice(place // 2 * head_size, (place // 2 + 1) * head_size)
+            qkv_bias[:, start : start + head_size] = value_bias[head : head + 1, taken]
     for load in loads:
         load.wait()
 
     def first_norm(step, carry):
         block = step // 2
         part = pl.ds(pl.multiple_of(lax.rem(step, 2) * 128, 128), 128)
-        segments = segments_ref[block, part]
+        segments = segments_ref[pl.ds(pl.multiple_of(step * 128, 128), 128)]
         normed, _ = centre_rows(normed_rows[block, part].astype(jnp.float32))
         normed_rows[block, part] = (
             normed * (1.0 + picked(vectors_ref, 1, segments, model_width))
@@ -952,7 +995,6 @@
 
     lax.fori_loop(0, 2 * blocks, first_norm, 0)
     gather_out.relay(0)
-    gather_fc1.start(1)
 
     def project_in(block, carry):
         rows = pl.ds(pl.multiple_of(block * tok_rows, tok_rows), tok_rows)
@@ -968,7 +1010,6 @@
 
     lax.fori_loop(0, blocks, project_in, 0)
     gather_fc1.relay(0)
-    gather_fc1.start(2)
 
     def turn(head, carry):
         value_columns[head] = parts[3 * head + 2].astype(jnp.float32).T.astype(jnp.bfloat16)
@@ -978,9 +1019,8 @@
 
     def attend(block):
         rows = pl.ds(pl.multiple_of(block * tok_rows, tok_rows), tok_rows)
-        same = jnp.broadcast_to(keys_image[...], (seq_len, tok_rows)) == jnp.broadcast_to(
-            rows_image[block], (seq_len, tok_rows)
-        )
+        keys = jnp.concatenate([segments_ref[...]] * (tok_rows // 128), axis=1)
+        same = keys == jnp.broadcast_to(segment_row[:, rows], keys.shape)
         bias[...] = jnp.where(same, 0.0, MASKED)
 
         def one_head(head, carry):
@@ -1024,10 +1064,8 @@
     project(partner)
     reduce_attn.send_pair()
     gather_fc1.relay(1)
-    gather_fc2.start(0)
     attend_pair(sibling, -direction)
     gather_fc1.relay(2)
-    gather_fc2.start(1)
     project(sibling)
     reduce_attn.second.start()
     project(member)
@@ -1039,8 +1077,9 @@
     def scale_cotangent(step, carry):
         block = step // 2
         part = pl.ds(pl.multiple_of(lax.rem(step, 2) * 128, 128), 128)
+        segments = segments_ref[pl.ds(pl.multiple_of(step * 128, 128), 128)]
         grad = (
-            picked(vectors_ref, 5, segments_ref[block, part], model_width)
+            picked(vectors_ref, 5, segments, model_width)
             * ffn_rows[block, part].astype(jnp.float32)
         ).astype(jnp.bfloat16)
         ffn_rows[block, part] = grad
@@ -1050,12 +1089,13 @@
     ffn_bias[...] = jnp.zeros_like(ffn_bias)
     lax.fori_loop(0, 2 * blocks, scale_cotangent, 0)
     gather_fc2.relay(0)
-    gather_fc2.start(2)
     reduce_attn.settle()
 
     def second_norm(block, carry):
         part = pl.ds(pl.multiple_of(block * 128, 128), 128)
-        segments = segments_ref[member, part]
+        segments = segments_ref[
+            pl.ds(pl.multiple_of(member * tok_rows + block * 128, 128), 128)
+        ]
         out = reduce_attn.rows(part) + bias_ref[0:1]
         after = patches_ref[part].astype(jnp.float32) + (
             picked(vectors_ref, 2, segments, model_width) * out
@@ -1073,20 +1113,11 @@
     gather_hidden.start()
     reduce_attn.finish()
     gather_fc2.relay(1)
-    gather_fc2.relay(2)
     gather_fc1.finish()
-    gather_fc2.finish()
     hidden_width = active_rows.shape[2]
     fc1 = fc1_full.reshape(model_width, hidden_width)
     fc2 = fc2_full.reshape(model_width, hidden_width)
 
-    def through_fc2(block, carry):
-        active_grad[block] = jnp.dot(
-            ffn_rows[block], fc2[...], preferred_element_type=jnp.float32
-        )
-        return carry
-
-    lax.fori_loop(0, HEAD_PARTS, through_fc2, 0)
     inner_bias[...] = jnp.zeros_like(inner_bias)
 
     def feed(block, carry):
@@ -1097,13 +1128,19 @@
         bent = jnp.tanh(TANH_COEFF * (inner + 0.044715 * square * inner))
         half = 0.5 * (1.0 + bent)
         active_rows[block] = (inner * half).astype(jnp.bfloat16)
-        slope = half + 0.5 * inner * (1.0 - bent * bent) * (
+        active_grad[block] = half + 0.5 * inner * (1.0 - bent * bent) * (
             TANH_COEFF * (1.0 + 3.0 * 0.044715 * square)
         )
-        grad = (active_grad[block] * slope).astype(jnp.bfloat16)
+        return carry
+
+    def through_fc2(block, carry):
+        grad = (
+            jnp.dot(ffn_rows[block], fc2[...], preferred_element_type=jnp.float32)
+            * active_grad[block]
+        ).astype(jnp.bfloat16)
         inner_grad[block] = grad
         inner_bias[...] += jnp.sum(
-            grad.astype(jnp.float32).reshape(tok_rows // 8, 8, inner.shape[1]), axis=0
+            grad.astype(jnp.float32).reshape(tok_rows // 8, 8, hidden_width), axis=0
         )
         return carry
 
@@ -1113,18 +1150,20 @@
 
     gather_hidden.wait_sibling()
     lax.fori_loop(0, 2, lambda step, carry: feed(member + step * direction, carry), 0)
+    gather_fc2.relay(2)
     gather_hidden.wait_partner()
     gather_hidden.wait_opposite()
-
-    def feed_far(step, carry):
-        block = opposite - step * direction
-        feed(block, carry)
+    lax.fori_loop(0, 2, lambda step, carry: feed(opposite - step * direction, carry), 0)
+    gather_fc2.finish()
+
+    def turn_back(block, carry):
+        through_fc2(block, carry)
         return return_fc1(block, carry)
 
-    lax.fori_loop(0, 2, feed_far, 0)
+    lax.fori_loop(0, 2, lambda step, carry: turn_back(opposite - step * direction, carry), 0)
     reduce_hidden.first.start()
     reduce_hidden.send_pair()
-    lax.fori_loop(0, 2, lambda step, carry: return_fc1(sibling - step * direction, carry), 0)
+    lax.fori_loop(0, 2, lambda step, carry: turn_back(sibling - step * direction, carry), 0)
     reduce_hidden.second.start()
 
     def forward_fc2(block, carry):
@@ -1143,7 +1182,9 @@
 
     def second_back(block, carry):
         part = pl.ds(pl.multiple_of(block * 128, 128), 128)
-        segments = segments_ref[member, part]
+        segments = segments_ref[
+            pl.ds(pl.multiple_of(member * tok_rows + block * 128, 128), 128)
+        ]
         grad = reduce_hidden.rows(part)
         normed, factor = centre_rows(after_ref[part])
         weighted = grad * (1.0 + picked(vectors_ref, 4, segments, model_width))
@@ -1156,7 +1197,7 @@
         attn_grad[member, part] = (
             picked(vectors_ref, 2, segments, model_width) * total
         ).astype(jnp.bfloat16)
-        hot = hot_ref[:, part]
+        hot = slot_hot(segment_row, member * tok_rows + block * 128)
         for index, term in enumerate((total * attn_out[part], grad, grad * normed)):
             slot_sums[index] += jnp.dot(
                 hot, term, precision=HIGH, preferred_element_type=jnp.float32
@@ -1181,7 +1222,7 @@
     reduce_hidden.finish()
 
 
-def core(head_size, *args):
+def core(slot_count, head_size, *args):
     shape = jax.ShapeDtypeStruct
     patches_full, w_qkv, out_shard, fc1_shard = args[:4]
     blocks, tok_rows, model_width = patches_full.shape
@@ -1201,6 +1242,8 @@
     return pl.pallas_call(
         core_kernel,
         out_shape=[
+            shape((seq_len, 128), jnp.int32),
+            shape((6, slot_count, model_width), full),
             rows_low,
             shape((3 * head_local, seq_len, HEAD_LANES), low),
             shape((head_local, blocks, 1, tok_rows), full),
@@ -1217,9 +1260,10 @@
             shape((third, hidden_width), full),
             shape((third, hidden_width), full),
         ],
-        in_specs=[ANY_SPEC] + [VMEM_SPEC] * 13,
-        out_specs=[VMEM_SPEC] * 15,
+        in_specs=[ANY_SPEC] + [VMEM_SPEC] * 11,
+        out_specs=[VMEM_SPEC] * 17,
         scratch_shapes=[
+            pltpu.VMEM((1, args[1].shape[1]), full),
             group_low,
             group_low,
             hidden_low,
@@ -1266,8 +1310,8 @@
     grad_ref,
     out_ref,
     totals_ref,
-    keys_image,
-    rows_image,
+    segment_row,
+    segments_ref,
     fc2_part,
     fc1_part,
     hidden_rows,
@@ -1277,25 +1321,23 @@
     patches_ref,
     after_ref,
     vectors_ref,
-    segments_ref,
-    hot_ref,
     sums_ref,
-    silu_ref,
-    slope_ref,
-    bucket_ref,
-    label_ref,
+    condition_ref,
+    ids_all,
     ada_ref,
     ffn_ref,
     block_ref,
     cotangent_ref,
-    ffn_bias,
+    bias_rows,
+    fc2_head,
+    fc2_neck,
     block_out,
     patches_grad,
     time_grad,
     class_grad,
     ada_grad,
     ada_bias,
-    fc2_tail,
+    fc2_grad,
     fc1_grad,
     qkv_grad,
     out_grad,
@@ -1322,6 +1364,7 @@
     mods_sibling,
     mods_pair,
     mods_partner,
+    mods_low,
     mods_cols,
     bias_all,
     silu_part,
@@ -1357,9 +1400,11 @@
         for copy in copies:
             copy.wait()
 
-    third = fc2_tail.shape[0]
+    third = fc2_head.shape[0]
+    fc2_grad[0:third] = fc2_head[...]
+    fc2_grad[third : 2 * third] = fc2_neck[...]
     units = row_reduces(
-        [(fc2_part, 0, fc2_tail)]
+        [(fc2_part, 0, fc2_grad.at[pl.ds(2 * third, third)])]
         + [(fc1_part, chunk, fc1_grad.at[pl.ds(chunk * third, third)]) for chunk in range(3)]
         + [(out_part, 0, out_grad)]
         + [(qkv_part, chunk, qkv_grad.at[pl.ds(chunk * third, third)]) for chunk in range(3)],
@@ -1411,9 +1456,8 @@
 
     for block in range(blocks):
         rows = pl.ds(block * tok_rows, tok_rows)
-        same = jnp.broadcast_to(keys_image[...], (seq_len, tok_rows)) == jnp.broadcast_to(
-            rows_image[block], (seq_len, tok_rows)
-        )
+        keys = jnp.concatenate([segments_ref[...]] * (tok_rows // 128), axis=1)
+        same = keys == jnp.broadcast_to(segment_row[:, rows], keys.shape)
         bias[...] = jnp.where(same, 0.0, MASKED)
 
         def one_head(head, carry):
@@ -1495,11 +1539,12 @@
 
     def rows_out(block, carry):
         part = pl.ds(pl.multiple_of(block * 128, 128), 128)
-        ffn = reduce_ffn.rows(part) + ffn_bias[0:1]
-        gate = picked(vectors_ref, 5, segments_ref[member, part], model_width)
+        ffn = reduce_ffn.rows(part) + bias_rows[2:3]
+        place = pl.multiple_of(member * tok_rows + block * 128, 128)
+        gate = picked(vectors_ref, 5, segments_ref[pl.ds(place, 128)], model_width)
         block_out[part] = (block_ref[part] + gate * ffn).astype(jnp.bfloat16)
         slot_sums[2] += jnp.dot(
-            hot_ref[:, part],
+            slot_hot(segment_row, place),
             cotangent_ref[part].astype(jnp.float32) * ffn,
             precision=HIGH,
             preferred_element_type=jnp.float32,
@@ -1516,13 +1561,16 @@
         part = pl.ds(pl.multiple_of(block * 128, 128), 128)
         grad = reduce_rows.rows(part)
         normed, factor = centre_rows(patches_ref[part].astype(jnp.float32))
-        weighted = grad * (1.0 + picked(vectors_ref, 1, segments_ref[member, part], model_width))
+        place = pl.multiple_of(member * tok_rows + block * 128, 128)
+        weighted = grad * (
+            1.0 + picked(vectors_ref, 1, segments_ref[pl.ds(place, 128)], model_width)
+        )
         patches_grad[part] = after_ref[part] + factor * (
             weighted
             - jnp.mean(weighted, axis=1, keepdims=True)
             - normed * jnp.mean(weighted * normed, axis=1, keepdims=True)
         )
-        hot = hot_ref[:, part]
+        hot = slot_hot(segment_row, place)
         slot_sums[0] += jnp.dot(hot, grad, precision=HIGH, preferred_element_type=jnp.float32)
         slot_sums[1] += jnp.dot(
             hot, grad * normed, precision=HIGH, preferred_element_type=jnp.float32
@@ -1546,7 +1594,7 @@
     beside.start()
     units[6].send_pair()
     beside.wait()
-    mods_pair[...] = mods_own[...] + mods_sibling[...]
+    mods_pair[...] = (mods_own[...] + mods_sibling[...]).astype(jnp.bfloat16)
     across = to_head(mods_pair, mods_partner, pair_send.at[1], pair_recv.at[1], partner)
     across.start()
     units[2].finish()
@@ -1554,21 +1602,23 @@
     settle(bias_copies)
     bias_sum[...] = jnp.sum(bias_all[...], axis=0)
     across.wait()
-    mods_own[...] = (
-        (mods_pair[...] + mods_partner[...]).astype(jnp.bfloat16).astype(jnp.float32)
-    )
-    copies = spread(0, lambda other: mods_own.at[other], mods_cols)
-    mods_cols[row] = mods_own[row]
+    mods_low[...] = (
+        mods_pair[...].astype(jnp.float32) + mods_partner[...].astype(jnp.float32)
+    ).astype(jnp.bfloat16)
+    copies = spread(0, lambda other: mods_low.at[other], mods_cols)
+    mods_cols[row] = mods_low[row]
     units[7].send_pair()
     units[4].finish()
     settle(copies)
     slots = ROW_PARTS * SLOT_ROWS
-    cols = mods_cols[...].reshape(slots, ada_width)
+    cols = mods_cols[...].astype(jnp.float32).reshape(slots, ada_width)
     low = cols.astype(jnp.bfloat16)
+    condition = condition_ref[...].reshape(slots, condition_ref.shape[2])
+    bent = 1.0 / (1.0 + jnp.exp(-condition))
     silu_part[...] = times_transposed(low, ada_ref[...]).reshape(silu_part.shape)
     copies = spread(2, lambda other: silu_part.at[other], silu_in)
     silu_in[row] = silu_part[row]
-    ada_grad[...] = jnp.dot(silu_ref[...], low, preferred_element_type=jnp.float32)
+    ada_grad[...] = contract_rows((condition * bent).astype(jnp.bfloat16), low)
     ada_bias[...] = jnp.broadcast_to(jnp.sum(cols, axis=0, keepdims=True), ada_bias.shape)
     settle(copies)
     summed = jnp.sum(silu_in[...], axis=0)
@@ -1579,21 +1629,19 @@
     units[6].finish()
     units[7].finish()
     settle(copies)
-    grad_condition = silu_all[...].reshape(slots, silu_all.shape[2]) * slope_ref[...]
-    time_grad[...] = jnp.dot(
-        bucket_ref[...], grad_condition, precision=HIGH, preferred_element_type=jnp.float32
-    )
-    class_grad[...] = jnp.dot(
-        label_ref[...], grad_condition, precision=HIGH, preferred_element_type=jnp.float32
-    )
+    grad_condition = silu_all[...].reshape(slots, silu_all.shape[2]) * (
+        bent * (1.0 + condition * (1.0 - bent))
+    )
+    for target, hot in zip((time_grad, class_grad), table_hots(ids_all, time_grad.shape[1])):
+        target[...] = contract_rows_exact(grad_condition, hot.astype(jnp.float32))
     reduce_rows.finish()
     reduce_ffn.finish()
 
 
 def rear(*args):
     shape = jax.ShapeDtypeStruct
-    grads, w_out, totals, grad_w_fc2, w_qkv, biases, buckets, w_ada = (
-        args[place] for place in (1, 2, 3, 6, 9, 11, 20, 22)
+    grads, w_out, totals, grad_w_fc2, w_qkv, biases, ids_all, w_ada = (
+        args[place] for place in (1, 2, 3, 6, 9, 11, 17, 18)
     )
     blocks, tok_rows, model_width = grads.shape
     width = w_qkv.shape[1]
@@ -1603,12 +1651,13 @@
     width_part = 3 * third
     out_width = w_out.shape[1]
     depth, ada_width = w_ada.shape
-    table_rows = buckets.shape[0]
+    table_rows = ids_all.shape[2]
     low = jnp.bfloat16
     full = jnp.float32
     heads_wide = pltpu.VMEM((head_local, seq_len, HEAD_LANES), full)
     slotted = (ROW_PARTS, SLOT_ROWS)
     wide = pltpu.VMEM(slotted + (ada_width,), full)
+    wide_low = pltpu.VMEM(slotted + (ada_width,), low)
     narrow = pltpu.VMEM(slotted + (depth,), full)
     sizes = (
         [(third, hidden_width)] * 4 + [(width_part, out_width)] + [(third, width)] * 3
@@ -1618,17 +1667,17 @@
         out_shape=[
             shape((tok_rows, model_width), low),
             shape((tok_rows, model_width), full),
-            shape((table_rows, depth), full),
-            shape((table_rows, depth), full),
+            shape((depth, table_rows), full),
+            shape((depth, table_rows), full),
             shape((depth, ada_width), full),
             shape((SLOT_ROWS, ada_width), full),
-            shape((third, hidden_width), full),
+            shape((width_part, hidden_width), full),
             shape((width_part, hidden_width), full),
             shape((width_part, width), full),
             shape((width_part, out_width), full),
             shape(biases.shape, full),
         ],
-        in_specs=[VMEM_SPEC] * 27,
+        in_specs=[VMEM_SPEC] * 25,
         out_specs=[VMEM_SPEC] * 11,
         scratch_shapes=[
             pltpu.VMEM((head_local, seq_len, HEAD_LANES), low),
@@ -1650,7 +1699,8 @@
         ]
         * 2
         + [pltpu.VMEM((3, SLOT_ROWS, model_width), full)]
-        + [wide] * 5
+        + [wide] * 2
+        + [wide_low] * 4
         + [pltpu.VMEM((ROW_PARTS,) + biases.shape, full)]
         + [narrow] * 3
         + [
@@ -1689,57 +1739,18 @@
     class_labels,
     cotangent,
 ):
-    head_parts = lax.axis_size("heads")
-    member = lax.axis_index("heads")
-    tok_rows = patches.shape[0]
     model_width = patches.shape[1]
-    seq_count = segment_ids.shape[0]
-    seq_len = segment_ids.shape[1]
     slot_count = image_lengths.shape[1]
-    image_count = seq_count * slot_count
-    group_rows = tok_rows * head_parts
     head_local = b_qv.shape[0]
     head_size = b_qv.shape[1] // 2
-    block_rows = min(BLOCK_LIMIT, seq_len)
-    scale_factor = 1.0 / math.sqrt(head_size)
-    row_parts = lax.axis_size("rows")
-    table_rows = time_table.shape[0]
-    ada_width = w_ada.shape[1]
-    every_slot = row_parts * SLOT_ROWS
-    slot_pad = jnp.full((SLOT_ROWS - slot_count,), -1, jnp.int32)
-    ids = jnp.broadcast_to(
-        jnp.concatenate([bucket_ids[0], slot_pad, class_labels[0], slot_pad])[:, None],
-        (2 * SLOT_ROWS, table_rows),
-    )
     qkv_full, patches_full, condition, mods, ids_all = front(
-        ids, time_table, class_table, w_ada, patches, w_qkv
+        bucket_ids, class_labels, time_table.T, class_table.T, w_ada, patches, w_qkv
     )
     qkv_cols = qkv_full.reshape(model_width, w_qkv.shape[1])
-    condition = condition.reshape(every_slot, condition.shape[2])
-    silu_value, silu_pull = jax.vjp(silu_plain, condition)
-    silu_low = silu_value.astype(jnp.bfloat16)
-    mods_all = mods[:, :slot_count].transpose(1, 0, 2).reshape(
-        slot_count, row_parts * ada_width
-    ) + b_ada.astype(jnp.float32)
-    own_segments = lax.dynamic_slice_in_dim(segment_ids[0], member * tok_rows, tok_rows)[:, None]
-    token_hot = (own_segments == jnp.arange(SLOT_ROWS, dtype=jnp.int32)[None, :]).astype(
-        jnp.float32
-    )
-    zero_bias = jnp.zeros((head_local, head_size), b_qv.dtype)
-    qkv_bias = (
-        jnp.concatenate([b_qv[:, :head_size], zero_bias, b_qv[:, head_size:]], axis=1)
-        .reshape(head_local * 3 * head_size)
-        .astype(jnp.float32)
-    )
-    slot_ends = jnp.cumsum(image_lengths, axis=1)
-    places = jnp.arange(seq_len, dtype=jnp.int32)
-    image_of = jnp.sum((places[None, :, None] >= slot_ends[:, None, :]).astype(jnp.int32), axis=2)
-
-    vectors = mods_all.reshape(slot_count, 6, model_width).transpose(1, 0, 2)
-    segments = segment_ids.reshape(head_parts, tok_rows, 1)
-    keys_image = image_of.reshape(seq_len, 1)
-    rows_image = image_of.reshape(head_parts, 1, tok_rows)
+    biases = jnp.stack([b_out, b_fc1, b_fc2]).astype(jnp.float32)
     (
+        segments,
+        vectors,
         rows_one,
         parts,
         totals,
@@ -1756,6 +1767,7 @@
         fc2_head,
         fc2_neck,
     ) = core(
+        slot_count,
         head_size,
         patches_full,
         qkv_cols,
@@ -1764,18 +1776,12 @@
         w_fc2,
         cotangent,
         patches,
-        segments,
-        keys_image,
-        rows_image,
-        token_hot.T,
-        vectors,
-        jnp.stack([b_out, b_fc1]).astype(jnp.float32),
-        qkv_bias[None, :],
-    )
-    all_ids = ids_all[:, :, 0]
-    table_places = lax.axis_index("rows") * table_rows + jnp.arange(table_rows, dtype=jnp.int32)
-    bucket_hot = table_places[:, None] == all_ids[:, :SLOT_ROWS].reshape(every_slot)[None, :]
-    label_hot = table_places[:, None] == all_ids[:, SLOT_ROWS:].reshape(every_slot)[None, :]
+        segment_ids,
+        mods,
+        b_ada.astype(jnp.float32).reshape(6, model_width),
+        biases,
+        b_qv.astype(jnp.float32),
+    )
     (
         block_out,
         grad_patches,
@@ -1783,7 +1789,7 @@
         grad_class,
         grad_w_ada,
         grad_b_ada,
-        fc2_tail,
+        grad_w_fc2,
         grad_w_fc1,
         grad_w_qkv,
         grad_w_out,
@@ -1793,8 +1799,8 @@
         attn_rows_grad,
         out_cols,
         totals,
-        keys_image,
-        rows_image,
+        segment_ids,
+        segments,
         grad_w_fc2,
         grad_w_fc1,
         rows_one,
@@ -1804,22 +1810,21 @@
         patches,
         grad_after,
         vectors,
-        segments,
-        token_hot.T,
         sums,
-        silu_low.T,
-        silu_pull(jnp.ones_like(condition))[0],
-        bucket_hot.astype(jnp.float32),
-        label_hot.astype(jnp.float32),
+        condition,
+        ids_all,
         w_ada,
         ffn_part,
         after_attn,
         cotangent,
-        b_fc2.astype(jnp.float32)[None, :],
-    )
-    grad_w_fc2 = jnp.concatenate([fc2_head, fc2_neck, fc2_tail], axis=0)
+        biases,
+        fc2_head,
+        fc2_neck,
+    )
+    grad_time = grad_time.T
+    grad_class = grad_class.T
     grad_b_ada = grad_b_ada[0]
-    bias_rows = model_width // row_parts
+    bias_rows = model_width // lax.axis_size("rows")
     row_start = lax.axis_index("rows") * bias_rows
     grad_b_fc1 = bias_all[0]
     grad_b_fc2 = lax.dynamic_slice_in_dim(bias_all[1], row_start, bias_rows)

time: 362 us -> 330 us (0.912)
  Pallas kernels: 322 us -> 310 us
  local copies, waits for them, and re-layouts: 27.6 us -> 16.9 us
  other arithmetic: 10.1 us -> 2.57 us
    pallas_call x1, Pallas kernels: 156 us -> 145 us  [core(): pl.pallas_call(core_kernel, out_shape=[shape((seq_len, 128), jnp.int32),...]
    unnamed x25 -> x23, local copies, waits for them, and re-layouts: 12.3 us -> 9.8 us
where the time goes in v7:
time: 330 us
  Pallas kernels  310 us (94%)
  local copies, waits for them, and re-layouts  16.9 us (5%)
    pallas_call x1, Pallas kernels, core(): pl.pallas_call(core_kernel, out_shape=[shape((seq_len, 128), jnp.int32),...  145 us
    pallas_call x1, Pallas kernels, rear(): pl.pallas_call(rear_kernel, out_shape=[shape((tok_rows, model_width), low...  116 us
    pallas_call x1, Pallas kernels, front(): pl.pallas_call(front_kernel, out_shape=(shape((ROW_PARTS,) + w_qkv.shape,...  48.7 us
    unnamed x23, local copies, waits for them, and re-layouts  9.8 us

profile of v7, /device:TPU:0, one launch (start us, length us, event | category | flops | bytes accessed | tf_op | source)
XLA Modules:
  0.0 330.0 jit_solution(18145047293923210798)
XLA Ops:
  0.6 48.7 %front.1 = (bf16[8,144,864]{2,1,0:T(8,128)(2,1)}, bf16[4,256,1152]{2,1,0:T(8,128)(2,1)}, f32[8,8,288]{2,1,0:T(8,128)}, f32[8,8,864]{2,1,0:T(8,128)}, s32[8,16,128]{2,1,0:T(8,128)}) custom-call(s32[1,4]{1,0:T(1,128)} %bucket_ref.1, s32[1,4]{1,0:T(1,128)} %label_ref.1, bf16[288,128]{1,0:T(8,128)(2,1)} %bitcast.15, bf16[288,128]{1,0:T(8,128)(2,1)} %bitcast.16, ...), custom_call_target="tpu_custom_call" | custom-call | tf_op jit(solution)/shard_map/front/pallas_call | solution.py:650
  49.4 0.7 stack.12
  50.1 0.7 stack.13
  50.8 0.7 stack.14
  51.5 0.6 maximum_convert_fusion.bias_ref.bias_rows
  52.1 1.4 reshape.42.ada_bias
  53.4 1.3 convert_element_type.8.value_bias
  54.7 145.2 %core.1 = (s32[1024,128]{1,0:T(8,128)}, f32[6,4,1152]{2,1,0:T(4,128)}, bf16[4,256,1152]{2,1,0:T(8,128)(2,1)}, bf16[12,1024,128]{2,1,0:T(8,128)(2,1)}, f32[4,4,1,...) custom-call(bf16[4,256,1152]{2,1,0:T(8,128)(2,1)} %get-tuple-element, ...), custom_call_target="tpu_custom_call" | custom-call | tf_op jit(solution)/shard_map/core/pallas_call | solution.py:1242
  200.0 115.8 %rear.1 = (bf16[256,1152]{1,0:T(8,128)(2,1)}, f32[256,1152]{1,0:T(8,128)}, f32[288,128]{1,0:T(8,128)}, f32[288,128]{1,0:T(8,128)}, f32[288,864]{1,0:T(8,128)}, /...) custom-call(bf16[12,1024,128]{2,1,0:T(8,128)(2,1)} %get-tuple-elemen, ...), custom_call_target="tpu_custom_call" | custom-call | tf_op jit(solution)/shard_map/rear/pallas_call | solution.py:1665
  315.8 0.0 copy-start.6
  315.8 0.0 copy-start.5
  315.8 0.0 copy-start
  315.8 1.5 fusion
  317.4 0.6 constant_dynamic-slice_fusion
  318.0 1.4 slice_reduce_fusion.1
  319.4 0.1 reshape_squeeze.3
  319.5 0.7 pad_maximum_fusion
  320.2 1.9 copy.44
  322.1 0.0 copy-start.3
  322.1 2.4 copy.45
  324.5 0.0 copy-done.6
  324.5 0.0 copy-start.4
  324.5 0.0 copy-start.2
  324.5 0.7 copy.46
  325.2 0.0 copy-done.5
  325.2 0.7 copy.47
  325.8 0.0 copy-done
  325.8 0.0 copy-start.1
  325.8 1.0 copy.48
  326.8 0.0 copy-done.3
  326.8 0.8 copy.49
  327.6 0.0 copy-done.4
  327.6 0.7 copy.50
  328.3 0.0 copy-done.2
  328.3 0.8 copy.51
  329.1 0.0 copy-done.1
  329.1 0.8 copy.52
  (1 shorter events, 0.0 us)
Async XLA Ops:
  315.8 8.7 %copy-start.6 = (f32[288,128]{1,0:T(8,128)S(1)}, f32[288,128]{1,0:T(8,128)}, u32[]{:S(2)}) copy-start(f32[288,128]{1,0:T(8,128)} %get-tuple-element.71) | copy-start | bytes 442372
  315.8 9.3 %copy-start.5 = (f32[288,128]{1,0:T(8,128)S(1)}, f32[288,128]{1,0:T(8,128)}, u32[]{:S(2)}) copy-start(f32[288,128]{1,0:T(8,128)} %get-tuple-element.72) | copy-start | bytes 442372
  315.8 10.0 %copy-start = (f32[288,864]{1,0:T(8,128)S(1)}, f32[288,864]{1,0:T(8,128)}, u32[]{:S(2)}) copy-start(f32[288,864]{1,0:T(8,128)} %get-tuple-element.107) | copy-start | bytes 2985988
  322.1 4.7 %copy-start.3 = (f32[144,864]{1,0:T(8,128)S(1)}, f32[144,864]{1,0:T(8,128)}, u32[]{:S(2)}) copy-start(f32[144,864]{1,0:T(8,128)} %get-tuple-element.109) | copy-start | bytes 1492996
  324.5 3.1 copy-start.4
  324.5 3.8 %copy-start.2 = (f32[144,1152]{1,0:T(8,128)S(1)}, f32[144,1152]{1,0:T(8,128)}, u32[]{:S(2)}) copy-start(f32[144,1152]{1,0:T(8,128)} %get-tuple-element.113) | copy-start | bytes 1990660
  325.8 3.3 copy-start.1

commit v8 on v7

--- a/solution.py
+++ b/solution.py
@@ -434,6 +434,7 @@
         self.level = self.row // 2
         self.side = lax.rem(self.row, 2)
         self.mate = self.row + 1 - 2 * self.side
+        above = lax.rem(self.level + 1, 4) * 2 + self.side
         size = shard.shape[0] // chunks
         self.own = pltpu.make_async_copy(shard, full.at[self.row], local_sem)
         self.straight = []
@@ -441,48 +442,38 @@
         for chunk in range(chunks):
             part = pl.ds(chunk * size, size)
             straight = []
-            across = [
-                to_row(
-                    shard.at[part],
-                    full.at[self.row, part],
-                    sends.at[chunk, 3],
-                    recvs.at[chunk, 3],
-                    self.mate,
-                )
-            ]
-            for step in range(1, 4):
-                target = lax.rem(self.level + step, 4) * 2 + self.side
+            across = []
+            for step in range(4):
                 origin = lax.rem(self.level + 4 - step, 4) * 2 + self.side
-                straight.append(
-                    to_row(
-                        shard.at[part],
-                        full.at[self.row, part],
-                        sends.at[chunk, step - 1],
-                        recvs.at[chunk, step - 1],
-                        target,
-                    )
-                )
+                source = shard.at[part] if step == 0 else full.at[origin, part]
+                target = full.at[origin, part]
                 across.append(
                     to_row(
-                        full.at[origin, part],
-                        full.at[origin, part],
+                        source,
+                        target,
                         sends.at[chunk, 3 + step],
                         recvs.at[chunk, 3 + step],
                         self.mate,
                     )
                 )
+                if step < 3:
+                    straight.append(
+                        to_row(
+                            source, target, sends.at[chunk, step], recvs.at[chunk, step], above
+                        )
+                    )
             self.straight.append(straight)
             self.across.append(across)
 
     def start(self, chunk):
-        for copy in self.straight[chunk]:
-            copy.start()
+        self.straight[chunk][0].start()
         self.across[chunk][0].start()
 
-    def relay(self, chunk):
-        for step in range(3):
-            self.straight[chunk][step].wait_recv()
-            self.across[chunk][1 + step].start()
+    def hop(self, chunk, step):
+        self.straight[chunk][step].wait_recv()
+        if step < 2:
+            self.straight[chunk][step + 1].start()
+        self.across[chunk][step + 1].start()
 
     def finish(self):
         self.own.wait()
@@ -608,12 +599,15 @@
     copies = spread(1, lambda other: cond_part.at[other], cond_in)
     gather_qkv.start(1)
     cond_in[row] = cond_part[row]
+    gather_qkv.hop(0, 0)
     settle(copies)
     condition = jnp.sum(cond_in[...], axis=0)
     cond_all[row] = condition
     cond_part[row] = condition
     copies = spread(2, lambda other: cond_part.at[row], cond_all)
-    gather_qkv.relay(0)
+    gather_qkv.start(2)
+    gather_qkv.hop(1, 0)
+    gather_qkv.hop(0, 1)
     settle(copies)
     every = cond_all[...].reshape(slots, cond_all.shape[2])
     silu_low = (every / (1.0 + jnp.exp(-every))).astype(jnp.bfloat16)
@@ -621,9 +615,10 @@
         silu_low, ada_ref[...], preferred_element_type=jnp.float32
     ).reshape(mods_part.shape)
     copies = spread(3, lambda other: mods_part.at[other], mods_in)
-    gather_qkv.start(2)
     mods_in[row] = mods_part[row]
-    gather_qkv.relay(1)
+    gather_qkv.hop(2, 0)
+    gather_qkv.hop(1, 1)
+    gather_qkv.hop(0, 2)
     settle(copies)
     beside = to_head(mods_in, mods_sibling, pair_send.at[0], pair_recv.at[0], sibling)
     beside.start()
@@ -633,9 +628,11 @@
     across = to_head(mods_pair, mods_partner, pair_send.at[1], pair_recv.at[1], partner)
     across.start()
     gather_patches.wait_partner()
-    gather_qkv.relay(2)
+    gather_qkv.hop(2, 1)
+    gather_qkv.hop(1, 2)
     across.wait()
     mods_ref[...] = mods_pair[...] + mods_partner[...]
+    gather_qkv.hop(2, 2)
     gather_patches.wait_opposite()
     gather_patches.finish()
     gather_qkv.finish()
@@ -946,9 +943,8 @@
     gather_out.start(0)
     gather_fc1.own.start()
     gather_fc2.own.start()
-    for gather in (gather_fc1, gather_fc2):
-        for chunk in range(3):
-            gather.start(chunk)
+    for chunk in range(3):
+        gather_fc1.start(chunk)
     gather_cotangent.start()
     reduce_attn = HeadReduce(
         group_part, beside_in, pair_rows, across_in, reduce_send.at[0], reduce_recv.at[0]
@@ -994,7 +990,10 @@
         return carry
 
     lax.fori_loop(0, 2 * blocks, first_norm, 0)
-    gather_out.relay(0)
+    gather_out.hop(0, 0)
+    gather_fc1.hop(0, 0)
+    gather_fc1.hop(1, 0)
+    gather_fc2.start(0)
 
     def project_in(block, carry):
         rows = pl.ds(pl.multiple_of(block * tok_rows, tok_rows), tok_rows)
@@ -1009,7 +1008,10 @@
         return carry
 
     lax.fori_loop(0, blocks, project_in, 0)
-    gather_fc1.relay(0)
+    gather_out.hop(0, 1)
+    gather_fc1.hop(2, 0)
+    gather_fc1.hop(0, 1)
+    gather_fc2.start(1)
 
     def turn(head, carry):
         value_columns[head] = parts[3 * head + 2].astype(jnp.float32).T.astype(jnp.bfloat16)
@@ -1046,26 +1048,31 @@
             ]
         mixed[block] = active_grad[1, :, 0 : head_local * head_size].astype(jnp.bfloat16)
 
-    def attend_pair(base, factor):
-        def one(step, carry):
-            attend(base + step * factor)
-            return carry
-
-        lax.fori_loop(0, 2, one, 0)
-
     def project(block):
         group_part[block] = times_transposed(mixed[block], out_w[...]).astype(jnp.bfloat16)
 
-    attend_pair(opposite, -direction)
+    attend(opposite)
+    gather_out.hop(0, 2)
+    gather_fc1.hop(1, 1)
+    gather_fc2.hop(0, 0)
+    gather_fc2.start(2)
+    attend(partner)
+    gather_fc1.hop(2, 1)
+    gather_fc1.hop(0, 2)
     gather_out.finish()
     out_w[...] = out_full[...].reshape(out_w.shape)
     project(opposite)
     reduce_attn.first.start()
     project(partner)
     reduce_attn.send_pair()
-    gather_fc1.relay(1)
-    attend_pair(sibling, -direction)
-    gather_fc1.relay(2)
+    gather_fc2.hop(1, 0)
+    attend(sibling)
+    gather_fc1.hop(1, 2)
+    gather_fc2.hop(0, 1)
+    gather_fc2.hop(2, 0)
+    attend(member)
+    gather_fc1.hop(2, 2)
+    gather_fc2.hop(1, 1)
     project(sibling)
     reduce_attn.second.start()
     project(member)
@@ -1088,7 +1095,8 @@
 
     ffn_bias[...] = jnp.zeros_like(ffn_bias)
     lax.fori_loop(0, 2 * blocks, scale_cotangent, 0)
-    gather_fc2.relay(0)
+    gather_fc2.hop(0, 2)
+    gather_fc2.hop(2, 1)
     reduce_attn.settle()
 
     def second_norm(block, carry):
@@ -1112,7 +1120,8 @@
     lax.fori_loop(0, tok_rows // 128, second_norm, 0)
     gather_hidden.start()
     reduce_attn.finish()
-    gather_fc2.relay(1)
+    gather_fc2.hop(1, 2)
+    gather_fc2.hop(2, 2)
     gather_fc1.finish()
     hidden_width = active_rows.shape[2]
     fc1 = fc1_full.reshape(model_width, hidden_width)
@@ -1150,7 +1159,6 @@
 
     gather_hidden.wait_sibling()
     lax.fori_loop(0, 2, lambda step, carry: feed(member + step * direction, carry), 0)
-    gather_fc2.relay(2)
     gather_hidden.wait_partner()
     gather_hidden.wait_opposite()
     lax.fori_loop(0, 2, lambda step, carry: feed(opposite - step * direction, carry), 0)

time: 330 us -> 320 us (0.970)
  Pallas kernels: 310 us -> 300 us
    pallas_call x1, Pallas kernels: 145 us -> 134 us  [core(): pl.pallas_call(core_kernel, out_shape=[shape((seq_len, 128), jnp.int32),...]
where the time goes in v8:
time: 320 us
  Pallas kernels  300 us (94%)
  local copies, waits for them, and re-layouts  16.9 us (5%)
    pallas_call x1, Pallas kernels, core(): pl.pallas_call(core_kernel, out_shape=[shape((seq_len, 128), jnp.int32),...  134 us
    pallas_call x1, Pallas kernels, rear(): pl.pallas_call(rear_kernel, out_shape=[shape((tok_rows, model_width), low...  115 us
    pallas_call x1, Pallas kernels, front(): pl.pallas_call(front_kernel, out_shape=(shape((ROW_PARTS,) + w_qkv.shape,...  50.4 us
    unnamed x23, local copies, waits for them, and re-layouts  9.8 us

profile of v8, /device:TPU:0, one launch (start us, length us, event | category | flops | bytes accessed | tf_op | source)
XLA Modules:
  0.0 319.7 jit_solution(294291941983802426)
XLA Ops:
  0.6 50.4 %front.1 = (bf16[8,144,864]{2,1,0:T(8,128)(2,1)}, bf16[4,256,1152]{2,1,0:T(8,128)(2,1)}, f32[8,8,288]{2,1,0:T(8,128)}, f32[8,8,864]{2,1,0:T(8,128)}, s32[8,16,128]{2,1,0:T(8,128)}) custom-call(s32[1,4]{1,0:T(1,128)} %bucket_ref.1, s32[1,4]{1,0:T(1,128)} %label_ref.1, bf16[288,128]{1,0:T(8,128)(2,1)} %bitcast.15, bf16[288,128]{1,0:T(8,128)(2,1)} %bitcast.16, ...), custom_call_target="tpu_custom_call" | custom-call | tf_op jit(solution)/shard_map/front/pallas_call | solution.py:647
  51.0 0.7 stack.12
  51.7 0.7 stack.13
  52.4 0.7 stack.14
  53.1 0.6 maximum_convert_fusion.bias_ref.bias_rows
  53.7 1.4 reshape.42.ada_bias
  55.1 1.3 convert_element_type.8.value_bias
  56.4 134.0 %core.1 = (s32[1024,128]{1,0:T(8,128)}, f32[6,4,1152]{2,1,0:T(4,128)}, bf16[4,256,1152]{2,1,0:T(8,128)(2,1)}, bf16[12,1024,128]{2,1,0:T(8,128)(2,1)}, f32[4,4,1,...) custom-call(bf16[4,256,1152]{2,1,0:T(8,128)(2,1)} %get-tuple-element, ...), custom_call_target="tpu_custom_call" | custom-call | tf_op jit(solution)/shard_map/core/pallas_call | solution.py:1250
  190.3 115.2 %rear.1 = (bf16[256,1152]{1,0:T(8,128)(2,1)}, f32[256,1152]{1,0:T(8,128)}, f32[288,128]{1,0:T(8,128)}, f32[288,128]{1,0:T(8,128)}, f32[288,864]{1,0:T(8,128)}, /...) custom-call(bf16[12,1024,128]{2,1,0:T(8,128)(2,1)} %get-tuple-elemen, ...), custom_call_target="tpu_custom_call" | custom-call | tf_op jit(solution)/shard_map/rear/pallas_call | solution.py:1673
  305.6 0.0 copy-start.6
  305.6 0.0 copy-start.5
  305.6 0.0 copy-start
  305.6 1.5 fusion
  307.1 0.6 constant_dynamic-slice_fusion
  307.8 1.4 slice_reduce_fusion.1
  309.2 0.1 reshape_squeeze.3
  309.3 0.7 pad_maximum_fusion
  309.9 1.9 copy.44
  311.9 0.0 copy-start.3
  311.9 2.4 copy.45
  314.3 0.0 copy-done.6
  314.3 0.0 copy-start.4
  314.3 0.0 copy-start.2
  314.3 0.7 copy.46
  314.9 0.0 copy-done.5
  314.9 0.7 copy.47
  315.6 0.0 copy-done
  315.6 0.0 copy-start.1
  315.6 1.0 copy.48
  316.6 0.0 copy-done.3
  316.6 0.8 copy.49
  317.4 0.0 copy-done.4
  317.4 0.7 copy.50
  318.0 0.0 copy-done.2
  318.1 0.8 copy.51
  318.9 0.0 copy-done.1
  318.9 0.8 copy.52
  (1 shorter events, 0.0 us)
Async XLA Ops:
  305.6 8.7 %copy-start.6 = (f32[288,128]{1,0:T(8,128)S(1)}, f32[288,128]{1,0:T(8,128)}, u32[]{:S(2)}) copy-start(f32[288,128]{1,0:T(8,128)} %get-tuple-element.71) | copy-start | bytes 442372
  305.6 9.3 %copy-start.5 = (f32[288,128]{1,0:T(8,128)S(1)}, f32[288,128]{1,0:T(8,128)}, u32[]{:S(2)}) copy-start(f32[288,128]{1,0:T(8,128)} %get-tuple-element.72) | copy-start | bytes 442372
  305.6 10.0 %copy-start = (f32[288,864]{1,0:T(8,128)S(1)}, f32[288,864]{1,0:T(8,128)}, u32[]{:S(2)}) copy-start(f32[288,864]{1,0:T(8,128)} %get-tuple-element.107) | copy-start | bytes 2985988
  311.9 4.7 %copy-start.3 = (f32[144,864]{1,0:T(8,128)S(1)}, f32[144,864]{1,0:T(8,128)}, u32[]{:S(2)}) copy-start(f32[144,864]{1,0:T(8,128)} %get-tuple-element.109) | copy-start | bytes 1492996
  314.3 3.1 copy-start.4
  314.3 3.8 %copy-start.2 = (f32[144,1152]{1,0:T(8,128)S(1)}, f32[144,1152]{1,0:T(8,128)}, u32[]{:S(2)}) copy-start(f32[144,1152]{1,0:T(8,128)} %get-tuple-element.113) | copy-start | bytes 1990660
  315.6 3.3 %copy-start.1 = (f32[144,1152]{1,0:T(8,128)S(1)}, f32[144,1152]{1,0:T(8,128)}, u32[]{:S(2)}) copy-start(f32[144,1152]{1,0:T(8,128)} %get-tuple-element.115) | copy-start | bytes 1990660

commit v9 on v8

--- a/solution.py
+++ b/solution.py
@@ -865,7 +865,6 @@
     patches_ref,
     segment_row,
     mods_ref,
-    ada_bias,
     bias_ref,
     value_bias,
     segments_ref,
@@ -886,6 +885,7 @@
     fc2_head,
     fc2_neck,
     qkv_bias,
+    head_bias,
     ffn_rows,
     hidden_rows,
     inner_grad,
@@ -968,13 +968,14 @@
             unit // 3, 0:slot_count, unit % 3 * fine : (unit % 3 + 1) * fine
         ]
     for part_index in range(6):
-        vectors_ref[part_index] += ada_bias[part_index : part_index + 1]
+        vectors_ref[part_index] += bias_ref[part_index : part_index + 1]
     qkv_bias[...] = jnp.zeros_like(qkv_bias)
+    head_bias[...] = value_bias[...].astype(jnp.float32)
     for head in range(head_local):
         for place in (0, 2):
             start = (3 * head + place) * head_size
             taken = slice(place // 2 * head_size, (place // 2 + 1) * head_size)
-            qkv_bias[:, start : start + head_size] = value_bias[head : head + 1, taken]
+            qkv_bias[:, start : start + head_size] = head_bias[head : head + 1, taken]
     for load in loads:
         load.wait()
 
@@ -1104,7 +1105,7 @@
         segments = segments_ref[
             pl.ds(pl.multiple_of(member * tok_rows + block * 128, 128), 128)
         ]
-        out = reduce_attn.rows(part) + bias_ref[0:1]
+        out = reduce_attn.rows(part) + bias_ref[6:7]
         after = patches_ref[part].astype(jnp.float32) + (
             picked(vectors_ref, 2, segments, model_width) * out
         )
@@ -1132,7 +1133,7 @@
     def feed(block, carry):
         inner = jnp.dot(
             hidden_rows[block], fc1[...], preferred_element_type=jnp.float32
-        ) + bias_ref[1:2]
+        ) + bias_ref[7:8]
         square = inner * inner
         bent = jnp.tanh(TANH_COEFF * (inner + 0.044715 * square * inner))
         half = 0.5 * (1.0 + bent)
@@ -1268,10 +1269,11 @@
             shape((third, hidden_width), full),
             shape((third, hidden_width), full),
         ],
-        in_specs=[ANY_SPEC] + [VMEM_SPEC] * 11,
+        in_specs=[ANY_SPEC] + [VMEM_SPEC] * 10,
         out_specs=[VMEM_SPEC] * 17,
         scratch_shapes=[
             pltpu.VMEM((1, args[1].shape[1]), full),
+            pltpu.VMEM(args[-1].shape, full),
             group_low,
             group_low,
             hidden_low,
@@ -1547,7 +1549,7 @@
 
     def rows_out(block, carry):
         part = pl.ds(pl.multiple_of(block * 128, 128), 128)
-        ffn = reduce_ffn.rows(part) + bias_rows[2:3]
+        ffn = reduce_ffn.rows(part) + bias_rows[8:9]
         place = pl.multiple_of(member * tok_rows + block * 128, 128)
         gate = picked(vectors_ref, 5, segments_ref[pl.ds(place, 128)], model_width)
         block_out[part] = (block_ref[part] + gate * ffn).astype(jnp.bfloat16)
@@ -1755,7 +1757,9 @@
         bucket_ids, class_labels, time_table.T, class_table.T, w_ada, patches, w_qkv
     )
     qkv_cols = qkv_full.reshape(model_width, w_qkv.shape[1])
-    biases = jnp.stack([b_out, b_fc1, b_fc2]).astype(jnp.float32)
+    biases = (
+        jnp.concatenate([b_ada, b_out, b_fc1, b_fc2]).astype(jnp.float32).reshape(9, model_width)
+    )
     (
         segments,
         vectors,
@@ -1786,9 +1790,8 @@
         patches,
         segment_ids,
         mods,
-        b_ada.astype(jnp.float32).reshape(6, model_width),
         biases,
-        b_qv.astype(jnp.float32),
+        b_qv,
     )
     (
         block_out,

time: 320 us -> 316 us (0.988)
  no operation moved by 1% of the time
where the time goes in v9:
time: 316 us
  Pallas kernels  300 us (95%)
  local copies, waits for them, and re-layouts  14.1 us (4%)
    pallas_call x1, Pallas kernels, core(): pl.pallas_call(core_kernel, out_shape=[shape((seq_len, 128), jnp.int32),...  134 us
    pallas_call x1, Pallas kernels, rear(): pl.pallas_call(rear_kernel, out_shape=[shape((tok_rows, model_width), low...  115 us
    pallas_call x1, Pallas kernels, front(): pl.pallas_call(front_kernel, out_shape=(shape((ROW_PARTS,) + w_qkv.shape,...  50.4 us
    unnamed x23, local copies, waits for them, and re-layouts  9.8 us

profile of v9, /device:TPU:0, one launch (start us, length us, event | category | flops | bytes accessed | tf_op | source)
XLA Modules:
  0.0 315.8 jit_solution(13122654904153729805)
XLA Ops:
  0.6 50.4 %front.1 = (bf16[8,144,864]{2,1,0:T(8,128)(2,1)}, bf16[4,256,1152]{2,1,0:T(8,128)(2,1)}, f32[8,8,288]{2,1,0:T(8,128)}, f32[8,8,864]{2,1,0:T(8,128)}, s32[8,16,128]{2,1,0:T(8,128)}) custom-call(s32[1,4]{1,0:T(1,128)} %bucket_ref.1, s32[1,4]{1,0:T(1,128)} %label_ref.1, bf16[288,128]{1,0:T(8,128)(2,1)} %bitcast.15, bf16[288,128]{1,0:T(8,128)(2,1)} %bitcast.16, ...), custom_call_target="tpu_custom_call" | custom-call | tf_op jit(solution)/shard_map/front/pallas_call | solution.py:647
  51.0 0.8 maximum_convert_fusion
  51.8 0.6 reshape.38.bias_ref.bias_rows
  52.4 133.9 %core.1 = (s32[1024,128]{1,0:T(8,128)}, f32[6,4,1152]{2,1,0:T(4,128)}, bf16[4,256,1152]{2,1,0:T(8,128)(2,1)}, bf16[12,1024,128]{2,1,0:T(8,128)(2,1)}, f32[4,4,1,...) custom-call(bf16[4,256,1152]{2,1,0:T(8,128)(2,1)} %get-tuple-element, ...), custom_call_target="tpu_custom_call" | custom-call | tf_op jit(solution)/shard_map/core/pallas_call | solution.py:1251
  186.3 115.3 %rear.1 = (bf16[256,1152]{1,0:T(8,128)(2,1)}, f32[256,1152]{1,0:T(8,128)}, f32[288,128]{1,0:T(8,128)}, f32[288,128]{1,0:T(8,128)}, f32[288,864]{1,0:T(8,128)}, /...) custom-call(bf16[12,1024,128]{2,1,0:T(8,128)(2,1)} %get-tuple-elemen, ...), custom_call_target="tpu_custom_call" | custom-call | tf_op jit(solution)/shard_map/rear/pallas_call | solution.py:1675
  301.6 0.0 copy-start.6
  301.6 0.0 copy-start.5
  301.7 0.0 copy-start
  301.7 1.5 fusion
  303.2 0.6 constant_dynamic-slice_fusion
  303.8 1.4 slice_reduce_fusion.1
  305.2 0.1 reshape_squeeze.3
  305.3 0.7 pad_maximum_fusion
  306.0 1.9 copy.44
  307.9 0.0 copy-start.3
  307.9 2.4 copy.45
  310.3 0.0 copy-done.6
  310.3 0.0 copy-start.4
  310.3 0.0 copy-start.2
  310.3 0.7 copy.46
  311.0 0.0 copy-done.5
  311.0 0.7 copy.47
  311.7 0.0 copy-done
  311.7 0.0 copy-start.1
  311.7 1.0 copy.48
  312.6 0.0 copy-done.3
  312.6 0.8 copy.49
  313.4 0.0 copy-done.4
  313.4 0.7 copy.50
  314.1 0.0 copy-done.2
  314.1 0.8 copy.51
  314.9 0.0 copy-done.1
  314.9 0.8 copy.52
  (1 shorter events, 0.0 us)
Async XLA Ops:
  301.6 8.7 %copy-start.6 = (f32[288,128]{1,0:T(8,128)S(1)}, f32[288,128]{1,0:T(8,128)}, u32[]{:S(2)}) copy-start(f32[288,128]{1,0:T(8,128)} %get-tuple-element.71) | copy-start | bytes 442372
  301.6 9.3 %copy-start.5 = (f32[288,128]{1,0:T(8,128)S(1)}, f32[288,128]{1,0:T(8,128)}, u32[]{:S(2)}) copy-start(f32[288,128]{1,0:T(8,128)} %get-tuple-element.72) | copy-start | bytes 442372
  301.7 10.0 %copy-start = (f32[288,864]{1,0:T(8,128)S(1)}, f32[288,864]{1,0:T(8,128)}, u32[]{:S(2)}) copy-start(f32[288,864]{1,0:T(8,128)} %get-tuple-element.107) | copy-start | bytes 2985988
  307.9 4.7 %copy-start.3 = (f32[144,864]{1,0:T(8,128)S(1)}, f32[144,864]{1,0:T(8,128)}, u32[]{:S(2)}) copy-start(f32[144,864]{1,0:T(8,128)} %get-tuple-element.109) | copy-start | bytes 1492996
  310.3 3.1 copy-start.4
  310.3 3.8 %copy-start.2 = (f32[144,1152]{1,0:T(8,128)S(1)}, f32[144,1152]{1,0:T(8,128)}, u32[]{:S(2)}) copy-start(f32[144,1152]{1,0:T(8,128)} %get-tuple-element.113) | copy-start | bytes 1990660
  311.7 3.3 %copy-start.1 = (f32[144,1152]{1,0:T(8,128)S(1)}, f32[144,1152]{1,0:T(8,128)}, u32[]{:S(2)}) copy-start(f32[144,1152]{1,0:T(8,128)} %get-tuple-element.115) | copy-start | bytes 1990660

commit v10 on v9

--- a/solution.py
+++ b/solution.py
@@ -737,15 +737,15 @@
             partial.at[:, 1 - self.side, self.part], self.mate_in, sends.at[0], recvs.at[0], mate
         )
         self.straight = []
-        for step in range(1, 4):
-            target = lax.rem(self.level + step, 4)
+        above = lax.rem(self.level + 1, 4) * 2 + self.side
+        for step in range(3):
             self.straight.append(
                 to_row(
-                    self.pair.at[target],
-                    self.straight_in.at[step - 1],
-                    sends.at[step],
-                    recvs.at[step],
-                    target * 2 + self.side,
+                    self.pair.at[lax.rem(self.level + 3 - step, 4)],
+                    self.straight_in.at[step],
+                    sends.at[1 + step],
+                    recvs.at[1 + step],
+                    above,
                 )
             )
 
@@ -763,17 +763,20 @@
             return carry
 
         lax.fori_loop(0, 4, one, 0)
-        for copy in self.straight:
-            copy.start()
+        self.straight[0].start()
+
+    def hop(self, step):
+        self.straight[step].wait_recv()
+        block = lax.rem(self.level + 2 - step, 4)
+        self.pair[block] = (
+            self.pair[block].astype(jnp.float32) + self.straight_in[step].astype(jnp.float32)
+        ).astype(jnp.bfloat16)
+        self.straight[step + 1].start()
 
     def finish(self):
-        for copy in self.straight:
-            copy.wait_recv()
-        self.total[...] = (
-            self.pair[self.level].astype(jnp.float32)
-            + self.straight_in[0].astype(jnp.float32)
-            + self.straight_in[1].astype(jnp.float32)
-            + self.straight_in[2].astype(jnp.float32)
+        self.straight[2].wait_recv()
+        self.total[...] = self.pair[self.level].astype(jnp.float32) + self.straight_in[2].astype(
+            jnp.float32
         )
         self.beside.wait_send()
         for copy in self.straight:
@@ -1221,9 +1224,13 @@
     bias_sums[0:1] = jnp.sum(inner_bias[...], axis=0, keepdims=True)
     bias_sums[1:2] = jnp.sum(ffn_bias[...], axis=0, keepdims=True)
     gather_grad.wait_sibling()
+    reduces[0].hop(0)
+    reduces[0].hop(1)
+    reduces[1].send_pair()
     gather_grad.wait_partner()
     gather_grad.wait_opposite()
-    reduces[1].send_pair()
+    reduces[1].hop(0)
+    reduces[1].hop(1)
     for unit in reduces:
         unit.finish()
     gather_hidden.finish()
@@ -1493,6 +1500,10 @@
         units[block].send_pair()
         if block < 2:
             units[block + 3].start()
+        if block > 0:
+            units[block - 1].hop(0)
+        if block > 1:
+            units[block - 2].hop(1)
 
     def pack(block, carry):
         rows = pl.ds(pl.multiple_of(block * tok_rows, tok_rows), tok_rows)
@@ -1514,6 +1525,8 @@
         return carry
 
     lax.fori_loop(0, blocks, pack, 0)
+    units[3].hop(0)
+    units[2].hop(1)
     direction = sibling - member
 
     def project_back(block):
@@ -1544,6 +1557,7 @@
     bias_copies = spread(1, lambda other: bias_own.at[2], bias_all)
     bias_all[row] = bias_own[2]
     units[4].send_pair()
+    units[3].hop(1)
     slot_sums[...] = jnp.zeros_like(slot_sums)
     reduce_ffn.settle()
 
@@ -1564,6 +1578,7 @@
     lax.fori_loop(0, tok_rows // 128, rows_out, 0)
     units[0].finish()
     units[1].finish()
+    units[4].hop(0)
     units[5].send_pair()
     reduce_rows.settle()
 
@@ -1602,6 +1617,8 @@
         mods_own[unit // 3, :, unit % 3 * fine : (unit % 3 + 1) * fine] = source
     beside = to_head(mods_own, mods_sibling, pair_send.at[0], pair_recv.at[0], sibling)
     beside.start()
+    units[5].hop(0)
+    units[4].hop(1)
     units[6].send_pair()
     beside.wait()
     mods_pair[...] = (mods_own[...] + mods_sibling[...]).astype(jnp.bfloat16)
@@ -1609,6 +1626,7 @@
     across.start()
     units[2].finish()
     units[3].finish()
+    units[5].hop(1)
     settle(bias_copies)
     bias_sum[...] = jnp.sum(bias_all[...], axis=0)
     across.wait()
@@ -1617,6 +1635,7 @@
     ).astype(jnp.bfloat16)
     copies = spread(0, lambda other: mods_low.at[other], mods_cols)
     mods_cols[row] = mods_low[row]
+    units[6].hop(0)
     units[7].send_pair()
     units[4].finish()
     settle(copies)
@@ -1629,12 +1648,15 @@
     copies = spread(2, lambda other: silu_part.at[other], silu_in)
     silu_in[row] = silu_part[row]
     ada_grad[...] = contract_rows((condition * bent).astype(jnp.bfloat16), low)
+    units[7].hop(0)
+    units[6].hop(1)
     ada_bias[...] = jnp.broadcast_to(jnp.sum(cols, axis=0, keepdims=True), ada_bias.shape)
     settle(copies)
     summed = jnp.sum(silu_in[...], axis=0)
     silu_all[row] = summed
     silu_part[row] = summed
     copies = spread(3, lambda other: silu_part.at[row], silu_all)
+    units[7].hop(1)
     units[5].finish()
     units[6].finish()
     units[7].finish()
@@ -1838,8 +1860,9 @@
     bias_rows = model_width // lax.axis_size("rows")
     row_start = lax.axis_index("rows") * bias_rows
     grad_b_fc1 = bias_all[0]
-    grad_b_fc2 = lax.dynamic_slice_in_dim(bias_all[1], row_start, bias_rows)
-    grad_b_out = lax.dynamic_slice_in_dim(bias_all[2], row_start, bias_rows)
+    bias_own = lax.dynamic_slice(bias_all, (1, row_start), (2, bias_rows))
+    grad_b_fc2 = bias_own[0]
+    grad_b_out = bias_own[1]
     bias_terms = bias_all[3, : head_local * 3 * head_size].reshape(head_local, 3, head_size)
     grad_b_qv = jnp.concatenate([bias_terms[:, 0], bias_terms[:, 2]], axis=1)
     return (

time: 316 us -> 316 us (level)
  no operation moved by 1% of the time
where the time goes in v10:
time: 316 us; the launch traced here: 315 us
  Pallas kernels  298 us (94%)
  local copies, waits for them, and re-layouts  14.8 us (5%)
    pallas_call x1, Pallas kernels, core(): pl.pallas_call(core_kernel, out_shape=[shape((seq_len, 128), jnp.int32),...  135 us
    pallas_call x1, Pallas kernels, rear(): pl.pallas_call(rear_kernel, out_shape=[shape((tok_rows, model_width), low...  113 us
    pallas_call x1, Pallas kernels, front(): pl.pallas_call(front_kernel, out_shape=(shape((ROW_PARTS,) + w_qkv.shape,...  50.4 us
    unnamed x23, local copies, waits for them, and re-layouts  9.8 us

profile of v10, /device:TPU:0, one launch (start us, length us, event | category | flops | bytes accessed | tf_op | source)
XLA Modules:
  0.0 315.3 jit_solution(9679548244197846938)
XLA Ops:
  0.6 50.4 %front.1 = (bf16[8,144,864]{2,1,0:T(8,128)(2,1)}, bf16[4,256,1152]{2,1,0:T(8,128)(2,1)}, f32[8,8,288]{2,1,0:T(8,128)}, f32[8,8,864]{2,1,0:T(8,128)}, s32[8,16,128]{2,1,0:T(8,128)}) custom-call(s32[1,4]{1,0:T(1,128)} %bucket_ref.1, s32[1,4]{1,0:T(1,128)} %label_ref.1, bf16[288,128]{1,0:T(8,128)(2,1)} %bitcast.15, bf16[288,128]{1,0:T(8,128)(2,1)} %bitcast.16, ...), custom_call_target="tpu_custom_call" | custom-call | tf_op jit(solution)/shard_map/front/pallas_call | solution.py:647
  51.0 0.8 maximum_convert_fusion
  51.8 0.6 reshape.36.bias_ref.bias_rows
  52.4 134.6 %core.1 = (s32[1024,128]{1,0:T(8,128)}, f32[6,4,1152]{2,1,0:T(4,128)}, bf16[4,256,1152]{2,1,0:T(8,128)(2,1)}, bf16[12,1024,128]{2,1,0:T(8,128)(2,1)}, f32[4,4,1,...) custom-call(bf16[4,256,1152]{2,1,0:T(8,128)(2,1)} %get-tuple-element, ...), custom_call_target="tpu_custom_call" | custom-call | tf_op jit(solution)/shard_map/core/pallas_call | solution.py:1258
  187.0 113.4 %rear.1 = (bf16[256,1152]{1,0:T(8,128)(2,1)}, f32[256,1152]{1,0:T(8,128)}, f32[288,128]{1,0:T(8,128)}, f32[288,128]{1,0:T(8,128)}, f32[288,864]{1,0:T(8,128)}, /...) custom-call(bf16[12,1024,128]{2,1,0:T(8,128)(2,1)} %get-tuple-elemen, ...), custom_call_target="tpu_custom_call" | custom-call | tf_op jit(solution)/shard_map/rear/pallas_call | solution.py:1697
  300.4 0.0 copy-start.6
  300.5 0.0 copy-start.5
  300.5 0.0 copy-start
  300.5 1.5 slice_reduce_fusion.1
  302.0 0.1 reshape_squeeze.3
  302.1 0.7 pad_maximum_fusion
  302.7 1.4 constant_dynamic-slice_fusion
  304.1 1.4 slice_reduce_fusion
  305.5 1.9 copy.44
  307.5 0.0 copy-start.3
  307.5 2.4 copy.45
  309.9 0.0 copy-done.6
  309.9 0.0 copy-start.4
  309.9 0.0 copy-start.2
  309.9 0.7 copy.46
  310.5 0.0 copy-done.5
  310.5 0.7 copy.47
  311.2 0.0 copy-done
  311.2 0.0 copy-start.1
  311.2 1.0 copy.48
  312.2 0.0 copy-done.3
  312.2 0.8 copy.49
  313.0 0.0 copy-done.4
  313.0 0.7 copy.50
  313.6 0.0 copy-done.2
  313.7 0.8 copy.51
  314.5 0.0 copy-done.1
  314.5 0.8 copy.52
  (1 shorter events, 0.0 us)
Async XLA Ops:
  300.4 9.4 %copy-start.6 = (f32[288,128]{1,0:T(8,128)S(1)}, f32[288,128]{1,0:T(8,128)}, u32[]{:S(2)}) copy-start(f32[288,128]{1,0:T(8,128)} %get-tuple-element.71) | copy-start | bytes 442372
  300.5 10.1 %copy-start.5 = (f32[288,128]{1,0:T(8,128)S(1)}, f32[288,128]{1,0:T(8,128)}, u32[]{:S(2)}) copy-start(f32[288,128]{1,0:T(8,128)} %get-tuple-element.72) | copy-start | bytes 442372
  300.5 10.7 %copy-start = (f32[288,864]{1,0:T(8,128)S(1)}, f32[288,864]{1,0:T(8,128)}, u32[]{:S(2)}) copy-start(f32[288,864]{1,0:T(8,128)} %get-tuple-element.104) | copy-start | bytes 2985988
  307.5 4.7 %copy-start.3 = (f32[144,864]{1,0:T(8,128)S(1)}, f32[144,864]{1,0:T(8,128)}, u32[]{:S(2)}) copy-start(f32[144,864]{1,0:T(8,128)} %get-tuple-element.106) | copy-start | bytes 1492996
  309.9 3.1 copy-start.4
  309.9 3.8 %copy-start.2 = (f32[144,1152]{1,0:T(8,128)S(1)}, f32[144,1152]{1,0:T(8,128)}, u32[]{:S(2)}) copy-start(f32[144,1152]{1,0:T(8,128)} %get-tuple-element.110) | copy-start | bytes 1990660
  311.2 3.3 %copy-start.1 = (f32[144,1152]{1,0:T(8,128)S(1)}, f32[144,1152]{1,0:T(8,128)}, u32[]{:S(2)}) copy-start(f32[144,1152]{1,0:T(8,128)} %get-tuple-element.112) | copy-start | bytes 1990660
